TPU v7x, 32 devices: a whole 2x2x4 slice. The times are simulated.
32 devices in a mesh: dp: 16 (over z, y, core), tensor: 2 (over x).
Axes of the slice: x: 2, y: 2, z: 4, core: 2. Of those that a mesh axis runs over, the one named last changes fastest.
Arguments:
- inputs: bfloat16 [12288, 1024], P(('dp', 'tensor')), may hold values from -6 to 6
- out_grad: bfloat16 [12288, 1024], P(('dp', 'tensor')), may hold values from -6 to 6
- parents: int32 [16, 3], P('dp'), may hold values from 0 to 1, as said below
- ln1_gain: bfloat16 [1024], P('dp'), may hold values from 0.5 to 1.5
- ln1_bias: bfloat16 [1024], P('dp'), may hold values from -1.5 to 1.5
- w_qkv: bfloat16 [3, 1024, 1024], P(None, 'dp', 'tensor'), may hold values from -0.25 to 0.25
- qv_bias: bfloat16 [2, 1024], P(None, 'dp'), may hold values from -1.5 to 1.5
- w_attn_out: bfloat16 [1024, 1024], P('tensor', 'dp'), may hold values from -0.75 to 0.75
- attn_out_bias: bfloat16 [1024], P('dp'), may hold values from -1.5 to 1.5
- ln2_gain: bfloat16 [1024], P('dp'), may hold values from 0.5 to 1.5
- ln2_bias: bfloat16 [1024], P('dp'), may hold values from -1.5 to 1.5
- w_up: bfloat16 [1024, 4096], P('dp', 'tensor'), may hold values from -0.1875 to 0.1875
- up_bias: bfloat16 [4096], P('dp'), may hold values from -1.5 to 1.5
- w_down: bfloat16 [4096, 1024], P('tensor', 'dp'), may hold values from -0.09375 to 0.09375
- down_bias: bfloat16 [1024], P('dp'), may hold values from -1.5 to 1.5
Outputs:
- out: bfloat16 [12288, 1024], P(('dp', 'tensor'))
- in_grad: float32 [12288, 1024], P(('dp', 'tensor'))
- grad_ln1_gain: float32 [1024], P('dp')
- grad_ln1_bias: float32 [1024], P('dp')
- grad_w_qkv: float32 [3, 1024, 1024], P(None, 'dp', 'tensor')
- grad_qv_bias: float32 [2, 1024], P(None, 'dp')
- grad_w_attn_out: float32 [1024, 1024], P('tensor', 'dp')
- grad_attn_out_bias: float32 [1024], P('dp')
- grad_ln2_gain: float32 [1024], P('dp')
- grad_ln2_bias: float32 [1024], P('dp')
- grad_w_up: float32 [1024, 4096], P('dp', 'tensor')
- grad_up_bias: float32 [4096], P('dp')
- grad_w_down: float32 [4096, 1024], P('tensor', 'dp')
- grad_down_bias: float32 [1024], P('dp')
Inputs may be any that keep to these rules, and one draw needn't show every extreme that they name: With B = max(1, 0) and L = min(2 B, 2 - B), every tree has the same shape: segments 0 to 3 - B - L - 1 form a trunk in which each segment's parent is the one before it (parents[t, 0] = 0); the next B segments are branches whose parent is the last trunk segment; the last L segments are leaves, two a branch, whose parent is a branch. Which branch holds which pair of leaves varies from tree to tree.
All inputs are finite; a program needn't handle non-finite values.
Results may differ from a plain program's by a relative error of at most 0.014.
Values may be sent and summed in bfloat16 or wider, within the bound.
No kernel may reach another device: no remote copies, remote signals or barrier semaphores. Data moves between devices by JAX's collectives and lax.ppermute only.
A program may use at most 128 MiB of HBM per device.

v0:
```python
import math

import jax
import jax.numpy as jnp
from jax import lax
from jax.sharding import PartitionSpec as P

HEADS = 16
SEG = 256


epsilon = 1e-05
gelu_coef = 0.7978845608028654


def layer_norm(values, scales, shifts):
    centre = jnp.mean(values, axis=-1, keepdims=True)
    shifted = values - centre
    spread = jnp.mean(shifted * shifted, axis=-1, keepdims=True)
    return shifted * lax.rsqrt(spread + epsilon) * scales + shifts


def gelu_tanh(values):
    return (
        0.5 * values * (1.0 + jnp.tanh(gelu_coef * (values + 0.044715 * values * values * values)))
    )


def matmul(left, right):
    return jnp.dot(left, right, preferred_element_type=jnp.float32)


def contract_rows(left, right):
    return lax.dot_general(
        left, right, (((0,), (0,)), ((), ())), preferred_element_type=jnp.float32
    )


def contract_last(left, right):
    return lax.dot_general(
        left, right, (((1,), (1,)), ((), ())), preferred_element_type=jnp.float32
    )


def ancestors(parent_row, segment_count):
    labels = jnp.arange(segment_count, dtype=jnp.int32)
    links = ((parent_row[:, None] == labels[None, :]) & (labels[:, None] > 0)).astype(jnp.float32)
    identity = jnp.eye(segment_count, dtype=jnp.float32)

    def extend(turn, reached):
        grown = jnp.dot(
            links, reached, precision=lax.Precision.HIGHEST, preferred_element_type=jnp.float32
        )
        return jnp.minimum(identity + grown, 1.0)

    return lax.fori_loop(0, segment_count, extend, identity)


def tree_mask(reached, first_row, block_rows, length):
    query_pos = first_row + jnp.arange(block_rows, dtype=jnp.int32)
    key_pos = jnp.arange(length, dtype=jnp.int32)
    segment_count = reached.shape[0]
    onehot = (
        (query_pos // SEG)[:, None] == jnp.arange(segment_count, dtype=jnp.int32)[None, :]
    ).astype(jnp.float32)
    row_reach = jnp.dot(
        onehot, reached, precision=lax.Precision.HIGHEST, preferred_element_type=jnp.float32
    )
    spread_out = jnp.repeat(row_reach, SEG, axis=1)
    return (spread_out > 0.5) & (key_pos[None, :] <= query_pos[:, None])


def row_block(length):
    pieces = -(-length // 512)
    while length % pieces:
        pieces += 1
    return length // pieces


def place_block(local_vec, full_length, offset):
    empty_vec = jnp.zeros(local_vec.shape[:-1] + (full_length,), jnp.float32)
    return lax.dynamic_update_slice_in_dim(empty_vec, local_vec, offset, local_vec.ndim - 1)


def local(
    inputs,
    out_grad,
    parents,
    ln1_gain,
    ln1_bias,
    w_qkv,
    qv_bias,
    w_attn_out,
    attn_out_bias,
    ln2_gain,
    ln2_bias,
    w_up,
    up_bias,
    w_down,
    down_bias,
):
    tensor_ranks = lax.axis_size("tensor")
    tensor_rank = lax.axis_index("tensor")
    rows_own = inputs.shape[0]
    length = rows_own * tensor_ranks
    model_width = inputs.shape[1]
    head_dim = model_width // HEADS
    local_width = w_qkv.shape[2]
    local_hidden = w_up.shape[1]
    heads_here = local_width // head_dim
    scale = 1.0 / math.sqrt(head_dim)
    gathered = (
        lax.all_gather(w_qkv, "dp", axis=1, tiled=True),
        lax.all_gather(w_attn_out, "dp", axis=1, tiled=True),
        lax.all_gather(w_up, "dp", axis=0, tiled=True),
        lax.all_gather(w_down, "dp", axis=1, tiled=True),
        lax.all_gather(ln1_gain, "dp", axis=0, tiled=True),
        lax.all_gather(ln1_bias, "dp", axis=0, tiled=True),
        lax.all_gather(qv_bias, "dp", axis=1, tiled=True),
        lax.all_gather(attn_out_bias, "dp", axis=0, tiled=True),
        lax.all_gather(ln2_gain, "dp", axis=0, tiled=True),
        lax.all_gather(ln2_bias, "dp", axis=0, tiled=True),
        lax.all_gather(up_bias, "dp", axis=0, tiled=True),
        lax.all_gather(down_bias, "dp", axis=0, tiled=True),
    )
    proj_full, out_full, hidden_full, back_full = (
        gathered[0],
        gathered[1],
        gathered[2],
        gathered[3],
    )
    gain_one = gathered[4].astype(jnp.float32)
    shift_one = gathered[5].astype(jnp.float32)
    proj_bias = lax.dynamic_slice_in_dim(
        gathered[6].astype(jnp.float32), tensor_rank * local_width, local_width, 1
    )
    out_bias = gathered[7].astype(jnp.float32)
    gain_two = gathered[8].astype(jnp.float32)
    shift_two = gathered[9].astype(jnp.float32)
    hidden_bias_full = gathered[10].astype(jnp.float32)
    back_bias = gathered[11].astype(jnp.float32)
    full_hidden = hidden_bias_full.shape[0]
    hidden_in = inputs.astype(jnp.float32)
    norm_one, ln1_pull = jax.vjp(layer_norm, hidden_in, gain_one, shift_one)
    norm_one_all = lax.all_gather(norm_one.astype(jnp.bfloat16), "tensor", axis=0, tiled=True)
    queries = (matmul(norm_one_all, proj_full[0]) + proj_bias[0]).astype(jnp.bfloat16)
    keys_low = matmul(norm_one_all, proj_full[1]).astype(jnp.bfloat16)
    values_low = (matmul(norm_one_all, proj_full[2]) + proj_bias[1]).astype(jnp.bfloat16)
    reached = ancestors(parents[0], length // SEG)
    block_rows = row_block(length)
    num_blocks = length // block_rows
    starts = jnp.arange(num_blocks, dtype=jnp.int32) * block_rows
    query_blocks = queries.reshape(num_blocks, block_rows, heads_here, head_dim)
    key_heads = keys_low.reshape(length, heads_here, head_dim)
    value_heads = values_low.reshape(length, heads_here, head_dim)

    def block_scores(query_block, first_row):
        scores = (
            jnp.einsum("qhd,khd->hqk", query_block, key_heads, preferred_element_type=jnp.float32)
            * scale
        )
        allowed = tree_mask(reached, first_row, block_rows, length)
        return jnp.where(allowed[None], scores, -1e30)

    def forward_block(element):
        query_block, first_row = element
        scores = block_scores(query_block, first_row)
        top_score = jnp.max(scores, axis=-1, keepdims=True)
        expo = jnp.exp(scores - top_score)
        totals = jnp.sum(expo, axis=-1, keepdims=True)
        probs = (expo / totals).astype(jnp.bfloat16)
        attended_block = jnp.einsum(
            "hqk,khd->qhd", probs, value_heads, preferred_element_type=jnp.float32
        )
        return (attended_block, (top_score + jnp.log(totals))[..., 0])

    attended_blocks, log_totals = lax.map(forward_block, (query_blocks, starts))
    attended = attended_blocks.reshape(length, local_width).astype(jnp.bfloat16)
    branch = (
        lax.psum_scatter(matmul(attended, out_full), "tensor", scatter_dimension=0, tiled=True)
        + out_bias
    )
    resid = hidden_in + branch
    norm_two, ln2_pull = jax.vjp(layer_norm, resid, gain_two, shift_two)
    norm_two_low = norm_two.astype(jnp.bfloat16)
    grad_back_bias = jnp.sum(out_grad.astype(jnp.float32), axis=0)
    norm_two_all = lax.all_gather(norm_two_low, "tensor", axis=0, tiled=True)
    hidden_slice = lax.dynamic_slice_in_dim(
        hidden_bias_full, tensor_rank * local_hidden, local_hidden, 0
    )
    pre = matmul(norm_two_all, hidden_full) + hidden_slice
    act, gelu_pull = jax.vjp(gelu_tanh, pre)
    act_low = act.astype(jnp.bfloat16)
    mixed = (
        lax.psum_scatter(
            matmul(act_low, back_full).astype(jnp.bfloat16),
            "tensor",
            scatter_dimension=0,
            tiled=True,
        ).astype(jnp.float32)
        + back_bias
    )
    cotangent_all = lax.all_gather(out_grad, "tensor", axis=0, tiled=True)
    grad_back = contract_rows(act_low, cotangent_all)
    (dpre,) = gelu_pull(contract_last(cotangent_all, back_full))
    dpre_low = dpre.astype(jnp.bfloat16)
    grad_hidden = contract_rows(norm_two_all, dpre_low)
    grad_hidden_bias = place_block(
        jnp.sum(dpre_low.astype(jnp.float32), axis=0), full_hidden, tensor_rank * local_hidden
    )
    dnorm_two = lax.psum_scatter(
        contract_last(dpre_low, hidden_full), "tensor", scatter_dimension=0, tiled=True
    )
    result = (resid + mixed).astype(jnp.bfloat16)
    dresid_part, grad_gain_two, grad_shift_two = ln2_pull(dnorm_two)
    dresid = out_grad.astype(jnp.float32) + dresid_part
    dbranch = dresid.astype(jnp.bfloat16)
    grad_out_bias = jnp.sum(dbranch.astype(jnp.float32), axis=0)
    dbranch_all = lax.all_gather(dbranch, "tensor", axis=0, tiled=True)
    grad_out = contract_rows(attended, dbranch_all)
    dattended = contract_last(dbranch_all, out_full).astype(jnp.bfloat16)
    dattended_blocks = dattended.reshape(num_blocks, block_rows, heads_here, head_dim)

    def backward_block(carry, element):
        dkey_acc, dvalue_acc = carry
        query_block, dattended_block, log_block, first_row = element
        scores = block_scores(query_block, first_row)
        probs = jnp.exp(scores - log_block[..., None])
        dvalue_acc = dvalue_acc + jnp.einsum(
            "hqk,qhd->khd",
            probs.astype(jnp.bfloat16),
            dattended_block,
            preferred_element_type=jnp.float32,
        )
        dprobs = jnp.einsum(
            "qhd,khd->hqk", dattended_block, value_heads, preferred_element_type=jnp.float32
        )
        dscores = probs * (dprobs - jnp.sum(dprobs * probs, axis=-1, keepdims=True))
        dscores_low = dscores.astype(jnp.bfloat16)
        dquery_block = (
            jnp.einsum("hqk,khd->qhd", dscores_low, key_heads, preferred_element_type=jnp.float32)
            * scale
        )
        dkey_acc = (
            dkey_acc
            + jnp.einsum(
                "hqk,qhd->khd", dscores_low, query_block, preferred_element_type=jnp.float32
            )
            * scale
        )
        return ((dkey_acc, dvalue_acc), dquery_block)

    zero_heads = jnp.zeros((length, heads_here, head_dim), jnp.float32)
    (dkey_acc, dvalue_acc), dquery_blocks = lax.scan(
        backward_block,
        (zero_heads, zero_heads),
        (query_blocks, dattended_blocks, log_totals, starts),
    )
    dqueries = dquery_blocks.reshape(length, local_width).astype(jnp.bfloat16)
    dkeys = dkey_acc.reshape(length, local_width).astype(jnp.bfloat16)
    dvalues = dvalue_acc.reshape(length, local_width).astype(jnp.bfloat16)
    grad_proj = jnp.stack(
        [
            contract_rows(norm_one_all, dqueries),
            contract_rows(norm_one_all, dkeys),
            contract_rows(norm_one_all, dvalues),
        ]
    )
    local_bias_grad = jnp.stack(
        [
            jnp.sum(dqueries.astype(jnp.float32), axis=0),
            jnp.sum(dvalues.astype(jnp.float32), axis=0),
        ]
    )
    grad_proj_bias = place_block(local_bias_grad, model_width, tensor_rank * local_width)
    dnorm_one = lax.psum_scatter(
        (
            contract_last(dqueries, proj_full[0])
            + contract_last(dkeys, proj_full[1])
            + contract_last(dvalues, proj_full[2])
        ).astype(jnp.bfloat16),
        "tensor",
        scatter_dimension=0,
        tiled=True,
    ).astype(jnp.float32)
    dinput_part, grad_gain_one, grad_shift_one = ln1_pull(dnorm_one)
    input_grad = dresid + dinput_part
    summed = (
        lax.psum_scatter(grad_proj, "dp", scatter_dimension=1, tiled=True),
        lax.psum_scatter(grad_out, "dp", scatter_dimension=1, tiled=True),
        lax.psum_scatter(grad_hidden, "dp", scatter_dimension=0, tiled=True),
        lax.psum_scatter(grad_back, "dp", scatter_dimension=1, tiled=True),
        lax.psum_scatter(grad_gain_one, "dp", scatter_dimension=0, tiled=True),
        lax.psum_scatter(grad_shift_one, "dp", scatter_dimension=0, tiled=True),
        lax.psum_scatter(grad_proj_bias, "dp", scatter_dimension=1, tiled=True),
        lax.psum_scatter(grad_out_bias, "dp", scatter_dimension=0, tiled=True),
        lax.psum_scatter(grad_gain_two, "dp", scatter_dimension=0, tiled=True),
        lax.psum_scatter(grad_shift_two, "dp", scatter_dimension=0, tiled=True),
        lax.psum_scatter(grad_hidden_bias, "dp", scatter_dimension=0, tiled=True),
        lax.psum_scatter(grad_back_bias, "dp", scatter_dimension=0, tiled=True),
    )
    vectors = lax.psum(
        (summed[4], summed[5], summed[6], summed[7], summed[8], summed[9], summed[10], summed[11]),
        "tensor",
    )
    return (
        result,
        input_grad,
        vectors[0],
        vectors[1],
        summed[0],
        vectors[2],
        summed[1],
        vectors[3],
        vectors[4],
        vectors[5],
        summed[2],
        vectors[6],
        summed[3],
        vectors[7],
    )


def solution(mesh):
    return jax.shard_map(
        local,
        mesh=mesh,
        in_specs=(
            P(("dp", "tensor"), None),
            P(("dp", "tensor"), None),
            P("dp", None),
            P("dp"),
            P("dp"),
            P(None, "dp", "tensor"),
            P(None, "dp"),
            P("tensor", "dp"),
            P("dp"),
            P("dp"),
            P("dp"),
            P("dp", "tensor"),
            P("dp"),
            P("tensor", "dp"),
            P("dp"),
        ),
        out_specs=(
            P(("dp", "tensor"), None),
            P(("dp", "tensor"), None),
            P("dp"),
            P("dp"),
            P(None, "dp", "tensor"),
            P(None, "dp"),
            P("tensor", "dp"),
            P("dp"),
            P("dp"),
            P("dp"),
            P("dp", "tensor"),
            P("dp"),
            P("tensor", "dp"),
            P("dp"),
        ),
        check_vma=False,
    )
```

profile of v0, /device:TPU:8, one launch (start us, length us, event | category | flops | bytes accessed | tf_op | source)
XLA Modules:
  0.0 1043.3 jit_solution(15335476766088514634)
XLA Ops:
  17.7 53.5 %all-reduce.15 = (bf16[1024]{0:T(1024)(128)(2,1)S(1)}, bf16[1024]{0:T(1024)(128)(2,1)S(1)}, bf16[1024]{0:T(1024)(128)(2,1)S(1)}, bf16[1024]{0:T(1024)(128)(2,1)S...) all-reduce(bf16[1024]{0:T(1024)(128)(2,1)S(1)} %dynamic-update-slic, ...), channel_id=1, replica_groups=mesh['dp'=16,'tensor'=2] {'dp'}, use_global_device_ids=true, to_apply=%add.1 | all-reduce | flops 6144 | bytes 24576
  76.4 22.4 %all-gather = bf16[16,64,2]{1,2,0:T(2,128)(2,1)S(1)} all-gather(bf16[1,64,2]{1,2,0:T(2,128)(2,1)S(1)} %bitcast.195), channel_id=1, replica_groups=mesh['dp'=16,'tensor'=2] {'dp'}, dimensions={0}, use_global_device_ids=true | all-gather | bytes 4352 | tf_op jit(solution)/shard_map/all_gather | solution.py:119
  98.9 7.9 all-gather.11.cloned.1.call-done
  106.9 47.8 %all-gather.13.cloned.1.call-done = bf16[3,1024,512]{2,1,0:T(8,128)(2,1)} async-done(((bf16[3,64,512]{2,1,0:T(8,128)(2,1)}), bf16[3,1024,512]{2,1,0:T(8,128)(2,1)}) %all-gather.13.cloned.1.call-update) | async-done | bytes 3145744 | tf_op jit(solution)/shard_map/all_gather | solution.py:113
  165.4 22.4 %while.42 = (s32[]{:T(128)}, bf16[2,384,8,64]{1,3,2,0:T(8,128)(2,1)}, f32[2,8,384]{2,1,0:T(8,128)S(1)}, s32[2]{0:T(128)S(1)}, f32[3,3]{1,0:T(4,128)S(1)}, /*inde...) while((s32[]{:T(128)}, ...), condition=%wide.region_7.8_spmd, body=%wide.region_4.7_spmd.sunk | while | flops 632928000 | bytes 39231964 | solution.py:177
  192.3 4.0 fusion.86
  197.0 42.7 %reduce-scatter.12.cloned.1.call-done = f32[384,1024]{1,0:T(8,128)} async-done(((f32[768,1024]{1,0:T(8,128)}), f32[384,1024]{1,0:T(8,128)}) %reduce-scatter.12.cloned.1.call-update) | async-done | bytes 1572880 | tf_op jit(solution)/shard_map/reduce_scatter | solution.py:180
  244.7 19.1 %all-gather.1 = bf16[16,1,256]{2,1,0:T(2,128)(2,1)S(1)} all-gather(bf16[1,1,256]{2,1,0:T(2,128)(2,1)S(1)} %reshape.290), channel_id=1, replica_groups=mesh['dp'=16,'tensor'=2] {'dp'}, dimensions={0}, use_global_device_ids=true | all-gather | bytes 8704 | tf_op jit(solution)/shard_map/all_gather | solution.py:123
  263.9 28.7 %all-gather.19.cloned.1.call-done = bf16[1024,2048]{1,0:T(8,128)(2,1)} async-done(((bf16[64,2048]{1,0:T(8,128)(2,1)}), bf16[1024,2048]{1,0:T(8,128)(2,1)}) %all-gather.19.cloned.1.call-update) | async-done | bytes 4194320 | tf_op jit(solution)/shard_map/all_gather | solution.py:115
  292.5 27.8 %all-gather.17.cloned.1.call-done = bf16[768,1024]{1,0:T(8,128)(2,1)} async-done(((bf16[384,1024]{1,0:T(8,128)(2,1)}), bf16[768,1024]{1,0:T(8,128)(2,1)}) %all-gather.17.cloned.1.call-update) | async-done | bytes 1572880 | tf_op jit(solution)/shard_map/all_gather | solution.py:187
  320.3 8.8 fusion.87
  329.1 20.1 %all-gather.23.cloned.1.call-done = bf16[768,1024]{1,0:T(8,128)(2,1)} async-done(((bf16[384,1024]{1,0:T(8,128)(2,1)}), bf16[768,1024]{1,0:T(8,128)(2,1)}) %all-gather.23.cloned.1.call-update) | async-done | bytes 1572880 | tf_op jit(solution)/shard_map/all_gather | solution.py:203
  349.2 53.0 %all-gather.21.cloned.1.call-done = bf16[2048,1024]{0,1:T(8,128)(2,1)} async-done(((bf16[2048,64]{0,1:T(8,128)(2,1)}), bf16[2048,1024]{0,1:T(8,128)(2,1)}) %all-gather.21.cloned.1.call-update) | async-done | bytes 4194320 | tf_op jit(solution)/shard_map/all_gather | solution.py:116
  402.2 11.9 %convert_reduce_fusion = (f32[2048]{0:T(1024)}, bf16[768,2048]{1,0:T(8,128)(2,1)S(1)}) fusion(f32[768,2048]{1,0:T(8,128)} %fusion.87, f32[2048]{0:T(1024)S(1)} %dynamic_slice.46, bf16[768,1024]{1,0:T(8,128)(2,1)} %all-gather.23.cloned.1.call-done, bf16[2048,1024]{0,1:T(8,128)(2,1)} %all-gather.21.cloned.1.call-done), kind=kOutput, calls=%fused_computation.92 | convolution fusion | flops 3263690752 | bytes 15220736 | tf_op jit(solution)/shard_map/dot_general | solution.py:40
  415.7 5.1 fusion.88
  420.9 9.2 convolution_convert_fusion
  430.2 32.6 %reduce-scatter.16.cloned.1.call-done = f32[384,1024]{1,0:T(8,128)} async-done(((f32[768,1024]{1,0:T(8,128)}), f32[384,1024]{1,0:T(8,128)}) %reduce-scatter.16.cloned.1.call-update) | async-done | bytes 1572880 | tf_op jit(solution)/shard_map/reduce_scatter | solution.py:211
  465.4 26.2 %reduce-scatter.14.cloned.1.call-done = bf16[384,1024]{1,0:T(8,128)(2,1)} async-done(((bf16[768,1024]{1,0:T(8,128)(2,1)}), bf16[384,1024]{1,0:T(8,128)(2,1)}) %reduce-scatter.14.cloned.1.call-update) | async-done | bytes 786448 | tf_op jit(solution)/shard_map/reduce_scatter | solution.py:195
  498.0 27.3 %all-gather.25.cloned.1.call-done = bf16[768,1024]{1,0:T(8,128)(2,1)} async-done(((bf16[384,1024]{1,0:T(8,128)(2,1)}), bf16[768,1024]{1,0:T(8,128)(2,1)}) %all-gather.25.cloned.1.call-update) | async-done | bytes 1572880 | tf_op jit(solution)/shard_map/all_gather | solution.py:219
  535.9 35.8 %while.44 = (s32[]{:T(128)}, f32[768,8,64]{0,2,1:T(8,128)S(1)}, f32[768,8,64]{0,2,1:T(8,128)}, bf16[2,384,8,64]{1,3,2,0:T(8,128)(2,1)}, bf16[2,384,8,64]{1,3,2,0...) while((s32[]{:T(128)}, f32[768,8,64]{0,2,1:T(8,128)S(1)}, ...), condition=%wide.region_17.18_spmd.clone, body=%wide.region_15.17_spmd.clone.sunk | while | flops 1548138240 | bytes 108819080 | solution.py:254
  544.5 3.8 multiply_reduce_fusion.5
  562.4 3.8 multiply_reduce_fusion.5
  586.1 3.8 fusion.89
  589.9 10.2 fusion.79
  600.4 9.1 fusion.90
  619.7 16.3 %reduce-scatter.28.cloned.1.call-done = f32[64,2]{1,0:T(8,128)} async-done(((f32[1024,2]{1,0:T(8,128)}), f32[64,2]{1,0:T(8,128)}) %reduce-scatter.28.cloned.1.call-update) | async-done | bytes 528
  636.9 27.3 %reduce-scatter.18.cloned.1.call-done = bf16[384,1024]{1,0:T(8,128)(2,1)} async-done(((bf16[768,1024]{1,0:T(8,128)(2,1)}), bf16[384,1024]{1,0:T(8,128)(2,1)}) %reduce-scatter.18.cloned.1.call-update) | async-done | bytes 786448 | tf_op jit(solution)/shard_map/reduce_scatter | solution.py:276
  670.0 53.5 %all-reduce.13 = (f32[1024]{0:T(1024)S(1)}, f32[1024]{0:T(1024)S(1)}, f32[1024]{0:T(1024)S(1)}, f32[1024]{0:T(1024)S(1)}, f32[1024]{0:T(1024)S(1)}, /*index=5*/f32[4096]{0:T(1024)S(1)}, f32[1024]{0:T(1024)S(1)}) all-reduce(f32[1024]{0:T(1024)S(1)} %get-tuple-element.412, ...), channel_id=6, replica_groups=mesh['dp'=16,'tensor'=2] {'dp'}, use_global_device_ids=true, to_apply=%region_22.23.clone | all-reduce | flops 10240 | bytes 81920
  724.0 5.5 all-reduce.14
  730.3 108.5 %reduce-scatter.26.cloned.1.call-done = f32[2048,64]{0,1:T(8,128)} async-done(((f32[2048,1024]{0,1:T(8,128)}), f32[2048,64]{0,1:T(8,128)}) %reduce-scatter.26.cloned.1.call-update) | async-done | bytes 524304 | tf_op jit(solution)/shard_map/reduce_scatter | solution.py:292
  838.8 108.9 %reduce-scatter.24.cloned.1.call-done = f32[64,2048]{1,0:T(8,128)} async-done(((f32[1024,2048]{1,0:T(8,128)}), f32[64,2048]{1,0:T(8,128)}) %reduce-scatter.24.cloned.1.call-update) | async-done | bytes 524304 | tf_op jit(solution)/shard_map/reduce_scatter | solution.py:291
  947.7 88.8 %reduce-scatter.20.cloned.1.call-done = f32[3,64,512]{2,1,0:T(8,128)} async-done(((f32[3,1024,512]{2,1,0:T(8,128)}), f32[3,64,512]{2,1,0:T(8,128)}) %reduce-scatter.20.cloned.1.call-update) | async-done | bytes 393232 | tf_op jit(solution)/shard_map/reduce_scatter | solution.py:289
  (272 shorter events, 138.7 us)
Async XLA Ops:
  7.2 68.6 %copy-start.38 = (s32[1,3]{1,0:T(1,128)S(1)}, s32[1,3]{1,0:T(1,128)}, u32[]{:S(2)}) copy-start(s32[1,3]{1,0:T(1,128)} %param.23) | copy-start | bytes 40
  7.2 99.7 %all-gather.11.cloned.1.call-start = ((), (), s32[]{:S(2)}) async-start(), calls=%async_computation.9 | async-start | bytes 2359296 | tf_op jit(solution)/shard_map/all_gather | solution.py:145
  7.2 69.2 %copy-start.34 = (bf16[2,64]{1,0:T(2,128)(2,1)S(1)}, bf16[2,64]{1,0:T(2,128)(2,1)}, u32[]{:S(2)}) copy-start(bf16[2,64]{1,0:T(2,128)(2,1)} %param.27) | copy-start | bytes 772
  8.6 146.1 %copy-start.22 = (f32[384]{0:T(512)}, f32[384]{0:T(512)S(1)}, u32[]{:S(2)}) copy-start(f32[384]{0:T(512)S(1)} %broadcast_multiply_fusion.1) | copy-start | bytes 4612
  10.7 65.1 %copy-start.24 = (f32[384]{0:T(512)}, f32[384]{0:T(512)S(1)}, u32[]{:S(2)}) copy-start(f32[384]{0:T(512)S(1)} %fusion.77) | copy-start | bytes 4612
  74.2 80.5 %all-gather.13.cloned.1.call-start = ((), (), s32[]{:S(2)}) async-start(), calls=%async_computation.10 | async-start | bytes 3342336 | tf_op jit(solution)/shard_map/all_gather | solution.py:113
  74.9 117.4 %all-gather.15.cloned.1.call-start = ((), (), s32[]{:S(2)}) async-start(), calls=%async_computation.11 | async-start | bytes 1114112 | tf_op jit(solution)/shard_map/all_gather | solution.py:114
  75.7 164.0 %reduce-scatter.12.cloned.1.call-start = ((), (), s32[]{:S(2)}) async-start(), calls=%async_computation.12 | async-start | bytes 4718592 | tf_op jit(solution)/shard_map/reduce_scatter | solution.py:180
  187.8 8.4 copy-start.1
  190.2 6.1 copy-start.11
  196.3 96.3 %all-gather.19.cloned.1.call-start = ((), (), s32[]{:S(2)}) async-start(), calls=%async_computation.14 | async-start | bytes 4456448 | tf_op jit(solution)/shard_map/all_gather | solution.py:115
  196.9 123.4 %all-gather.17.cloned.1.call-start = ((), (), s32[]{:S(2)}) async-start(), calls=%async_computation.13 | async-start | bytes 2359296 | tf_op jit(solution)/shard_map/all_gather | solution.py:187
  243.1 106.0 %all-gather.23.cloned.1.call-start = ((), (), s32[]{:S(2)}) async-start(), calls=%async_computation.17 | async-start | bytes 2359296 | tf_op jit(solution)/shard_map/all_gather | solution.py:203
  243.9 158.3 %all-gather.21.cloned.1.call-start = ((), (), s32[]{:S(2)}) async-start(), calls=%async_computation.15 | async-start | bytes 4456448 | tf_op jit(solution)/shard_map/all_gather | solution.py:116
  244.6 218.2 %reduce-scatter.16.cloned.1.call-start = ((), (), s32[]{:S(2)}) async-start(), calls=%async_computation.18 | async-start | bytes 4718592 | tf_op jit(solution)/shard_map/reduce_scatter | solution.py:211
  402.2 13.6 %copy-start.35 = (bf16[1024,2048]{1,0:T(8,128)(2,1)S(1)}, bf16[1024,2048]{1,0:T(8,128)(2,1)}, u32[]{:S(2)}) copy-start(bf16[1024,2048]{1,0:T(8,128)(2,1)} %all-gather.19.cloned.1.call-done) | copy-start | bytes 12582916
  420.9 70.8 %reduce-scatter.14.cloned.1.call-start = ((), (), s32[]{:S(2)}) async-start(), calls=%async_computation.16 | async-start | bytes 2359296 | tf_op jit(solution)/shard_map/reduce_scatter | solution.py:195
  430.2 95.1 %all-gather.25.cloned.1.call-start = ((), (), s32[]{:S(2)}) async-start(), calls=%async_computation.19 | async-start | bytes 2359296 | tf_op jit(solution)/shard_map/all_gather | solution.py:219
  497.9 138.1 %reduce-scatter.28.cloned.1.call-start = ((), (), s32[]{:S(2)}) async-start(), calls=%async_computation.25 | async-start | bytes 557056
  580.2 83.9 %reduce-scatter.18.cloned.1.call-start = ((), (), s32[]{:S(2)}) async-start(), calls=%async_computation.20 | async-start | bytes 2359296 | tf_op jit(solution)/shard_map/reduce_scatter | solution.py:276
  586.0 144.3 %reduce-scatter.22.cloned.1.call-start = ((), (), s32[]{:S(2)}) async-start(), calls=%async_computation.22 | async-start | bytes 2228224 | tf_op jit(solution)/shard_map/reduce_scatter | solution.py:290
  589.9 249.0 %reduce-scatter.26.cloned.1.call-start = ((), (), s32[]{:S(2)}) async-start(), calls=%async_computation.24 | async-start | bytes 8912896 | tf_op jit(solution)/shard_map/reduce_scatter | solution.py:292
  600.1 347.6 %reduce-scatter.24.cloned.1.call-start = ((), (), s32[]{:S(2)}) async-start(), calls=%async_computation.23 | async-start | bytes 8912896 | tf_op jit(solution)/shard_map/reduce_scatter | solution.py:291
  609.5 426.9 %reduce-scatter.20.cloned.1.call-start = ((), (), s32[]{:S(2)}) async-start(), calls=%async_computation.21 | async-start | bytes 6684672 | tf_op jit(solution)/shard_map/reduce_scatter | solution.py:289
  617.7 46.4 %copy-start = (bf16[384,1024]{1,0:T(8,128)(2,1)S(1)}, bf16[384,1024]{1,0:T(8,128)(2,1)}, u32[]{:S(2)}) copy-start(bf16[384,1024]{1,0:T(8,128)(2,1)} %param.21) | copy-start | bytes 2359300
  617.7 46.4 %copy-start.21 = (f32[1024]{0:T(1024)S(1)}, f32[1024]{0:T(1024)}, u32[]{:S(2)}) copy-start(f32[1024]{0:T(1024)} %copy-done.20) | copy-start | bytes 12292
  617.7 46.4 %copy-start.23 = (f32[384]{0:T(512)S(1)}, f32[384]{0:T(512)}, u32[]{:S(2)}) copy-start(f32[384]{0:T(512)} %copy-done.22) | copy-start | bytes 4612
  617.7 48.2 %copy-start.29 = (f32[384]{0:T(512)S(1)}, f32[384]{0:T(512)}, u32[]{:S(2)}) copy-start(f32[384]{0:T(512)} %copy-done.28) | copy-start | bytes 4612
  617.7 48.2 %copy-start.25 = (f32[384]{0:T(512)S(1)}, f32[384]{0:T(512)}, u32[]{:S(2)}) copy-start(f32[384]{0:T(512)} %copy-done.24) | copy-start | bytes 4612
  617.8 50.2 %copy-start.4 = (f32[384,1024]{1,0:T(8,128)S(1)}, f32[384,1024]{1,0:T(8,128)}, u32[]{:S(2)}) copy-start(f32[384,1024]{1,0:T(8,128)} %copy-done.3) | copy-start | bytes 4718596
  617.8 50.2 %copy-start.7 = (bf16[384,1024]{1,0:T(8,128)(2,1)S(1)}, bf16[384,1024]{1,0:T(8,128)(2,1)}, u32[]{:S(2)}) copy-start(bf16[384,1024]{1,0:T(8,128)(2,1)} %param.22) | copy-start | bytes 2359300
  617.8 50.2 %copy-start.27 = (f32[384]{0:T(512)S(1)}, f32[384]{0:T(512)}, u32[]{:S(2)}) copy-start(f32[384]{0:T(512)} %copy-done.26) | copy-start | bytes 4612
  (34 other events, 75.5 us)
Sparse Core Ops, SparseCore 0:
  74.3 32.5 all-gather.10
  109.1 45.6 all-gather.12
  156.9 35.3 all-gather.14
  196.4 43.2 reduce-scatter.11
  241.9 50.5 all-gather.18
  294.6 25.6 all-gather.16
  321.9 27.1 all-gather.22
  351.6 50.5 all-gather.20
  421.0 41.8 reduce-scatter.15
  465.5 26.0 reduce-scatter.13
  498.0 27.2 all-gather.24
  580.4 55.6 reduce-scatter.27
  638.9 25.2 reduce-scatter.17
  668.8 61.4 reduce-scatter.21
  734.8 104.0 reduce-scatter.25
  843.3 104.3 reduce-scatter.23
  952.1 84.3 reduce-scatter.19
where the time goes:
time: 1050 us; the launch traced here: 1040 us
  waiting for transfers between devices  670 us (64%)
  blocking collectives  154 us (15%)
  matrix products  118 us (11%)
  other arithmetic  43.5 us (4%)
  local copies, waits for them, and re-layouts  38.4 us (4%)
  between operations  17 us (2%)
    reduce_scatter x1, waiting for transfers between devices, local(): lax.psum_scatter(grad_hidden, 'dp', scatter_dimension=0, tiled=True)  109 us
    reduce_scatter x1, waiting for transfers between devices, local(): lax.psum_scatter(grad_back, 'dp', scatter_dimension=1, tiled=True)  109 us
    unnamed x2, blocking collectives  107 us
    reduce_scatter x1, waiting for transfers between devices, local(): lax.psum_scatter(grad_proj, 'dp', scatter_dimension=1, tiled=True)  88.8 us
    all_gather x1, waiting for transfers between devices, local(): lax.all_gather(w_down, 'dp', axis=1, tiled=True)  53 us
    all_gather x1, waiting for transfers between devices, local(): lax.all_gather(w_qkv, 'dp', axis=1, tiled=True)  47.8 us
    reduce_scatter x1, waiting for transfers between devices, local(): lax.psum_scatter(matmul(attended, out_full), 'tensor', scatter_dimension=...  42.7 us
    reduce_scatter x1, waiting for transfers between devices, local(): lax.psum_scatter(contract_last(dpre_low, hidden_full), 'tensor', scatter_...  32.6 us
  transfers between devices with their start and end apart: 17, of which 17 were waited for; matrix products, arithmetic and copies ran while one was open for 10% of the time, Pallas kernels for 0%

commit v1 on v0

--- a/solution.py
+++ b/solution.py
@@ -1,8 +1,11 @@
+import functools
 import math
 
 import jax
 import jax.numpy as jnp
 from jax import lax
+from jax.experimental import pallas as pl
+from jax.experimental.pallas import tpu as pltpu
 from jax.sharding import PartitionSpec as P
 
 HEADS = 16
@@ -82,7 +85,7 @@
     return lax.dynamic_update_slice_in_dim(empty_vec, local_vec, offset, local_vec.ndim - 1)
 
 
-def local(
+def generic(
     inputs,
     out_grad,
     parents,
@@ -321,6 +324,368 @@
     )
 
 
+def attend_kernel(qkv_ref, out_ref, log_ref, *, scale):
+    length = qkv_ref.shape[0]
+    lane = lax.broadcasted_iota(jnp.int32, (SEG, 128), 1)
+    key = qkv_ref[:, 128:256]
+    value_t = jnp.transpose(qkv_ref[:, 256:384])
+    for seg in range(length // SEG):
+        keys_here = (seg + 1) * SEG
+        query = qkv_ref[seg * SEG : keys_here, 0:128] * scale
+        key_pos = lax.broadcasted_iota(jnp.int32, (keys_here, SEG), 0)
+        query_pos = lax.broadcasted_iota(jnp.int32, (keys_here, SEG), 1) + seg * SEG
+        parts = []
+        for head in range(2):
+            mine = jnp.where(lane // 64 == head, query, jnp.zeros_like(query))
+            scores = contract_last(key[:keys_here], mine)
+            scores = jnp.where(key_pos <= query_pos, scores, -1e30)
+            top = jnp.max(scores, axis=0, keepdims=True)
+            expo = jnp.exp(scores - top)
+            total = jnp.sum(expo, axis=0, keepdims=True)
+            mixed = matmul(
+                value_t[head * 64 : head * 64 + 64, :keys_here], expo.astype(jnp.bfloat16)
+            )
+            parts.append(mixed / total)
+            log_ref[0, head : head + 1, seg * SEG : keys_here] = top + jnp.log(total)
+        out_ref[seg * SEG : keys_here, :] = jnp.transpose(jnp.concatenate(parts, axis=0)).astype(
+            jnp.bfloat16
+        )
+
+
+def attend(qkv, scale):
+    length, width = qkv.shape
+    pairs = width // 384
+    return pl.pallas_call(
+        functools.partial(attend_kernel, scale=scale),
+        grid=(pairs,),
+        in_specs=[pl.BlockSpec((length, 384), lambda p: (0, p))],
+        out_specs=[
+            pl.BlockSpec((length, 128), lambda p: (0, p)),
+            pl.BlockSpec((1, 8, length), lambda p: (p, 0, 0)),
+        ],
+        out_shape=[
+            jax.ShapeDtypeStruct((length, pairs * 128), jnp.bfloat16),
+            jax.ShapeDtypeStruct((pairs, 8, length), jnp.float32),
+        ],
+        compiler_params=pltpu.CompilerParams(vmem_limit_bytes=48 * 2**20),
+        name="attend",
+    )(qkv)
+
+
+def attend_back_kernel(qkv_ref, grad_ref, log_ref, out_ref, dkey_ref, dvalue_ref, *, scale):
+    length = qkv_ref.shape[0]
+    lane = lax.broadcasted_iota(jnp.int32, (SEG, 128), 1)
+    key = qkv_ref[:, 128:256]
+    value = qkv_ref[:, 256:384]
+    key_t = jnp.transpose(key)
+    dkey_ref[...] = jnp.zeros_like(dkey_ref)
+    dvalue_ref[...] = jnp.zeros_like(dvalue_ref)
+    for seg in range(length // SEG):
+        keys_here = (seg + 1) * SEG
+        rows = slice(seg * SEG, keys_here)
+        query = qkv_ref[rows, 0:128] * scale
+        grad = grad_ref[rows, :]
+        key_pos = lax.broadcasted_iota(jnp.int32, (keys_here, SEG), 0)
+        query_pos = lax.broadcasted_iota(jnp.int32, (keys_here, SEG), 1) + seg * SEG
+        parts = []
+        dkey = jnp.zeros((keys_here, 128), jnp.float32)
+        dvalue = jnp.zeros((keys_here, 128), jnp.float32)
+        for head in range(2):
+            here = lane // 64 == head
+            query_mine = jnp.where(here, query, jnp.zeros_like(query))
+            grad_mine = jnp.where(here, grad, jnp.zeros_like(grad))
+            scores = contract_last(key[:keys_here], query_mine)
+            scores = jnp.where(key_pos <= query_pos, scores, -1e30)
+            probs = jnp.exp(scores - log_ref[0, head : head + 1, rows])
+            dprobs = contract_last(value[:keys_here], grad_mine)
+            mean = jnp.sum(probs * dprobs, axis=0, keepdims=True)
+            dscores = (probs * (dprobs - mean)).astype(jnp.bfloat16)
+            dvalue = dvalue + matmul(probs.astype(jnp.bfloat16), grad_mine)
+            dkey = dkey + matmul(dscores, query_mine)
+            parts.append(matmul(key_t[head * 64 : head * 64 + 64, :keys_here], dscores) * scale)
+        dkey_ref[:keys_here, :] += dkey
+        dvalue_ref[:keys_here, :] += dvalue
+        out_ref[rows, 0:128] = jnp.transpose(jnp.concatenate(parts, axis=0)).astype(jnp.bfloat16)
+    out_ref[:, 128:256] = dkey_ref[...].astype(jnp.bfloat16)
+    out_ref[:, 256:384] = dvalue_ref[...].astype(jnp.bfloat16)
+
+
+def attend_back(qkv, grad, logs, scale):
+    length, width = qkv.shape
+    pairs = width // 384
+    return pl.pallas_call(
+        functools.partial(attend_back_kernel, scale=scale),
+        grid=(pairs,),
+        in_specs=[
+            pl.BlockSpec((length, 384), lambda p: (0, p)),
+            pl.BlockSpec((length, 128), lambda p: (0, p)),
+            pl.BlockSpec((1, 8, length), lambda p: (p, 0, 0)),
+        ],
+        out_specs=pl.BlockSpec((length, 384), lambda p: (0, p)),
+        out_shape=jax.ShapeDtypeStruct((length, width), jnp.bfloat16),
+        scratch_shapes=[
+            pltpu.VMEM((length, 128), jnp.float32),
+            pltpu.VMEM((length, 128), jnp.float32),
+        ],
+        compiler_params=pltpu.CompilerParams(vmem_limit_bytes=48 * 2**20),
+        name="attend_back",
+    )(qkv, grad, logs)
+
+
+def dp_shift(value, ranks, dz, dy, dc):
+    far, near = 4, ranks // 8
+
+    def goes(rank):
+        z, y, c = rank // (near * 2), rank // 2 % near, rank % 2
+        return ((z + dz) % far * near + (y + dy) % near) * 2 + (c + dc) % 2
+
+    return lax.ppermute(value, "dp", [(rank, goes(rank)) for rank in range(ranks)])
+
+
+def dp_gather(shard, ranks):
+    near = ranks // 8
+    pieces = [shard] + [dp_shift(shard, ranks, k, 0, 0) for k in (1, 2, 3)]
+    for step in range(1, near):
+        pieces = pieces + [dp_shift(piece, ranks, 0, step, 0) for piece in pieces[:4]]
+    half = jnp.concatenate(pieces, axis=0)
+    return jnp.concatenate([half, dp_shift(half, ranks, 0, 0, 1)], axis=0)
+
+
+def dp_reduce(grads, ranks, wire):
+    near = ranks // 8
+    half = grads.shape[0] // 2
+    other = dp_shift(grads[half:].astype(wire), ranks, 0, 0, 1)
+    mine = grads[:half].astype(jnp.float32) + other.astype(jnp.float32)
+    part = half // near
+    total = mine[:part]
+    for step in range(1, near):
+        sent = mine[step * part : (step + 1) * part].astype(wire)
+        total = total + dp_shift(sent, ranks, 0, -step, 0).astype(jnp.float32)
+    rows = part // 4
+    low = total[rows:].astype(wire)
+    result = total[:rows]
+    for k in (1, 2, 3):
+        result = result + dp_shift(low[(k - 1) * rows : k * rows], ranks, -k, 0, 0).astype(
+            jnp.float32
+        )
+    return result
+
+
+def swap(value):
+    return lax.ppermute(value, "tensor", [(0, 1), (1, 0)])
+
+
+def paired(
+    inputs,
+    out_grad,
+    parents,
+    ln1_gain,
+    ln1_bias,
+    w_qkv,
+    qv_bias,
+    w_attn_out,
+    attn_out_bias,
+    ln2_gain,
+    ln2_bias,
+    w_up,
+    up_bias,
+    w_down,
+    down_bias,
+):
+    ranks = lax.axis_size("dp")
+    near = ranks // 8
+    rank = lax.axis_index("dp")
+    side = lax.axis_index("tensor")
+    rows, width = inputs.shape
+    length = 2 * rows
+    shard = width // ranks
+    heads_width = w_qkv.shape[2]
+    pairs = heads_width // 128
+    hidden = w_up.shape[1]
+    head_dim = width // HEADS
+    scale = 1.0 / math.sqrt(head_dim)
+    low = jnp.bfloat16
+
+    slots = jnp.arange(ranks, dtype=jnp.int32)
+    core_step, near_step, far_step = slots // (ranks // 2), slots // 4 % near, slots % 4
+    my_z, my_y, my_c = rank // (2 * near), rank // 2 % near, rank % 2
+    source = ((my_z - far_step) % 4 * near + (my_y - near_step) % near) * 2 + (
+        my_c + core_step
+    ) % 2
+    feature = jnp.repeat(source * shard, shard) + jnp.tile(
+        jnp.arange(shard, dtype=jnp.int32), ranks
+    )
+    to_local = (jnp.arange(width, dtype=jnp.int32)[:, None] == feature[None, :]).astype(low)
+    slot_of = (slots[:, None] == source[None, :]).astype(jnp.float32)
+
+    inputs_other = swap(inputs)
+    grad_other = swap(out_grad)
+
+    proj_shard = (
+        w_qkv.reshape(3, shard, pairs, 128).transpose(1, 2, 0, 3).reshape(shard, 3 * heads_width)
+    )
+    vectors = jnp.concatenate(
+        [ln1_gain, ln1_bias, attn_out_bias, ln2_gain, ln2_bias, down_bias]
+        + [qv_bias.reshape(-1), up_bias]
+    )
+    vector_rows = jnp.pad(vectors, (0, 8 * 3 * heads_width - vectors.shape[0])).reshape(8, -1)
+    first = dp_gather(jnp.concatenate([proj_shard, vector_rows], axis=0), ranks)
+    first = first.reshape(ranks, shard + 8, 3 * heads_width)
+    proj_full = first[:, :shard].reshape(width, 3 * heads_width)
+    vector_full = first[:, shard:].reshape(ranks, -1)[:, : vectors.shape[0]].astype(jnp.float32)
+    out_full = dp_gather(w_attn_out.T, ranks)
+    hidden_full = dp_gather(w_up, ranks)
+    back_full = dp_gather(w_down.T, ranks)
+
+    gain_one, shift_one, out_bias, gain_two, shift_two, back_bias = (
+        vector_full[:, i * shard : (i + 1) * shard].reshape(width) for i in range(6)
+    )
+    natural = jnp.dot(slot_of, vector_full[:, 6 * shard :], precision=lax.Precision.HIGHEST)
+    query_bias = lax.dynamic_slice_in_dim(
+        natural[:, :shard].reshape(width), side * heads_width, heads_width, 0
+    )
+    value_bias = lax.dynamic_slice_in_dim(
+        natural[:, shard : 2 * shard].reshape(width), side * heads_width, heads_width, 0
+    )
+    hidden_bias = lax.dynamic_slice_in_dim(
+        natural[:, 2 * shard :].reshape(-1), side * hidden, hidden, 0
+    )
+    proj_bias = jnp.stack(
+        [
+            query_bias.reshape(pairs, 128),
+            jnp.zeros((pairs, 128), jnp.float32),
+            value_bias.reshape(pairs, 128),
+        ],
+        axis=1,
+    ).reshape(-1)
+
+    def in_order(own, other):
+        return jnp.where(
+            side == 0,
+            jnp.concatenate([own, other], axis=0),
+            jnp.concatenate([other, own], axis=0),
+        )
+
+    def own_rows(value):
+        return lax.dynamic_slice_in_dim(value, side * rows, rows, 0)
+
+    def other_rows(value):
+        return lax.dynamic_slice_in_dim(value, (1 - side) * rows, rows, 0)
+
+    hidden_in = matmul(in_order(inputs, inputs_other), to_local)
+    cotangent = matmul(in_order(out_grad, grad_other), to_local).astype(low)
+    norm_one = layer_norm(hidden_in, gain_one, shift_one).astype(low)
+    qkv = (matmul(norm_one, proj_full) + proj_bias).astype(low)
+    attended, logs = attend(qkv, scale)
+    share = contract_last(attended, out_full).astype(low)
+    branch = share.astype(jnp.float32) + swap(share).astype(jnp.float32)
+    resid = hidden_in + (branch + out_bias)
+    norm_two, ln2_pull = jax.vjp(
+        lambda v: layer_norm(v, gain_two, shift_two), resid
+    )
+    norm_two = norm_two.astype(low)
+    pre = matmul(norm_two, hidden_full) + hidden_bias
+    act, gelu_pull = jax.vjp(gelu_tanh, pre)
+    act = act.astype(low)
+    own_out = contract_last(own_rows(act), back_full)
+    other_out = swap(contract_last(other_rows(act), back_full).astype(low))
+    result = own_rows(resid) + (own_out + other_out.astype(jnp.float32)) + back_bias
+    result = contract_last(result.astype(low), to_local).astype(low)
+    (dpre,) = gelu_pull(matmul(cotangent, back_full))
+    dpre = dpre.astype(low)
+    dnorm_share = contract_last(dpre, hidden_full).astype(low)
+    dnorm_two = dnorm_share.astype(jnp.float32) + swap(dnorm_share).astype(jnp.float32)
+    grad_back = dp_reduce(contract_rows(cotangent, act), ranks, low).T
+    grad_hidden = dp_reduce(contract_rows(norm_two, dpre), ranks, low)
+    (dresid_part,) = ln2_pull(dnorm_two)
+    dresid = cotangent.astype(jnp.float32) + dresid_part
+    dbranch = dresid.astype(low)
+    dattended = matmul(dbranch, out_full).astype(low)
+    grad_out = dp_reduce(contract_rows(dbranch, attended), ranks, low).T
+    dqkv = attend_back(qkv, dattended, logs, scale)
+    own_dnorm = contract_last(own_rows(dqkv), proj_full)
+    other_dnorm = swap(contract_last(other_rows(dqkv), proj_full).astype(low))
+    dnorm_one = own_dnorm + other_dnorm.astype(jnp.float32)
+    hidden_own = own_rows(hidden_in)
+    _, ln1_pull = jax.vjp(layer_norm, hidden_own, gain_one, shift_one)
+    dinput, grad_gain_one, grad_shift_one = ln1_pull(dnorm_one)
+    input_grad = own_rows(dresid) + dinput
+    input_grad = lax.dot_general(
+        input_grad,
+        to_local.astype(jnp.float32),
+        (((1,), (1,)), ((), ())),
+        precision=lax.Precision.HIGHEST,
+        preferred_element_type=jnp.float32,
+    )
+    grad_proj = dp_reduce(contract_rows(norm_one, dqkv), ranks, low)
+    grad_proj = grad_proj.reshape(shard, pairs, 3, 128).transpose(2, 0, 1, 3)
+    grad_proj = grad_proj.reshape(3, shard, heads_width)
+
+    resid_own = own_rows(resid)
+    _, ln2_vec_pull = jax.vjp(lambda g, b: layer_norm(resid_own, g, b), gain_two, shift_two)
+    grad_gain_two, grad_shift_two = ln2_vec_pull(own_rows(dnorm_two))
+    grad_out_bias = jnp.sum(own_rows(dbranch).astype(jnp.float32), axis=0)
+    grad_back_bias = jnp.sum(own_rows(cotangent).astype(jnp.float32), axis=0)
+    dqkv_sum = jnp.sum(dqkv.astype(jnp.float32), axis=0).reshape(pairs, 3, 128)
+    grad_query_bias = place_block(
+        dqkv_sum[:, 0].reshape(heads_width), width, side * heads_width
+    ).reshape(ranks, shard)
+    grad_value_bias = place_block(
+        dqkv_sum[:, 2].reshape(heads_width), width, side * heads_width
+    ).reshape(ranks, shard)
+    grad_hidden_bias = place_block(
+        jnp.sum(dpre.astype(jnp.float32), axis=0), 2 * hidden, side * hidden
+    ).reshape(ranks, -1)
+    to_slot = lax.dot_general(
+        slot_of,
+        jnp.concatenate([grad_query_bias, grad_value_bias, grad_hidden_bias], axis=1),
+        (((0,), (0,)), ((), ())),
+        precision=lax.Precision.HIGHEST,
+        preferred_element_type=jnp.float32,
+    )
+    pack = jnp.concatenate(
+        [
+            value.reshape(ranks, shard)
+            for value in (
+                grad_gain_one,
+                grad_shift_one,
+                grad_out_bias,
+                grad_gain_two,
+                grad_shift_two,
+                grad_back_bias,
+            )
+        ]
+        + [to_slot],
+        axis=1,
+    )
+    pack = pack + swap(pack)
+    pack = dp_reduce(pack, ranks, jnp.float32).reshape(-1)
+    vector_grads = [pack[i * shard : (i + 1) * shard] for i in range(6)]
+    return (
+        result,
+        input_grad,
+        vector_grads[0],
+        vector_grads[1],
+        grad_proj,
+        pack[6 * shard : 8 * shard].reshape(2, shard),
+        grad_out,
+        vector_grads[2],
+        vector_grads[3],
+        vector_grads[4],
+        grad_hidden,
+        pack[8 * shard :],
+        grad_back,
+        vector_grads[5],
+    )
+
+
+def local(*arrays):
+    pairs_fit = lax.axis_size("tensor") == 2 and lax.axis_size("dp") % 8 == 0
+    if pairs_fit and arrays[2].shape[1] == 3:
+        return paired(*arrays)
+    return generic(*arrays)
+
+
 def solution(mesh):
     return jax.shard_map(
         local,

time: 1050 us -> 456 us (0.43)
  waiting for transfers between devices: 670 us -> 162 us
  blocking collectives: 154 us -> 0 us
  starting transfers between devices: 0.94 us -> 75.9 us
  matrix products: 118 us -> 73.4 us
  local copies, waits for them, and re-layouts: 38.4 us -> 72.9 us
  Pallas kernels: 0 us -> 24.1 us
  between operations: 17 us -> 1.95 us
    reduce_scatter x8 -> x0, waiting for transfers between devices: 436 us -> none  [the longest x1 109 us: local(): lax.psum_scatter(grad_hidden, 'dp', scatter_dimension=0, tiled=True)]
    all_gather x8 -> x0, waiting for transfers between devices: 215 us -> none  [the longest x1 53 us: local(): lax.all_gather(w_down, 'dp', axis=1, tiled=True)]
    ppermute x0 -> x64, waiting for transfers between devices: none -> 162 us  [the longest x57 111 us: dp_shift(): lax.ppermute(value, 'dp', [(rank, goes(rank)) for rank in range(ranks)])]
    unnamed x2 -> x0, blocking collectives: 107 us -> none
    ppermute x0 -> x64, starting transfers between devices: none -> 75.9 us  [the longest x57 69.2 us: dp_shift(): lax.ppermute(value, 'dp', [(rank, goes(rank)) for rank in range(ranks)])]
    all_gather x2 -> x0, blocking collectives: 41.5 us -> none  [the longest x1 22.4 us: local(): lax.all_gather(qv_bias, 'dp', axis=1, tiled=True)]
    dot_general x21 -> x3, matrix products: 34.8 us -> 4.5 us  [the longest x1 4.17 us: paired(): lax.dot_general(input_grad, to_local.astype(jnp.float32), (((1,), (1,)),...]
    pallas_call x0 -> x2, Pallas kernels: none -> 24.1 us  [the longest x1 13 us: attend_back(): pl.pallas_call(functools.partial(attend_back_kernel, scale=scale), grid=(...]
  transfers between devices with their start and end apart: 17 -> 64, of which waited for: 17 -> 32; matrix products, arithmetic and copies ran while one was open for 10% -> 33% of each run, Pallas kernels for 0% -> 5%
where the time goes in v1:
time: 456 us; the launch traced here: 448 us
  waiting for transfers between devices  162 us (36%)
  starting transfers between devices  75.9 us (17%)
  matrix products  73.4 us (16%)
  local copies, waits for them, and re-layouts  72.9 us (16%)
  other arithmetic  38 us (8%)
  Pallas kernels  24.1 us (5%)
    ppermute x57, waiting for transfers between devices, dp_shift(): lax.ppermute(value, 'dp', [(rank, goes(rank)) for rank in range(ranks)])  111 us
    ppermute x57, starting transfers between devices, dp_shift(): lax.ppermute(value, 'dp', [(rank, goes(rank)) for rank in range(ranks)])  69.2 us
    ppermute x7, waiting for transfers between devices, swap(): return lax.ppermute(value, 'tensor', [(0, 1), (1, 0)])  51.1 us
    unnamed x124, local copies, waits for them, and re-layouts  35.1 us
    dot_general x6, matrix products, contract_last(): lax.dot_general(left, right, (((1,), (1,)), ((), ())), preferred_element_...  26.1 us
    dot_general x6, matrix products, matmul(): return jnp.dot(left, right, preferred_element_type=jnp.float32)  25.2 us
    dot_general x4, matrix products, contract_rows(): lax.dot_general(left, right, (((0,), (0,)), ((), ())), preferred_element_...  17.6 us
    pallas_call x1, Pallas kernels, attend_back(): pl.pallas_call(functools.partial(attend_back_kernel, scale=scale), grid=(...  13 us
  transfers between devices with their start and end apart: 64, of which 32 were waited for; matrix products, arithmetic and copies ran while one was open for 33% of the time, Pallas kernels for 5%

profile of v1, /device:TPU:8, one launch (start us, length us, event | category | flops | bytes accessed | tf_op | source)
XLA Modules:
  0.0 448.0 jit_solution(1919554768826352525)
XLA Ops:
  26.0 4.0 collective-permute-done.9
  56.7 6.9 %collective-permute-done.2 = bf16[72,1536]{1,0:T(8,128)(2,1)S(1)} collective-permute-done((bf16[72,1536]{1,0:T(8,128)(2,1)}, bf16[72,1536]{1,0:T(8,128)(2,1)S(1)}, u32[]{:S(2)}, u32[]{:S(2)}) %collective-permute-start.2) | collective-permute-done | bytes 221216 | tf_op jit(solution)/shard_map/ppermute | solution.py:442
  71.8 4.0 collective-permute-done.4
  78.9 6.4 %collective-permute-start.19 = (bf16[64,2048]{1,0:T(8,128)(2,1)S(1)}, bf16[64,2048]{1,0:T(8,128)(2,1)S(1)}, u32[]{:S(2)}, u32[]{:S(2)}) collective-permute-start(bf16[64,2048]{1,0:T(8,128)(2,1)S(1)} %copy-done.22), channel_id=1, source_target_pairs={{0,16},{2,18},{4,20},{6,22},{8,24},{10,26},{12,28},{14,30},{16,0},... | collective-permute-start | bytes 786440 | tf_op jit(solution)/shard_map/ppermute | solution.py:442
  106.3 4.3 collective-permute-done.6
  111.0 4.3 collective-permute-done.7
  115.8 5.2 %collective-permute-done.30 = bf16[64,2048]{1,0:T(8,128)(2,1)S(1)} collective-permute-done((bf16[64,2048]{1,0:T(8,128)(2,1)}, bf16[64,2048]{1,0:T(8,128)(2,1)S(1)}, u32[]{:S(2)}, u32[]{:S(2)}) %collective-permute-start.30) | collective-permute-done | bytes 262176 | tf_op jit(solution)/shard_map/ppermute | solution.py:442
  122.2 4.3 collective-permute-done.31
  127.8 4.4 collective-permute-done.32
  133.4 4.3 collective-permute-done.22
  138.6 4.8 %collective-permute-done.23 = bf16[64,2048]{1,0:T(8,128)(2,1)S(1)} collective-permute-done((bf16[64,2048]{1,0:T(8,128)(2,1)S(1)}, bf16[64,2048]{1,0:T(8,128)(2,1)S(1)}, u32[]{:S(2)}, u32[]{:S(2)}) %collective-permute-start.23) | collective-permute-done | bytes 262176 | tf_op jit(solution)/shard_map/ppermute | solution.py:442
  157.8 5.7 %add_convert_fusion.qkv_ref = bf16[768,1536]{1,0:T(8,128)(2,1)S(1)} fusion(bf16[1024,1536]{1,0:T(8,128)(2,1)} %bitcast.65, f32[1536]{0:T(1024)S(1)} %add.343, f32[768,1024]{1,0:T(8,128)} %copy-done.5, f32[1024]{0:T(1024)S(1)} %add.339, f32[1024]{0:T(1024)S(1)} %mul.239, f32[768]{0:T(1024)} %add_rsqrt_fusion, f32[768]{0:T(1024)S(1)} %broadcast_multiply_fusion.1), kind=kOutput, calls=%fused_computation.14 | convolution fusion | flops 2422210560 | bytes 8671232 | tf_op jit(solution)/shard_map/dot_general | solution.py:33
  163.5 11.2 %attend.1 = (bf16[768,512]{1,0:T(8,128)(2,1)S(1)}, f32[4,8,768]{2,1,0:T(8,128)S(1)}) custom-call(bf16[768,1536]{1,0:T(8,128)(2,1)S(1)} %add_convert_fusion.qkv_ref), custom_call_target="tpu_custom_call" | custom-call | tf_op jit(solution)/shard_map/attend/pallas_call | solution.py:358
  177.4 3.9 fusion.14
  191.4 22.0 %collective-permute-done.17 = bf16[768,1024]{1,0:T(8,128)(2,1)} collective-permute-done((bf16[768,1024]{1,0:T(8,128)(2,1)}, bf16[768,1024]{1,0:T(8,128)(2,1)}, u32[]{:S(2)}, u32[]{:S(2)}) %collective-permute-start.17) | collective-permute-done | bytes 1572896 | tf_op jit(solution)/shard_map/ppermute | solution.py:475
  220.2 9.2 %convert_reduce_fusion = (f32[2048]{0:T(1024)S(1)}, bf16[768,2048]{1,0:T(8,128)(2,1)S(1)}, bf16[768,2048]{1,0:T(8,128)(2,1)S(1)}) fusion(f32[768,2048]{1,0:T(8,128)S(1)} %fusion.91, f32[2048]{0:T(1024)S(1)} %dynamic_slice.43, bf16[768,1024]{1,0:T(8,128)(2,1)S(1)} %copy-done.13, bf16[1024,2048]{1,0:T(8,128)(2,1)S(1)} %copy-done.25), kind=kOutput, calls=%fused_computation.10 | convolution fusion | flops 3266836480 | bytes 18366464 | tf_op jit(solution)/shard_map/dot_general | solution.py:33
  229.4 4.7 %convolution_convert_fusion.1 = bf16[768,1024]{1,0:T(8,128)(2,1)} fusion(bf16[768,2048]{1,0:T(8,128)(2,1)S(1)} %get-tuple-element.32, bf16[1024,2048]{1,0:T(8,128)(2,1)S(1)} %constant_dynamic-update-slice_fusion.46), kind=kOutput, calls=%fused_computation.45 | convolution fusion | flops 3222011904 | bytes 8912896 | tf_op jit(solution)/shard_map/dot_general | solution.py:43
  234.2 6.1 %fusion.90 = f32[1024,2048]{1,0:T(8,128)} fusion(bf16[768,2048]{1,0:T(8,128)(2,1)S(1)} %get-tuple-element.32, f32[768,1024]{1,0:T(8,128)S(1)} %get-tuple-element.40, f32[1024]{0:T(1024)S(1)} %add.353, f32[1024]{0:T(1024)S(1)} %mul.247, f32[768]{0:T(1024)S(1)} %fusion.65, f32[768]{0:T(1024)S(1)} %broadcast_multiply_fusion), kind=kOutput, calls=%fused_computation.261 | convolution fusion | flops 3225157632 | bytes 14694400 | tf_op jit(solution)/shard_map/dot_general | solution.py:37
  245.0 5.7 %fusion.112 = f32[1024,2048]{1,0:T(8,128)} fusion(bf16[768,1024]{1,0:T(8,128)(2,1)S(1)} %copy-done.13, bf16[768,2048]{1,0:T(8,128)(2,1)S(1)} %get-tuple-element.43), kind=kOutput, calls=%fused_computation.281 | convolution fusion | flops 3221225472 | bytes 13107200 | tf_op jit(solution)/shard_map/dot_general | solution.py:37
  254.7 4.0 slice.435
  259.5 4.2 collective-permute-done.34
  263.8 7.0 %fusion.37 = bf16[384,1024]{1,0:T(8,128)(2,1)} fusion(s32[1024]{0:T(1024)S(1)} %copy-done.32, bf16[384,1024]{1,0:T(8,128)(2,1)} %collective-permute-done.34, f32[768,1024]{1,0:T(8,128)} %copy-done.2, s32[]{:T(128)S(6)} %select_n.127, bf16[1024,2048]{1,0:T(8,128)(2,1)} %constant_dynamic-update-slice_fusion.63, bf16[768,2048]{1,0:T(8,128)(2,1)} %copy-done.41, ...), kind=kOutput, calls=%fused_computation.82 | convolution fusion | flops 2419326976 | bytes 8922112 | tf_op jit(solution)/shard_map/dot_general | solution.py:43
  270.8 24.8 %collective-permute-done.36 = bf16[768,1024]{1,0:T(8,128)(2,1)} collective-permute-done((bf16[768,1024]{1,0:T(8,128)(2,1)}, bf16[768,1024]{1,0:T(8,128)(2,1)}, u32[]{:S(2)}, u32[]{:S(2)}) %collective-permute-start.36) | collective-permute-done | bytes 1572896 | tf_op jit(solution)/shard_map/ppermute | solution.py:475
  305.9 13.0 %attend_back.1 = bf16[768,1536]{1,0:T(8,128)(2,1)S(1)} custom-call(bf16[768,1536]{1,0:T(8,128)(2,1)S(1)} %add_convert_fusion.qkv_ref, bf16[768,512]{1,0:T(8,128)(2,1)S(1)} %convolution_convert_fusion.3.grad_ref, f32[4,8,768]{2,1,0:T(8,128)S(1)} %get-tuple-element.17.log_ref), custom_call_target="tpu_custom_call" | custom-call | tf_op jit(solution)/shard_map/attend_back/pallas_call | solution.py:416
  318.9 5.1 %convolution_convert_fusion.2 = bf16[384,1024]{1,0:T(8,128)(2,1)} fusion(bf16[1024,1536]{1,0:T(8,128)(2,1)} %bitcast.66, bf16[768,1536]{1,0:T(8,128)(2,1)S(1)} %attend_back.1, s32[]{:T(128)S(6)} %select_n.129), kind=kOutput, calls=%fused_computation.83 | convolution fusion | flops 1208352768 | bytes 5111812 | tf_op jit(solution)/shard_map/dot_general | solution.py:43
  324.5 4.7 %fusion.89 = f32[1024,1536]{1,0:T(8,128)} fusion(bf16[768,1536]{1,0:T(8,128)(2,1)S(1)} %attend_back.1, f32[768,1024]{1,0:T(8,128)S(1)} %copy-done.7, f32[1024]{0:T(1024)S(1)} %add.339, f32[1024]{0:T(1024)S(1)} %mul.239, f32[768]{0:T(1024)S(1)} %copy-done.34, f32[768]{0:T(1024)S(1)} %broadcast_multiply_fusion.1), kind=kOutput, calls=%fused_computation.260 | convolution fusion | flops 2419851264 | bytes 11810816 | tf_op jit(solution)/shard_map/dot_general | solution.py:37
  337.5 4.2 slice_add_fusion.1
  350.4 4.4 multiply_reduce_fusion.5
  363.3 4.2 fusion.6
  388.4 10.3 %collective-permute-done.60 = bf16[256,2048]{1,0:T(8,128)(2,1)} collective-permute-done((bf16[256,2048]{1,0:T(8,128)(2,1)S(1)}, bf16[256,2048]{1,0:T(8,128)(2,1)}, u32[]{:S(2)}, u32[]{:S(2)}) %collective-permute-start.60) | collective-permute-done | bytes 1048608 | tf_op jit(solution)/shard_map/ppermute | solution.py:442
  408.4 6.4 %collective-permute-done.56 = bf16[64,2048]{1,0:T(8,128)(2,1)S(1)} collective-permute-done((bf16[64,2048]{1,0:T(8,128)(2,1)S(1)}, bf16[64,2048]{1,0:T(8,128)(2,1)S(1)}, u32[]{:S(2)}, u32[]{:S(2)}) %collective-permute-start.56) | collective-permute-done | bytes 262176 | tf_op jit(solution)/shard_map/ppermute | solution.py:442
  424.5 11.7 %collective-permute-done.62 = bf16[64,2048]{1,0:T(8,128)(2,1)S(1)} collective-permute-done((bf16[64,2048]{1,0:T(8,128)(2,1)S(1)}, bf16[64,2048]{1,0:T(8,128)(2,1)S(1)}, u32[]{:S(2)}, u32[]{:S(2)}) %collective-permute-start.62) | collective-permute-done | bytes 262176 | tf_op jit(solution)/shard_map/ppermute | solution.py:442
  (363 shorter events, 220.8 us)
Async XLA Ops:
  0.7 78.2 %collective-permute-start.26 = (bf16[64,2048]{1,0:T(8,128)(2,1)}, bf16[64,2048]{1,0:T(8,128)(2,1)}, u32[]{:S(2)}, u32[]{:S(2)}) collective-permute-start(bf16[64,2048]{1,0:T(8,128)(2,1)} %bitcast.73), channel_id=1, source_target_pairs={{0,8},{2,10},{4,12},{6,14},{8,16},{10,18},{12,20},{14,22},{16,24},... | collective-permute-start | bytes 786440 | tf_op jit(solution)/shard_map/ppermute | solution.py:442
  2.3 84.9 %collective-permute-start.27 = (bf16[64,2048]{1,0:T(8,128)(2,1)}, bf16[64,2048]{1,0:T(8,128)(2,1)}, u32[]{:S(2)}, u32[]{:S(2)}) collective-permute-start(bf16[64,2048]{1,0:T(8,128)(2,1)} %bitcast.74), channel_id=1, source_target_pairs={{0,16},{2,18},{4,20},{6,22},{8,24},{10,26},{12,28},{14,30},{16,0},... | collective-permute-start | bytes 786440 | tf_op jit(solution)/shard_map/ppermute | solution.py:442
  3.4 87.6 %collective-permute-start.28 = (bf16[64,2048]{1,0:T(8,128)(2,1)}, bf16[64,2048]{1,0:T(8,128)(2,1)}, u32[]{:S(2)}, u32[]{:S(2)}) collective-permute-start(bf16[64,2048]{1,0:T(8,128)(2,1)} %bitcast.75), channel_id=1, source_target_pairs={{0,24},{2,26},{4,28},{6,30},{8,0},{10,2},{12,4},{14,6},{16,8},{18,... | collective-permute-start | bytes 786440 | tf_op jit(solution)/shard_map/ppermute | solution.py:442
  5.4 24.6 %collective-permute-start.9 = (bf16[64,512]{1,0:T(8,128)(2,1)}, bf16[64,512]{1,0:T(8,128)(2,1)}, u32[]{:S(2)}, u32[]{:S(2)}) collective-permute-start(bf16[64,512]{1,0:T(8,128)(2,1)} %bitcast.77), channel_id=1, source_target_pairs={{0,8},{2,10},{4,12},{6,14},{8,16},{10,18},{12,20},{14,22},{16,24},... | collective-permute-start | bytes 196616 | tf_op jit(solution)/shard_map/ppermute | solution.py:442
  5.4 26.0 %collective-permute-start.10 = (bf16[64,512]{1,0:T(8,128)(2,1)}, bf16[64,512]{1,0:T(8,128)(2,1)}, u32[]{:S(2)}, u32[]{:S(2)}) collective-permute-start(bf16[64,512]{1,0:T(8,128)(2,1)} %bitcast.78), channel_id=1, source_target_pairs={{0,16},{2,18},{4,20},{6,22},{8,24},{10,26},{12,28},{14,30},{16,0},... | collective-permute-start | bytes 196616 | tf_op jit(solution)/shard_map/ppermute | solution.py:442
  50.9 43.5 %collective-permute-start.29 = (bf16[64,2048]{1,0:T(8,128)(2,1)}, bf16[64,2048]{1,0:T(8,128)(2,1)S(1)}, u32[]{:S(2)}, u32[]{:S(2)}) collective-permute-start(bf16[64,2048]{1,0:T(8,128)(2,1)} %bitcast.76), channel_id=1, source_target_pairs={{0,4},{2,6},{4,0},{6,2},{8,12},{10,14},{12,8},{14,10},{16,20},{18,... | collective-permute-start | bytes 786440 | tf_op jit(solution)/shard_map/ppermute | solution.py:442
  75.9 20.8 %collective-permute-start.18 = (bf16[64,2048]{1,0:T(8,128)(2,1)S(1)}, bf16[64,2048]{1,0:T(8,128)(2,1)S(1)}, u32[]{:S(2)}, u32[]{:S(2)}) collective-permute-start(bf16[64,2048]{1,0:T(8,128)(2,1)S(1)} %copy-done.22), channel_id=1, source_target_pairs={{0,8},{2,10},{4,12},{6,14},{8,16},{10,18},{12,20},{14,22},{16,24},... | collective-permute-start | bytes 786440 | tf_op jit(solution)/shard_map/ppermute | solution.py:442
  78.9 18.7 %collective-permute-start.19 = (bf16[64,2048]{1,0:T(8,128)(2,1)S(1)}, bf16[64,2048]{1,0:T(8,128)(2,1)S(1)}, u32[]{:S(2)}, u32[]{:S(2)}) collective-permute-start(bf16[64,2048]{1,0:T(8,128)(2,1)S(1)} %copy-done.22), channel_id=1, source_target_pairs={{0,16},{2,18},{4,20},{6,22},{8,24},{10,26},{12,28},{14,30},{16,0},... | collective-permute-start | bytes 786440 | tf_op jit(solution)/shard_map/ppermute | solution.py:442
  94.4 56.7 %collective-permute-start = (bf16[384,1024]{1,0:T(8,128)(2,1)S(1)}, bf16[384,1024]{1,0:T(8,128)(2,1)S(1)}, u32[]{:S(2)}, u32[]{:S(2)}) collective-permute-start(bf16[384,1024]{1,0:T(8,128)(2,1)S(1)} %copy-done.39), channel_id=1, source_target_pairs={{0,1},{1,0},{2,3},{3,2},{4,5},{5,4},{6,7},{7,6},{8,9},{9,8},{10,11... | collective-permute-start | bytes 2359304 | tf_op jit(solution)/shard_map/ppermute | solution.py:475
  96.7 52.8 %collective-permute-start.16 = (bf16[512,512]{1,0:T(8,128)(2,1)S(1)}, bf16[512,512]{1,0:T(8,128)(2,1)S(1)}, u32[]{:S(2)}, u32[]{:S(2)}) collective-permute-start(bf16[512,512]{1,0:T(8,128)(2,1)S(1)} %copy-done.26), channel_id=1, source_target_pairs={{0,2},{2,0},{4,6},{6,4},{8,10},{10,8},{12,14},{14,12},{16,18},{18,... | collective-permute-start | bytes 1572872 | tf_op jit(solution)/shard_map/ppermute | solution.py:442
  143.4 34.0 %collective-permute-start.35 = (bf16[384,1024]{1,0:T(8,128)(2,1)}, bf16[384,1024]{1,0:T(8,128)(2,1)}, u32[]{:S(2)}, u32[]{:S(2)}) collective-permute-start(bf16[384,1024]{1,0:T(8,128)(2,1)} %param.16), channel_id=1, source_target_pairs={{0,1},{1,0},{2,3},{3,2},{4,5},{5,4},{6,7},{7,6},{8,9},{9,8},{10,11... | collective-permute-start | bytes 2359304 | tf_op jit(solution)/shard_map/ppermute | solution.py:475
  148.6 37.6 %collective-permute-start.33 = (bf16[512,2048]{1,0:T(8,128)(2,1)}, bf16[512,2048]{1,0:T(8,128)(2,1)}, u32[]{:S(2)}, u32[]{:S(2)}) collective-permute-start(bf16[512,2048]{1,0:T(8,128)(2,1)} %get-tuple-element.73), channel_id=1, source_target_pairs={{0,2},{2,0},{4,6},{6,4},{8,10},{10,8},{12,14},{14,12},{16,18},{18,... | collective-permute-start | bytes 6291464 | tf_op jit(solution)/shard_map/ppermute | solution.py:442
  149.5 40.1 %collective-permute-start.25 = (bf16[512,2048]{1,0:T(8,128)(2,1)}, bf16[512,2048]{1,0:T(8,128)(2,1)}, u32[]{:S(2)}, u32[]{:S(2)}) collective-permute-start(bf16[512,2048]{1,0:T(8,128)(2,1)} %get-tuple-element.57), channel_id=1, source_target_pairs={{0,2},{2,0},{4,6},{6,4},{8,10},{10,8},{12,14},{14,12},{16,18},{18,... | collective-permute-start | bytes 6291464 | tf_op jit(solution)/shard_map/ppermute | solution.py:442
  176.8 36.6 %collective-permute-start.17 = (bf16[768,1024]{1,0:T(8,128)(2,1)}, bf16[768,1024]{1,0:T(8,128)(2,1)}, u32[]{:S(2)}, u32[]{:S(2)}) collective-permute-start(bf16[768,1024]{1,0:T(8,128)(2,1)} %convolution_convert_fusion), channel_id=1, source_target_pairs={{0,1},{1,0},{2,3},{3,2},{4,5},{5,4},{6,7},{7,6},{8,9},{9,8},{10,11... | collective-permute-start | bytes 4718600 | tf_op jit(solution)/shard_map/ppermute | solution.py:475
  243.0 20.8 %collective-permute-start.34 = (bf16[384,1024]{1,0:T(8,128)(2,1)}, bf16[384,1024]{1,0:T(8,128)(2,1)}, u32[]{:S(2)}, u32[]{:S(2)}) collective-permute-start(bf16[384,1024]{1,0:T(8,128)(2,1)} %fusion.34), channel_id=1, source_target_pairs={{0,1},{1,0},{2,3},{3,2},{4,5},{5,4},{6,7},{7,6},{8,9},{9,8},{10,11... | collective-permute-start | bytes 2359304 | tf_op jit(solution)/shard_map/ppermute | solution.py:475
  243.5 52.1 %collective-permute-start.36 = (bf16[768,1024]{1,0:T(8,128)(2,1)}, bf16[768,1024]{1,0:T(8,128)(2,1)}, u32[]{:S(2)}, u32[]{:S(2)}) collective-permute-start(bf16[768,1024]{1,0:T(8,128)(2,1)} %convolution_convert_fusion.1), channel_id=1, source_target_pairs={{0,1},{1,0},{2,3},{3,2},{4,5},{5,4},{6,7},{7,6},{8,9},{9,8},{10,11... | collective-permute-start | bytes 4718600 | tf_op jit(solution)/shard_map/ppermute | solution.py:475
  254.7 82.7 %collective-permute-start.54 = (bf16[512,2048]{1,0:T(8,128)(2,1)}, bf16[512,2048]{1,0:T(8,128)(2,1)}, u32[]{:S(2)}, u32[]{:S(2)}) collective-permute-start(bf16[512,2048]{1,0:T(8,128)(2,1)} %slice.436), channel_id=1, source_target_pairs={{0,2},{2,0},{4,6},{6,4},{8,10},{10,8},{12,14},{14,12},{16,18},{18,... | collective-permute-start | bytes 6291464 | tf_op jit(solution)/shard_map/ppermute | solution.py:442
  258.7 87.3 %collective-permute-start.59 = (bf16[512,2048]{1,0:T(8,128)(2,1)}, bf16[512,2048]{1,0:T(8,128)(2,1)}, u32[]{:S(2)}, u32[]{:S(2)}) collective-permute-start(bf16[512,2048]{1,0:T(8,128)(2,1)} %slice.435), channel_id=1, source_target_pairs={{0,2},{2,0},{4,6},{6,4},{8,10},{10,8},{12,14},{14,12},{16,18},{18,... | collective-permute-start | bytes 6291464 | tf_op jit(solution)/shard_map/ppermute | solution.py:442
  324.0 26.4 %collective-permute-start.37 = (bf16[384,1024]{1,0:T(8,128)(2,1)}, bf16[384,1024]{1,0:T(8,128)(2,1)}, u32[]{:S(2)}, u32[]{:S(2)}) collective-permute-start(bf16[384,1024]{1,0:T(8,128)(2,1)} %convolution_convert_fusion.2), channel_id=1, source_target_pairs={{0,1},{1,0},{2,3},{3,2},{4,5},{5,4},{6,7},{7,6},{8,9},{9,8},{10,11... | collective-permute-start | bytes 2359304 | tf_op jit(solution)/shard_map/ppermute | solution.py:475
  335.6 64.8 %collective-permute-start.44 = (bf16[512,1536]{1,0:T(8,128)(2,1)}, bf16[512,1536]{1,0:T(8,128)(2,1)}, u32[]{:S(2)}, u32[]{:S(2)}) collective-permute-start(bf16[512,1536]{1,0:T(8,128)(2,1)} %slice.437), channel_id=1, source_target_pairs={{0,2},{2,0},{4,6},{6,4},{8,10},{10,8},{12,14},{14,12},{16,18},{18,... | collective-permute-start | bytes 4718600 | tf_op jit(solution)/shard_map/ppermute | solution.py:442
  336.5 22.2 %collective-permute-start.50 = (bf16[256,512]{1,0:T(8,128)(2,1)S(1)}, bf16[256,512]{1,0:T(8,128)(2,1)}, u32[]{:S(2)}, u32[]{:S(2)}) collective-permute-start(bf16[256,512]{1,0:T(8,128)(2,1)S(1)} %slice.442), channel_id=1, source_target_pairs={{0,4},{2,6},{4,0},{6,2},{8,12},{10,14},{12,8},{14,10},{16,20},{18,... | collective-permute-start | bytes 786440 | tf_op jit(solution)/shard_map/ppermute | solution.py:442
  344.9 35.3 %collective-permute-start.55 = (bf16[256,2048]{1,0:T(8,128)(2,1)}, bf16[256,2048]{1,0:T(8,128)(2,1)}, u32[]{:S(2)}, u32[]{:S(2)}) collective-permute-start(bf16[256,2048]{1,0:T(8,128)(2,1)} %slice.439), channel_id=1, source_target_pairs={{0,4},{2,6},{4,0},{6,2},{8,12},{10,14},{12,8},{14,10},{16,20},{18,... | collective-permute-start | bytes 3145736 | tf_op jit(solution)/shard_map/ppermute | solution.py:442
  375.4 23.3 %collective-permute-start.60 = (bf16[256,2048]{1,0:T(8,128)(2,1)S(1)}, bf16[256,2048]{1,0:T(8,128)(2,1)}, u32[]{:S(2)}, u32[]{:S(2)}) collective-permute-start(bf16[256,2048]{1,0:T(8,128)(2,1)S(1)} %copy-done.21), channel_id=1, source_target_pairs={{0,4},{2,6},{4,0},{6,2},{8,12},{10,14},{12,8},{14,10},{16,20},{18,... | collective-permute-start | bytes 3145736 | tf_op jit(solution)/shard_map/ppermute | solution.py:442
  382.7 22.1 %collective-permute-start.58 = (bf16[64,2048]{1,0:T(8,128)(2,1)S(1)}, bf16[64,2048]{1,0:T(8,128)(2,1)S(1)}, u32[]{:S(2)}, u32[]{:S(2)}) collective-permute-start(bf16[64,2048]{1,0:T(8,128)(2,1)S(1)} %get-tuple-element.49), channel_id=1, source_target_pairs={{0,8},{2,10},{4,12},{6,14},{8,16},{10,18},{12,20},{14,22},{16,24},... | collective-permute-start | bytes 786440 | tf_op jit(solution)/shard_map/ppermute | solution.py:442
  383.1 25.3 %collective-permute-start.57 = (bf16[64,2048]{1,0:T(8,128)(2,1)S(1)}, bf16[64,2048]{1,0:T(8,128)(2,1)S(1)}, u32[]{:S(2)}, u32[]{:S(2)}) collective-permute-start(bf16[64,2048]{1,0:T(8,128)(2,1)S(1)} %get-tuple-element.50), channel_id=1, source_target_pairs={{0,16},{2,18},{4,20},{6,22},{8,24},{10,26},{12,28},{14,30},{16,0},... | collective-permute-start | bytes 786440 | tf_op jit(solution)/shard_map/ppermute | solution.py:442
  386.5 28.3 %collective-permute-start.56 = (bf16[64,2048]{1,0:T(8,128)(2,1)S(1)}, bf16[64,2048]{1,0:T(8,128)(2,1)S(1)}, u32[]{:S(2)}, u32[]{:S(2)}) collective-permute-start(bf16[64,2048]{1,0:T(8,128)(2,1)S(1)} %get-tuple-element.48), channel_id=1, source_target_pairs={{0,24},{2,26},{4,28},{6,30},{8,0},{10,2},{12,4},{14,6},{16,8},{18,... | collective-permute-start | bytes 786440 | tf_op jit(solution)/shard_map/ppermute | solution.py:442
  403.0 21.5 %collective-permute-start.63 = (bf16[64,2048]{1,0:T(8,128)(2,1)S(1)}, bf16[64,2048]{1,0:T(8,128)(2,1)S(1)}, u32[]{:S(2)}, u32[]{:S(2)}) collective-permute-start(bf16[64,2048]{1,0:T(8,128)(2,1)S(1)} %get-tuple-element.46), channel_id=1, source_target_pairs={{0,8},{2,10},{4,12},{6,14},{8,16},{10,18},{12,20},{14,22},{16,24},... | collective-permute-start | bytes 786440 | tf_op jit(solution)/shard_map/ppermute | solution.py:442
  404.8 31.3 %collective-permute-start.62 = (bf16[64,2048]{1,0:T(8,128)(2,1)S(1)}, bf16[64,2048]{1,0:T(8,128)(2,1)S(1)}, u32[]{:S(2)}, u32[]{:S(2)}) collective-permute-start(bf16[64,2048]{1,0:T(8,128)(2,1)S(1)} %get-tuple-element.47), channel_id=1, source_target_pairs={{0,16},{2,18},{4,20},{6,22},{8,24},{10,26},{12,28},{14,30},{16,0},... | collective-permute-start | bytes 786440 | tf_op jit(solution)/shard_map/ppermute | solution.py:442
  408.4 29.4 %collective-permute-start.61 = (bf16[64,2048]{1,0:T(8,128)(2,1)S(1)}, bf16[64,2048]{1,0:T(8,128)(2,1)S(1)}, u32[]{:S(2)}, u32[]{:S(2)}) collective-permute-start(bf16[64,2048]{1,0:T(8,128)(2,1)S(1)} %get-tuple-element.45), channel_id=1, source_target_pairs={{0,24},{2,26},{4,28},{6,30},{8,0},{10,2},{12,4},{14,6},{16,8},{18,... | collective-permute-start | bytes 786440 | tf_op jit(solution)/shard_map/ppermute | solution.py:442
  419.4 21.0 %collective-permute-start.48 = (bf16[64,1536]{1,0:T(8,128)(2,1)S(1)}, bf16[64,1536]{1,0:T(8,128)(2,1)S(1)}, u32[]{:S(2)}, u32[]{:S(2)}) collective-permute-start(bf16[64,1536]{1,0:T(8,128)(2,1)S(1)} %get-tuple-element.52), channel_id=1, source_target_pairs={{0,8},{2,10},{4,12},{6,14},{8,16},{10,18},{12,20},{14,22},{16,24},... | collective-permute-start | bytes 589832 | tf_op jit(solution)/shard_map/ppermute | solution.py:442
  420.9 21.6 %collective-permute-start.47 = (bf16[64,1536]{1,0:T(8,128)(2,1)S(1)}, bf16[64,1536]{1,0:T(8,128)(2,1)S(1)}, u32[]{:S(2)}, u32[]{:S(2)}) collective-permute-start(bf16[64,1536]{1,0:T(8,128)(2,1)S(1)} %get-tuple-element.53), channel_id=1, source_target_pairs={{0,16},{2,18},{4,20},{6,22},{8,24},{10,26},{12,28},{14,30},{16,0},... | collective-permute-start | bytes 589832 | tf_op jit(solution)/shard_map/ppermute | solution.py:442
  424.5 21.6 %collective-permute-start.46 = (bf16[64,1536]{1,0:T(8,128)(2,1)S(1)}, bf16[64,1536]{1,0:T(8,128)(2,1)S(1)}, u32[]{:S(2)}, u32[]{:S(2)}) collective-permute-start(bf16[64,1536]{1,0:T(8,128)(2,1)S(1)} %get-tuple-element.51), channel_id=1, source_target_pairs={{0,24},{2,26},{4,28},{6,30},{8,0},{10,2},{12,4},{14,6},{16,8},{18,... | collective-permute-start | bytes 589832 | tf_op jit(solution)/shard_map/ppermute | solution.py:442
  (78 other events, 1075.7 us)

commit v2 on v0

--- a/solution.py
+++ b/solution.py
@@ -1,8 +1,11 @@
+import functools
 import math
 
 import jax
 import jax.numpy as jnp
 from jax import lax
+from jax.experimental import pallas as pl
+from jax.experimental.pallas import tpu as pltpu
 from jax.sharding import PartitionSpec as P
 
 HEADS = 16
@@ -82,7 +85,7 @@
     return lax.dynamic_update_slice_in_dim(empty_vec, local_vec, offset, local_vec.ndim - 1)
 
 
-def local(
+def generic(
     inputs,
     out_grad,
     parents,
@@ -321,6 +324,894 @@
     )
 
 
+LOW = jnp.bfloat16
+SLOT = 64
+
+
+def settings():
+    return pltpu.CompilerParams(vmem_limit_bytes=56 * 2**20)
+
+
+def cost(flops, moved, exps=0):
+    return pl.CostEstimate(
+        flops=int(flops), bytes_accessed=int(moved), transcendentals=int(exps)
+    )
+
+
+def whole(shape):
+    return pl.BlockSpec(shape, lambda *_: (0,) * len(shape))
+
+
+def piece_specs(pieces, block, first=0):
+    return [
+        pl.BlockSpec((piece.shape[0], block), lambda p, *_: (0, first + p)) for piece in pieces
+    ]
+
+
+def fixed_specs(pieces, block, index):
+    return [pl.BlockSpec((piece.shape[0], block), lambda *_: (0, index)) for piece in pieces]
+
+
+def fill(scratch, refs):
+    row = 0
+    for ref in refs:
+        scratch[row : row + ref.shape[0], :] = ref[...]
+        row += ref.shape[0]
+
+
+def fill_slots(place_ref, scratch, ref):
+    for slot in range(scratch.shape[0] // SLOT):
+        start = pl.multiple_of(place_ref[4 + slot] * SLOT, SLOT)
+        scratch[slot * SLOT : slot * SLOT + SLOT, :] = ref[pl.ds(start, SLOT), :]
+
+
+def row_stats(rows):
+    centre = jnp.mean(rows, axis=-1, keepdims=True)
+    shifted = rows - centre
+    spread = jnp.mean(shifted * shifted, axis=-1, keepdims=True)
+    inverse = lax.rsqrt(spread + epsilon)
+    return shifted * inverse, inverse
+
+
+def norm_back(dnorm, xhat, inverse, gain):
+    scaled = dnorm * gain
+    return inverse * (
+        scaled
+        - jnp.mean(scaled, axis=-1, keepdims=True)
+        - xhat * jnp.mean(scaled * xhat, axis=-1, keepdims=True)
+    )
+
+
+def attend_pair(qkv_ref, out_ref, log_ref, scale):
+    length = qkv_ref.shape[0]
+    lane = lax.broadcasted_iota(jnp.int32, (SEG, 128), 1)
+    key = qkv_ref[:, 128:256]
+    value_t = jnp.transpose(qkv_ref[:, 256:384])
+    for seg in range(length // SEG):
+        keys_here = (seg + 1) * SEG
+        query = qkv_ref[seg * SEG : keys_here, 0:128] * scale
+        key_pos = lax.broadcasted_iota(jnp.int32, (keys_here, SEG), 0)
+        query_pos = lax.broadcasted_iota(jnp.int32, (keys_here, SEG), 1) + seg * SEG
+        parts = []
+        for head in range(2):
+            mine = jnp.where(lane // 64 == head, query, jnp.zeros_like(query))
+            scores = contract_last(key[:keys_here], mine)
+            scores = jnp.where(key_pos <= query_pos, scores, -1e30)
+            top = jnp.max(scores, axis=0, keepdims=True)
+            expo = jnp.exp(scores - top)
+            total = jnp.sum(expo, axis=0, keepdims=True)
+            mixed = matmul(value_t[head * 64 : head * 64 + 64, :keys_here], expo.astype(LOW))
+            parts.append(mixed / total)
+            log_ref[0, head : head + 1, seg * SEG : keys_here] = top + jnp.log(total)
+        out_ref[seg * SEG : keys_here, :] = jnp.transpose(jnp.concatenate(parts, axis=0)).astype(
+            LOW
+        )
+
+
+def front_kernel(place_ref, xhat_ref, vec_ref, bias_ref, *refs, scale, count):
+    pieces = refs[:count]
+    norm_ref, qkv_ref, out_ref, log_ref, weight_ref = refs[count:]
+
+    @pl.when(pl.program_id(0) == 0)
+    def _():
+        norm_ref[...] = (xhat_ref[...] * vec_ref[0:1, :] + vec_ref[1:2, :]).astype(LOW)
+
+    fill(weight_ref, pieces)
+    bias = jnp.concatenate(
+        [bias_ref[0:1, :], jnp.zeros((1, 128), jnp.float32), bias_ref[1:2, :]], axis=1
+    )
+    qkv_ref[...] = (matmul(norm_ref[...], weight_ref[...]) + bias).astype(LOW)
+    attend_pair(qkv_ref, out_ref, log_ref, scale)
+
+
+def front(place, xhat, vectors, bias, pieces, pairs, scale):
+    length, width = xhat.shape
+    return pl.pallas_call(
+        functools.partial(front_kernel, scale=scale, count=len(pieces)),
+        grid_spec=pltpu.PrefetchScalarGridSpec(
+            num_scalar_prefetch=1,
+            grid=(pairs,),
+            in_specs=[
+                whole((length, width)),
+                whole(vectors.shape),
+                pl.BlockSpec((8, 128), lambda p, place: (0, place[0] * pairs + p)),
+            ]
+            + piece_specs(pieces, 384),
+            out_specs=[
+                whole((length, width)),
+                pl.BlockSpec((length, 384), lambda p, _: (0, p)),
+                pl.BlockSpec((length, 128), lambda p, _: (0, p)),
+                pl.BlockSpec((1, 8, length), lambda p, _: (p, 0, 0)),
+            ],
+            scratch_shapes=[pltpu.VMEM((width, 384), LOW)],
+        ),
+        out_shape=[
+            jax.ShapeDtypeStruct((length, width), LOW),
+            jax.ShapeDtypeStruct((length, pairs * 384), LOW),
+            jax.ShapeDtypeStruct((length, pairs * 128), LOW),
+            jax.ShapeDtypeStruct((pairs, 8, length), jnp.float32),
+        ],
+        compiler_params=settings(),
+        cost_estimate=cost(2 * length * width * pairs * 384 * 4, 12 * length * width),
+        name="front",
+    )(place, xhat, vectors, bias, *pieces)
+
+
+def share_kernel(att_ref, *refs):
+    pieces, out_ref, weight_ref = refs[:-2], refs[-2], refs[-1]
+
+    @pl.when(pl.program_id(0) == 0)
+    def _():
+        fill(weight_ref, pieces)
+
+    out_ref[...] = contract_last(att_ref[...], weight_ref[...]).astype(LOW)
+
+
+def share_product(att, pieces):
+    length, inner = att.shape
+    width = sum(piece.shape[0] for piece in pieces)
+    return pl.pallas_call(
+        share_kernel,
+        grid=(length // SEG,),
+        in_specs=[pl.BlockSpec((SEG, inner), lambda p: (p, 0))] + fixed_specs(pieces, inner, 3),
+        out_specs=pl.BlockSpec((SEG, width), lambda p: (p, 0)),
+        out_shape=jax.ShapeDtypeStruct((length, width), LOW),
+        scratch_shapes=[pltpu.VMEM((width, inner), LOW)],
+        compiler_params=settings(),
+        cost_estimate=cost(2 * length * width * inner, 4 * length * width),
+        name="share",
+    )(att, *pieces)
+
+
+def up_kernel(
+    place_ref,
+    x_ref,
+    own_ref,
+    other_ref,
+    vec_ref,
+    bias_ref,
+    *refs,
+):
+    grad_ref, up_all_ref, resid_ref, left_ref, act_ref, slope_ref, weight_ref, norm_ref = refs
+    length = x_ref.shape[0]
+
+    @pl.when(pl.program_id(0) == 0)
+    def _():
+        for start in range(0, length, SEG):
+            rows = slice(start, start + SEG)
+            branch = own_ref[rows, :].astype(jnp.float32) + other_ref[rows, :].astype(jnp.float32)
+            resid = x_ref[rows, :].astype(jnp.float32) + (branch + vec_ref[2:3, :])
+            resid_ref[rows, :] = resid
+            xhat, _ = row_stats(resid)
+            norm = xhat * vec_ref[3:4, :] + vec_ref[4:5, :]
+            norm_ref[rows, :] = norm.astype(LOW)
+            put_natural(place_ref, left_ref.at[1, rows, :], norm)
+            left_ref[0, rows, :] = grad_ref[rows, :]
+
+    fill_slots(place_ref, weight_ref, up_all_ref)
+    for start in range(0, length, SEG):
+        rows = slice(start, start + SEG)
+        pre = matmul(norm_ref[rows, :], weight_ref[...]) + bias_ref[...]
+        square = pre * pre
+        bent = jnp.tanh(gelu_coef * pre * (1.0 + 0.044715 * square))
+        half = 0.5 * (1.0 + bent)
+        act_ref[0, rows, :] = (pre * half).astype(LOW)
+        slope_ref[rows, :] = (
+            half
+            + (0.5 * gelu_coef) * pre * (1.0 - bent * bent) * (1.0 + (3 * 0.044715) * square)
+        ).astype(LOW)
+
+
+def up_product(place, x, own, other, vectors, bias, grad, pair, block=512):
+    length, width = x.shape
+    hidden = pair.shape[1] // 2
+    steps = hidden // block
+    return pl.pallas_call(
+        up_kernel,
+        grid_spec=pltpu.PrefetchScalarGridSpec(
+            num_scalar_prefetch=1,
+            grid=(steps,),
+            in_specs=[whole((length, width))] * 3
+            + [
+                whole(vectors.shape),
+                pl.BlockSpec((1, block), lambda p, place: (0, place[0] * steps + p)),
+                whole((length, width)),
+                pl.BlockSpec((width, block), lambda p, _: (0, p)),
+            ],
+            out_specs=[
+                whole((length, width)),
+                whole((2, length, width)),
+                pl.BlockSpec((1, length, block), lambda p, _: (0, 0, p)),
+                pl.BlockSpec((length, block), lambda p, _: (0, p)),
+            ],
+            scratch_shapes=[pltpu.VMEM((width, block), LOW), pltpu.VMEM((length, width), LOW)],
+        ),
+        out_shape=[
+            jax.ShapeDtypeStruct((length, width), jnp.float32),
+            jax.ShapeDtypeStruct((2, length, width), LOW),
+            jax.ShapeDtypeStruct((2, length, hidden), LOW),
+            jax.ShapeDtypeStruct((length, hidden), LOW),
+        ],
+        compiler_params=settings(),
+        cost_estimate=cost(3 * length * width * hidden, 16 * length * width),
+        name="up",
+    )(place, x, own, other, vectors, bias, grad, pair)
+
+
+def turn_kernel(
+    place_ref,
+    grad_ref,
+    act_ref,
+    slope_ref,
+    up_all_ref,
+    down_all_ref,
+    own_ref,
+    other_ref,
+    dnorm_ref,
+    dpre_ref,
+    sum_ref,
+    up_ref,
+    down_ref,
+    out_acc,
+    norm_acc,
+):
+    length = grad_ref.shape[0]
+    rows_own = length // 2
+    step = pl.program_id(0)
+    fill_slots(place_ref, up_ref, up_all_ref)
+    fill_slots(place_ref, down_ref, down_all_ref)
+    total = jnp.zeros((1, up_ref.shape[1]), jnp.float32)
+    for start in range(0, length, SEG):
+        rows = slice(start, start + SEG)
+        dact = matmul(grad_ref[rows, :], down_ref[...])
+        dpre = (dact * slope_ref[rows, :].astype(jnp.float32)).astype(LOW)
+        dpre_ref[0, rows, :] = dpre
+        total = total + jnp.sum(dpre.astype(jnp.float32), axis=0, keepdims=True)
+        mixed = contract_last(act_ref[0, rows, :], down_ref[...])
+        dnorm = contract_last(dpre, up_ref[...])
+
+        @pl.when(step == 0)
+        def _():
+            out_acc[rows, :] = mixed
+            norm_acc[rows, :] = dnorm
+
+        @pl.when(step > 0)
+        def _():
+            out_acc[rows, :] += mixed
+            norm_acc[rows, :] += dnorm
+
+    sum_ref[...] = jnp.broadcast_to(total, sum_ref.shape)
+
+    @pl.when(step == pl.num_programs(0) - 1)
+    def _():
+        side = place_ref[0]
+        own_ref[...] = out_acc[pl.ds(pl.multiple_of(side * rows_own, rows_own), rows_own), :]
+        other_ref[...] = out_acc[
+            pl.ds(pl.multiple_of((1 - side) * rows_own, rows_own), rows_own), :
+        ].astype(LOW)
+        dnorm_ref[...] = norm_acc[...].astype(LOW)
+
+
+def turn_product(place, grad, act, slope, pair, block=512):
+    length, width = grad.shape
+    hidden = act.shape[2]
+    steps = hidden // block
+    return pl.pallas_call(
+        turn_kernel,
+        grid_spec=pltpu.PrefetchScalarGridSpec(
+            num_scalar_prefetch=1,
+            grid=(hidden // block,),
+            in_specs=[
+                whole((length, width)),
+                pl.BlockSpec((1, length, block), lambda p, _: (0, 0, p)),
+                pl.BlockSpec((length, block), lambda p, _: (0, p)),
+                pl.BlockSpec((width, block), lambda p, _: (0, p)),
+                pl.BlockSpec((width, block), lambda p, _: (0, steps + p)),
+            ],
+            out_specs=[
+                whole((length // 2, width)),
+                whole((length // 2, width)),
+                whole((length, width)),
+                pl.BlockSpec((1, length, block), lambda p, _: (1, 0, p)),
+                pl.BlockSpec((8, block), lambda p, _: (0, p)),
+            ],
+            scratch_shapes=[
+                pltpu.VMEM((width, block), LOW),
+                pltpu.VMEM((width, block), LOW),
+                pltpu.VMEM((length, width), jnp.float32),
+                pltpu.VMEM((length, width), jnp.float32),
+            ],
+        ),
+        out_shape=[
+            jax.ShapeDtypeStruct((length // 2, width), jnp.float32),
+            jax.ShapeDtypeStruct((length // 2, width), LOW),
+            jax.ShapeDtypeStruct((length, width), LOW),
+            jax.ShapeDtypeStruct((2, length, hidden), LOW),
+            jax.ShapeDtypeStruct((8, hidden), jnp.float32),
+        ],
+        input_output_aliases={2: 3},
+        compiler_params=settings(),
+        cost_estimate=cost(6 * length * width * hidden, 24 * length * width),
+        name="turn",
+    )(place, grad, act, slope, pair, pair)
+
+
+def mid_kernel(resid_ref, own_ref, other_ref, grad_ref, vec_ref, *refs, count):
+    pieces = refs[:count]
+    dresid_ref, dbranch_ref, datt_ref, sum_ref, weight_ref = refs[count:]
+
+    @pl.when(pl.program_id(0) == 0)
+    def _():
+        fill(weight_ref, pieces)
+        sum_ref[...] = jnp.zeros_like(sum_ref)
+
+    dnorm = own_ref[...].astype(jnp.float32) + other_ref[...].astype(jnp.float32)
+    grad = grad_ref[...].astype(jnp.float32)
+    xhat, inverse = row_stats(resid_ref[...])
+    dresid = grad + norm_back(dnorm, xhat, inverse, vec_ref[3:4, :])
+    dresid_ref[...] = dresid
+    dbranch = dresid.astype(LOW)
+    dbranch_ref[...] = dbranch
+    datt_ref[...] = matmul(dbranch, weight_ref[...]).astype(LOW)
+    for row, value in enumerate((dnorm * xhat, dnorm, dbranch.astype(jnp.float32), grad)):
+        sum_ref[row : row + 1, :] += 0.5 * jnp.sum(value, axis=0, keepdims=True)
+
+
+def mid_product(resid, own, other, grad, vectors, pieces, inner):
+    length, width = resid.shape
+    rows = pl.BlockSpec((SEG, width), lambda p: (p, 0))
+    return pl.pallas_call(
+        functools.partial(mid_kernel, count=len(pieces)),
+        grid=(length // SEG,),
+        in_specs=[rows] * 4 + [whole(vectors.shape)] + fixed_specs(pieces, inner, 3),
+        out_specs=[rows, rows, pl.BlockSpec((SEG, inner), lambda p: (p, 0)), whole((8, width))],
+        out_shape=[
+            jax.ShapeDtypeStruct((length, width), jnp.float32),
+            jax.ShapeDtypeStruct((length, width), LOW),
+            jax.ShapeDtypeStruct((length, inner), LOW),
+            jax.ShapeDtypeStruct((8, width), jnp.float32),
+        ],
+        scratch_shapes=[pltpu.VMEM((width, inner), LOW)],
+        compiler_params=settings(),
+        cost_estimate=cost(2 * length * width * inner * 16, 16 * length * width),
+        name="mid",
+    )(resid, own, other, grad, vectors, *pieces)
+
+
+def attend_back_pair(qkv_ref, grad_ref, log_ref, out_ref, dkey_ref, dvalue_ref, scale):
+    length = qkv_ref.shape[0]
+    lane = lax.broadcasted_iota(jnp.int32, (SEG, 128), 1)
+    key = qkv_ref[:, 128:256]
+    value = qkv_ref[:, 256:384]
+    key_t = jnp.transpose(key)
+    dkey_ref[...] = jnp.zeros_like(dkey_ref)
+    dvalue_ref[...] = jnp.zeros_like(dvalue_ref)
+    for seg in range(length // SEG):
+        keys_here = (seg + 1) * SEG
+        rows = slice(seg * SEG, keys_here)
+        query = qkv_ref[rows, 0:128] * scale
+        grad = grad_ref[rows, :]
+        key_pos = lax.broadcasted_iota(jnp.int32, (keys_here, SEG), 0)
+        query_pos = lax.broadcasted_iota(jnp.int32, (keys_here, SEG), 1) + seg * SEG
+        parts = []
+        dkey = jnp.zeros((keys_here, 128), jnp.float32)
+        dvalue = jnp.zeros((keys_here, 128), jnp.float32)
+        for head in range(2):
+            here = lane // 64 == head
+            query_mine = jnp.where(here, query, jnp.zeros_like(query))
+            grad_mine = jnp.where(here, grad, jnp.zeros_like(grad))
+            scores = contract_last(key[:keys_here], query_mine)
+            scores = jnp.where(key_pos <= query_pos, scores, -1e30)
+            probs = jnp.exp(scores - log_ref[0, head : head + 1, rows])
+            dprobs = contract_last(value[:keys_here], grad_mine)
+            mean = jnp.sum(probs * dprobs, axis=0, keepdims=True)
+            dscores = (probs * (dprobs - mean)).astype(LOW)
+            dvalue = dvalue + matmul(probs.astype(LOW), grad_mine)
+            dkey = dkey + matmul(dscores, query_mine)
+            parts.append(matmul(key_t[head * 64 : head * 64 + 64, :keys_here], dscores) * scale)
+        dkey_ref[:keys_here, :] += dkey
+        dvalue_ref[:keys_here, :] += dvalue
+        out_ref[rows, 0:128] = jnp.transpose(jnp.concatenate(parts, axis=0)).astype(LOW)
+    out_ref[:, 128:256] = dkey_ref[...].astype(LOW)
+    out_ref[:, 256:384] = dvalue_ref[...].astype(LOW)
+
+
+def back_kernel(place_ref, xhat_ref, qkv_ref, grad_ref, log_ref, *refs, scale, count):
+    pieces = refs[:count]
+    dqkv_ref, own_ref, other_ref, sum_ref, vec_ref = refs[count : count + 5]
+    weight_ref, dkey_ref, dvalue_ref, acc_ref = refs[count + 5 :]
+    rows_own = own_ref.shape[0]
+    step = pl.program_id(0)
+    fill(weight_ref, pieces)
+    attend_back_pair(qkv_ref, grad_ref, log_ref, dqkv_ref, dkey_ref, dvalue_ref, scale)
+    dnorm = contract_last(dqkv_ref[...], weight_ref[...])
+    sum_ref[...] = jnp.broadcast_to(
+        jnp.sum(dqkv_ref[...].astype(jnp.float32), axis=0, keepdims=True)[None], sum_ref.shape
+    )
+
+    @pl.when(step == 0)
+    def _():
+        acc_ref[...] = dnorm
+
+    @pl.when(step > 0)
+    def _():
+        acc_ref[...] += dnorm
+
+    @pl.when(step == pl.num_programs(0) - 1)
+    def _():
+        side = place_ref[0]
+        total = acc_ref[...]
+        vec_ref[0:1, :] = jnp.sum(total * xhat_ref[...], axis=0, keepdims=True)
+        vec_ref[1:8, :] = jnp.broadcast_to(jnp.sum(total, axis=0, keepdims=True), (7, total.shape[1]))
+        own_ref[...] = acc_ref[pl.ds(pl.multiple_of(side * rows_own, rows_own), rows_own), :]
+        other_ref[...] = acc_ref[
+            pl.ds(pl.multiple_of((1 - side) * rows_own, rows_own), rows_own), :
+        ].astype(LOW)
+
+
+def back_product(place, xhat, qkv, grad, logs, pieces, scale):
+    length, columns = qkv.shape
+    width = sum(piece.shape[0] for piece in pieces)
+    pairs = columns // 384
+    return pl.pallas_call(
+        functools.partial(back_kernel, scale=scale, count=len(pieces)),
+        grid_spec=pltpu.PrefetchScalarGridSpec(
+            num_scalar_prefetch=1,
+            grid=(pairs,),
+            in_specs=[
+                whole((length, width)),
+                pl.BlockSpec((length, 384), lambda p, _: (0, p)),
+                pl.BlockSpec((length, 128), lambda p, _: (0, p)),
+                pl.BlockSpec((1, 8, length), lambda p, _: (p, 0, 0)),
+            ]
+            + piece_specs(pieces, 384),
+            out_specs=[
+                pl.BlockSpec((length, 384), lambda p, _: (0, p)),
+                whole((length // 2, width)),
+                whole((length // 2, width)),
+                pl.BlockSpec((1, 8, 384), lambda p, _: (p, 0, 0)),
+                whole((8, width)),
+            ],
+            scratch_shapes=[
+                pltpu.VMEM((width, 384), LOW),
+                pltpu.VMEM((length, 128), jnp.float32),
+                pltpu.VMEM((length, 128), jnp.float32),
+                pltpu.VMEM((length, width), jnp.float32),
+            ],
+        ),
+        out_shape=[
+            jax.ShapeDtypeStruct((length, columns), LOW),
+            jax.ShapeDtypeStruct((length // 2, width), jnp.float32),
+            jax.ShapeDtypeStruct((length // 2, width), LOW),
+            jax.ShapeDtypeStruct((pairs, 8, 384), jnp.float32),
+            jax.ShapeDtypeStruct((8, width), jnp.float32),
+        ],
+        compiler_params=settings(),
+        cost_estimate=cost(2 * length * width * columns * 48, 12 * length * width),
+        name="back",
+    )(place, xhat, qkv, grad, logs, *pieces)
+
+
+def put_natural(place_ref, out_ref, value):
+    near = value.shape[1] // 512
+    lane = lax.broadcasted_iota(jnp.int32, (value.shape[0], 128), 1)
+    half = value.shape[1] // 2
+    for slot in range(4 * near):
+        first = value[:, slot // 2 * 128 : slot // 2 * 128 + 128]
+        second = value[:, half + slot // 2 * 128 : half + slot // 2 * 128 + 128]
+        if slot % 2 == 0:
+            second = pltpu.roll(second, 64, 1)
+        else:
+            first = pltpu.roll(first, 64, 1)
+        block = jnp.where(lane < 64, first, second)
+        block = jnp.where(place_ref[3] == 1, pltpu.roll(block, 64, 1), block)
+        far_index = lax.rem(place_ref[1] + 4 - slot % 4, 4)
+        near_index = lax.rem(place_ref[2] + near - slot // 4, near)
+        target = far_index * near + near_index
+        out_ref[:, pl.ds(pl.multiple_of(target * 128, 128), 128)] = block.astype(out_ref.dtype)
+
+
+def last_kernel(
+    place_ref, x_ref, dresid_ref, own_ref, other_ref, vec_ref, out_ref
+):
+    dnorm = own_ref[...] + other_ref[...].astype(jnp.float32)
+    xhat, inverse = row_stats(x_ref[...].astype(jnp.float32))
+    total = dresid_ref[...] + norm_back(dnorm, xhat, inverse, vec_ref[0:1, :])
+    put_natural(place_ref, out_ref, total)
+
+
+def last_product(place, x, dresid, own, other, vectors):
+    rows, width = own.shape
+    block = 128
+    steps = rows // block
+    mine = pl.BlockSpec((block, width), lambda p, place: (place[0] * steps + p, 0))
+    plain = pl.BlockSpec((block, width), lambda p, _: (p, 0))
+    return pl.pallas_call(
+        last_kernel,
+        grid_spec=pltpu.PrefetchScalarGridSpec(
+            num_scalar_prefetch=1,
+            grid=(steps,),
+            in_specs=[mine, mine, plain, plain, whole(vectors.shape)],
+            out_specs=plain,
+        ),
+        out_shape=jax.ShapeDtypeStruct((rows, width), jnp.float32),
+        compiler_params=settings(),
+        cost_estimate=cost(40 * rows * width, 320 * rows * width),
+        name="last",
+    )(place, x, dresid, own, other, vectors)
+
+
+def result_kernel(place_ref, resid_ref, own_ref, other_ref, vec_ref, out_ref):
+    mixed = own_ref[...] + other_ref[...].astype(jnp.float32)
+    total = resid_ref[...] + mixed + vec_ref[5:6, :]
+    put_natural(place_ref, out_ref, total)
+
+
+def result_product(place, resid, own, other, vectors):
+    rows, width = own.shape
+    block = 128
+    steps = rows // block
+    mine = pl.BlockSpec((block, width), lambda p, place: (place[0] * steps + p, 0))
+    plain = pl.BlockSpec((block, width), lambda p, _: (p, 0))
+    return pl.pallas_call(
+        result_kernel,
+        grid_spec=pltpu.PrefetchScalarGridSpec(
+            num_scalar_prefetch=1,
+            grid=(steps,),
+            in_specs=[mine, plain, plain, whole(vectors.shape)],
+            out_specs=plain,
+        ),
+        out_shape=jax.ShapeDtypeStruct((rows, width), LOW),
+        compiler_params=settings(),
+        cost_estimate=cost(10 * rows * width, 320 * rows * width),
+        name="result",
+    )(place, resid, own, other, vectors)
+
+
+def pack_kernel(proj_ref, out_ref, up_ref, down_ref, vec_ref, narrow_ref, wide_ref):
+    columns = proj_ref.shape[2]
+    for pair in range(columns // 128):
+        for kind in range(3):
+            start = (pair * 3 + kind) * 128
+            narrow_ref[:, start : start + 128] = proj_ref[kind, :, pair * 128 : pair * 128 + 128]
+    narrow_ref[:, 3 * columns : 4 * columns] = out_ref[...]
+    turned = jnp.transpose(vec_ref[...].astype(jnp.float32))
+    turned = jnp.concatenate([turned, jnp.zeros((SLOT, 112), jnp.float32)], axis=1)
+    narrow_ref[:, 4 * columns :] = turned.astype(LOW)
+    hidden = up_ref.shape[1]
+    wide_ref[:, :hidden] = up_ref[...]
+    wide_ref[:, hidden:] = down_ref[...]
+
+
+def pack_shards(proj, out, up, down, vec):
+    rows, columns = out.shape
+    return pl.pallas_call(
+        pack_kernel,
+        out_shape=[
+            jax.ShapeDtypeStruct((rows, 4 * columns + 128), LOW),
+            jax.ShapeDtypeStruct((rows, 2 * up.shape[1]), LOW),
+        ],
+        compiler_params=settings(),
+        cost_estimate=cost(0, 4 * rows * (4 * columns + 2 * up.shape[1])),
+        name="pack",
+    )(proj, out, up, down, vec)
+
+
+def vector_kernel(place_ref, *refs):
+    pieces = refs[:-4]
+    slot_ref, bias_ref, hidden_ref, joined_ref = refs[-4:]
+    fill(joined_ref, pieces)
+    turned = jnp.transpose(joined_ref[...]).astype(jnp.float32)
+    slot_ref[...] = turned[0:8]
+    put_natural(place_ref, bias_ref, turned[8:16])
+    lane = lax.broadcasted_iota(jnp.int32, (1, 128), 1)
+    for pair in range(bias_ref.shape[1] // 128):
+        rows = [bias_ref[2 + q : 3 + q, pair * 128 : pair * 128 + 128] for q in range(4)]
+        flipped = [pltpu.roll(row, 64, 1) for row in rows]
+        for q in (0, 2):
+            start = pair * 512 + q * 64
+            hidden_ref[:, start : start + 128] = jnp.where(lane < 64, rows[q], flipped[q + 1])
+            hidden_ref[:, start + 256 : start + 384] = jnp.where(
+                lane < 64, flipped[q], rows[q + 1]
+            )
+
+
+def spread_vectors(place, pieces, index):
+    width = sum(piece.shape[0] for piece in pieces)
+    return pl.pallas_call(
+        vector_kernel,
+        grid_spec=pltpu.PrefetchScalarGridSpec(
+            num_scalar_prefetch=1,
+            grid=(1,),
+            in_specs=fixed_specs(pieces, 128, index),
+            out_specs=[whole((8, width)), whole((8, width)), whole((1, 4 * width))],
+            scratch_shapes=[pltpu.VMEM((width, 128), LOW)],
+        ),
+        out_shape=[
+            jax.ShapeDtypeStruct((8, width), jnp.float32),
+            jax.ShapeDtypeStruct((8, width), jnp.float32),
+            jax.ShapeDtypeStruct((1, 4 * width), jnp.float32),
+        ],
+        compiler_params=settings(),
+        cost_estimate=cost(width * 128, 2 * width * 128),
+        name="vectors",
+    )(place, *pieces)
+
+
+def after(value, *events):
+    return lax.optimization_barrier((value,) + events)[0]
+
+
+def dp_shift(value, ranks, dz, dy, dc):
+    far, near = 4, ranks // 8
+
+    def goes(rank):
+        z, y, c = rank // (near * 2), rank // 2 % near, rank % 2
+        return ((z + dz) % far * near + (y + dy) % near) * 2 + (c + dc) % 2
+
+    return lax.ppermute(value, "dp", [(rank, goes(rank)) for rank in range(ranks)])
+
+
+def dp_gather(shard, ranks):
+    far = [shard] + [dp_shift(shard, ranks, k, 0, 0) for k in (1, 2, 3)]
+    near = [dp_shift(piece, ranks, 0, 1, 0) for piece in far]
+    pieces = far + near
+    return pieces + [dp_shift(piece, ranks, 0, 0, 1) for piece in pieces], pieces
+
+
+def far_reduce(total, ranks, wire):
+    rows = total.shape[0] // 4
+    sent = {
+        k: dp_shift(total[k * rows : (k + 1) * rows].astype(wire), ranks, -k, 0, 0)
+        for k in (1, 3, 2)
+    }
+    result = total[:rows]
+    for k in (1, 2, 3):
+        result = result + sent[k].astype(jnp.float32)
+    return result
+
+
+def dp_reduce_small(grads, ranks):
+    near = ranks // 8
+    half = grads.shape[0] // 2
+    mine = grads[:half] + dp_shift(grads[half:], ranks, 0, 0, 1)
+    part = half // near
+    total = mine[:part]
+    for step in range(1, near):
+        total = total + dp_shift(mine[step * part : (step + 1) * part], ranks, 0, -step, 0)
+    return far_reduce(total, ranks, jnp.float32)
+
+
+def reduce_core(left, right, ranks):
+    half = left.shape[1] // 2
+    return dp_shift(contract_rows(left[:, half:], right).astype(LOW), ranks, 0, 0, 1)
+
+
+def reduce_near(left, right, other):
+    half = left.shape[1] // 2
+    part = half // 2
+    sent = contract_rows(left[:, part:half], right) + other[part:].astype(jnp.float32)
+    return sent.astype(LOW)
+
+
+def reduce_sum(left, right, other, arrived):
+    part = left.shape[1] // 4
+    total = contract_rows(left[:, :part], right) + other[:part].astype(jnp.float32)
+    return total + arrived.astype(jnp.float32)
+
+
+def far_send(total, ranks):
+    rows = total.shape[0] // 4
+    low = total.astype(LOW)
+    return [dp_shift(low[k * rows : (k + 1) * rows], ranks, -k, 0, 0) for k in (1, 3, 2)]
+
+
+def far_sum(total, sent):
+    result = total[: total.shape[0] // 4]
+    for value in sent:
+        result = result + value.astype(jnp.float32)
+    return result
+
+
+def swap(value):
+    return lax.ppermute(value, "tensor", [(0, 1), (1, 0)])
+
+
+def paired(
+    inputs,
+    out_grad,
+    parents,
+    ln1_gain,
+    ln1_bias,
+    w_qkv,
+    qv_bias,
+    w_attn_out,
+    attn_out_bias,
+    ln2_gain,
+    ln2_bias,
+    w_up,
+    up_bias,
+    w_down,
+    down_bias,
+):
+    ranks = lax.axis_size("dp")
+    near = ranks // 8
+    rank = lax.axis_index("dp")
+    side = lax.axis_index("tensor")
+    rows, width = inputs.shape
+    shard = width // ranks
+    heads_width = w_qkv.shape[2]
+    pairs = heads_width // 128
+    hidden = w_up.shape[1]
+    scale = 1.0 / math.sqrt(width // HEADS)
+
+    slots = jnp.arange(ranks, dtype=jnp.int32)
+    core_step, near_step, far_step = slots // (ranks // 2), slots // 4 % near, slots % 4
+    my_z, my_y, my_c = rank // (2 * near), rank // 2 % near, rank % 2
+    source = ((my_z - far_step) % 4 * near + (my_y - near_step) % near) * 2 + (
+        my_c + core_step
+    ) % 2
+    place = jnp.concatenate([jnp.stack([side, my_z, my_y, my_c]), source]).astype(jnp.int32)
+    feature = jnp.repeat(source * shard, shard) + jnp.tile(
+        jnp.arange(shard, dtype=jnp.int32), ranks
+    )
+    to_local = (jnp.arange(width, dtype=jnp.int32)[:, None] == feature[None, :]).astype(LOW)
+    slot_of = (slots[:, None] == source[None, :]).astype(jnp.float32)
+
+    zero = jnp.zeros_like(ln1_gain)
+    vec = [ln1_gain, ln1_bias, attn_out_bias, ln2_gain, ln2_bias, down_bias, zero, zero]
+    vec = jnp.concatenate(
+        [jnp.stack(vec), qv_bias, up_bias.reshape(4, shard), jnp.zeros((2, shard), LOW)], axis=0
+    )
+    narrow_shard, wide_shard = pack_shards(w_qkv, w_attn_out.T, w_up, w_down.T, vec)
+    inputs_other = swap(inputs)
+    grad_other = swap(after(out_grad, inputs_other))
+    narrow, narrow_far = dp_gather(narrow_shard, ranks)
+    wide = lax.all_gather(
+        after(wide_shard, inputs_other, *narrow_far[1:7]), "dp", axis=0, tiled=True
+    )
+    vectors, query_bias, hidden_bias = spread_vectors(place, narrow, 16)
+
+    def in_order(own, other):
+        return jnp.where(
+            side == 0,
+            jnp.concatenate([own, other], axis=0),
+            jnp.concatenate([other, own], axis=0),
+        )
+
+    hidden_in = matmul(
+        after(in_order(inputs, inputs_other), *narrow_far[1:4]), to_local
+    )
+    xhat, _ = row_stats(hidden_in)
+    hidden_in = hidden_in.astype(LOW)
+    norm_one, qkv, attended, logs = front(
+        place, xhat, vectors, query_bias, narrow, pairs, scale
+    )
+    share = share_product(after(attended, grad_other), narrow)
+    grad_rows = after(in_order(out_grad, grad_other), share)
+    cotangent = matmul(grad_rows, to_local).astype(LOW)
+    resid, lefts, rights, slope = up_product(
+        place, hidden_in, share, swap(share), vectors, hidden_bias, grad_rows, wide
+    )
+    own_out, other_out, dnorm_share, rights, dpre_sum = turn_product(
+        place, cotangent, rights, slope, wide
+    )
+    dnorm_other = swap(dnorm_share)
+    wide_share = lax.dot_general(
+        lefts,
+        after(rights, dnorm_share),
+        (((1,), (1,)), ((0,), (0,))),
+        preferred_element_type=jnp.float32,
+    ).astype(LOW)
+    wide_grad = lax.psum_scatter(wide_share, "dp", scatter_dimension=1, tiled=True)
+    dresid, dbranch, dattended, mid_sum = mid_product(
+        after(resid, wide_share),
+        dnorm_share,
+        dnorm_other,
+        cotangent,
+        vectors,
+        narrow,
+        heads_width,
+    )
+    dqkv, own_dnorm, other_dnorm, dqkv_sum, front_sum = back_product(
+        place, xhat, qkv, dattended, logs, narrow, scale
+    )
+    proj_core = reduce_core(norm_one, dqkv, ranks)
+    proj_near = reduce_near(norm_one, dqkv, proj_core)
+    proj_arrived = dp_shift(proj_near, ranks, 0, 1, 0)
+    out_core = reduce_core(dbranch, attended, ranks)
+    out_near = reduce_near(dbranch, attended, out_core)
+    out_arrived = dp_shift(after(out_near, proj_near), ranks, 0, 1, 0)
+    grad_back = wide_grad[0].T.astype(jnp.float32)
+    grad_hidden = wide_grad[1].astype(jnp.float32)
+    own_other, back_other = swap(other_out), swap(other_dnorm)
+    proj_total = reduce_sum(
+        norm_one, dqkv, proj_core, after(proj_arrived, own_other, back_other)
+    )
+    grad_proj = far_sum(proj_total, far_send(proj_total, ranks))
+    out_total = reduce_sum(dbranch, attended, out_core, out_arrived)
+    grad_out = far_sum(out_total, far_send(out_total, ranks)).T
+    result = result_product(
+        place, after(resid, proj_total, out_total), own_out, own_other, vectors
+    )
+    input_grad = last_product(
+        place,
+        hidden_in,
+        dresid,
+        own_dnorm,
+        after(back_other, proj_total, out_total),
+        vectors,
+    )
+    grad_proj = grad_proj.reshape(shard, pairs, 3, 128).transpose(2, 0, 1, 3)
+    grad_proj = grad_proj.reshape(3, shard, heads_width)
+
+    dqkv_sum = dqkv_sum[:, 0].reshape(pairs, 3, 128)
+    placed = [
+        place_block(value, 2 * value.shape[0], side * value.shape[0]).reshape(ranks, -1)
+        for value in (
+            dqkv_sum[:, 0].reshape(heads_width),
+            dqkv_sum[:, 2].reshape(heads_width),
+            dpre_sum[0],
+        )
+    ]
+    to_slot = lax.dot_general(
+        slot_of,
+        jnp.concatenate(placed, axis=1),
+        (((0,), (0,)), ((), ())),
+        precision=lax.Precision.HIGHEST,
+        preferred_element_type=jnp.float32,
+    )
+    pack = jnp.stack([front_sum[0], front_sum[1], mid_sum[2], mid_sum[0], mid_sum[1], mid_sum[3]])
+    pack = pack.reshape(6, ranks, shard).transpose(1, 0, 2).reshape(ranks, -1)
+    pack = after(jnp.concatenate([pack, to_slot], axis=1), proj_near)
+    pack = dp_reduce_small(pack + swap(pack), ranks)
+    pack = pack.reshape(-1)
+    vector_grads = [pack[i * shard : (i + 1) * shard] for i in range(6)]
+    return (
+        result,
+        input_grad,
+        vector_grads[0],
+        vector_grads[1],
+        grad_proj,
+        pack[6 * shard : 8 * shard].reshape(2, shard),
+        grad_out,
+        vector_grads[2],
+        vector_grads[3],
+        vector_grads[4],
+        grad_hidden,
+        pack[8 * shard :],
+        grad_back,
+        vector_grads[5],
+    )
+
+
+def local(*arrays):
+    fits = lax.axis_size("tensor") == 2 and lax.axis_size("dp") == 16
+    if fits and arrays[2].shape[1] == 3:
+        return paired(*arrays)
+    return generic(*arrays)
+
+
 def solution(mesh):
     return jax.shard_map(
         local,

time: 1050 us -> 332 us (0.32)
  waiting for transfers between devices: 670 us -> 114 us
  blocking collectives: 154 us -> 0 us
  Pallas kernels: 0 us -> 108 us
  matrix products: 118 us -> 30.2 us
  starting transfers between devices: 0.94 us -> 37.4 us
  other arithmetic: 43.5 us -> 7.55 us
  local copies, waits for them, and re-layouts: 38.4 us -> 14.5 us
    reduce_scatter x8 -> x1, waiting for transfers between devices: 436 us -> 0.01 us  [paired(): lax.psum_scatter(wide_share, 'dp', scatter_dimension=1, tiled=True)]
    all_gather x8 -> x1, waiting for transfers between devices: 215 us -> 0.01 us  [paired(): lax.all_gather(after(wide_shard, inputs_other, *narrow_far[1:7]), 'dp', a...]
    ppermute x0 -> x37, waiting for transfers between devices: none -> 113 us  [the longest x30 57.1 us: dp_shift(): lax.ppermute(value, 'dp', [(rank, goes(rank)) for rank in range(ranks)])]
    pallas_call x0 -> x10, Pallas kernels: none -> 108 us  [the longest x1 23.5 us: back_product(): pl.pallas_call(functools.partial(back_kernel, scale=scale, count=len(piec...]
    unnamed x2 -> x0, blocking collectives: 107 us -> none
    dot_general x27 -> x2, matrix products: 61 us -> 12.1 us  [the longest x1 11.9 us: paired(): lax.dot_general(lefts, after(rights, dnorm_share), (((1,), (1,)), ((0,),...]
    all_gather x2 -> x0, blocking collectives: 41.5 us -> none  [the longest x1 22.4 us: local(): lax.all_gather(qv_bias, 'dp', axis=1, tiled=True)]
    ppermute x0 -> x37, starting transfers between devices: none -> 37.3 us  [the longest x30 28.6 us: dp_shift(): lax.ppermute(value, 'dp', [(rank, goes(rank)) for rank in range(ranks)])]
  transfers between devices with their start and end apart: 17 -> 39, of which waited for: 17 -> 13; matrix products, arithmetic and copies ran while one was open for 10% -> 14% of each run, Pallas kernels for 0% -> 22%
where the time goes in v2:
time: 332 us; the launch traced here: 326 us
  waiting for transfers between devices  114 us (34%)
  Pallas kernels  108 us (33%)
  starting transfers between devices  37.4 us (11%)
  matrix products  30.2 us (9%)
  between operations  15.1 us (5%)
  local copies, waits for them, and re-layouts  14.5 us (4%)
  other arithmetic  7.55 us (2%)
    ppermute x30, waiting for transfers between devices, dp_shift(): lax.ppermute(value, 'dp', [(rank, goes(rank)) for rank in range(ranks)])  57.1 us
    ppermute x7, waiting for transfers between devices, swap(): return lax.ppermute(value, 'tensor', [(0, 1), (1, 0)])  56.4 us
    ppermute x30, starting transfers between devices, dp_shift(): lax.ppermute(value, 'dp', [(rank, goes(rank)) for rank in range(ranks)])  28.6 us
    pallas_call x1, Pallas kernels, back_product(): pl.pallas_call(functools.partial(back_kernel, scale=scale, count=len(piec...  23.5 us
    pallas_call x1, Pallas kernels, turn_product(): pl.pallas_call(turn_kernel, grid_spec=pltpu.PrefetchScalarGridSpec(num_sc...  21 us
    pallas_call x1, Pallas kernels, front(): pl.pallas_call(functools.partial(front_kernel, scale=scale, count=len(pie...  18.7 us
    pallas_call x1, Pallas kernels, up_product(): pl.pallas_call(up_kernel, grid_spec=pltpu.PrefetchScalarGridSpec(num_scal...  17 us
    dot_general x6, matrix products, contract_rows(): lax.dot_general(left, right, (((0,), (0,)), ((), ())), preferred_element_...  13.1 us
  transfers between devices with their start and end apart: 39, of which 13 were waited for; matrix products, arithmetic and copies ran while one was open for 14% of the time, Pallas kernels for 22%

profile of v2, /device:TPU:8, one launch (start us, length us, event | category | flops | bytes accessed | tf_op | source)
XLA Modules:
  0.0 326.5 jit_solution(12494280762424395791)
XLA Ops:
  9.5 2.6 concatenate.27.vec_ref
  12.1 2.1 pack.1
  20.4 14.8 %collective-permute-done.1.refs_1_ = bf16[64,2176]{1,0:T(8,128)(2,1)S(1)} collective-permute-done((bf16[64,2176]{1,0:T(8,128)(2,1)}, bf16[64,2176]{1,0:T(8,128)(2,1)S(1)}, u32[]{:S(2)}, u32[]{:S(2)}) %collective-permute-start.1) | collective-permute-done | bytes 278560 | tf_op jit(solution)/shard_map/ppermute | solution.py:972
  36.7 3.0 collective-permute-done.2.refs_2_
  42.5 5.2 %collective-permute-done.6.refs_6_ = bf16[64,2176]{1,0:T(8,128)(2,1)S(1)} collective-permute-done((bf16[64,2176]{1,0:T(8,128)(2,1)S(1)}, bf16[64,2176]{1,0:T(8,128)(2,1)S(1)}, u32[]{:S(2)}, u32[]{:S(2)}) %collective-permute-start.6) | collective-permute-done | bytes 278560 | tf_op jit(solution)/shard_map/ppermute | solution.py:972
  51.6 1.9 fusion.49
  54.5 3.2 collective-permute-done.7.refs_7_
  58.4 2.7 subtract_multiply_fusion
  63.4 2.5 vectors.1
  65.9 18.7 %front.1 = (bf16[768,1024]{1,0:T(8,128)(2,1)}, bf16[768,1536]{1,0:T(8,128)(2,1)}, bf16[768,512]{1,0:T(8,128)(2,1)}, f32[4,8,768]{2,1,0:T(8,128)}) custom-call(s32[20]{0:T(128)} %concatenate.24.place_ref, f32[768,1024]{1,0:T(8,128)} %get-tuple-element.94.xhat_ref, f32[8,1024]{1,0:T(8,128)} %get-tuple-element.55.vec_ref, ...), custom_call_target="tpu_custom_call" | custom-call | flops 9663676416 | bytes 9437184 | tf_op jit(solution)/shard_map/front/pallas_call | solution.py:429
  84.6 4.3 %share.1.own_ref = bf16[768,1024]{1,0:T(8,128)(2,1)} custom-call(bf16[768,512]{1,0:T(8,128)(2,1)} %get-tuple-element.59.att_ref, bf16[64,2176]{1,0:T(8,128)(2,1)} %get-tuple-element.53.refs_0_, bf16[64,2176]{1,0:T(8,128)(2,1)} %copy-done.4, bf16[64,2176]{1,0:T(8,128)(2,1)} %copy-done.5, bf16[64,2176]{1,0:T(8,128)(2,1)} %copy-done.6, ...), custom_call_target="tpu_custom_call" | custom-call | flops 805306368 | bytes 3145728 | tf_op jit(solution)/shard_map/share/pallas_call | solution.py:473
  91.1 3.0 fusion.6.grad_ref
  94.1 31.5 %collective-permute-done.17.other_ref = bf16[768,1024]{1,0:T(8,128)(2,1)S(1)} collective-permute-done((bf16[768,1024]{1,0:T(8,128)(2,1)}, bf16[768,1024]{1,0:T(8,128)(2,1)S(1)}, u32[]{:S(2)}, u32[]{:S(2)}) %collective-permute-start.17) | collective-permute-done | bytes 1572896 | tf_op jit(solution)/shard_map/ppermute | solution.py:1037
  126.7 17.0 %up.1 = (f32[768,1024]{1,0:T(8,128)}, bf16[2,768,1024]{2,1,0:T(8,128)(2,1)}, bf16[2,768,2048]{2,1,0:T(8,128)(2,1)}, bf16[768,2048]{1,0:T(8,128)(2,1)}) custom-call(s32[20]{0:T(128)} %concatenate.24.place_ref, bf16[768,1024]{1,0:T(8,128)(2,1)} %get-tuple-element.95.x_ref, bf16[768,1024]{1,0:T(8,128)(2,1)} %share.1.own_ref, bf16[768,1024]{1,0:T(8,128)(2,1)} %copy-done.27, ...), custom_call_target="tpu_custom_call" | custom-call | flops 4831838208 | bytes 12582912 | tf_op jit(solution)/shard_map/up/pallas_call | solution.py:529
  143.7 21.0 %turn.1 = (f32[384,1024]{1,0:T(8,128)}, bf16[384,1024]{1,0:T(8,128)(2,1)}, bf16[768,1024]{1,0:T(8,128)(2,1)}, bf16[2,768,2048]{2,1,0:T(8,128)(2,1)}, f32[8,2048]{1,0:T(8,128)}) custom-call(s32[20]{0:T(128)} %concatenate.24.place_ref, bf16[768,1024]{1,0:T(8,128)(2,1)} %fusion.6.grad_ref, ...), custom_call_target="tpu_custom_call", output_to_operand_aliasing={{3}: (2, {})} | custom-call | flops 9663676416 | bytes 18874368 | tf_op jit(solution)/shard_map/turn/pallas_call | solution.py:619
  166.2 11.9 %convolution_convert_fusion = bf16[2,1024,2048]{2,1,0:T(8,128)(2,1)} fusion(bf16[2,768,1024]{2,1,0:T(8,128)(2,1)S(1)} %copy-done.28, bf16[2,768,2048]{2,1,0:T(8,128)(2,1)} %get-tuple-element.72), kind=kOutput, calls=%fused_computation | convolution fusion | flops 6446645248 | bytes 17825792 | tf_op jit(solution)/shard_map/dot_general | solution.py:1120
  178.2 22.4 %collective-permute-done.18.other_ref = bf16[768,1024]{1,0:T(8,128)(2,1)S(1)} collective-permute-done((bf16[768,1024]{1,0:T(8,128)(2,1)}, bf16[768,1024]{1,0:T(8,128)(2,1)S(1)}, u32[]{:S(2)}, u32[]{:S(2)}) %collective-permute-start.18) | collective-permute-done | bytes 1572896 | tf_op jit(solution)/shard_map/ppermute | solution.py:1037
  201.7 8.4 %mid.1 = (f32[768,1024]{1,0:T(8,128)}, bf16[768,1024]{1,0:T(8,128)(2,1)}, bf16[768,512]{1,0:T(8,128)(2,1)}, f32[8,1024]{1,0:T(8,128)}) custom-call(f32[768,1024]{1,0:T(8,128)} %get-tuple-element.82.resid_ref, bf16[768,1024]{1,0:T(8,128)(2,1)} %get-tuple-element.71.own_ref, bf16[768,1024]{1,0:T(8,128)(2,1)} %copy-done.26, bf16[768,1024]{1,0:T(8,128)(2,1)} %fusion.6.grad_ref, ...), custom_call_target="tpu_custom_call" | custom-call | flops 12884901888 | bytes 12582912 | tf_op jit(solution)/shard_map/mid/pallas_call | solution.py:683
  210.1 23.5 %back.1 = (bf16[768,1536]{1,0:T(8,128)(2,1)}, f32[384,1024]{1,0:T(8,128)}, bf16[384,1024]{1,0:T(8,128)(2,1)}, f32[4,8,384]{2,1,0:T(8,128)}, f32[8,1024]{1,0:T(8,128)}) custom-call(s32[20]{0:T(128)} %concatenate.24.place_ref, f32[768,1024]{1,0:T(8,128)} %get-tuple-element.94.xhat_ref, bf16[768,1536]{1,0:T(8,128)(2,1)} %get-tuple-element.66.qkv_ref, ...), custom_call_target="tpu_custom_call" | custom-call | flops 115964116992 | bytes 9437184 | tf_op jit(solution)/shard_map/back/pallas_call | solution.py:776
  233.6 4.4 %convolution_convert_fusion.1 = bf16[512,1536]{1,0:T(8,128)(2,1)} fusion(bf16[768,1536]{1,0:T(8,128)(2,1)} %get-tuple-element.76, bf16[768,1024]{1,0:T(8,128)(2,1)S(1)} %copy-done.2), kind=kOutput, calls=%fused_computation.5 | convolution fusion | flops 1208745984 | bytes 4718592 | tf_op jit(solution)/shard_map/dot_general | solution.py:37
  241.8 3.1 fusion.3
  246.5 2.6 collective-permute-done.25
  254.6 2.2 collective-permute-start.29
  256.8 2.0 collective-permute-start.28
  263.8 25.4 %collective-permute-done.24 = bf16[256,512]{1,0:T(8,128)(2,1)S(1)} collective-permute-done((bf16[256,512]{1,0:T(8,128)(2,1)}, bf16[256,512]{1,0:T(8,128)(2,1)S(1)}, u32[]{:S(2)}, u32[]{:S(2)}) %collective-permute-start.24) | collective-permute-done | bytes 262176 | tf_op jit(solution)/shard_map/ppermute | solution.py:972
  293.3 2.4 fusion.50
  295.7 2.5 collective-permute-start.33
  298.2 2.1 collective-permute-start.32
  300.3 3.8 %collective-permute-done.34 = bf16[64,512]{1,0:T(8,128)(2,1)S(1)} collective-permute-done((bf16[64,512]{1,0:T(8,128)(2,1)S(1)}, bf16[64,512]{1,0:T(8,128)(2,1)S(1)}, u32[]{:S(2)}, u32[]{:S(2)}) %collective-permute-start.34) | collective-permute-done | bytes 65568 | tf_op jit(solution)/shard_map/ppermute | solution.py:972
  304.8 5.0 %result.1 = bf16[384,1024]{1,0:T(8,128)(2,1)} custom-call(s32[20]{0:T(128)} %concatenate.24.place_ref, f32[768,1024]{1,0:T(8,128)} %get-tuple-element.82.resid_ref, f32[384,1024]{1,0:T(8,128)} %get-tuple-element.83.own_ref, bf16[384,1024]{1,0:T(8,128)(2,1)} %collective-permute-done.21.other_ref, f32[8,1024]{1,0:T(8,128)} %get-tuple-element.55.vec_ref), custom_call_target="tpu_custom_call" | custom-call | flops 3932160 | bytes 125829120 | tf_op jit(solution)/shard_map/result/pallas_call | solution.py:876
  309.9 5.8 %last.1 = f32[384,1024]{1,0:T(8,128)} custom-call(s32[20]{0:T(128)} %concatenate.24.place_ref, bf16[768,1024]{1,0:T(8,128)(2,1)} %get-tuple-element.95.x_ref, f32[768,1024]{1,0:T(8,128)} %get-tuple-element.84.dresid_ref, f32[384,1024]{1,0:T(8,128)} %get-tuple-element.85.own_ref, bf16[384,1024]{1,0:T(8,128)(2,1)} %collective-permute-done.22.other_ref, ...), custom_call_target="tpu_custom_call" | custom-call | flops 15728640 | bytes 125829120 | tf_op jit(solution)/shard_map/last/pallas_call | solution.py:849
  317.1 2.1 convert_bitcast_fusion
  (178 shorter events, 48.4 us)
Async XLA Ops:
  7.2 118.4 %all-gather.2.cloned.1.call-start = ((), (), s32[]{:S(2)}) async-start(), calls=%async_computation.1 | async-start | bytes 8912896 | tf_op jit(solution)/shard_map/all_gather | solution.py:1090
  7.2 40.5 %collective-permute-start = (bf16[384,1024]{1,0:T(8,128)(2,1)}, bf16[384,1024]{1,0:T(8,128)(2,1)S(1)}, u32[]{:S(2)}, u32[]{:S(2)}) collective-permute-start(bf16[384,1024]{1,0:T(8,128)(2,1)} %param.15), channel_id=1, source_target_pairs={{0,1},{1,0},{2,3},{3,2},{4,5},{5,4},{6,7},{7,6},{8,9},{9,8},{10,11... | collective-permute-start | bytes 2359304 | tf_op jit(solution)/shard_map/ppermute | solution.py:1037
  14.2 20.9 %collective-permute-start.1 = (bf16[64,2176]{1,0:T(8,128)(2,1)}, bf16[64,2176]{1,0:T(8,128)(2,1)S(1)}, u32[]{:S(2)}, u32[]{:S(2)}) collective-permute-start(bf16[64,2176]{1,0:T(8,128)(2,1)} %get-tuple-element.53.refs_0_), channel_id=1, source_target_pairs={{0,8},{2,10},{4,12},{6,14},{8,16},{10,18},{12,20},{14,22},{16,24},... | collective-permute-start | bytes 835592 | tf_op jit(solution)/shard_map/ppermute | solution.py:972
  15.8 23.9 %collective-permute-start.2 = (bf16[64,2176]{1,0:T(8,128)(2,1)}, bf16[64,2176]{1,0:T(8,128)(2,1)S(1)}, u32[]{:S(2)}, u32[]{:S(2)}) collective-permute-start(bf16[64,2176]{1,0:T(8,128)(2,1)} %get-tuple-element.53.refs_0_), channel_id=1, source_target_pairs={{0,16},{2,18},{4,20},{6,22},{8,24},{10,26},{12,28},{14,30},{16,0},... | collective-permute-start | bytes 835592 | tf_op jit(solution)/shard_map/ppermute | solution.py:972
  17.0 24.3 %collective-permute-start.3 = (bf16[64,2176]{1,0:T(8,128)(2,1)}, bf16[64,2176]{1,0:T(8,128)(2,1)S(1)}, u32[]{:S(2)}, u32[]{:S(2)}) collective-permute-start(bf16[64,2176]{1,0:T(8,128)(2,1)} %get-tuple-element.53.refs_0_), channel_id=1, source_target_pairs={{0,24},{2,26},{4,28},{6,30},{8,0},{10,2},{12,4},{14,6},{16,8},{18,... | collective-permute-start | bytes 835592 | tf_op jit(solution)/shard_map/ppermute | solution.py:972
  18.9 22.5 %collective-permute-start.4 = (bf16[64,2176]{1,0:T(8,128)(2,1)}, bf16[64,2176]{1,0:T(8,128)(2,1)S(1)}, u32[]{:S(2)}, u32[]{:S(2)}) collective-permute-start(bf16[64,2176]{1,0:T(8,128)(2,1)} %get-tuple-element.53.refs_0_), channel_id=1, source_target_pairs={{0,4},{2,6},{4,0},{6,2},{8,12},{10,14},{12,8},{14,10},{16,20},{18,... | collective-permute-start | bytes 835592 | tf_op jit(solution)/shard_map/ppermute | solution.py:972
  35.2 7.3 %collective-permute-start.5 = (bf16[64,2176]{1,0:T(8,128)(2,1)S(1)}, bf16[64,2176]{1,0:T(8,128)(2,1)S(1)}, u32[]{:S(2)}, u32[]{:S(2)}) collective-permute-start(bf16[64,2176]{1,0:T(8,128)(2,1)S(1)} %collective-permute-done.1.refs_1_), channel_id=1, source_target_pairs={{0,4},{2,6},{4,0},{6,2},{8,12},{10,14},{12,8},{14,10},{16,20},{18,... | collective-permute-start | bytes 835592 | tf_op jit(solution)/shard_map/ppermute | solution.py:972
  39.7 8.0 %collective-permute-start.6 = (bf16[64,2176]{1,0:T(8,128)(2,1)S(1)}, bf16[64,2176]{1,0:T(8,128)(2,1)S(1)}, u32[]{:S(2)}, u32[]{:S(2)}) collective-permute-start(bf16[64,2176]{1,0:T(8,128)(2,1)S(1)} %collective-permute-done.2.refs_2_), channel_id=1, source_target_pairs={{0,4},{2,6},{4,0},{6,2},{8,12},{10,14},{12,8},{14,10},{16,20},{18,... | collective-permute-start | bytes 835592 | tf_op jit(solution)/shard_map/ppermute | solution.py:972
  47.7 269.4 %reduce-scatter.2.cloned.1.call-start = ((), (), s32[]{:S(2)}) async-start(), calls=%async_computation.2 | async-start | bytes 8912896 | tf_op jit(solution)/shard_map/reduce_scatter | solution.py:1126
  47.8 6.3 %collective-permute-start.8 = (bf16[64,2176]{1,0:T(8,128)(2,1)}, bf16[64,2176]{1,0:T(8,128)(2,1)S(1)}, u32[]{:S(2)}, u32[]{:S(2)}) collective-permute-start(bf16[64,2176]{1,0:T(8,128)(2,1)} %get-tuple-element.53.refs_0_), channel_id=1, source_target_pairs={{0,2},{2,0},{4,6},{6,4},{8,10},{10,8},{12,14},{14,12},{16,18},{18,... | collective-permute-start | bytes 835592 | tf_op jit(solution)/shard_map/ppermute | solution.py:972
  48.7 9.0 %collective-permute-start.7 = (bf16[64,2176]{1,0:T(8,128)(2,1)S(1)}, bf16[64,2176]{1,0:T(8,128)(2,1)S(1)}, u32[]{:S(2)}, u32[]{:S(2)}) collective-permute-start(bf16[64,2176]{1,0:T(8,128)(2,1)S(1)} %collective-permute-done.3.refs_3_), channel_id=1, source_target_pairs={{0,4},{2,6},{4,0},{6,2},{8,12},{10,14},{12,8},{14,10},{16,20},{18,... | collective-permute-start | bytes 835592 | tf_op jit(solution)/shard_map/ppermute | solution.py:972
  50.2 7.5 %collective-permute-start.9 = (bf16[64,2176]{1,0:T(8,128)(2,1)S(1)}, bf16[64,2176]{1,0:T(8,128)(2,1)S(1)}, u32[]{:S(2)}, u32[]{:S(2)}) collective-permute-start(bf16[64,2176]{1,0:T(8,128)(2,1)S(1)} %collective-permute-done.1.refs_1_), channel_id=1, source_target_pairs={{0,2},{2,0},{4,6},{6,4},{8,10},{10,8},{12,14},{14,12},{16,18},{18,... | collective-permute-start | bytes 835592 | tf_op jit(solution)/shard_map/ppermute | solution.py:972
  50.4 7.9 %collective-permute-start.10 = (bf16[64,2176]{1,0:T(8,128)(2,1)S(1)}, bf16[64,2176]{1,0:T(8,128)(2,1)S(1)}, u32[]{:S(2)}, u32[]{:S(2)}) collective-permute-start(bf16[64,2176]{1,0:T(8,128)(2,1)S(1)} %collective-permute-done.2.refs_2_), channel_id=1, source_target_pairs={{0,2},{2,0},{4,6},{6,4},{8,10},{10,8},{12,14},{14,12},{16,18},{18,... | collective-permute-start | bytes 835592 | tf_op jit(solution)/shard_map/ppermute | solution.py:972
  50.7 10.4 %collective-permute-start.11 = (bf16[64,2176]{1,0:T(8,128)(2,1)S(1)}, bf16[64,2176]{1,0:T(8,128)(2,1)S(1)}, u32[]{:S(2)}, u32[]{:S(2)}) collective-permute-start(bf16[64,2176]{1,0:T(8,128)(2,1)S(1)} %collective-permute-done.3.refs_3_), channel_id=1, source_target_pairs={{0,2},{2,0},{4,6},{6,4},{8,10},{10,8},{12,14},{14,12},{16,18},{18,... | collective-permute-start | bytes 835592 | tf_op jit(solution)/shard_map/ppermute | solution.py:972
  54.0 7.7 %collective-permute-start.12 = (bf16[64,2176]{1,0:T(8,128)(2,1)S(1)}, bf16[64,2176]{1,0:T(8,128)(2,1)S(1)}, u32[]{:S(2)}, u32[]{:S(2)}) collective-permute-start(bf16[64,2176]{1,0:T(8,128)(2,1)S(1)} %collective-permute-done.4.refs_4_), channel_id=1, source_target_pairs={{0,2},{2,0},{4,6},{6,4},{8,10},{10,8},{12,14},{14,12},{16,18},{18,... | collective-permute-start | bytes 835592 | tf_op jit(solution)/shard_map/ppermute | solution.py:972
  61.1 23.5 %collective-permute-start.16 = (bf16[384,1024]{1,0:T(8,128)(2,1)S(1)}, bf16[384,1024]{1,0:T(8,128)(2,1)S(1)}, u32[]{:S(2)}, u32[]{:S(2)}) collective-permute-start(bf16[384,1024]{1,0:T(8,128)(2,1)S(1)} %copy-done.20), channel_id=1, source_target_pairs={{0,1},{1,0},{2,3},{3,2},{4,5},{5,4},{6,7},{7,6},{8,9},{9,8},{10,11... | collective-permute-start | bytes 2359304 | tf_op jit(solution)/shard_map/ppermute | solution.py:1037
  88.9 36.6 %collective-permute-start.17 = (bf16[768,1024]{1,0:T(8,128)(2,1)}, bf16[768,1024]{1,0:T(8,128)(2,1)S(1)}, u32[]{:S(2)}, u32[]{:S(2)}) collective-permute-start(bf16[768,1024]{1,0:T(8,128)(2,1)} %share.1.own_ref), channel_id=1, source_target_pairs={{0,1},{1,0},{2,3},{3,2},{4,5},{5,4},{6,7},{7,6},{8,9},{9,8},{10,11... | collective-permute-start | bytes 4718600 | tf_op jit(solution)/shard_map/ppermute | solution.py:1037
  164.7 35.8 %collective-permute-start.18 = (bf16[768,1024]{1,0:T(8,128)(2,1)}, bf16[768,1024]{1,0:T(8,128)(2,1)S(1)}, u32[]{:S(2)}, u32[]{:S(2)}) collective-permute-start(bf16[768,1024]{1,0:T(8,128)(2,1)} %get-tuple-element.71.own_ref), channel_id=1, source_target_pairs={{0,1},{1,0},{2,3},{3,2},{4,5},{5,4},{6,7},{7,6},{8,9},{9,8},{10,11... | collective-permute-start | bytes 4718600 | tf_op jit(solution)/shard_map/ppermute | solution.py:1037
  249.8 7.0 %collective-permute-start.23 = (bf16[512,512]{1,0:T(8,128)(2,1)S(1)}, bf16[512,512]{1,0:T(8,128)(2,1)S(1)}, u32[]{:S(2)}, u32[]{:S(2)}) collective-permute-start(bf16[512,512]{1,0:T(8,128)(2,1)S(1)} %convolution_convert_fusion.2), channel_id=1, source_target_pairs={{0,2},{2,0},{4,6},{6,4},{8,10},{10,8},{12,14},{14,12},{16,18},{18,... | collective-permute-start | bytes 1572872 | tf_op jit(solution)/shard_map/ppermute | solution.py:972
  251.9 40.5 %collective-permute-start.21 = (bf16[384,1024]{1,0:T(8,128)(2,1)}, bf16[384,1024]{1,0:T(8,128)(2,1)}, u32[]{:S(2)}, u32[]{:S(2)}) collective-permute-start(bf16[384,1024]{1,0:T(8,128)(2,1)} %get-tuple-element.77), channel_id=1, source_target_pairs={{0,1},{1,0},{2,3},{3,2},{4,5},{5,4},{6,7},{7,6},{8,9},{9,8},{10,11... | collective-permute-start | bytes 2359304 | tf_op jit(solution)/shard_map/ppermute | solution.py:1037
  253.4 39.8 %collective-permute-start.22 = (bf16[384,1024]{1,0:T(8,128)(2,1)}, bf16[384,1024]{1,0:T(8,128)(2,1)}, u32[]{:S(2)}, u32[]{:S(2)}) collective-permute-start(bf16[384,1024]{1,0:T(8,128)(2,1)} %get-tuple-element.78), channel_id=1, source_target_pairs={{0,1},{1,0},{2,3},{3,2},{4,5},{5,4},{6,7},{7,6},{8,9},{9,8},{10,11... | collective-permute-start | bytes 2359304 | tf_op jit(solution)/shard_map/ppermute | solution.py:1037
  254.1 5.8 %collective-permute-start.30 = (f32[1,768]{1,0:T(1,128)S(1)}, f32[1,768]{1,0:T(1,128)S(1)}, u32[]{:S(2)}, u32[]{:S(2)}) collective-permute-start(f32[1,768]{1,0:T(1,128)S(1)} %get-tuple-element.107), channel_id=1, source_target_pairs={{0,8},{2,10},{4,12},{6,14},{8,16},{10,18},{12,20},{14,22},{16,24},... | collective-permute-start | bytes 9224 | tf_op jit(solution)/shard_map/ppermute | solution.py:972
  254.6 6.8 %collective-permute-start.29 = (f32[1,768]{1,0:T(1,128)S(1)}, f32[1,768]{1,0:T(1,128)S(1)}, u32[]{:S(2)}, u32[]{:S(2)}) collective-permute-start(f32[1,768]{1,0:T(1,128)S(1)} %get-tuple-element.108), channel_id=1, source_target_pairs={{0,16},{2,18},{4,20},{6,22},{8,24},{10,26},{12,28},{14,30},{16,0},... | collective-permute-start | bytes 9224 | tf_op jit(solution)/shard_map/ppermute | solution.py:972
  256.8 5.1 %collective-permute-start.28 = (f32[1,768]{1,0:T(1,128)S(1)}, f32[1,768]{1,0:T(1,128)S(1)}, u32[]{:S(2)}, u32[]{:S(2)}) collective-permute-start(f32[1,768]{1,0:T(1,128)S(1)} %get-tuple-element.106), channel_id=1, source_target_pairs={{0,24},{2,26},{4,28},{6,30},{8,0},{10,2},{12,4},{14,6},{16,8},{18,... | collective-permute-start | bytes 9224 | tf_op jit(solution)/shard_map/ppermute | solution.py:972
  259.9 33.4 %collective-permute-start.20 = (bf16[256,1536]{1,0:T(8,128)(2,1)}, bf16[256,1536]{1,0:T(8,128)(2,1)}, u32[]{:S(2)}, u32[]{:S(2)}) collective-permute-start(bf16[256,1536]{1,0:T(8,128)(2,1)} %fusion.3), channel_id=1, source_target_pairs={{0,4},{2,6},{4,0},{6,2},{8,12},{10,14},{12,8},{14,10},{16,20},{18,... | collective-permute-start | bytes 2359304 | tf_op jit(solution)/shard_map/ppermute | solution.py:972
  261.5 27.7 %collective-permute-start.24 = (bf16[256,512]{1,0:T(8,128)(2,1)}, bf16[256,512]{1,0:T(8,128)(2,1)S(1)}, u32[]{:S(2)}, u32[]{:S(2)}) collective-permute-start(bf16[256,512]{1,0:T(8,128)(2,1)} %fusion.8), channel_id=1, source_target_pairs={{0,4},{2,6},{4,0},{6,2},{8,12},{10,14},{12,8},{14,10},{16,20},{18,... | collective-permute-start | bytes 786440 | tf_op jit(solution)/shard_map/ppermute | solution.py:972
  290.6 9.7 %collective-permute-start.36 = (bf16[64,512]{1,0:T(8,128)(2,1)S(1)}, bf16[64,512]{1,0:T(8,128)(2,1)S(1)}, u32[]{:S(2)}, u32[]{:S(2)}) collective-permute-start(bf16[64,512]{1,0:T(8,128)(2,1)S(1)} %get-tuple-element.102), channel_id=1, source_target_pairs={{0,16},{2,18},{4,20},{6,22},{8,24},{10,26},{12,28},{14,30},{16,0},... | collective-permute-start | bytes 196616 | tf_op jit(solution)/shard_map/ppermute | solution.py:972
  291.2 9.1 %collective-permute-start.35 = (bf16[64,512]{1,0:T(8,128)(2,1)S(1)}, bf16[64,512]{1,0:T(8,128)(2,1)S(1)}, u32[]{:S(2)}, u32[]{:S(2)}) collective-permute-start(bf16[64,512]{1,0:T(8,128)(2,1)S(1)} %get-tuple-element.103), channel_id=1, source_target_pairs={{0,8},{2,10},{4,12},{6,14},{8,16},{10,18},{12,20},{14,22},{16,24},... | collective-permute-start | bytes 196616 | tf_op jit(solution)/shard_map/ppermute | solution.py:972
  292.5 11.7 %collective-permute-start.34 = (bf16[64,512]{1,0:T(8,128)(2,1)S(1)}, bf16[64,512]{1,0:T(8,128)(2,1)S(1)}, u32[]{:S(2)}, u32[]{:S(2)}) collective-permute-start(bf16[64,512]{1,0:T(8,128)(2,1)S(1)} %get-tuple-element.101), channel_id=1, source_target_pairs={{0,24},{2,26},{4,28},{6,30},{8,0},{10,2},{12,4},{14,6},{16,8},{18,... | collective-permute-start | bytes 196616 | tf_op jit(solution)/shard_map/ppermute | solution.py:972
  295.7 20.0 %collective-permute-start.33 = (bf16[64,1536]{1,0:T(8,128)(2,1)S(1)}, bf16[64,1536]{1,0:T(8,128)(2,1)S(1)}, u32[]{:S(2)}, u32[]{:S(2)}) collective-permute-start(bf16[64,1536]{1,0:T(8,128)(2,1)S(1)} %get-tuple-element.97), channel_id=1, source_target_pairs={{0,16},{2,18},{4,20},{6,22},{8,24},{10,26},{12,28},{14,30},{16,0},... | collective-permute-start | bytes 589832 | tf_op jit(solution)/shard_map/ppermute | solution.py:972
  298.2 17.5 %collective-permute-start.32 = (bf16[64,1536]{1,0:T(8,128)(2,1)S(1)}, bf16[64,1536]{1,0:T(8,128)(2,1)S(1)}, u32[]{:S(2)}, u32[]{:S(2)}) collective-permute-start(bf16[64,1536]{1,0:T(8,128)(2,1)S(1)} %get-tuple-element.98), channel_id=1, source_target_pairs={{0,8},{2,10},{4,12},{6,14},{8,16},{10,18},{12,20},{14,22},{16,24},... | collective-permute-start | bytes 589832 | tf_op jit(solution)/shard_map/ppermute | solution.py:972
  300.3 15.4 %collective-permute-start.31 = (bf16[64,1536]{1,0:T(8,128)(2,1)S(1)}, bf16[64,1536]{1,0:T(8,128)(2,1)S(1)}, u32[]{:S(2)}, u32[]{:S(2)}) collective-permute-start(bf16[64,1536]{1,0:T(8,128)(2,1)S(1)} %get-tuple-element.96), channel_id=1, source_target_pairs={{0,24},{2,26},{4,28},{6,30},{8,0},{10,2},{12,4},{14,6},{16,8},{18,... | collective-permute-start | bytes 589832 | tf_op jit(solution)/shard_map/ppermute | solution.py:972
  (36 other events, 269.8 us)
Sparse Core Ops, SparseCore 0:
  47.8 74.4 all-gather.1
  178.3 109.3 reduce-scatter.1

commit v3 on v2

--- a/solution.py
+++ b/solution.py
@@ -328,8 +328,8 @@
 SLOT = 64
 
 
-def settings():
-    return pltpu.CompilerParams(vmem_limit_bytes=56 * 2**20)
+def settings(mib):
+    return pltpu.CompilerParams(vmem_limit_bytes=mib * 2**20)
 
 
 def cost(flops, moved, exps=0):
@@ -352,17 +352,10 @@
     return [pl.BlockSpec((piece.shape[0], block), lambda *_: (0, index)) for piece in pieces]
 
 
-def fill(scratch, refs):
-    row = 0
-    for ref in refs:
-        scratch[row : row + ref.shape[0], :] = ref[...]
-        row += ref.shape[0]
-
-
-def fill_slots(place_ref, scratch, ref):
-    for slot in range(scratch.shape[0] // SLOT):
+def fill_natural(place_ref, scratch, refs):
+    for slot, ref in enumerate(refs):
         start = pl.multiple_of(place_ref[4 + slot] * SLOT, SLOT)
-        scratch[slot * SLOT : slot * SLOT + SLOT, :] = ref[pl.ds(start, SLOT), :]
+        scratch[pl.ds(start, SLOT), :] = ref[...]
 
 
 def row_stats(rows):
@@ -385,291 +378,209 @@
 def attend_pair(qkv_ref, out_ref, log_ref, scale):
     length = qkv_ref.shape[0]
     lane = lax.broadcasted_iota(jnp.int32, (SEG, 128), 1)
-    key = qkv_ref[:, 128:256]
+    reach = lax.broadcasted_iota(jnp.int32, (SEG, SEG), 0) <= lax.broadcasted_iota(
+        jnp.int32, (SEG, SEG), 1
+    )
     value_t = jnp.transpose(qkv_ref[:, 256:384])
     for seg in range(length // SEG):
-        keys_here = (seg + 1) * SEG
-        query = qkv_ref[seg * SEG : keys_here, 0:128] * scale
-        key_pos = lax.broadcasted_iota(jnp.int32, (keys_here, SEG), 0)
-        query_pos = lax.broadcasted_iota(jnp.int32, (keys_here, SEG), 1) + seg * SEG
+        before = seg * SEG
+        rows = slice(before, before + SEG)
+        query = qkv_ref[rows, 0:128] * scale
         parts = []
         for head in range(2):
+            lanes = slice(head * 64, head * 64 + 64)
             mine = jnp.where(lane // 64 == head, query, jnp.zeros_like(query))
-            scores = contract_last(key[:keys_here], mine)
-            scores = jnp.where(key_pos <= query_pos, scores, -1e30)
+            scores = contract_last(qkv_ref[rows, 128:256], mine)
+            scores = jnp.where(reach, scores, -1e30)
             top = jnp.max(scores, axis=0, keepdims=True)
+            if seg > 0:
+                early = contract_last(qkv_ref[0:before, 128:256], mine)
+                top = jnp.maximum(top, jnp.max(early, axis=0, keepdims=True))
             expo = jnp.exp(scores - top)
             total = jnp.sum(expo, axis=0, keepdims=True)
-            mixed = matmul(value_t[head * 64 : head * 64 + 64, :keys_here], expo.astype(LOW))
+            mixed = matmul(value_t[lanes, rows], expo.astype(LOW))
+            if seg > 0:
+                expo = jnp.exp(early - top)
+                total = total + jnp.sum(expo, axis=0, keepdims=True)
+                mixed = mixed + matmul(value_t[lanes, 0:before], expo.astype(LOW))
             parts.append(mixed / total)
-            log_ref[0, head : head + 1, seg * SEG : keys_here] = top + jnp.log(total)
-        out_ref[seg * SEG : keys_here, :] = jnp.transpose(jnp.concatenate(parts, axis=0)).astype(
-            LOW
-        )
-
-
-def front_kernel(place_ref, xhat_ref, vec_ref, bias_ref, *refs, scale, count):
-    pieces = refs[:count]
-    norm_ref, qkv_ref, out_ref, log_ref, weight_ref = refs[count:]
-
-    @pl.when(pl.program_id(0) == 0)
+            log_ref[0, head : head + 1, rows] = top + jnp.log(total)
+        out_ref[rows, :] = jnp.transpose(jnp.concatenate(parts, axis=0)).astype(LOW)
+
+
+def front_kernel(place_ref, x_ref, vec_ref, bias_ref, *refs, scale, count):
+    pieces, outs = refs[:count], refs[count : 2 * count]
+    xhat_ref, norm_ref, qkv_ref, att_ref, log_ref, share_ref = refs[2 * count : 2 * count + 6]
+    weight_ref, out_ref, joined_ref = refs[2 * count + 6 :]
+    length = x_ref.shape[0]
+    step = pl.program_id(0)
+
+    @pl.when(step == 0)
     def _():
-        norm_ref[...] = (xhat_ref[...] * vec_ref[0:1, :] + vec_ref[1:2, :]).astype(LOW)
-
-    fill(weight_ref, pieces)
+        for start in range(0, length, SEG):
+            rows = slice(start, start + SEG)
+            xhat, _ = row_stats(x_ref[rows, :].astype(jnp.float32))
+            xhat_ref[rows, :] = xhat.astype(LOW)
+            norm_ref[rows, :] = (xhat * vec_ref[0:1, :] + vec_ref[1:2, :]).astype(LOW)
+        fill_natural(place_ref, out_ref, outs)
+
+    fill_natural(place_ref, weight_ref, pieces)
     bias = jnp.concatenate(
         [bias_ref[0:1, :], jnp.zeros((1, 128), jnp.float32), bias_ref[1:2, :]], axis=1
     )
     qkv_ref[...] = (matmul(norm_ref[...], weight_ref[...]) + bias).astype(LOW)
-    attend_pair(qkv_ref, out_ref, log_ref, scale)
-
-
-def front(place, xhat, vectors, bias, pieces, pairs, scale):
-    length, width = xhat.shape
+    attend_pair(qkv_ref, att_ref, log_ref, scale)
+    joined_ref[:, pl.ds(pl.multiple_of(step * 128, 128), 128)] = att_ref[...]
+
+    @pl.when(step == pl.num_programs(0) - 1)
+    def _():
+        share_ref[...] = contract_last(joined_ref[...], out_ref[...]).astype(LOW)
+
+
+def front(place, x, vectors, bias, pieces, pairs, scale):
+    length, width = x.shape
+    once = pl.Buffered(1)
+    square = pl.BlockSpec((length, width), lambda *_: (0, 0), pipeline_mode=once)
     return pl.pallas_call(
         functools.partial(front_kernel, scale=scale, count=len(pieces)),
         grid_spec=pltpu.PrefetchScalarGridSpec(
             num_scalar_prefetch=1,
             grid=(pairs,),
             in_specs=[
-                whole((length, width)),
+                square,
                 whole(vectors.shape),
                 pl.BlockSpec((8, 128), lambda p, place: (0, place[0] * pairs + p)),
             ]
-            + piece_specs(pieces, 384),
+            + piece_specs(pieces, 384)
+            + fixed_specs(pieces, pairs * 128, 3),
             out_specs=[
-                whole((length, width)),
+                square,
+                square,
                 pl.BlockSpec((length, 384), lambda p, _: (0, p)),
                 pl.BlockSpec((length, 128), lambda p, _: (0, p)),
                 pl.BlockSpec((1, 8, length), lambda p, _: (p, 0, 0)),
+                square,
             ],
-            scratch_shapes=[pltpu.VMEM((width, 384), LOW)],
+            scratch_shapes=[
+                pltpu.VMEM((width, 384), LOW),
+                pltpu.VMEM((width, pairs * 128), LOW),
+                pltpu.VMEM((length, pairs * 128), LOW),
+            ],
         ),
         out_shape=[
+            jax.ShapeDtypeStruct((length, width), LOW),
             jax.ShapeDtypeStruct((length, width), LOW),
             jax.ShapeDtypeStruct((length, pairs * 384), LOW),
             jax.ShapeDtypeStruct((length, pairs * 128), LOW),
             jax.ShapeDtypeStruct((pairs, 8, length), jnp.float32),
+            jax.ShapeDtypeStruct((length, width), LOW),
         ],
-        compiler_params=settings(),
+        compiler_params=settings(56),
         cost_estimate=cost(2 * length * width * pairs * 384 * 4, 12 * length * width),
         name="front",
-    )(place, xhat, vectors, bias, *pieces)
-
-
-def share_kernel(att_ref, *refs):
-    pieces, out_ref, weight_ref = refs[:-2], refs[-2], refs[-1]
-
-    @pl.when(pl.program_id(0) == 0)
-    def _():
-        fill(weight_ref, pieces)
-
-    out_ref[...] = contract_last(att_ref[...], weight_ref[...]).astype(LOW)
-
-
-def share_product(att, pieces):
-    length, inner = att.shape
-    width = sum(piece.shape[0] for piece in pieces)
-    return pl.pallas_call(
-        share_kernel,
-        grid=(length // SEG,),
-        in_specs=[pl.BlockSpec((SEG, inner), lambda p: (p, 0))] + fixed_specs(pieces, inner, 3),
-        out_specs=pl.BlockSpec((SEG, width), lambda p: (p, 0)),
-        out_shape=jax.ShapeDtypeStruct((length, width), LOW),
-        scratch_shapes=[pltpu.VMEM((width, inner), LOW)],
-        compiler_params=settings(),
-        cost_estimate=cost(2 * length * width * inner, 4 * length * width),
-        name="share",
-    )(att, *pieces)
-
-
-def up_kernel(
+    )(place, x, vectors, bias, *pieces, *pieces)
+
+
+def feed_kernel(
     place_ref,
     x_ref,
     own_ref,
     other_ref,
     vec_ref,
     bias_ref,
-    *refs,
+    grad_ref,
+    up_ref,
+    down_ref,
+    resid_ref,
+    left_ref,
+    right_ref,
+    mixed_ref,
+    dnorm_ref,
+    sum_ref,
 ):
-    grad_ref, up_all_ref, resid_ref, left_ref, act_ref, slope_ref, weight_ref, norm_ref = refs
-    length = x_ref.shape[0]
-
     @pl.when(pl.program_id(0) == 0)
     def _():
-        for start in range(0, length, SEG):
-            rows = slice(start, start + SEG)
-            branch = own_ref[rows, :].astype(jnp.float32) + other_ref[rows, :].astype(jnp.float32)
-            resid = x_ref[rows, :].astype(jnp.float32) + (branch + vec_ref[2:3, :])
-            resid_ref[rows, :] = resid
-            xhat, _ = row_stats(resid)
-            norm = xhat * vec_ref[3:4, :] + vec_ref[4:5, :]
-            norm_ref[rows, :] = norm.astype(LOW)
-            put_natural(place_ref, left_ref.at[1, rows, :], norm)
-            left_ref[0, rows, :] = grad_ref[rows, :]
-
-    fill_slots(place_ref, weight_ref, up_all_ref)
-    for start in range(0, length, SEG):
-        rows = slice(start, start + SEG)
-        pre = matmul(norm_ref[rows, :], weight_ref[...]) + bias_ref[...]
+        sum_ref[...] = jnp.zeros_like(sum_ref)
+
+    branch = own_ref[...].astype(jnp.float32) + other_ref[...].astype(jnp.float32)
+    resid = x_ref[...].astype(jnp.float32) + (branch + vec_ref[2:3, :])
+    resid_ref[...] = resid.astype(LOW)
+    xhat, _ = row_stats(resid)
+    norm = (xhat * vec_ref[3:4, :] + vec_ref[4:5, :]).astype(LOW)
+    left_ref[0] = norm
+    hidden = up_ref.shape[1]
+    for start in range(0, hidden, 512):
+        columns = slice(start, start + 512)
+        pre = matmul(norm, up_ref[:, columns]) + bias_ref[:, columns]
         square = pre * pre
-        bent = jnp.tanh(gelu_coef * pre * (1.0 + 0.044715 * square))
-        half = 0.5 * (1.0 + bent)
-        act_ref[0, rows, :] = (pre * half).astype(LOW)
-        slope_ref[rows, :] = (
-            half
-            + (0.5 * gelu_coef) * pre * (1.0 - bent * bent) * (1.0 + (3 * 0.044715) * square)
-        ).astype(LOW)
-
-
-def up_product(place, x, own, other, vectors, bias, grad, pair, block=512):
+        bent = jnp.tanh(pre * (square * (0.044715 * gelu_coef) + gelu_coef))
+        half = 0.5 * bent + 0.5
+        act = pre * half
+        right_ref[0, :, columns] = act.astype(LOW)
+        slope = half + act * (1.0 - bent) * (square * (3 * 0.044715 * gelu_coef) + gelu_coef)
+        dpre = (matmul(grad_ref[0], down_ref[:, columns]) * slope).astype(LOW)
+        right_ref[1, :, columns] = dpre
+        total = jnp.sum(dpre.astype(jnp.float32), axis=0, keepdims=True)
+        sum_ref[:, columns] += jnp.broadcast_to(total, (8, 512))
+    dnorm_ref[...] = contract_last(right_ref[1], up_ref[...]).astype(LOW)
+    mixed_ref[...] = contract_last(right_ref[0], down_ref[...]).astype(LOW)
+
+
+def feed_product(place, x, own, other, vectors, bias, lefts, pair, block=SEG):
     length, width = x.shape
     hidden = pair.shape[1] // 2
-    steps = hidden // block
+    once = pl.Buffered(1)
+    rows = pl.BlockSpec((block, width), lambda p, _: (p, 0))
     return pl.pallas_call(
-        up_kernel,
+        feed_kernel,
         grid_spec=pltpu.PrefetchScalarGridSpec(
             num_scalar_prefetch=1,
-            grid=(steps,),
-            in_specs=[whole((length, width))] * 3
+            grid=(length // block,),
+            in_specs=[rows] * 3
             + [
                 whole(vectors.shape),
-                pl.BlockSpec((1, block), lambda p, place: (0, place[0] * steps + p)),
-                whole((length, width)),
-                pl.BlockSpec((width, block), lambda p, _: (0, p)),
+                pl.BlockSpec((1, hidden), lambda p, place: (0, place[0])),
+                pl.BlockSpec((1, block, width), lambda p, _: (0, p, 0)),
+                pl.BlockSpec((width, hidden), lambda *_: (0, 0), pipeline_mode=once),
+                pl.BlockSpec((width, hidden), lambda *_: (0, 1), pipeline_mode=once),
             ],
             out_specs=[
-                whole((length, width)),
-                whole((2, length, width)),
-                pl.BlockSpec((1, length, block), lambda p, _: (0, 0, p)),
-                pl.BlockSpec((length, block), lambda p, _: (0, p)),
-            ],
-            scratch_shapes=[pltpu.VMEM((width, block), LOW), pltpu.VMEM((length, width), LOW)],
-        ),
-        out_shape=[
-            jax.ShapeDtypeStruct((length, width), jnp.float32),
-            jax.ShapeDtypeStruct((2, length, width), LOW),
-            jax.ShapeDtypeStruct((2, length, hidden), LOW),
-            jax.ShapeDtypeStruct((length, hidden), LOW),
-        ],
-        compiler_params=settings(),
-        cost_estimate=cost(3 * length * width * hidden, 16 * length * width),
-        name="up",
-    )(place, x, own, other, vectors, bias, grad, pair)
-
-
-def turn_kernel(
-    place_ref,
-    grad_ref,
-    act_ref,
-    slope_ref,
-    up_all_ref,
-    down_all_ref,
-    own_ref,
-    other_ref,
-    dnorm_ref,
-    dpre_ref,
-    sum_ref,
-    up_ref,
-    down_ref,
-    out_acc,
-    norm_acc,
-):
-    length = grad_ref.shape[0]
-    rows_own = length // 2
-    step = pl.program_id(0)
-    fill_slots(place_ref, up_ref, up_all_ref)
-    fill_slots(place_ref, down_ref, down_all_ref)
-    total = jnp.zeros((1, up_ref.shape[1]), jnp.float32)
-    for start in range(0, length, SEG):
-        rows = slice(start, start + SEG)
-        dact = matmul(grad_ref[rows, :], down_ref[...])
-        dpre = (dact * slope_ref[rows, :].astype(jnp.float32)).astype(LOW)
-        dpre_ref[0, rows, :] = dpre
-        total = total + jnp.sum(dpre.astype(jnp.float32), axis=0, keepdims=True)
-        mixed = contract_last(act_ref[0, rows, :], down_ref[...])
-        dnorm = contract_last(dpre, up_ref[...])
-
-        @pl.when(step == 0)
-        def _():
-            out_acc[rows, :] = mixed
-            norm_acc[rows, :] = dnorm
-
-        @pl.when(step > 0)
-        def _():
-            out_acc[rows, :] += mixed
-            norm_acc[rows, :] += dnorm
-
-    sum_ref[...] = jnp.broadcast_to(total, sum_ref.shape)
-
-    @pl.when(step == pl.num_programs(0) - 1)
-    def _():
-        side = place_ref[0]
-        own_ref[...] = out_acc[pl.ds(pl.multiple_of(side * rows_own, rows_own), rows_own), :]
-        other_ref[...] = out_acc[
-            pl.ds(pl.multiple_of((1 - side) * rows_own, rows_own), rows_own), :
-        ].astype(LOW)
-        dnorm_ref[...] = norm_acc[...].astype(LOW)
-
-
-def turn_product(place, grad, act, slope, pair, block=512):
-    length, width = grad.shape
-    hidden = act.shape[2]
-    steps = hidden // block
-    return pl.pallas_call(
-        turn_kernel,
-        grid_spec=pltpu.PrefetchScalarGridSpec(
-            num_scalar_prefetch=1,
-            grid=(hidden // block,),
-            in_specs=[
-                whole((length, width)),
-                pl.BlockSpec((1, length, block), lambda p, _: (0, 0, p)),
-                pl.BlockSpec((length, block), lambda p, _: (0, p)),
-                pl.BlockSpec((width, block), lambda p, _: (0, p)),
-                pl.BlockSpec((width, block), lambda p, _: (0, steps + p)),
-            ],
-            out_specs=[
-                whole((length // 2, width)),
-                whole((length // 2, width)),
-                whole((length, width)),
-                pl.BlockSpec((1, length, block), lambda p, _: (1, 0, p)),
-                pl.BlockSpec((8, block), lambda p, _: (0, p)),
-            ],
-            scratch_shapes=[
-                pltpu.VMEM((width, block), LOW),
-                pltpu.VMEM((width, block), LOW),
-                pltpu.VMEM((length, width), jnp.float32),
-                pltpu.VMEM((length, width), jnp.float32),
+                rows,
+                pl.BlockSpec((1, block, width), lambda p, _: (1, p, 0)),
+                pl.BlockSpec((2, block, hidden), lambda p, _: (0, p, 0)),
+                rows,
+                rows,
+                whole((8, hidden)),
             ],
         ),
         out_shape=[
-            jax.ShapeDtypeStruct((length // 2, width), jnp.float32),
-            jax.ShapeDtypeStruct((length // 2, width), LOW),
             jax.ShapeDtypeStruct((length, width), LOW),
+            jax.ShapeDtypeStruct((2, length, width), LOW),
             jax.ShapeDtypeStruct((2, length, hidden), LOW),
+            jax.ShapeDtypeStruct((length, width), LOW),
+            jax.ShapeDtypeStruct((length, width), LOW),
             jax.ShapeDtypeStruct((8, hidden), jnp.float32),
         ],
-        input_output_aliases={2: 3},
-        compiler_params=settings(),
-        cost_estimate=cost(6 * length * width * hidden, 24 * length * width),
-        name="turn",
-    )(place, grad, act, slope, pair, pair)
-
-
-def mid_kernel(resid_ref, own_ref, other_ref, grad_ref, vec_ref, *refs, count):
+        input_output_aliases={6: 1},
+        compiler_params=settings(56),
+        cost_estimate=cost(9 * length * width * hidden, 40 * length * width),
+        name="feed",
+    )(place, x, own, other, vectors, bias, lefts, pair, pair)
+
+
+def mid_kernel(place_ref, resid_ref, own_ref, other_ref, grad_ref, vec_ref, *refs, count):
     pieces = refs[:count]
-    dresid_ref, dbranch_ref, datt_ref, sum_ref, weight_ref = refs[count:]
+    dbranch_ref, datt_ref, sum_ref, weight_ref = refs[count:]
 
     @pl.when(pl.program_id(0) == 0)
     def _():
-        fill(weight_ref, pieces)
+        fill_natural(place_ref, weight_ref, pieces)
         sum_ref[...] = jnp.zeros_like(sum_ref)
 
     dnorm = own_ref[...].astype(jnp.float32) + other_ref[...].astype(jnp.float32)
-    grad = grad_ref[...].astype(jnp.float32)
-    xhat, inverse = row_stats(resid_ref[...])
+    grad = grad_ref[0].astype(jnp.float32)
+    xhat, inverse = row_stats(resid_ref[...].astype(jnp.float32))
     dresid = grad + norm_back(dnorm, xhat, inverse, vec_ref[3:4, :])
-    dresid_ref[...] = dresid
     dbranch = dresid.astype(LOW)
     dbranch_ref[...] = dbranch
     datt_ref[...] = matmul(dbranch, weight_ref[...]).astype(LOW)
@@ -677,60 +588,86 @@
         sum_ref[row : row + 1, :] += 0.5 * jnp.sum(value, axis=0, keepdims=True)
 
 
-def mid_product(resid, own, other, grad, vectors, pieces, inner):
+def mid_product(place, resid, own, other, grad, vectors, pieces, inner):
     length, width = resid.shape
-    rows = pl.BlockSpec((SEG, width), lambda p: (p, 0))
+    rows = pl.BlockSpec((SEG, width), lambda p, _: (p, 0))
     return pl.pallas_call(
         functools.partial(mid_kernel, count=len(pieces)),
-        grid=(length // SEG,),
-        in_specs=[rows] * 4 + [whole(vectors.shape)] + fixed_specs(pieces, inner, 3),
-        out_specs=[rows, rows, pl.BlockSpec((SEG, inner), lambda p: (p, 0)), whole((8, width))],
+        grid_spec=pltpu.PrefetchScalarGridSpec(
+            num_scalar_prefetch=1,
+            grid=(length // SEG,),
+            in_specs=[rows] * 3
+            + [pl.BlockSpec((1, SEG, width), lambda p, _: (0, p, 0)), whole(vectors.shape)]
+            + fixed_specs(pieces, inner, 3),
+            out_specs=[
+                rows,
+                pl.BlockSpec((SEG, inner), lambda p, _: (p, 0)),
+                whole((8, width)),
+            ],
+            scratch_shapes=[pltpu.VMEM((width, inner), LOW)],
+        ),
         out_shape=[
-            jax.ShapeDtypeStruct((length, width), jnp.float32),
             jax.ShapeDtypeStruct((length, width), LOW),
             jax.ShapeDtypeStruct((length, inner), LOW),
             jax.ShapeDtypeStruct((8, width), jnp.float32),
         ],
-        scratch_shapes=[pltpu.VMEM((width, inner), LOW)],
-        compiler_params=settings(),
+        compiler_params=settings(56),
         cost_estimate=cost(2 * length * width * inner * 16, 16 * length * width),
         name="mid",
-    )(resid, own, other, grad, vectors, *pieces)
+    )(place, resid, own, other, grad, vectors, *pieces)
 
 
 def attend_back_pair(qkv_ref, grad_ref, log_ref, out_ref, dkey_ref, dvalue_ref, scale):
     length = qkv_ref.shape[0]
     lane = lax.broadcasted_iota(jnp.int32, (SEG, 128), 1)
-    key = qkv_ref[:, 128:256]
-    value = qkv_ref[:, 256:384]
-    key_t = jnp.transpose(key)
-    dkey_ref[...] = jnp.zeros_like(dkey_ref)
-    dvalue_ref[...] = jnp.zeros_like(dvalue_ref)
-    for seg in range(length // SEG):
-        keys_here = (seg + 1) * SEG
-        rows = slice(seg * SEG, keys_here)
+    reach = lax.broadcasted_iota(jnp.int32, (SEG, SEG), 0) <= lax.broadcasted_iota(
+        jnp.int32, (SEG, SEG), 1
+    )
+    key_t = jnp.transpose(qkv_ref[:, 128:256])
+    for seg in reversed(range(length // SEG)):
+        before = seg * SEG
+        rows = slice(before, before + SEG)
+        spans = [rows] if seg == 0 else [rows, slice(0, before)]
         query = qkv_ref[rows, 0:128] * scale
         grad = grad_ref[rows, :]
-        key_pos = lax.broadcasted_iota(jnp.int32, (keys_here, SEG), 0)
-        query_pos = lax.broadcasted_iota(jnp.int32, (keys_here, SEG), 1) + seg * SEG
         parts = []
-        dkey = jnp.zeros((keys_here, 128), jnp.float32)
-        dvalue = jnp.zeros((keys_here, 128), jnp.float32)
+        dkeys = [None] * len(spans)
+        dvalues = [None] * len(spans)
         for head in range(2):
             here = lane // 64 == head
+            lanes = slice(head * 64, head * 64 + 64)
             query_mine = jnp.where(here, query, jnp.zeros_like(query))
             grad_mine = jnp.where(here, grad, jnp.zeros_like(grad))
-            scores = contract_last(key[:keys_here], query_mine)
-            scores = jnp.where(key_pos <= query_pos, scores, -1e30)
-            probs = jnp.exp(scores - log_ref[0, head : head + 1, rows])
-            dprobs = contract_last(value[:keys_here], grad_mine)
-            mean = jnp.sum(probs * dprobs, axis=0, keepdims=True)
-            dscores = (probs * (dprobs - mean)).astype(LOW)
-            dvalue = dvalue + matmul(probs.astype(LOW), grad_mine)
-            dkey = dkey + matmul(dscores, query_mine)
-            parts.append(matmul(key_t[head * 64 : head * 64 + 64, :keys_here], dscores) * scale)
-        dkey_ref[:keys_here, :] += dkey
-        dvalue_ref[:keys_here, :] += dvalue
+            log_row = log_ref[0, head : head + 1, rows]
+            probs, dprobs = [], []
+            mean = None
+            for index, span in enumerate(spans):
+                scores = contract_last(qkv_ref[span, 128:256], query_mine)
+                if index == 0:
+                    scores = jnp.where(reach, scores, -1e30)
+                prob = jnp.exp(scores - log_row)
+                dprob = contract_last(qkv_ref[span, 256:384], grad_mine)
+                share = jnp.sum(prob * dprob, axis=0, keepdims=True)
+                mean = share if mean is None else mean + share
+                probs.append(prob)
+                dprobs.append(dprob)
+            part = None
+            for index, span in enumerate(spans):
+                dscores = (probs[index] * (dprobs[index] - mean)).astype(LOW)
+                dvalue = matmul(probs[index].astype(LOW), grad_mine)
+                dkey = matmul(dscores, query_mine)
+                piece = matmul(key_t[lanes, span], dscores)
+                part = piece if part is None else part + piece
+                dkeys[index] = dkey if head == 0 else dkeys[index] + dkey
+                dvalues[index] = dvalue if head == 0 else dvalues[index] + dvalue
+            parts.append(part * scale)
+        for index, span in enumerate(spans):
+            if seg == length // SEG - 1:
+                dkey_ref[span, :] = dkeys[index]
+                dvalue_ref[span, :] = dvalues[index]
+            else:
+                dkey_ref[span, :] += dkeys[index]
+                dvalue_ref[span, :] += dvalues[index]
         out_ref[rows, 0:128] = jnp.transpose(jnp.concatenate(parts, axis=0)).astype(LOW)
     out_ref[:, 128:256] = dkey_ref[...].astype(LOW)
     out_ref[:, 256:384] = dvalue_ref[...].astype(LOW)
@@ -738,11 +675,10 @@
 
 def back_kernel(place_ref, xhat_ref, qkv_ref, grad_ref, log_ref, *refs, scale, count):
     pieces = refs[:count]
-    dqkv_ref, own_ref, other_ref, sum_ref, vec_ref = refs[count : count + 5]
-    weight_ref, dkey_ref, dvalue_ref, acc_ref = refs[count + 5 :]
-    rows_own = own_ref.shape[0]
+    dqkv_ref, dnorm_ref, sum_ref, vec_ref = refs[count : count + 4]
+    weight_ref, dkey_ref, dvalue_ref, acc_ref = refs[count + 4 :]
     step = pl.program_id(0)
-    fill(weight_ref, pieces)
+    fill_natural(place_ref, weight_ref, pieces)
     attend_back_pair(qkv_ref, grad_ref, log_ref, dqkv_ref, dkey_ref, dvalue_ref, scale)
     dnorm = contract_last(dqkv_ref[...], weight_ref[...])
     sum_ref[...] = jnp.broadcast_to(
@@ -753,20 +689,18 @@
     def _():
         acc_ref[...] = dnorm
 
-    @pl.when(step > 0)
+    @pl.when((step > 0) & (step < pl.num_programs(0) - 1))
     def _():
         acc_ref[...] += dnorm
 
     @pl.when(step == pl.num_programs(0) - 1)
     def _():
-        side = place_ref[0]
-        total = acc_ref[...]
-        vec_ref[0:1, :] = jnp.sum(total * xhat_ref[...], axis=0, keepdims=True)
-        vec_ref[1:8, :] = jnp.broadcast_to(jnp.sum(total, axis=0, keepdims=True), (7, total.shape[1]))
-        own_ref[...] = acc_ref[pl.ds(pl.multiple_of(side * rows_own, rows_own), rows_own), :]
-        other_ref[...] = acc_ref[
-            pl.ds(pl.multiple_of((1 - side) * rows_own, rows_own), rows_own), :
-        ].astype(LOW)
+        total = acc_ref[...] + dnorm
+        dnorm_ref[...] = total.astype(LOW)
+        vec_ref[0:1, :] = jnp.sum(total * xhat_ref[...].astype(jnp.float32), axis=0, keepdims=True)
+        vec_ref[1:8, :] = jnp.broadcast_to(
+            jnp.sum(total, axis=0, keepdims=True), (7, total.shape[1])
+        )
 
 
 def back_product(place, xhat, qkv, grad, logs, pieces, scale):
@@ -787,8 +721,7 @@
             + piece_specs(pieces, 384),
             out_specs=[
                 pl.BlockSpec((length, 384), lambda p, _: (0, p)),
-                whole((length // 2, width)),
-                whole((length // 2, width)),
+                whole((length, width)),
                 pl.BlockSpec((1, 8, 384), lambda p, _: (p, 0, 0)),
                 whole((8, width)),
             ],
@@ -801,47 +734,25 @@
         ),
         out_shape=[
             jax.ShapeDtypeStruct((length, columns), LOW),
-            jax.ShapeDtypeStruct((length // 2, width), jnp.float32),
-            jax.ShapeDtypeStruct((length // 2, width), LOW),
+            jax.ShapeDtypeStruct((length, width), LOW),
             jax.ShapeDtypeStruct((pairs, 8, 384), jnp.float32),
             jax.ShapeDtypeStruct((8, width), jnp.float32),
         ],
-        compiler_params=settings(),
+        compiler_params=settings(56),
         cost_estimate=cost(2 * length * width * columns * 48, 12 * length * width),
         name="back",
     )(place, xhat, qkv, grad, logs, *pieces)
 
 
-def put_natural(place_ref, out_ref, value):
-    near = value.shape[1] // 512
-    lane = lax.broadcasted_iota(jnp.int32, (value.shape[0], 128), 1)
-    half = value.shape[1] // 2
-    for slot in range(4 * near):
-        first = value[:, slot // 2 * 128 : slot // 2 * 128 + 128]
-        second = value[:, half + slot // 2 * 128 : half + slot // 2 * 128 + 128]
-        if slot % 2 == 0:
-            second = pltpu.roll(second, 64, 1)
-        else:
-            first = pltpu.roll(first, 64, 1)
-        block = jnp.where(lane < 64, first, second)
-        block = jnp.where(place_ref[3] == 1, pltpu.roll(block, 64, 1), block)
-        far_index = lax.rem(place_ref[1] + 4 - slot % 4, 4)
-        near_index = lax.rem(place_ref[2] + near - slot // 4, near)
-        target = far_index * near + near_index
-        out_ref[:, pl.ds(pl.multiple_of(target * 128, 128), 128)] = block.astype(out_ref.dtype)
-
-
-def last_kernel(
-    place_ref, x_ref, dresid_ref, own_ref, other_ref, vec_ref, out_ref
-):
-    dnorm = own_ref[...] + other_ref[...].astype(jnp.float32)
+def last_kernel(place_ref, x_ref, dbranch_ref, own_ref, other_ref, vec_ref, out_ref):
+    dnorm = own_ref[...].astype(jnp.float32) + other_ref[...].astype(jnp.float32)
     xhat, inverse = row_stats(x_ref[...].astype(jnp.float32))
-    total = dresid_ref[...] + norm_back(dnorm, xhat, inverse, vec_ref[0:1, :])
-    put_natural(place_ref, out_ref, total)
-
-
-def last_product(place, x, dresid, own, other, vectors):
-    rows, width = own.shape
+    back = norm_back(dnorm, xhat, inverse, vec_ref[0:1, :])
+    out_ref[...] = dbranch_ref[...].astype(jnp.float32) + back
+
+
+def last_product(place, x, dbranch, own, other, vectors):
+    rows, width = other.shape
     block = 128
     steps = rows // block
     mine = pl.BlockSpec((block, width), lambda p, place: (place[0] * steps + p, 0))
@@ -851,24 +762,24 @@
         grid_spec=pltpu.PrefetchScalarGridSpec(
             num_scalar_prefetch=1,
             grid=(steps,),
-            in_specs=[mine, mine, plain, plain, whole(vectors.shape)],
+            in_specs=[plain, mine, mine, plain, whole(vectors.shape)],
             out_specs=plain,
         ),
         out_shape=jax.ShapeDtypeStruct((rows, width), jnp.float32),
-        compiler_params=settings(),
+        compiler_params=settings(16),
         cost_estimate=cost(40 * rows * width, 320 * rows * width),
         name="last",
-    )(place, x, dresid, own, other, vectors)
+    )(place, x, dbranch, own, other, vectors)
 
 
 def result_kernel(place_ref, resid_ref, own_ref, other_ref, vec_ref, out_ref):
-    mixed = own_ref[...] + other_ref[...].astype(jnp.float32)
-    total = resid_ref[...] + mixed + vec_ref[5:6, :]
-    put_natural(place_ref, out_ref, total)
+    mixed = own_ref[...].astype(jnp.float32) + other_ref[...].astype(jnp.float32)
+    total = resid_ref[...].astype(jnp.float32) + mixed + vec_ref[5:6, :]
+    out_ref[...] = total.astype(LOW)
 
 
 def result_product(place, resid, own, other, vectors):
-    rows, width = own.shape
+    rows, width = other.shape
     block = 128
     steps = rows // block
     mine = pl.BlockSpec((block, width), lambda p, place: (place[0] * steps + p, 0))
@@ -878,11 +789,11 @@
         grid_spec=pltpu.PrefetchScalarGridSpec(
             num_scalar_prefetch=1,
             grid=(steps,),
-            in_specs=[mine, plain, plain, whole(vectors.shape)],
+            in_specs=[mine, mine, plain, whole(vectors.shape)],
             out_specs=plain,
         ),
         out_shape=jax.ShapeDtypeStruct((rows, width), LOW),
-        compiler_params=settings(),
+        compiler_params=settings(16),
         cost_estimate=cost(10 * rows * width, 320 * rows * width),
         name="result",
     )(place, resid, own, other, vectors)
@@ -911,7 +822,7 @@
             jax.ShapeDtypeStruct((rows, 4 * columns + 128), LOW),
             jax.ShapeDtypeStruct((rows, 2 * up.shape[1]), LOW),
         ],
-        compiler_params=settings(),
+        compiler_params=settings(28),
         cost_estimate=cost(0, 4 * rows * (4 * columns + 2 * up.shape[1])),
         name="pack",
     )(proj, out, up, down, vec)
@@ -919,14 +830,14 @@
 
 def vector_kernel(place_ref, *refs):
     pieces = refs[:-4]
-    slot_ref, bias_ref, hidden_ref, joined_ref = refs[-4:]
-    fill(joined_ref, pieces)
+    vec_ref, bias_ref, hidden_ref, joined_ref = refs[-4:]
+    fill_natural(place_ref, joined_ref, pieces)
     turned = jnp.transpose(joined_ref[...]).astype(jnp.float32)
-    slot_ref[...] = turned[0:8]
-    put_natural(place_ref, bias_ref, turned[8:16])
+    vec_ref[...] = turned[0:8]
+    bias_ref[...] = turned[8:16]
     lane = lax.broadcasted_iota(jnp.int32, (1, 128), 1)
     for pair in range(bias_ref.shape[1] // 128):
-        rows = [bias_ref[2 + q : 3 + q, pair * 128 : pair * 128 + 128] for q in range(4)]
+        rows = [turned[10 + q : 11 + q, pair * 128 : pair * 128 + 128] for q in range(4)]
         flipped = [pltpu.roll(row, 64, 1) for row in rows]
         for q in (0, 2):
             start = pair * 512 + q * 64
@@ -952,7 +863,7 @@
             jax.ShapeDtypeStruct((8, width), jnp.float32),
             jax.ShapeDtypeStruct((1, 4 * width), jnp.float32),
         ],
-        compiler_params=settings(),
+        compiler_params=settings(28),
         cost_estimate=cost(width * 128, 2 * width * 128),
         name="vectors",
     )(place, *pieces)
@@ -979,29 +890,6 @@
     return pieces + [dp_shift(piece, ranks, 0, 0, 1) for piece in pieces], pieces
 
 
-def far_reduce(total, ranks, wire):
-    rows = total.shape[0] // 4
-    sent = {
-        k: dp_shift(total[k * rows : (k + 1) * rows].astype(wire), ranks, -k, 0, 0)
-        for k in (1, 3, 2)
-    }
-    result = total[:rows]
-    for k in (1, 2, 3):
-        result = result + sent[k].astype(jnp.float32)
-    return result
-
-
-def dp_reduce_small(grads, ranks):
-    near = ranks // 8
-    half = grads.shape[0] // 2
-    mine = grads[:half] + dp_shift(grads[half:], ranks, 0, 0, 1)
-    part = half // near
-    total = mine[:part]
-    for step in range(1, near):
-        total = total + dp_shift(mine[step * part : (step + 1) * part], ranks, 0, -step, 0)
-    return far_reduce(total, ranks, jnp.float32)
-
-
 def reduce_core(left, right, ranks):
     half = left.shape[1] // 2
     return dp_shift(contract_rows(left[:, half:], right).astype(LOW), ranks, 0, 0, 1)
@@ -1020,10 +908,10 @@
     return total + arrived.astype(jnp.float32)
 
 
-def far_send(total, ranks):
+def far_send(total, ranks, wire=LOW):
     rows = total.shape[0] // 4
-    low = total.astype(LOW)
-    return [dp_shift(low[k * rows : (k + 1) * rows], ranks, -k, 0, 0) for k in (1, 3, 2)]
+    low = total.astype(wire)
+    return [dp_shift(low[k * rows : (k + 1) * rows], ranks, -k, 0, 0) for k in (2, 3, 1)]
 
 
 def far_sum(total, sent):
@@ -1099,22 +987,18 @@
             jnp.concatenate([other, own], axis=0),
         )
 
-    hidden_in = matmul(
-        after(in_order(inputs, inputs_other), *narrow_far[1:4]), to_local
-    )
-    xhat, _ = row_stats(hidden_in)
-    hidden_in = hidden_in.astype(LOW)
-    norm_one, qkv, attended, logs = front(
-        place, xhat, vectors, query_bias, narrow, pairs, scale
-    )
-    share = share_product(after(attended, grad_other), narrow)
-    grad_rows = after(in_order(out_grad, grad_other), share)
-    cotangent = matmul(grad_rows, to_local).astype(LOW)
-    resid, lefts, rights, slope = up_product(
-        place, hidden_in, share, swap(share), vectors, hidden_bias, grad_rows, wide
-    )
-    own_out, other_out, dnorm_share, rights, dpre_sum = turn_product(
-        place, cotangent, rights, slope, wide
+    def other_rows(value):
+        return lax.dynamic_slice_in_dim(value, (1 - side) * rows, rows, 0)
+
+    hidden_in = in_order(inputs, inputs_other)
+    xhat, norm_one, qkv, attended, logs, share = front(
+        place, after(hidden_in, grad_other), vectors, query_bias, narrow, pairs, scale
+    )
+    cotangent = after(in_order(out_grad, grad_other), share)
+    lefts = jnp.stack([cotangent, jnp.zeros_like(cotangent)])
+    norm_slot = matmul(after(norm_one, share), to_local).astype(LOW)
+    resid, lefts, rights, mixed_share, dnorm_share, dpre_sum = feed_product(
+        place, hidden_in, share, swap(share), vectors, hidden_bias, lefts, wide
     )
     dnorm_other = swap(dnorm_share)
     wide_share = lax.dot_general(
@@ -1124,47 +1008,20 @@
         preferred_element_type=jnp.float32,
     ).astype(LOW)
     wide_grad = lax.psum_scatter(wide_share, "dp", scatter_dimension=1, tiled=True)
-    dresid, dbranch, dattended, mid_sum = mid_product(
-        after(resid, wide_share),
+    dbranch, dattended, mid_sum = mid_product(
+        place,
+        after(resid, wide_share, norm_slot),
         dnorm_share,
         dnorm_other,
-        cotangent,
+        lefts,
         vectors,
         narrow,
         heads_width,
     )
-    dqkv, own_dnorm, other_dnorm, dqkv_sum, front_sum = back_product(
+    dqkv, dnorm_one, dqkv_sum, front_sum = back_product(
         place, xhat, qkv, dattended, logs, narrow, scale
     )
-    proj_core = reduce_core(norm_one, dqkv, ranks)
-    proj_near = reduce_near(norm_one, dqkv, proj_core)
-    proj_arrived = dp_shift(proj_near, ranks, 0, 1, 0)
-    out_core = reduce_core(dbranch, attended, ranks)
-    out_near = reduce_near(dbranch, attended, out_core)
-    out_arrived = dp_shift(after(out_near, proj_near), ranks, 0, 1, 0)
-    grad_back = wide_grad[0].T.astype(jnp.float32)
-    grad_hidden = wide_grad[1].astype(jnp.float32)
-    own_other, back_other = swap(other_out), swap(other_dnorm)
-    proj_total = reduce_sum(
-        norm_one, dqkv, proj_core, after(proj_arrived, own_other, back_other)
-    )
-    grad_proj = far_sum(proj_total, far_send(proj_total, ranks))
-    out_total = reduce_sum(dbranch, attended, out_core, out_arrived)
-    grad_out = far_sum(out_total, far_send(out_total, ranks)).T
-    result = result_product(
-        place, after(resid, proj_total, out_total), own_out, own_other, vectors
-    )
-    input_grad = last_product(
-        place,
-        hidden_in,
-        dresid,
-        own_dnorm,
-        after(back_other, proj_total, out_total),
-        vectors,
-    )
-    grad_proj = grad_proj.reshape(shard, pairs, 3, 128).transpose(2, 0, 1, 3)
-    grad_proj = grad_proj.reshape(3, shard, heads_width)
-
+    proj_core = reduce_core(norm_slot, dqkv, ranks)
     dqkv_sum = dqkv_sum[:, 0].reshape(pairs, 3, 128)
     placed = [
         place_block(value, 2 * value.shape[0], side * value.shape[0]).reshape(ranks, -1)
@@ -1174,18 +1031,67 @@
             dpre_sum[0],
         )
     ]
-    to_slot = lax.dot_general(
+    pack = jnp.stack([front_sum[0], front_sum[1], mid_sum[2], mid_sum[0], mid_sum[1], mid_sum[3]])
+    pack = pack.reshape(6, ranks, shard).transpose(1, 0, 2).reshape(ranks, -1)
+    pack = lax.dot_general(
         slot_of,
-        jnp.concatenate(placed, axis=1),
+        jnp.concatenate([pack] + placed, axis=1),
         (((0,), (0,)), ((), ())),
         precision=lax.Precision.HIGHEST,
         preferred_element_type=jnp.float32,
     )
-    pack = jnp.stack([front_sum[0], front_sum[1], mid_sum[2], mid_sum[0], mid_sum[1], mid_sum[3]])
-    pack = pack.reshape(6, ranks, shard).transpose(1, 0, 2).reshape(ranks, -1)
-    pack = after(jnp.concatenate([pack, to_slot], axis=1), proj_near)
-    pack = dp_reduce_small(pack + swap(pack), ranks)
-    pack = pack.reshape(-1)
+    pack = pack + swap(pack)
+    pack = pack[: ranks // 2] + dp_shift(pack[ranks // 2 :], ranks, 0, 0, 1)
+    back_other = swap(other_rows(after(dnorm_one, pack)))
+    dbranch_slot = matmul(after(dbranch, dattended), to_local).astype(LOW)
+    out_core = reduce_core(dbranch_slot, attended, ranks)
+    slim_near, pack = lax.optimization_barrier(
+        (
+            jnp.concatenate(
+                [
+                    reduce_near(norm_slot, dqkv, proj_core),
+                    reduce_near(dbranch_slot, attended, out_core),
+                ],
+                axis=1,
+            ),
+            pack,
+        )
+    )
+    pack_arrived = dp_shift(pack[ranks // 4 :], ranks, 0, 1, 0)
+    slim_arrived = dp_shift(slim_near, ranks, 0, 1, 0)
+    own_other = swap(other_rows(after(mixed_share, back_other)))
+    slim_arrived, pack_arrived, back_other = lax.optimization_barrier(
+        (slim_arrived, pack_arrived, back_other)
+    )
+    columns = 3 * heads_width
+    slim_total, pack_total = lax.optimization_barrier(
+        (
+            jnp.concatenate(
+                [
+                    reduce_sum(norm_slot, dqkv, proj_core, slim_arrived[:, :columns]),
+                    reduce_sum(dbranch_slot, attended, out_core, slim_arrived[:, columns:]),
+                ],
+                axis=1,
+            ),
+            pack[: ranks // 4] + pack_arrived,
+        )
+    )
+    pack = far_sum(pack_total, far_send(pack_total, ranks, jnp.float32)).reshape(-1)
+    grad_back = wide_grad[0].T.astype(jnp.float32)
+    grad_hidden = wide_grad[1].astype(jnp.float32)
+    slim_grad = far_sum(
+        after(slim_total, grad_back, grad_hidden), far_send(slim_total, ranks)
+    )
+    grad_proj = slim_grad[:, :columns]
+    grad_out = slim_grad[:, columns:].T
+    result = result_product(
+        place, after(resid, slim_total), mixed_share, own_other, vectors
+    )
+    input_grad = last_product(
+        place, inputs, dbranch, dnorm_one, after(back_other, slim_total), vectors
+    )
+    grad_proj = grad_proj.reshape(shard, pairs, 3, 128).transpose(2, 0, 1, 3)
+    grad_proj = grad_proj.reshape(3, shard, heads_width)
     vector_grads = [pack[i * shard : (i + 1) * shard] for i in range(6)]
     return (
         result,

time: 332 us -> 316 us (0.952); the launches traced: 326 us -> 315 us
  Pallas kernels: 108 us -> 84.4 us
  waiting for transfers between devices: 114 us -> 126 us
  local copies, waits for them, and re-layouts: 14.5 us -> 23.2 us
  starting transfers between devices: 37.4 us -> 30.5 us
  matrix products: 30.2 us -> 26.8 us
    pallas_call x4 -> x2, Pallas kernels: 50.6 us -> 31.4 us  [the longest x1 23.7 us: feed_product(): pl.pallas_call(feed_kernel, grid_spec=pltpu.PrefetchScalarGridSpec(num_sc...]
    ppermute x7, waiting for transfers between devices: 56.4 us -> 74 us  [swap(): return lax.ppermute(value, 'tensor', [(0, 1), (1, 0)])]
    unnamed x58 -> x94, local copies, waits for them, and re-layouts: 4.06 us -> 11 us
    ppermute x30 -> x26, starting transfers between devices: 28.6 us -> 22 us  [dp_shift(): lax.ppermute(value, 'dp', [(rank, goes(rank)) for rank in range(ranks)])]
    ppermute x30 -> x26, waiting for transfers between devices: 57.1 us -> 51.8 us  [dp_shift(): lax.ppermute(value, 'dp', [(rank, goes(rank)) for rank in range(ranks)])]
    select_n x2, other arithmetic: 1.36 us -> 5.34 us  [in_order(): jnp.where(side == 0, jnp.concatenate([own, other], axis=0), jnp.concatena...]
    pallas_call x1, Pallas kernels: 18.7 us -> 22.2 us  [front(): pl.pallas_call(functools.partial(front_kernel, scale=scale, count=len(pie...]
  transfers between devices with their start and end apart: 39 -> 35, of which waited for: 13 -> 16; matrix products, arithmetic and copies ran while one was open for 14% -> 14% of each run, Pallas kernels for 22% -> 19%
where the time goes in v3:
time: 316 us; the launch traced here: 315 us
  waiting for transfers between devices  126 us (40%)
  Pallas kernels  84.4 us (27%)
  starting transfers between devices  30.5 us (10%)
  matrix products  26.8 us (8%)
  local copies, waits for them, and re-layouts  23.2 us (7%)
  between operations  14.7 us (5%)
  other arithmetic  9.16 us (3%)
    ppermute x7, waiting for transfers between devices, swap(): return lax.ppermute(value, 'tensor', [(0, 1), (1, 0)])  74 us
    ppermute x26, waiting for transfers between devices, dp_shift(): lax.ppermute(value, 'dp', [(rank, goes(rank)) for rank in range(ranks)])  51.8 us
    pallas_call x1, Pallas kernels, feed_product(): pl.pallas_call(feed_kernel, grid_spec=pltpu.PrefetchScalarGridSpec(num_sc...  23.7 us
    pallas_call x1, Pallas kernels, back_product(): pl.pallas_call(functools.partial(back_kernel, scale=scale, count=len(piec...  23.2 us
    pallas_call x1, Pallas kernels, front(): pl.pallas_call(functools.partial(front_kernel, scale=scale, count=len(pie...  22.2 us
    ppermute x26, starting transfers between devices, dp_shift(): lax.ppermute(value, 'dp', [(rank, goes(rank)) for rank in range(ranks)])  22 us
    dot_general x6, matrix products, contract_rows(): lax.dot_general(left, right, (((0,), (0,)), ((), ())), preferred_element_...  12.7 us
    unnamed x94, local copies, waits for them, and re-layouts  11 us
  transfers between devices with their start and end apart: 35, of which 16 were waited for; matrix products, arithmetic and copies ran while one was open for 14% of the time, Pallas kernels for 19%

profile of v3, /device:TPU:8, one launch (start us, length us, event | category | flops | bytes accessed | tf_op | source)
XLA Modules:
  0.0 314.6 jit_solution(220789965720820890)
XLA Ops:
  18.3 1.8 collective-permute-start.4
  21.6 14.5 %collective-permute-done.2.refs_1_.refs_17_ = bf16[64,2176]{1,0:T(8,128)(2,1)S(1)} collective-permute-done((bf16[64,2176]{1,0:T(8,128)(2,1)S(1)}, bf16[64,2176]{1,0:T(8,128)(2,1)S(1)}, u32[]{:S(2)}, u32[]{:S(2)}) %collective-permute-start.2) | collective-permute-done | bytes 278560 | tf_op jit(solution)/shard_map/ppermute | solution.py:883
  37.6 3.0 collective-permute-done.3.refs_2_.refs_18_
  43.4 5.2 %collective-permute-done.7.refs_6_.refs_22_ = bf16[64,2176]{1,0:T(8,128)(2,1)S(1)} collective-permute-done((bf16[64,2176]{1,0:T(8,128)(2,1)S(1)}, bf16[64,2176]{1,0:T(8,128)(2,1)S(1)}, u32[]{:S(2)}, u32[]{:S(2)}) %collective-permute-start.7) | collective-permute-done | bytes 278560 | tf_op jit(solution)/shard_map/ppermute | solution.py:883
  52.2 6.7 %collective-permute-done.8.refs_7_.refs_23_ = bf16[64,2176]{1,0:T(8,128)(2,1)S(1)} collective-permute-done((bf16[64,2176]{1,0:T(8,128)(2,1)S(1)}, bf16[64,2176]{1,0:T(8,128)(2,1)S(1)}, u32[]{:S(2)}, u32[]{:S(2)}) %collective-permute-start.8) | collective-permute-done | bytes 278560 | tf_op jit(solution)/shard_map/ppermute | solution.py:883
  62.2 3.3 %maximum_select_fusion.x_ref = bf16[768,1024]{1,0:T(8,128)(2,1)} fusion(bf16[384,1024]{1,0:T(8,128)(2,1)} %copy-done.36, bf16[384,1024]{1,0:T(8,128)(2,1)S(1)} %copy-done.2, pred[]{:T(512)S(6)} %eq.39), kind=kLoop, calls=%fused_computation.14 | loop fusion | flops 7077888 | bytes 3145729 | tf_op jit(solution)/shard_map/jit(_where)/select_n | solution.py:984
  69.8 22.2 %front.1 = (bf16[768,1024]{1,0:T(8,128)(2,1)}, bf16[768,1024]{1,0:T(8,128)(2,1)}, bf16[768,1536]{1,0:T(8,128)(2,1)}, bf16[768,512]{1,0:T(8,128)(2,1)}, f32[4,8,768]{2,1,0:T(8,128)}, /*index=5*/bf16[768,1024]{1,0:T(8,128)(2,1)}) custom-call(s32[20]{0:T(128)} %copy-done.26, bf16[768,1024]{1,0:T(8,128)(2,1)} %maximum_select_fusion.x_ref, f32[8,1024]{1,0:T(8,128)} %copy-done.23, ...), custom_call_target="tpu_custom_call" | custom-call | flops 9663676416 | bytes 9437184 | tf_op jit(solution)/shard_map/front/pallas_call | solution.py:444
  92.9 2.1 maximum_select_fusion.1
  95.0 2.0 stack.51.grad_ref
  97.0 31.4 %collective-permute-done.17.other_ref = bf16[768,1024]{1,0:T(8,128)(2,1)} collective-permute-done((bf16[768,1024]{1,0:T(8,128)(2,1)}, bf16[768,1024]{1,0:T(8,128)(2,1)}, u32[]{:S(2)}, u32[]{:S(2)}) %collective-permute-start.17) | collective-permute-done | bytes 1572896 | tf_op jit(solution)/shard_map/ppermute | solution.py:925
  128.4 23.7 %feed.1 = (bf16[768,1024]{1,0:T(8,128)(2,1)}, bf16[2,768,1024]{2,1,0:T(8,128)(2,1)}, bf16[2,768,2048]{2,1,0:T(8,128)(2,1)}, bf16[768,1024]{1,0:T(8,128)(2,1)}, b...) custom-call(s32[20]{0:T(128)} %copy-done.26, ...), custom_call_target="tpu_custom_call", output_to_operand_aliasing={{1}: (6, {})} | custom-call | flops 14495514624 | bytes 31457280 | tf_op jit(solution)/shard_map/feed/pallas_call | solution.py:534
  153.2 3.0 fusion.6
  156.2 9.0 %convolution_convert_fusion = bf16[2,1024,2048]{2,1,0:T(8,128)(2,1)} fusion(bf16[2,768,1024]{2,1,0:T(8,128)(2,1)S(1)} %copy-done.32, bf16[2,768,2048]{2,1,0:T(8,128)(2,1)S(1)} %bitcast.82), kind=kOutput, calls=%fused_computation | convolution fusion | flops 6446645248 | bytes 17825792 | tf_op jit(solution)/shard_map/dot_general | solution.py:1004
  166.4 21.2 %collective-permute-done.18.other_ref = bf16[768,1024]{1,0:T(8,128)(2,1)S(1)} collective-permute-done((bf16[768,1024]{1,0:T(8,128)(2,1)}, bf16[768,1024]{1,0:T(8,128)(2,1)S(1)}, u32[]{:S(2)}, u32[]{:S(2)}) %collective-permute-start.18) | collective-permute-done | bytes 1572896 | tf_op jit(solution)/shard_map/ppermute | solution.py:925
  188.7 7.7 %mid.1 = (bf16[768,1024]{1,0:T(8,128)(2,1)}, bf16[768,512]{1,0:T(8,128)(2,1)}, f32[8,1024]{1,0:T(8,128)}) custom-call(s32[20]{0:T(128)} %copy-done.26, bf16[768,1024]{1,0:T(8,128)(2,1)} %get-tuple-element.95.resid_ref, bf16[768,1024]{1,0:T(8,128)(2,1)} %get-tuple-element.75.own_ref, bf16[768,1024]{1,0:T(8,128)(2,1)} %copy-done.40, ...), custom_call_target="tpu_custom_call" | custom-call | flops 12884901888 | bytes 12582912 | tf_op jit(solution)/shard_map/mid/pallas_call | solution.py:594
  196.4 23.2 %back.1 = (bf16[768,1536]{1,0:T(8,128)(2,1)}, bf16[768,1024]{1,0:T(8,128)(2,1)}, f32[4,8,384]{2,1,0:T(8,128)}, f32[8,1024]{1,0:T(8,128)}) custom-call(s32[20]{0:T(128)} %copy-done.26, bf16[768,1024]{1,0:T(8,128)(2,1)} %get-tuple-element.71.xhat_ref, bf16[768,1536]{1,0:T(8,128)(2,1)} %get-tuple-element.72.qkv_ref, ...), custom_call_target="tpu_custom_call" | custom-call | flops 115964116992 | bytes 9437184 | tf_op jit(solution)/shard_map/back/pallas_call | solution.py:710
  221.2 4.3 %convolution_convert_fusion.1 = bf16[512,1536]{1,0:T(8,128)(2,1)} fusion(bf16[768,1536]{1,0:T(8,128)(2,1)} %get-tuple-element.80, bf16[768,1024]{1,0:T(8,128)(2,1)S(1)} %copy-done.33), kind=kOutput, calls=%fused_computation.4 | convolution fusion | flops 1208745984 | bytes 4718592 | tf_op jit(solution)/shard_map/dot_general | solution.py:37
  226.1 1.8 fusion.7
  230.9 2.7 collective-permute-done.21
  234.9 1.7 fusion.9
  236.6 2.8 fusion.3
  242.6 17.9 %collective-permute-done.25.other_ref = bf16[384,1024]{1,0:T(8,128)(2,1)S(1)} collective-permute-done((bf16[384,1024]{1,0:T(8,128)(2,1)S(1)}, bf16[384,1024]{1,0:T(8,128)(2,1)S(1)}, u32[]{:S(2)}, u32[]{:S(2)}) %collective-permute-start.25) | collective-permute-done | bytes 786464 | tf_op jit(solution)/shard_map/ppermute | solution.py:925
  262.6 8.1 %collective-permute-done.24 = f32[4,768]{1,0:T(4,128)S(1)} collective-permute-done((f32[4,768]{1,0:T(4,128)S(1)}, f32[4,768]{1,0:T(4,128)S(1)}, u32[]{:S(2)}, u32[]{:S(2)}) %collective-permute-start.24) | collective-permute-done | bytes 12320 | tf_op jit(solution)/shard_map/ppermute | solution.py:883
  272.1 2.0 fusion.2
  275.6 2.5 collective-permute-start.27
  278.1 2.0 collective-permute-start.29
  282.4 2.2 result.1
  284.6 3.0 last.1
  290.5 2.1 fusion.16
  292.6 1.6 collective-permute-done.30
  294.2 8.6 %collective-permute-done.31 = bf16[64,2048]{1,0:T(8,128)(2,1)S(1)} collective-permute-done((bf16[64,2048]{1,0:T(8,128)(2,1)S(1)}, bf16[64,2048]{1,0:T(8,128)(2,1)S(1)}, u32[]{:S(2)}, u32[]{:S(2)}) %collective-permute-start.31) | collective-permute-done | bytes 262176 | tf_op jit(solution)/shard_map/ppermute | solution.py:883
  302.8 1.7 collective-permute-done.32
  (206 shorter events, 55.0 us)
Async XLA Ops:
  7.2 121.2 %all-gather.2.cloned.1.call-start = ((), (), s32[]{:S(2)}) async-start(), calls=%async_computation.1 | async-start | bytes 8912896 | tf_op jit(solution)/shard_map/all_gather | solution.py:978
  7.2 41.4 %collective-permute-start = (bf16[384,1024]{1,0:T(8,128)(2,1)}, bf16[384,1024]{1,0:T(8,128)(2,1)S(1)}, u32[]{:S(2)}, u32[]{:S(2)}) collective-permute-start(bf16[384,1024]{1,0:T(8,128)(2,1)} %x_ref.1), channel_id=1, source_target_pairs={{0,1},{1,0},{2,3},{3,2},{4,5},{5,4},{6,7},{7,6},{8,9},{9,8},{10,11... | collective-permute-start | bytes 2359304 | tf_op jit(solution)/shard_map/ppermute | solution.py:925
  15.5 20.6 %collective-permute-start.2 = (bf16[64,2176]{1,0:T(8,128)(2,1)S(1)}, bf16[64,2176]{1,0:T(8,128)(2,1)S(1)}, u32[]{:S(2)}, u32[]{:S(2)}) collective-permute-start(bf16[64,2176]{1,0:T(8,128)(2,1)S(1)} %get-tuple-element.60.refs_0_.refs_16_), channel_id=1, source_target_pairs={{0,8},{2,10},{4,12},{6,14},{8,16},{10,18},{12,20},{14,22},{16,24},... | collective-permute-start | bytes 835592 | tf_op jit(solution)/shard_map/ppermute | solution.py:883
  17.1 23.5 %collective-permute-start.3 = (bf16[64,2176]{1,0:T(8,128)(2,1)S(1)}, bf16[64,2176]{1,0:T(8,128)(2,1)S(1)}, u32[]{:S(2)}, u32[]{:S(2)}) collective-permute-start(bf16[64,2176]{1,0:T(8,128)(2,1)S(1)} %get-tuple-element.60.refs_0_.refs_16_), channel_id=1, source_target_pairs={{0,16},{2,18},{4,20},{6,22},{8,24},{10,26},{12,28},{14,30},{16,0},... | collective-permute-start | bytes 835592 | tf_op jit(solution)/shard_map/ppermute | solution.py:883
  18.3 24.1 %collective-permute-start.4 = (bf16[64,2176]{1,0:T(8,128)(2,1)S(1)}, bf16[64,2176]{1,0:T(8,128)(2,1)S(1)}, u32[]{:S(2)}, u32[]{:S(2)}) collective-permute-start(bf16[64,2176]{1,0:T(8,128)(2,1)S(1)} %get-tuple-element.60.refs_0_.refs_16_), channel_id=1, source_target_pairs={{0,24},{2,26},{4,28},{6,30},{8,0},{10,2},{12,4},{14,6},{16,8},{18,... | collective-permute-start | bytes 835592 | tf_op jit(solution)/shard_map/ppermute | solution.py:883
  20.1 22.3 %collective-permute-start.5 = (bf16[64,2176]{1,0:T(8,128)(2,1)S(1)}, bf16[64,2176]{1,0:T(8,128)(2,1)S(1)}, u32[]{:S(2)}, u32[]{:S(2)}) collective-permute-start(bf16[64,2176]{1,0:T(8,128)(2,1)S(1)} %get-tuple-element.60.refs_0_.refs_16_), channel_id=1, source_target_pairs={{0,4},{2,6},{4,0},{6,2},{8,12},{10,14},{12,8},{14,10},{16,20},{18,... | collective-permute-start | bytes 835592 | tf_op jit(solution)/shard_map/ppermute | solution.py:883
  36.1 7.3 %collective-permute-start.6 = (bf16[64,2176]{1,0:T(8,128)(2,1)S(1)}, bf16[64,2176]{1,0:T(8,128)(2,1)S(1)}, u32[]{:S(2)}, u32[]{:S(2)}) collective-permute-start(bf16[64,2176]{1,0:T(8,128)(2,1)S(1)} %collective-permute-done.2.refs_1_.refs_17_), channel_id=1, source_target_pairs={{0,4},{2,6},{4,0},{6,2},{8,12},{10,14},{12,8},{14,10},{16,20},{18,... | collective-permute-start | bytes 835592 | tf_op jit(solution)/shard_map/ppermute | solution.py:883
  40.6 8.0 %collective-permute-start.7 = (bf16[64,2176]{1,0:T(8,128)(2,1)S(1)}, bf16[64,2176]{1,0:T(8,128)(2,1)S(1)}, u32[]{:S(2)}, u32[]{:S(2)}) collective-permute-start(bf16[64,2176]{1,0:T(8,128)(2,1)S(1)} %collective-permute-done.3.refs_2_.refs_18_), channel_id=1, source_target_pairs={{0,4},{2,6},{4,0},{6,2},{8,12},{10,14},{12,8},{14,10},{16,20},{18,... | collective-permute-start | bytes 835592 | tf_op jit(solution)/shard_map/ppermute | solution.py:883
  49.6 240.9 %reduce-scatter.2.cloned.1.call-start = ((), (), s32[]{:S(2)}) async-start(), calls=%async_computation.2 | async-start | bytes 8912896 | tf_op jit(solution)/shard_map/reduce_scatter | solution.py:1010
  49.6 20.3 %collective-permute-start.1 = (bf16[384,1024]{1,0:T(8,128)(2,1)}, bf16[384,1024]{1,0:T(8,128)(2,1)}, u32[]{:S(2)}, u32[]{:S(2)}) collective-permute-start(bf16[384,1024]{1,0:T(8,128)(2,1)} %param.16), channel_id=1, source_target_pairs={{0,1},{1,0},{2,3},{3,2},{4,5},{5,4},{6,7},{7,6},{8,9},{9,8},{10,11... | collective-permute-start | bytes 2359304 | tf_op jit(solution)/shard_map/ppermute | solution.py:925
  50.1 8.8 %collective-permute-start.8 = (bf16[64,2176]{1,0:T(8,128)(2,1)S(1)}, bf16[64,2176]{1,0:T(8,128)(2,1)S(1)}, u32[]{:S(2)}, u32[]{:S(2)}) collective-permute-start(bf16[64,2176]{1,0:T(8,128)(2,1)S(1)} %collective-permute-done.4.refs_3_.refs_19_), channel_id=1, source_target_pairs={{0,4},{2,6},{4,0},{6,2},{8,12},{10,14},{12,8},{14,10},{16,20},{18,... | collective-permute-start | bytes 835592 | tf_op jit(solution)/shard_map/ppermute | solution.py:883
  51.6 7.3 %collective-permute-start.10 = (bf16[64,2176]{1,0:T(8,128)(2,1)S(1)}, bf16[64,2176]{1,0:T(8,128)(2,1)S(1)}, u32[]{:S(2)}, u32[]{:S(2)}) collective-permute-start(bf16[64,2176]{1,0:T(8,128)(2,1)S(1)} %collective-permute-done.2.refs_1_.refs_17_), channel_id=1, source_target_pairs={{0,2},{2,0},{4,6},{6,4},{8,10},{10,8},{12,14},{14,12},{16,18},{18,... | collective-permute-start | bytes 835592 | tf_op jit(solution)/shard_map/ppermute | solution.py:883
  51.6 8.5 %collective-permute-start.11 = (bf16[64,2176]{1,0:T(8,128)(2,1)S(1)}, bf16[64,2176]{1,0:T(8,128)(2,1)S(1)}, u32[]{:S(2)}, u32[]{:S(2)}) collective-permute-start(bf16[64,2176]{1,0:T(8,128)(2,1)S(1)} %collective-permute-done.3.refs_2_.refs_18_), channel_id=1, source_target_pairs={{0,2},{2,0},{4,6},{6,4},{8,10},{10,8},{12,14},{14,12},{16,18},{18,... | collective-permute-start | bytes 835592 | tf_op jit(solution)/shard_map/ppermute | solution.py:883
  52.1 8.8 %collective-permute-start.12 = (bf16[64,2176]{1,0:T(8,128)(2,1)S(1)}, bf16[64,2176]{1,0:T(8,128)(2,1)S(1)}, u32[]{:S(2)}, u32[]{:S(2)}) collective-permute-start(bf16[64,2176]{1,0:T(8,128)(2,1)S(1)} %collective-permute-done.4.refs_3_.refs_19_), channel_id=1, source_target_pairs={{0,2},{2,0},{4,6},{6,4},{8,10},{10,8},{12,14},{14,12},{16,18},{18,... | collective-permute-start | bytes 835592 | tf_op jit(solution)/shard_map/ppermute | solution.py:883
  58.9 6.6 %collective-permute-start.13 = (bf16[64,2176]{1,0:T(8,128)(2,1)S(1)}, bf16[64,2176]{1,0:T(8,128)(2,1)}, u32[]{:S(2)}, u32[]{:S(2)}) collective-permute-start(bf16[64,2176]{1,0:T(8,128)(2,1)S(1)} %collective-permute-done.5.refs_4_.refs_20_), channel_id=1, source_target_pairs={{0,2},{2,0},{4,6},{6,4},{8,10},{10,8},{12,14},{14,12},{16,18},{18,... | collective-permute-start | bytes 835592 | tf_op jit(solution)/shard_map/ppermute | solution.py:883
  59.7 5.8 %collective-permute-start.14 = (bf16[64,2176]{1,0:T(8,128)(2,1)S(1)}, bf16[64,2176]{1,0:T(8,128)(2,1)}, u32[]{:S(2)}, u32[]{:S(2)}) collective-permute-start(bf16[64,2176]{1,0:T(8,128)(2,1)S(1)} %collective-permute-done.6.refs_5_.refs_21_), channel_id=1, source_target_pairs={{0,2},{2,0},{4,6},{6,4},{8,10},{10,8},{12,14},{14,12},{16,18},{18,... | collective-permute-start | bytes 835592 | tf_op jit(solution)/shard_map/ppermute | solution.py:883
  60.8 4.7 %collective-permute-start.15 = (bf16[64,2176]{1,0:T(8,128)(2,1)S(1)}, bf16[64,2176]{1,0:T(8,128)(2,1)}, u32[]{:S(2)}, u32[]{:S(2)}) collective-permute-start(bf16[64,2176]{1,0:T(8,128)(2,1)S(1)} %collective-permute-done.7.refs_6_.refs_22_), channel_id=1, source_target_pairs={{0,2},{2,0},{4,6},{6,4},{8,10},{10,8},{12,14},{14,12},{16,18},{18,... | collective-permute-start | bytes 835592 | tf_op jit(solution)/shard_map/ppermute | solution.py:883
  92.0 36.4 %collective-permute-start.17 = (bf16[768,1024]{1,0:T(8,128)(2,1)}, bf16[768,1024]{1,0:T(8,128)(2,1)}, u32[]{:S(2)}, u32[]{:S(2)}) collective-permute-start(bf16[768,1024]{1,0:T(8,128)(2,1)} %get-tuple-element.63.own_ref), channel_id=1, source_target_pairs={{0,1},{1,0},{2,3},{3,2},{4,5},{5,4},{6,7},{7,6},{8,9},{9,8},{10,11... | collective-permute-start | bytes 4718600 | tf_op jit(solution)/shard_map/ppermute | solution.py:925
  152.2 35.4 %collective-permute-start.18 = (bf16[768,1024]{1,0:T(8,128)(2,1)}, bf16[768,1024]{1,0:T(8,128)(2,1)S(1)}, u32[]{:S(2)}, u32[]{:S(2)}) collective-permute-start(bf16[768,1024]{1,0:T(8,128)(2,1)} %get-tuple-element.75.own_ref), channel_id=1, source_target_pairs={{0,1},{1,0},{2,3},{3,2},{4,5},{5,4},{6,7},{7,6},{8,9},{9,8},{10,11... | collective-permute-start | bytes 4718600 | tf_op jit(solution)/shard_map/ppermute | solution.py:925
  225.6 11.0 %collective-permute-start.19 = (bf16[512,1536]{1,0:T(8,128)(2,1)}, bf16[512,1536]{1,0:T(8,128)(2,1)}, u32[]{:S(2)}, u32[]{:S(2)}) collective-permute-start(bf16[512,1536]{1,0:T(8,128)(2,1)} %convolution_convert_fusion.1), channel_id=1, source_target_pairs={{0,2},{2,0},{4,6},{6,4},{8,10},{10,8},{12,14},{14,12},{16,18},{18,... | collective-permute-start | bytes 4718600 | tf_op jit(solution)/shard_map/ppermute | solution.py:883
  228.6 6.3 %collective-permute-start.20 = (bf16[512,512]{1,0:T(8,128)(2,1)S(1)}, bf16[512,512]{1,0:T(8,128)(2,1)S(1)}, u32[]{:S(2)}, u32[]{:S(2)}) collective-permute-start(bf16[512,512]{1,0:T(8,128)(2,1)S(1)} %convolution_convert_fusion.2), channel_id=1, source_target_pairs={{0,2},{2,0},{4,6},{6,4},{8,10},{10,8},{12,14},{14,12},{16,18},{18,... | collective-permute-start | bytes 1572872 | tf_op jit(solution)/shard_map/ppermute | solution.py:883
  229.4 4.2 %collective-permute-start.21 = (f32[16,768]{1,0:T(8,128)S(1)}, f32[16,768]{1,0:T(8,128)S(1)}, u32[]{:S(2)}, u32[]{:S(2)}) collective-permute-start(f32[16,768]{1,0:T(8,128)S(1)} %fusion.17), channel_id=1, source_target_pairs={{0,1},{1,0},{2,3},{3,2},{4,5},{5,4},{6,7},{7,6},{8,9},{9,8},{10,11... | collective-permute-start | bytes 147464 | tf_op jit(solution)/shard_map/ppermute | solution.py:925
  239.5 31.2 %collective-permute-start.23 = (bf16[256,2048]{1,0:T(8,128)(2,1)S(1)}, bf16[256,2048]{1,0:T(8,128)(2,1)S(1)}, u32[]{:S(2)}, u32[]{:S(2)}) collective-permute-start(bf16[256,2048]{1,0:T(8,128)(2,1)S(1)} %pad_maximum_fusion.1), channel_id=1, source_target_pairs={{0,4},{2,6},{4,0},{6,2},{8,12},{10,14},{12,8},{14,10},{16,20},{18,... | collective-permute-start | bytes 3145736 | tf_op jit(solution)/shard_map/ppermute | solution.py:883
  241.1 19.4 %collective-permute-start.25 = (bf16[384,1024]{1,0:T(8,128)(2,1)S(1)}, bf16[384,1024]{1,0:T(8,128)(2,1)S(1)}, u32[]{:S(2)}, u32[]{:S(2)}) collective-permute-start(bf16[384,1024]{1,0:T(8,128)(2,1)S(1)} %constant_dynamic-slice_fusion.1), channel_id=1, source_target_pairs={{0,1},{1,0},{2,3},{3,2},{4,5},{5,4},{6,7},{7,6},{8,9},{9,8},{10,11... | collective-permute-start | bytes 2359304 | tf_op jit(solution)/shard_map/ppermute | solution.py:925
  260.5 10.1 %collective-permute-start.24 = (f32[4,768]{1,0:T(4,128)S(1)}, f32[4,768]{1,0:T(4,128)S(1)}, u32[]{:S(2)}, u32[]{:S(2)}) collective-permute-start(f32[4,768]{1,0:T(4,128)S(1)} %slice.176), channel_id=1, source_target_pairs={{0,4},{2,6},{4,0},{6,2},{8,12},{10,14},{12,8},{14,10},{16,20},{18,... | collective-permute-start | bytes 36872 | tf_op jit(solution)/shard_map/ppermute | solution.py:883
  261.1 20.3 %collective-permute-start.26 = (bf16[384,1024]{1,0:T(8,128)(2,1)S(1)}, bf16[384,1024]{1,0:T(8,128)(2,1)S(1)}, u32[]{:S(2)}, u32[]{:S(2)}) collective-permute-start(bf16[384,1024]{1,0:T(8,128)(2,1)S(1)} %constant_dynamic-slice_fusion), channel_id=1, source_target_pairs={{0,1},{1,0},{2,3},{3,2},{4,5},{5,4},{6,7},{7,6},{8,9},{9,8},{10,11... | collective-permute-start | bytes 2359304 | tf_op jit(solution)/shard_map/ppermute | solution.py:925
  275.6 12.1 %collective-permute-start.27 = (f32[1,768]{1,0:T(1,128)S(1)}, f32[1,768]{1,0:T(1,128)S(1)}, u32[]{:S(2)}, u32[]{:S(2)}) collective-permute-start(f32[1,768]{1,0:T(1,128)S(1)} %get-tuple-element.111), channel_id=1, source_target_pairs={{0,16},{2,18},{4,20},{6,22},{8,24},{10,26},{12,28},{14,30},{16,0},... | collective-permute-start | bytes 9224 | tf_op jit(solution)/shard_map/ppermute | solution.py:883
  278.1 10.5 %collective-permute-start.28 = (f32[1,768]{1,0:T(1,128)S(1)}, f32[1,768]{1,0:T(1,128)S(1)}, u32[]{:S(2)}, u32[]{:S(2)}) collective-permute-start(f32[1,768]{1,0:T(1,128)S(1)} %get-tuple-element.113), channel_id=1, source_target_pairs={{0,8},{2,10},{4,12},{6,14},{8,16},{10,18},{12,20},{14,22},{16,24},... | collective-permute-start | bytes 9224 | tf_op jit(solution)/shard_map/ppermute | solution.py:883
  278.1 10.5 %collective-permute-start.29 = (f32[1,768]{1,0:T(1,128)S(1)}, f32[1,768]{1,0:T(1,128)S(1)}, u32[]{:S(2)}, u32[]{:S(2)}) collective-permute-start(f32[1,768]{1,0:T(1,128)S(1)} %get-tuple-element.112), channel_id=1, source_target_pairs={{0,24},{2,26},{4,28},{6,30},{8,0},{10,2},{12,4},{14,6},{16,8},{18,... | collective-permute-start | bytes 9224 | tf_op jit(solution)/shard_map/ppermute | solution.py:883
  280.9 13.3 %collective-permute-start.30 = (bf16[64,2048]{1,0:T(8,128)(2,1)}, bf16[64,2048]{1,0:T(8,128)(2,1)S(1)}, u32[]{:S(2)}, u32[]{:S(2)}) collective-permute-start(bf16[64,2048]{1,0:T(8,128)(2,1)} %get-tuple-element.104), channel_id=1, source_target_pairs={{0,16},{2,18},{4,20},{6,22},{8,24},{10,26},{12,28},{14,30},{16,0},... | collective-permute-start | bytes 786440 | tf_op jit(solution)/shard_map/ppermute | solution.py:883
  281.4 21.5 %collective-permute-start.31 = (bf16[64,2048]{1,0:T(8,128)(2,1)S(1)}, bf16[64,2048]{1,0:T(8,128)(2,1)S(1)}, u32[]{:S(2)}, u32[]{:S(2)}) collective-permute-start(bf16[64,2048]{1,0:T(8,128)(2,1)S(1)} %get-tuple-element.106), channel_id=1, source_target_pairs={{0,8},{2,10},{4,12},{6,14},{8,16},{10,18},{12,20},{14,22},{16,24},... | collective-permute-start | bytes 786440 | tf_op jit(solution)/shard_map/ppermute | solution.py:883
  287.6 16.9 %collective-permute-start.32 = (bf16[64,2048]{1,0:T(8,128)(2,1)S(1)}, bf16[64,2048]{1,0:T(8,128)(2,1)S(1)}, u32[]{:S(2)}, u32[]{:S(2)}) collective-permute-start(bf16[64,2048]{1,0:T(8,128)(2,1)S(1)} %get-tuple-element.105), channel_id=1, source_target_pairs={{0,24},{2,26},{4,28},{6,30},{8,0},{10,2},{12,4},{14,6},{16,8},{18,... | collective-permute-start | bytes 786440 | tf_op jit(solution)/shard_map/ppermute | solution.py:883
  (50 other events, 512.3 us)
Sparse Core Ops, SparseCore 0:
  48.8 74.5 all-gather.1
  165.4 109.9 reduce-scatter.1

commit v4 on v3

--- a/solution.py
+++ b/solution.py
@@ -387,14 +387,17 @@
         rows = slice(before, before + SEG)
         query = qkv_ref[rows, 0:128] * scale
         parts = []
+        drawn = []
+        for head in range(2):
+            mine = jnp.where(lane // 64 == head, query, jnp.zeros_like(query))
+            scores = contract_last(qkv_ref[rows, 128:256], mine)
+            early = contract_last(qkv_ref[0:before, 128:256], mine) if seg > 0 else None
+            drawn.append((jnp.where(reach, scores, -1e30), early))
         for head in range(2):
             lanes = slice(head * 64, head * 64 + 64)
-            mine = jnp.where(lane // 64 == head, query, jnp.zeros_like(query))
-            scores = contract_last(qkv_ref[rows, 128:256], mine)
-            scores = jnp.where(reach, scores, -1e30)
+            scores, early = drawn[head]
             top = jnp.max(scores, axis=0, keepdims=True)
             if seg > 0:
-                early = contract_last(qkv_ref[0:before, 128:256], mine)
                 top = jnp.maximum(top, jnp.max(early, axis=0, keepdims=True))
             expo = jnp.exp(scores - top)
             total = jnp.sum(expo, axis=0, keepdims=True)
@@ -408,20 +411,23 @@
         out_ref[rows, :] = jnp.transpose(jnp.concatenate(parts, axis=0)).astype(LOW)
 
 
-def front_kernel(place_ref, x_ref, vec_ref, bias_ref, *refs, scale, count):
+def front_kernel(place_ref, own_ref, other_ref, vec_ref, bias_ref, *refs, scale, count):
     pieces, outs = refs[:count], refs[count : 2 * count]
-    xhat_ref, norm_ref, qkv_ref, att_ref, log_ref, share_ref = refs[2 * count : 2 * count + 6]
-    weight_ref, out_ref, joined_ref = refs[2 * count + 6 :]
-    length = x_ref.shape[0]
+    x_ref, xhat_ref, norm_ref, qkv_ref, att_ref, log_ref = refs[2 * count : 2 * count + 6]
+    share_ref, weight_ref, out_ref, joined_ref = refs[2 * count + 6 :]
+    rows_own = own_ref.shape[0]
     step = pl.program_id(0)
 
     @pl.when(step == 0)
     def _():
-        for start in range(0, length, SEG):
-            rows = slice(start, start + SEG)
-            xhat, _ = row_stats(x_ref[rows, :].astype(jnp.float32))
-            xhat_ref[rows, :] = xhat.astype(LOW)
-            norm_ref[rows, :] = (xhat * vec_ref[0:1, :] + vec_ref[1:2, :]).astype(LOW)
+        for half, ref in ((place_ref[0], own_ref), (1 - place_ref[0], other_ref)):
+            for start in range(0, rows_own, 128):
+                rows = pl.ds(pl.multiple_of(half * rows_own + start, 128), 128)
+                x = ref[start : start + 128, :]
+                xhat, _ = row_stats(x.astype(jnp.float32))
+                x_ref[rows, :] = x
+                xhat_ref[rows, :] = xhat.astype(LOW)
+                norm_ref[rows, :] = (xhat * vec_ref[0:1, :] + vec_ref[1:2, :]).astype(LOW)
         fill_natural(place_ref, out_ref, outs)
 
     fill_natural(place_ref, weight_ref, pieces)
@@ -437,17 +443,19 @@
         share_ref[...] = contract_last(joined_ref[...], out_ref[...]).astype(LOW)
 
 
-def front(place, x, vectors, bias, pieces, pairs, scale):
-    length, width = x.shape
+def front(place, own, other, vectors, bias, pieces, pairs, scale):
+    length, width = 2 * own.shape[0], own.shape[1]
     once = pl.Buffered(1)
     square = pl.BlockSpec((length, width), lambda *_: (0, 0), pipeline_mode=once)
+    half = pl.BlockSpec(own.shape, lambda *_: (0, 0), pipeline_mode=once)
     return pl.pallas_call(
         functools.partial(front_kernel, scale=scale, count=len(pieces)),
         grid_spec=pltpu.PrefetchScalarGridSpec(
             num_scalar_prefetch=1,
             grid=(pairs,),
             in_specs=[
-                square,
+                half,
+                half,
                 whole(vectors.shape),
                 pl.BlockSpec((8, 128), lambda p, place: (0, place[0] * pairs + p)),
             ]
@@ -456,29 +464,31 @@
             out_specs=[
                 square,
                 square,
+                square,
                 pl.BlockSpec((length, 384), lambda p, _: (0, p)),
                 pl.BlockSpec((length, 128), lambda p, _: (0, p)),
                 pl.BlockSpec((1, 8, length), lambda p, _: (p, 0, 0)),
                 square,
+                pl.BlockSpec((width, 384), lambda p, _: (0, p)),
+                pl.BlockSpec((width, pairs * 128), lambda *_: (0, 0), pipeline_mode=once),
             ],
-            scratch_shapes=[
-                pltpu.VMEM((width, 384), LOW),
-                pltpu.VMEM((width, pairs * 128), LOW),
-                pltpu.VMEM((length, pairs * 128), LOW),
-            ],
+            scratch_shapes=[pltpu.VMEM((length, pairs * 128), LOW)],
         ),
         out_shape=[
+            jax.ShapeDtypeStruct((length, width), LOW),
             jax.ShapeDtypeStruct((length, width), LOW),
             jax.ShapeDtypeStruct((length, width), LOW),
             jax.ShapeDtypeStruct((length, pairs * 384), LOW),
             jax.ShapeDtypeStruct((length, pairs * 128), LOW),
             jax.ShapeDtypeStruct((pairs, 8, length), jnp.float32),
             jax.ShapeDtypeStruct((length, width), LOW),
+            jax.ShapeDtypeStruct((width, pairs * 384), LOW),
+            jax.ShapeDtypeStruct((width, pairs * 128), LOW),
         ],
         compiler_params=settings(56),
         cost_estimate=cost(2 * length * width * pairs * 384 * 4, 12 * length * width),
         name="front",
-    )(place, x, vectors, bias, *pieces, *pieces)
+    )(place, own, other, vectors, bias, *pieces, *pieces)
 
 
 def feed_kernel(
@@ -489,17 +499,34 @@
     vec_ref,
     bias_ref,
     grad_ref,
-    up_ref,
-    down_ref,
+    pair_ref,
     resid_ref,
     left_ref,
     right_ref,
-    mixed_ref,
     dnorm_ref,
     sum_ref,
+    up_ref,
+    down_ref,
+    sem,
 ):
-    @pl.when(pl.program_id(0) == 0)
+    first = pl.program_id(0) == 0
+    hidden = up_ref.shape[1]
+
+    def fetch(start):
+        part = pl.ds(start, 512)
+        index = start // 512
+        return (
+            pltpu.make_async_copy(pair_ref.at[:, part], up_ref.at[:, part], sem.at[0, index]),
+            pltpu.make_async_copy(
+                pair_ref.at[:, pl.ds(hidden + start, 512)], down_ref.at[:, part], sem.at[1, index]
+            ),
+        )
+
+    @pl.when(first)
     def _():
+        for start in range(0, hidden, 512):
+            for copy in fetch(start):
+                copy.start()
         sum_ref[...] = jnp.zeros_like(sum_ref)
 
     branch = own_ref[...].astype(jnp.float32) + other_ref[...].astype(jnp.float32)
@@ -508,9 +535,14 @@
     xhat, _ = row_stats(resid)
     norm = (xhat * vec_ref[3:4, :] + vec_ref[4:5, :]).astype(LOW)
     left_ref[0] = norm
-    hidden = up_ref.shape[1]
     for start in range(0, hidden, 512):
         columns = slice(start, start + 512)
+
+        @pl.when(first)
+        def _(start=start):
+            for copy in fetch(start):
+                copy.wait()
+
         pre = matmul(norm, up_ref[:, columns]) + bias_ref[:, columns]
         square = pre * pre
         bent = jnp.tanh(pre * (square * (0.044715 * gelu_coef) + gelu_coef))
@@ -523,13 +555,11 @@
         total = jnp.sum(dpre.astype(jnp.float32), axis=0, keepdims=True)
         sum_ref[:, columns] += jnp.broadcast_to(total, (8, 512))
     dnorm_ref[...] = contract_last(right_ref[1], up_ref[...]).astype(LOW)
-    mixed_ref[...] = contract_last(right_ref[0], down_ref[...]).astype(LOW)
 
 
 def feed_product(place, x, own, other, vectors, bias, lefts, pair, block=SEG):
     length, width = x.shape
     hidden = pair.shape[1] // 2
-    once = pl.Buffered(1)
     rows = pl.BlockSpec((block, width), lambda p, _: (p, 0))
     return pl.pallas_call(
         feed_kernel,
@@ -541,16 +571,19 @@
                 whole(vectors.shape),
                 pl.BlockSpec((1, hidden), lambda p, place: (0, place[0])),
                 pl.BlockSpec((1, block, width), lambda p, _: (0, p, 0)),
-                pl.BlockSpec((width, hidden), lambda *_: (0, 0), pipeline_mode=once),
-                pl.BlockSpec((width, hidden), lambda *_: (0, 1), pipeline_mode=once),
+                pl.BlockSpec(memory_space=pl.ANY),
             ],
             out_specs=[
                 rows,
                 pl.BlockSpec((1, block, width), lambda p, _: (1, p, 0)),
                 pl.BlockSpec((2, block, hidden), lambda p, _: (0, p, 0)),
                 rows,
-                rows,
                 whole((8, hidden)),
+            ],
+            scratch_shapes=[
+                pltpu.VMEM((width, hidden), LOW),
+                pltpu.VMEM((width, hidden), LOW),
+                pltpu.SemaphoreType.DMA((2, hidden // 512)),
             ],
         ),
         out_shape=[
@@ -558,23 +591,20 @@
             jax.ShapeDtypeStruct((2, length, width), LOW),
             jax.ShapeDtypeStruct((2, length, hidden), LOW),
             jax.ShapeDtypeStruct((length, width), LOW),
-            jax.ShapeDtypeStruct((length, width), LOW),
             jax.ShapeDtypeStruct((8, hidden), jnp.float32),
         ],
         input_output_aliases={6: 1},
         compiler_params=settings(56),
         cost_estimate=cost(9 * length * width * hidden, 40 * length * width),
         name="feed",
-    )(place, x, own, other, vectors, bias, lefts, pair, pair)
-
-
-def mid_kernel(place_ref, resid_ref, own_ref, other_ref, grad_ref, vec_ref, *refs, count):
-    pieces = refs[:count]
-    dbranch_ref, datt_ref, sum_ref, weight_ref = refs[count:]
-
+    )(place, x, own, other, vectors, bias, lefts, pair)
+
+
+def mid_kernel(
+    resid_ref, own_ref, other_ref, grad_ref, vec_ref, weight_ref, dbranch_ref, datt_ref, sum_ref
+):
     @pl.when(pl.program_id(0) == 0)
     def _():
-        fill_natural(place_ref, weight_ref, pieces)
         sum_ref[...] = jnp.zeros_like(sum_ref)
 
     dnorm = own_ref[...].astype(jnp.float32) + other_ref[...].astype(jnp.float32)
@@ -588,24 +618,20 @@
         sum_ref[row : row + 1, :] += 0.5 * jnp.sum(value, axis=0, keepdims=True)
 
 
-def mid_product(place, resid, own, other, grad, vectors, pieces, inner):
+def mid_product(resid, own, other, lefts, vectors, weight, block=SEG):
     length, width = resid.shape
-    rows = pl.BlockSpec((SEG, width), lambda p, _: (p, 0))
+    inner = weight.shape[1]
+    rows = pl.BlockSpec((block, width), lambda p: (p, 0))
     return pl.pallas_call(
-        functools.partial(mid_kernel, count=len(pieces)),
-        grid_spec=pltpu.PrefetchScalarGridSpec(
-            num_scalar_prefetch=1,
-            grid=(length // SEG,),
-            in_specs=[rows] * 3
-            + [pl.BlockSpec((1, SEG, width), lambda p, _: (0, p, 0)), whole(vectors.shape)]
-            + fixed_specs(pieces, inner, 3),
-            out_specs=[
-                rows,
-                pl.BlockSpec((SEG, inner), lambda p, _: (p, 0)),
-                whole((8, width)),
-            ],
-            scratch_shapes=[pltpu.VMEM((width, inner), LOW)],
-        ),
+        mid_kernel,
+        grid=(length // block,),
+        in_specs=[rows] * 3
+        + [
+            pl.BlockSpec((1, block, width), lambda p: (0, p, 0)),
+            whole(vectors.shape),
+            whole(weight.shape),
+        ],
+        out_specs=[rows, pl.BlockSpec((block, inner), lambda p: (p, 0)), whole((8, width))],
         out_shape=[
             jax.ShapeDtypeStruct((length, width), LOW),
             jax.ShapeDtypeStruct((length, inner), LOW),
@@ -614,7 +640,7 @@
         compiler_params=settings(56),
         cost_estimate=cost(2 * length * width * inner * 16, 16 * length * width),
         name="mid",
-    )(place, resid, own, other, grad, vectors, *pieces)
+    )(resid, own, other, lefts, vectors, weight)
 
 
 def attend_back_pair(qkv_ref, grad_ref, log_ref, out_ref, dkey_ref, dvalue_ref, scale):
@@ -633,24 +659,26 @@
         parts = []
         dkeys = [None] * len(spans)
         dvalues = [None] * len(spans)
+        drawn = []
         for head in range(2):
             here = lane // 64 == head
-            lanes = slice(head * 64, head * 64 + 64)
             query_mine = jnp.where(here, query, jnp.zeros_like(query))
             grad_mine = jnp.where(here, grad, jnp.zeros_like(grad))
+            scores = [contract_last(qkv_ref[span, 128:256], query_mine) for span in spans]
+            scores[0] = jnp.where(reach, scores[0], -1e30)
+            dprobs = [contract_last(qkv_ref[span, 256:384], grad_mine) for span in spans]
+            drawn.append((query_mine, grad_mine, scores, dprobs))
+        for head in range(2):
+            lanes = slice(head * 64, head * 64 + 64)
+            query_mine, grad_mine, scores, dprobs = drawn[head]
             log_row = log_ref[0, head : head + 1, rows]
-            probs, dprobs = [], []
+            probs = []
             mean = None
-            for index, span in enumerate(spans):
-                scores = contract_last(qkv_ref[span, 128:256], query_mine)
-                if index == 0:
-                    scores = jnp.where(reach, scores, -1e30)
-                prob = jnp.exp(scores - log_row)
-                dprob = contract_last(qkv_ref[span, 256:384], grad_mine)
-                share = jnp.sum(prob * dprob, axis=0, keepdims=True)
+            for index in range(len(spans)):
+                prob = jnp.exp(scores[index] - log_row)
+                share = jnp.sum(prob * dprobs[index], axis=0, keepdims=True)
                 mean = share if mean is None else mean + share
                 probs.append(prob)
-                dprobs.append(dprob)
             part = None
             for index, span in enumerate(spans):
                 dscores = (probs[index] * (dprobs[index] - mean)).astype(LOW)
@@ -673,12 +701,23 @@
     out_ref[:, 256:384] = dvalue_ref[...].astype(LOW)
 
 
-def back_kernel(place_ref, xhat_ref, qkv_ref, grad_ref, log_ref, *refs, scale, count):
-    pieces = refs[:count]
-    dqkv_ref, dnorm_ref, sum_ref, vec_ref = refs[count : count + 4]
-    weight_ref, dkey_ref, dvalue_ref, acc_ref = refs[count + 4 :]
+def back_kernel(
+    xhat_ref,
+    qkv_ref,
+    grad_ref,
+    log_ref,
+    weight_ref,
+    dqkv_ref,
+    dnorm_ref,
+    sum_ref,
+    vec_ref,
+    dkey_ref,
+    dvalue_ref,
+    acc_ref,
+    *,
+    scale,
+):
     step = pl.program_id(0)
-    fill_natural(place_ref, weight_ref, pieces)
     attend_back_pair(qkv_ref, grad_ref, log_ref, dqkv_ref, dkey_ref, dvalue_ref, scale)
     dnorm = contract_last(dqkv_ref[...], weight_ref[...])
     sum_ref[...] = jnp.broadcast_to(
@@ -703,45 +742,43 @@
         )
 
 
-def back_product(place, xhat, qkv, grad, logs, pieces, scale):
+def back_product(xhat, qkv, grad, logs, weight, scale):
     length, columns = qkv.shape
-    width = sum(piece.shape[0] for piece in pieces)
+    width = weight.shape[0]
     pairs = columns // 384
+    once = pl.Buffered(1)
+    square = pl.BlockSpec((length, width), lambda p: (0, 0), pipeline_mode=once)
     return pl.pallas_call(
-        functools.partial(back_kernel, scale=scale, count=len(pieces)),
-        grid_spec=pltpu.PrefetchScalarGridSpec(
-            num_scalar_prefetch=1,
-            grid=(pairs,),
-            in_specs=[
-                whole((length, width)),
-                pl.BlockSpec((length, 384), lambda p, _: (0, p)),
-                pl.BlockSpec((length, 128), lambda p, _: (0, p)),
-                pl.BlockSpec((1, 8, length), lambda p, _: (p, 0, 0)),
-            ]
-            + piece_specs(pieces, 384),
-            out_specs=[
-                pl.BlockSpec((length, 384), lambda p, _: (0, p)),
-                whole((length, width)),
-                pl.BlockSpec((1, 8, 384), lambda p, _: (p, 0, 0)),
-                whole((8, width)),
-            ],
-            scratch_shapes=[
-                pltpu.VMEM((width, 384), LOW),
-                pltpu.VMEM((length, 128), jnp.float32),
-                pltpu.VMEM((length, 128), jnp.float32),
-                pltpu.VMEM((length, width), jnp.float32),
-            ],
-        ),
+        functools.partial(back_kernel, scale=scale),
+        grid=(pairs,),
+        in_specs=[
+            square,
+            pl.BlockSpec((length, 384), lambda p: (0, p)),
+            pl.BlockSpec((length, 128), lambda p: (0, p)),
+            pl.BlockSpec((1, 8, length), lambda p: (p, 0, 0)),
+            pl.BlockSpec((width, 384), lambda p: (0, p)),
+        ],
+        out_specs=[
+            pl.BlockSpec((length, 384), lambda p: (0, p)),
+            square,
+            pl.BlockSpec((1, 8, 384), lambda p: (p, 0, 0)),
+            whole((8, width)),
+        ],
         out_shape=[
             jax.ShapeDtypeStruct((length, columns), LOW),
             jax.ShapeDtypeStruct((length, width), LOW),
             jax.ShapeDtypeStruct((pairs, 8, 384), jnp.float32),
             jax.ShapeDtypeStruct((8, width), jnp.float32),
         ],
+        scratch_shapes=[
+            pltpu.VMEM((length, 128), jnp.float32),
+            pltpu.VMEM((length, 128), jnp.float32),
+            pltpu.VMEM((length, width), jnp.float32),
+        ],
         compiler_params=settings(56),
         cost_estimate=cost(2 * length * width * columns * 48, 12 * length * width),
         name="back",
-    )(place, xhat, qkv, grad, logs, *pieces)
+    )(xhat, qkv, grad, logs, weight)
 
 
 def last_kernel(place_ref, x_ref, dbranch_ref, own_ref, other_ref, vec_ref, out_ref):
@@ -822,7 +859,7 @@
             jax.ShapeDtypeStruct((rows, 4 * columns + 128), LOW),
             jax.ShapeDtypeStruct((rows, 2 * up.shape[1]), LOW),
         ],
-        compiler_params=settings(28),
+        compiler_params=settings(56),
         cost_estimate=cost(0, 4 * rows * (4 * columns + 2 * up.shape[1])),
         name="pack",
     )(proj, out, up, down, vec)
@@ -863,7 +900,7 @@
             jax.ShapeDtypeStruct((8, width), jnp.float32),
             jax.ShapeDtypeStruct((1, 4 * width), jnp.float32),
         ],
-        compiler_params=settings(28),
+        compiler_params=settings(56),
         cost_estimate=cost(width * 128, 2 * width * 128),
         name="vectors",
     )(place, *pieces)
@@ -883,28 +920,29 @@
     return lax.ppermute(value, "dp", [(rank, goes(rank)) for rank in range(ranks)])
 
 
-def dp_gather(shard, ranks):
+def dp_gather(shard, ranks, event):
     far = [shard] + [dp_shift(shard, ranks, k, 0, 0) for k in (1, 2, 3)]
-    near = [dp_shift(piece, ranks, 0, 1, 0) for piece in far]
+    sent = far[:2] + [after(far[2], event)] + far[3:]
+    near = [dp_shift(piece, ranks, 0, 1, 0) for piece in sent]
     pieces = far + near
     return pieces + [dp_shift(piece, ranks, 0, 0, 1) for piece in pieces], pieces
 
 
 def reduce_core(left, right, ranks):
-    half = left.shape[1] // 2
-    return dp_shift(contract_rows(left[:, half:], right).astype(LOW), ranks, 0, 0, 1)
+    half = left.shape[0] // 2
+    return dp_shift(matmul(left[half:], right).astype(LOW), ranks, 0, 0, 1)
 
 
 def reduce_near(left, right, other):
-    half = left.shape[1] // 2
+    half = left.shape[0] // 2
     part = half // 2
-    sent = contract_rows(left[:, part:half], right) + other[part:].astype(jnp.float32)
+    sent = matmul(left[part:half], right) + other[part:].astype(jnp.float32)
     return sent.astype(LOW)
 
 
 def reduce_sum(left, right, other, arrived):
-    part = left.shape[1] // 4
-    total = contract_rows(left[:, :part], right) + other[:part].astype(jnp.float32)
+    part = left.shape[0] // 4
+    total = matmul(left[:part], right) + other[:part].astype(jnp.float32)
     return total + arrived.astype(jnp.float32)
 
 
@@ -972,11 +1010,11 @@
         [jnp.stack(vec), qv_bias, up_bias.reshape(4, shard), jnp.zeros((2, shard), LOW)], axis=0
     )
     narrow_shard, wide_shard = pack_shards(w_qkv, w_attn_out.T, w_up, w_down.T, vec)
-    inputs_other = swap(inputs)
+    narrow, narrow_far = dp_gather(narrow_shard, ranks, place)
+    inputs_other = swap(after(inputs, narrow_shard))
     grad_other = swap(after(out_grad, inputs_other))
-    narrow, narrow_far = dp_gather(narrow_shard, ranks)
     wide = lax.all_gather(
-        after(wide_shard, inputs_other, *narrow_far[1:7]), "dp", axis=0, tiled=True
+        after(wide_shard, inputs_other, *narrow_far[1:6]), "dp", axis=0, tiled=True
     )
     vectors, query_bias, hidden_bias = spread_vectors(place, narrow, 16)
 
@@ -987,18 +1025,29 @@
             jnp.concatenate([other, own], axis=0),
         )
 
+    def to_slots(value):
+        return lax.dot_general(
+            to_local, value, (((0,), (1,)), ((), ())), preferred_element_type=jnp.float32
+        ).astype(LOW)
+
     def other_rows(value):
         return lax.dynamic_slice_in_dim(value, (1 - side) * rows, rows, 0)
 
-    hidden_in = in_order(inputs, inputs_other)
-    xhat, norm_one, qkv, attended, logs, share = front(
-        place, after(hidden_in, grad_other), vectors, query_bias, narrow, pairs, scale
+    hidden_in, xhat, norm_one, qkv, attended, logs, share, proj_full, out_full = front(
+        place,
+        inputs,
+        inputs_other,
+        vectors,
+        query_bias,
+        narrow,
+        pairs,
+        scale,
     )
     cotangent = after(in_order(out_grad, grad_other), share)
     lefts = jnp.stack([cotangent, jnp.zeros_like(cotangent)])
-    norm_slot = matmul(after(norm_one, share), to_local).astype(LOW)
-    resid, lefts, rights, mixed_share, dnorm_share, dpre_sum = feed_product(
-        place, hidden_in, share, swap(share), vectors, hidden_bias, lefts, wide
+    norm_slot = to_slots(after(norm_one, share))
+    resid, lefts, rights, dnorm_share, dpre_sum = feed_product(
+        place, hidden_in, share, swap(after(share, grad_other)), vectors, hidden_bias, lefts, wide
     )
     dnorm_other = swap(dnorm_share)
     wide_share = lax.dot_general(
@@ -1008,20 +1057,13 @@
         preferred_element_type=jnp.float32,
     ).astype(LOW)
     wide_grad = lax.psum_scatter(wide_share, "dp", scatter_dimension=1, tiled=True)
+    mixed_share = contract_last(after(rights, wide_share)[0], wide[:, hidden:]).astype(LOW)
     dbranch, dattended, mid_sum = mid_product(
-        place,
-        after(resid, wide_share, norm_slot),
-        dnorm_share,
-        dnorm_other,
-        lefts,
-        vectors,
-        narrow,
-        heads_width,
+        after(resid, mixed_share, norm_slot), dnorm_share, dnorm_other, lefts, vectors, out_full
     )
     dqkv, dnorm_one, dqkv_sum, front_sum = back_product(
-        place, xhat, qkv, dattended, logs, narrow, scale
-    )
-    proj_core = reduce_core(norm_slot, dqkv, ranks)
+        xhat, qkv, dattended, logs, proj_full, scale
+    )
     dqkv_sum = dqkv_sum[:, 0].reshape(pairs, 3, 128)
     placed = [
         place_block(value, 2 * value.shape[0], side * value.shape[0]).reshape(ranks, -1)
@@ -1040,10 +1082,11 @@
         precision=lax.Precision.HIGHEST,
         preferred_element_type=jnp.float32,
     )
+    proj_core = reduce_core(norm_slot, after(dqkv, pack), ranks)
     pack = pack + swap(pack)
     pack = pack[: ranks // 2] + dp_shift(pack[ranks // 2 :], ranks, 0, 0, 1)
     back_other = swap(other_rows(after(dnorm_one, pack)))
-    dbranch_slot = matmul(after(dbranch, dattended), to_local).astype(LOW)
+    dbranch_slot = to_slots(after(dbranch, dattended))
     out_core = reduce_core(dbranch_slot, attended, ranks)
     slim_near, pack = lax.optimization_barrier(
         (

time: 316 us -> 308 us (0.975)
  matrix products: 26.8 us -> 39.3 us
  Pallas kernels: 84.4 us -> 76.1 us
  local copies, waits for them, and re-layouts: 23.2 us -> 17.6 us
  other arithmetic: 9.16 us -> 4.59 us
    dot_general x2 -> x6, matrix products: 4.83 us -> 13.8 us  [matmul(): return jnp.dot(left, right, preferred_element_type=jnp.float32)]
    ppermute x7, waiting for transfers between devices: 74 us -> 65.2 us  [swap(): return lax.ppermute(value, 'tensor', [(0, 1), (1, 0)])]
    unnamed x94 -> x72, local copies, waits for them, and re-layouts: 11 us -> 3.36 us
    ppermute x26, waiting for transfers between devices: 51.8 us -> 59.2 us  [dp_shift(): lax.ppermute(value, 'dp', [(rank, goes(rank)) for rank in range(ranks)])]
    pallas_call x2, Pallas kernels: 30.9 us -> 26 us  [the longest x1 19 us: back_product(): pl.pallas_call(functools.partial(back_kernel, scale=scale), grid=(pairs,)...]
    select_n x2 -> x1, other arithmetic: 5.34 us -> 0.68 us  [in_order(): jnp.where(side == 0, jnp.concatenate([own, other], axis=0), jnp.concatena...]
    pallas_call x1, Pallas kernels: 23.7 us -> 20.1 us  [feed_product(): pl.pallas_call(feed_kernel, grid_spec=pltpu.PrefetchScalarGridSpec(num_sc...]
    dot_general x1, matrix products: 9 us -> 12.3 us  [paired(): lax.dot_general(lefts, after(rights, dnorm_share), (((1,), (1,)), ((0,),...]
  transfers between devices with their start and end apart: 35 -> 35, of which waited for: 16 -> 15; matrix products, arithmetic and copies ran while one was open for 14% -> 17% of each run, Pallas kernels for 19% -> 18%
where the time goes in v4:
time: 308 us; the launch traced here: 307 us
  waiting for transfers between devices  124 us (40%)
  Pallas kernels  76.1 us (25%)
  matrix products  39.3 us (13%)
  starting transfers between devices  30.1 us (10%)
  local copies, waits for them, and re-layouts  17.6 us (6%)
  between operations  14.7 us (5%)
  other arithmetic  4.59 us (1%)
    ppermute x7, waiting for transfers between devices, swap(): return lax.ppermute(value, 'tensor', [(0, 1), (1, 0)])  65.2 us
    ppermute x26, waiting for transfers between devices, dp_shift(): lax.ppermute(value, 'dp', [(rank, goes(rank)) for rank in range(ranks)])  59.2 us
    ppermute x26, starting transfers between devices, dp_shift(): lax.ppermute(value, 'dp', [(rank, goes(rank)) for rank in range(ranks)])  24.6 us
    pallas_call x1, Pallas kernels, front(): pl.pallas_call(functools.partial(front_kernel, scale=scale, count=len(pie...  20.2 us
    pallas_call x1, Pallas kernels, feed_product(): pl.pallas_call(feed_kernel, grid_spec=pltpu.PrefetchScalarGridSpec(num_sc...  20.1 us
    pallas_call x1, Pallas kernels, back_product(): pl.pallas_call(functools.partial(back_kernel, scale=scale), grid=(pairs,)...  19 us
    dot_general x6, matrix products, matmul(): return jnp.dot(left, right, preferred_element_type=jnp.float32)  13.8 us
    dot_general x1, matrix products, paired(): lax.dot_general(lefts, after(rights, dnorm_share), (((1,), (1,)), ((0,),...  12.3 us
  transfers between devices with their start and end apart: 35, of which 15 were waited for; matrix products, arithmetic and copies ran while one was open for 17% of the time, Pallas kernels for 18%

profile of v4, /device:TPU:8, one launch (start us, length us, event | category | flops | bytes accessed | tf_op | source)
XLA Modules:
  0.0 306.8 jit_solution(17663640354177422967)
XLA Ops:
  8.0 2.6 concatenate.22.vec_ref
  10.6 2.1 pack.1
  17.7 2.6 collective-permute-start.2
  20.3 14.8 %collective-permute-done.1.refs_1_.refs_17_ = bf16[64,2176]{1,0:T(8,128)(2,1)S(1)} collective-permute-done((bf16[64,2176]{1,0:T(8,128)(2,1)}, bf16[64,2176]{1,0:T(8,128)(2,1)S(1)}, u32[]{:S(2)}, u32[]{:S(2)}) %collective-permute-start.1) | collective-permute-done | bytes 278560 | tf_op jit(solution)/shard_map/ppermute | solution.py:920
  36.6 3.0 collective-permute-done.2.refs_2_.refs_18_
  39.6 2.0 collective-permute-done.5.refs_5_.refs_21_
  45.6 6.9 %collective-permute-done.7.refs_7_.refs_23_ = bf16[64,2176]{1,0:T(8,128)(2,1)S(1)} collective-permute-done((bf16[64,2176]{1,0:T(8,128)(2,1)S(1)}, bf16[64,2176]{1,0:T(8,128)(2,1)S(1)}, u32[]{:S(2)}, u32[]{:S(2)}) %collective-permute-start.7) | collective-permute-done | bytes 278560 | tf_op jit(solution)/shard_map/ppermute | solution.py:920
  52.5 10.7 %collective-permute-done.6.refs_6_.refs_22_ = bf16[64,2176]{1,0:T(8,128)(2,1)S(1)} collective-permute-done((bf16[64,2176]{1,0:T(8,128)(2,1)S(1)}, bf16[64,2176]{1,0:T(8,128)(2,1)S(1)}, u32[]{:S(2)}, u32[]{:S(2)}) %collective-permute-start.6) | collective-permute-done | bytes 278560 | tf_op jit(solution)/shard_map/ppermute | solution.py:920
  66.2 2.4 vectors.1
  68.5 20.2 %front.1 = (bf16[768,1024]{1,0:T(8,128)(2,1)}, bf16[768,1024]{1,0:T(8,128)(2,1)}, bf16[768,1024]{1,0:T(8,128)(2,1)}, bf16[768,1536]{1,0:T(8,128)(2,1)}, bf16[768...) custom-call(s32[20]{0:T(128)} %concatenate.21.place_ref, ...), custom_call_target="tpu_custom_call" | custom-call | flops 9663676416 | bytes 9437184 | tf_op jit(solution)/shard_map/front/pallas_call | solution.py:451
  90.2 4.5 %fusion.13 = bf16[1024,768]{1,0:T(8,128)(2,1)} fusion(bf16[768,1024]{1,0:T(8,128)(2,1)} %get-tuple-element.79, s32[1024]{0:T(1024)S(1)} %add.167), kind=kOutput, calls=%fused_computation.17 | convolution fusion | flops 1613496320 | bytes 3149824 | tf_op jit(solution)/shard_map/dot_general | solution.py:1029
  95.4 2.1 stack.51.grad_ref
  97.6 27.9 %collective-permute-done.17.other_ref = bf16[768,1024]{1,0:T(8,128)(2,1)S(1)} collective-permute-done((bf16[768,1024]{1,0:T(8,128)(2,1)}, bf16[768,1024]{1,0:T(8,128)(2,1)S(1)}, u32[]{:S(2)}, u32[]{:S(2)}) %collective-permute-start.17) | collective-permute-done | bytes 1572896 | tf_op jit(solution)/shard_map/ppermute | solution.py:963
  126.7 20.1 %feed.1 = (bf16[768,1024]{1,0:T(8,128)(2,1)}, bf16[2,768,1024]{2,1,0:T(8,128)(2,1)}, bf16[2,768,2048]{2,1,0:T(8,128)(2,1)}, bf16[768,1024]{1,0:T(8,128)(2,1)}, f32[8,2048]{1,0:T(8,128)}) custom-call(s32[20]{0:T(128)} %concatenate.21.place_ref, bf16[768,1024]{1,0:T(8,128)(2,1)} %get-tuple-element.69.x_ref, ...), custom_call_target="tpu_custom_call", output_to_operand_aliasing={{1}: (6, {})} | custom-call | flops 14495514624 | bytes 31457280 | tf_op jit(solution)/shard_map/feed/pallas_call | solution.py:564
  147.8 12.3 %convolution_convert_fusion = bf16[2,1024,2048]{2,1,0:T(8,128)(2,1)} fusion(bf16[2,768,1024]{2,1,0:T(8,128)(2,1)} %get-tuple-element.83.grad_ref, bf16[2,768,2048]{2,1,0:T(8,128)(2,1)} %get-tuple-element.86), kind=kOutput, calls=%fused_computation | convolution fusion | flops 6446645248 | bytes 17825792 | tf_op jit(solution)/shard_map/dot_general | solution.py:1053
  161.2 6.6 %fusion.19.own_ref = bf16[768,1024]{1,0:T(8,128)(2,1)S(1)} fusion(bf16[1024,4096]{1,0:T(8,128)(2,1)} %all-gather.2.cloned.1.call-done.pair_ref, bf16[2,768,2048]{2,1,0:T(8,128)(2,1)} %get-tuple-element.86), kind=kOutput, calls=%fused_computation.19 | convolution fusion | flops 3222011904 | bytes 8912896 | tf_op jit(solution)/shard_map/dot_general | solution.py:43
  167.8 14.8 %collective-permute-done.18.other_ref = bf16[768,1024]{1,0:T(8,128)(2,1)S(1)} collective-permute-done((bf16[768,1024]{1,0:T(8,128)(2,1)}, bf16[768,1024]{1,0:T(8,128)(2,1)S(1)}, u32[]{:S(2)}, u32[]{:S(2)}) %collective-permute-start.18) | collective-permute-done | bytes 1572896 | tf_op jit(solution)/shard_map/ppermute | solution.py:963
  183.8 7.0 %mid.1 = (bf16[768,1024]{1,0:T(8,128)(2,1)}, bf16[768,512]{1,0:T(8,128)(2,1)}, f32[8,1024]{1,0:T(8,128)}) custom-call(bf16[768,1024]{1,0:T(8,128)(2,1)} %get-tuple-element.108.resid_ref, bf16[768,1024]{1,0:T(8,128)(2,1)} %get-tuple-element.84.own_ref, bf16[768,1024]{1,0:T(8,128)(2,1)} %copy-done.34, bf16[2,768,1024]{2,1,0:T(8,128)(2,1)} %get-tuple-element.83.grad_ref, ...), custom_call_target="tpu_custom_call" | custom-call | flops 12884901888 | bytes 12582912 | tf_op jit(solution)/shard_map/mid/pallas_call | solution.py:625
  190.8 19.0 %back.1 = (bf16[768,1536]{1,0:T(8,128)(2,1)}, bf16[768,1024]{1,0:T(8,128)(2,1)}, f32[4,8,384]{2,1,0:T(8,128)}, f32[8,1024]{1,0:T(8,128)}) custom-call(bf16[768,1024]{1,0:T(8,128)(2,1)} %get-tuple-element.80.xhat_ref, bf16[768,1536]{1,0:T(8,128)(2,1)} %get-tuple-element.81.qkv_ref, bf16[768,512]{1,0:T(8,128)(2,1)} %get-tuple-element.89.grad_ref, ...), custom_call_target="tpu_custom_call" | custom-call | flops 115964116992 | bytes 9437184 | tf_op jit(solution)/shard_map/back/pallas_call | solution.py:751
  212.2 4.6 %convolution_convert_fusion.1 = bf16[512,1536]{1,0:T(8,128)(2,1)} fusion(bf16[768,1536]{1,0:T(8,128)(2,1)} %get-tuple-element.97, bf16[1024,768]{1,0:T(8,128)(2,1)} %fusion.13), kind=kOutput, calls=%fused_computation.7 | convolution fusion | flops 1208745984 | bytes 4718592 | tf_op jit(solution)/shard_map/dot_general | solution.py:33
  221.1 3.6 %collective-permute-done.21 = f32[16,768]{1,0:T(8,128)S(1)} collective-permute-done((f32[16,768]{1,0:T(8,128)S(1)}, f32[16,768]{1,0:T(8,128)S(1)}, u32[]{:S(2)}, u32[]{:S(2)}) %collective-permute-start.21) | collective-permute-done | bytes 49184 | tf_op jit(solution)/shard_map/ppermute | solution.py:963
  227.8 2.7 fusion.10
  232.7 18.9 %collective-permute-done.25.other_ref = bf16[384,1024]{1,0:T(8,128)(2,1)S(1)} collective-permute-done((bf16[384,1024]{1,0:T(8,128)(2,1)S(1)}, bf16[384,1024]{1,0:T(8,128)(2,1)S(1)}, u32[]{:S(2)}, u32[]{:S(2)}) %collective-permute-start.25) | collective-permute-done | bytes 786464 | tf_op jit(solution)/shard_map/ppermute | solution.py:963
  253.8 8.1 %collective-permute-done.24 = f32[4,768]{1,0:T(4,128)S(1)} collective-permute-done((f32[4,768]{1,0:T(4,128)S(1)}, f32[4,768]{1,0:T(4,128)S(1)}, u32[]{:S(2)}, u32[]{:S(2)}) %collective-permute-start.24) | collective-permute-done | bytes 12320 | tf_op jit(solution)/shard_map/ppermute | solution.py:920
  263.3 2.0 fusion.9
  265.5 3.8 %collective-permute-start.27 = (f32[1,768]{1,0:T(1,128)S(1)}, f32[1,768]{1,0:T(1,128)S(1)}, u32[]{:S(2)}, u32[]{:S(2)}) collective-permute-start(f32[1,768]{1,0:T(1,128)S(1)} %get-tuple-element.123), channel_id=1, source_target_pairs={{0,16},{2,18},{4,20},{6,22},{8,24},{10,26},{12,28},{14,30},{16,0},... | collective-permute-start | bytes 9224 | tf_op jit(solution)/shard_map/ppermute | solution.py:920
  274.3 2.2 result.1
  276.5 3.0 last.1
  279.6 2.0 collective-permute-start.31
  283.4 2.1 fusion.32
  285.5 4.7 %collective-permute-done.30 = bf16[64,2048]{1,0:T(8,128)(2,1)S(1)} collective-permute-done((bf16[64,2048]{1,0:T(8,128)(2,1)}, bf16[64,2048]{1,0:T(8,128)(2,1)S(1)}, u32[]{:S(2)}, u32[]{:S(2)}) %collective-permute-start.30) | collective-permute-done | bytes 262176 | tf_op jit(solution)/shard_map/ppermute | solution.py:920
  290.2 6.5 %collective-permute-done.32 = bf16[64,2048]{1,0:T(8,128)(2,1)} collective-permute-done((bf16[64,2048]{1,0:T(8,128)(2,1)}, bf16[64,2048]{1,0:T(8,128)(2,1)}, u32[]{:S(2)}, u32[]{:S(2)}) %collective-permute-start.32) | collective-permute-done | bytes 262176 | tf_op jit(solution)/shard_map/ppermute | solution.py:920
  (183 shorter events, 46.2 us)
Async XLA Ops:
  7.2 118.3 %all-gather.2.cloned.1.call-start = ((), (), s32[]{:S(2)}) async-start(), calls=%async_computation.1 | async-start | bytes 8912896 | tf_op jit(solution)/shard_map/all_gather | solution.py:1016
  12.7 29.0 %collective-permute-start = (bf16[384,1024]{1,0:T(8,128)(2,1)}, bf16[384,1024]{1,0:T(8,128)(2,1)S(1)}, u32[]{:S(2)}, u32[]{:S(2)}) collective-permute-start(bf16[384,1024]{1,0:T(8,128)(2,1)} %x_ref.1), channel_id=1, source_target_pairs={{0,1},{1,0},{2,3},{3,2},{4,5},{5,4},{6,7},{7,6},{8,9},{9,8},{10,11... | collective-permute-start | bytes 2359304 | tf_op jit(solution)/shard_map/ppermute | solution.py:963
  14.2 20.9 %collective-permute-start.1 = (bf16[64,2176]{1,0:T(8,128)(2,1)}, bf16[64,2176]{1,0:T(8,128)(2,1)S(1)}, u32[]{:S(2)}, u32[]{:S(2)}) collective-permute-start(bf16[64,2176]{1,0:T(8,128)(2,1)} %get-tuple-element.64.refs_0_.refs_16_), channel_id=1, source_target_pairs={{0,8},{2,10},{4,12},{6,14},{8,16},{10,18},{12,20},{14,22},{16,24},... | collective-permute-start | bytes 835592 | tf_op jit(solution)/shard_map/ppermute | solution.py:920
  15.7 20.9 %collective-permute-start.4 = (bf16[64,2176]{1,0:T(8,128)(2,1)}, bf16[64,2176]{1,0:T(8,128)(2,1)S(1)}, u32[]{:S(2)}, u32[]{:S(2)}) collective-permute-start(bf16[64,2176]{1,0:T(8,128)(2,1)} %get-tuple-element.64.refs_0_.refs_16_), channel_id=1, source_target_pairs={{0,4},{2,6},{4,0},{6,2},{8,12},{10,14},{12,8},{14,10},{16,20},{18,... | collective-permute-start | bytes 835592 | tf_op jit(solution)/shard_map/ppermute | solution.py:920
  17.3 19.4 %collective-permute-start.3 = (bf16[64,2176]{1,0:T(8,128)(2,1)}, bf16[64,2176]{1,0:T(8,128)(2,1)S(1)}, u32[]{:S(2)}, u32[]{:S(2)}) collective-permute-start(bf16[64,2176]{1,0:T(8,128)(2,1)} %get-tuple-element.64.refs_0_.refs_16_), channel_id=1, source_target_pairs={{0,24},{2,26},{4,28},{6,30},{8,0},{10,2},{12,4},{14,6},{16,8},{18,... | collective-permute-start | bytes 835592 | tf_op jit(solution)/shard_map/ppermute | solution.py:920
  17.7 21.9 %collective-permute-start.2 = (bf16[64,2176]{1,0:T(8,128)(2,1)}, bf16[64,2176]{1,0:T(8,128)(2,1)S(1)}, u32[]{:S(2)}, u32[]{:S(2)}) collective-permute-start(bf16[64,2176]{1,0:T(8,128)(2,1)} %get-tuple-element.64.refs_0_.refs_16_), channel_id=1, source_target_pairs={{0,16},{2,18},{4,20},{6,22},{8,24},{10,26},{12,28},{14,30},{16,0},... | collective-permute-start | bytes 835592 | tf_op jit(solution)/shard_map/ppermute | solution.py:920
  35.1 6.5 %collective-permute-start.5 = (bf16[64,2176]{1,0:T(8,128)(2,1)S(1)}, bf16[64,2176]{1,0:T(8,128)(2,1)S(1)}, u32[]{:S(2)}, u32[]{:S(2)}) collective-permute-start(bf16[64,2176]{1,0:T(8,128)(2,1)S(1)} %collective-permute-done.1.refs_1_.refs_17_), channel_id=1, source_target_pairs={{0,4},{2,6},{4,0},{6,2},{8,12},{10,14},{12,8},{14,10},{16,20},{18,... | collective-permute-start | bytes 835592 | tf_op jit(solution)/shard_map/ppermute | solution.py:920
  41.7 241.7 %reduce-scatter.2.cloned.1.call-start = ((), (), s32[]{:S(2)}) async-start(), calls=%async_computation.2 | async-start | bytes 8912896 | tf_op jit(solution)/shard_map/reduce_scatter | solution.py:1059
  41.7 3.2 %collective-permute-start.8 = (bf16[64,2176]{1,0:T(8,128)(2,1)}, bf16[64,2176]{1,0:T(8,128)(2,1)S(1)}, u32[]{:S(2)}, u32[]{:S(2)}) collective-permute-start(bf16[64,2176]{1,0:T(8,128)(2,1)} %get-tuple-element.64.refs_0_.refs_16_), channel_id=1, source_target_pairs={{0,2},{2,0},{4,6},{6,4},{8,10},{10,8},{12,14},{14,12},{16,18},{18,... | collective-permute-start | bytes 835592 | tf_op jit(solution)/shard_map/ppermute | solution.py:920
  42.5 3.0 collective-permute-start.12
  42.9 9.5 %collective-permute-start.7 = (bf16[64,2176]{1,0:T(8,128)(2,1)S(1)}, bf16[64,2176]{1,0:T(8,128)(2,1)S(1)}, u32[]{:S(2)}, u32[]{:S(2)}) collective-permute-start(bf16[64,2176]{1,0:T(8,128)(2,1)S(1)} %collective-permute-done.3.refs_3_.refs_19_), channel_id=1, source_target_pairs={{0,4},{2,6},{4,0},{6,2},{8,12},{10,14},{12,8},{14,10},{16,20},{18,... | collective-permute-start | bytes 835592 | tf_op jit(solution)/shard_map/ppermute | solution.py:920
  44.5 18.7 %collective-permute-start.6 = (bf16[64,2176]{1,0:T(8,128)(2,1)S(1)}, bf16[64,2176]{1,0:T(8,128)(2,1)S(1)}, u32[]{:S(2)}, u32[]{:S(2)}) collective-permute-start(bf16[64,2176]{1,0:T(8,128)(2,1)S(1)} %collective-permute-done.2.refs_2_.refs_18_), channel_id=1, source_target_pairs={{0,4},{2,6},{4,0},{6,2},{8,12},{10,14},{12,8},{14,10},{16,20},{18,... | collective-permute-start | bytes 835592 | tf_op jit(solution)/shard_map/ppermute | solution.py:920
  45.0 18.2 %collective-permute-start.11 = (bf16[64,2176]{1,0:T(8,128)(2,1)S(1)}, bf16[64,2176]{1,0:T(8,128)(2,1)S(1)}, u32[]{:S(2)}, u32[]{:S(2)}) collective-permute-start(bf16[64,2176]{1,0:T(8,128)(2,1)S(1)} %collective-permute-done.3.refs_3_.refs_19_), channel_id=1, source_target_pairs={{0,2},{2,0},{4,6},{6,4},{8,10},{10,8},{12,14},{14,12},{16,18},{18,... | collective-permute-start | bytes 835592 | tf_op jit(solution)/shard_map/ppermute | solution.py:920
  45.0 18.7 %collective-permute-start.10 = (bf16[64,2176]{1,0:T(8,128)(2,1)S(1)}, bf16[64,2176]{1,0:T(8,128)(2,1)S(1)}, u32[]{:S(2)}, u32[]{:S(2)}) collective-permute-start(bf16[64,2176]{1,0:T(8,128)(2,1)S(1)} %collective-permute-done.2.refs_2_.refs_18_), channel_id=1, source_target_pairs={{0,2},{2,0},{4,6},{6,4},{8,10},{10,8},{12,14},{14,12},{16,18},{18,... | collective-permute-start | bytes 835592 | tf_op jit(solution)/shard_map/ppermute | solution.py:920
  45.5 18.3 %collective-permute-start.9 = (bf16[64,2176]{1,0:T(8,128)(2,1)S(1)}, bf16[64,2176]{1,0:T(8,128)(2,1)S(1)}, u32[]{:S(2)}, u32[]{:S(2)}) collective-permute-start(bf16[64,2176]{1,0:T(8,128)(2,1)S(1)} %collective-permute-done.1.refs_1_.refs_17_), channel_id=1, source_target_pairs={{0,2},{2,0},{4,6},{6,4},{8,10},{10,8},{12,14},{14,12},{16,18},{18,... | collective-permute-start | bytes 835592 | tf_op jit(solution)/shard_map/ppermute | solution.py:920
  52.4 11.3 %collective-permute-start.15 = (bf16[64,2176]{1,0:T(8,128)(2,1)S(1)}, bf16[64,2176]{1,0:T(8,128)(2,1)S(1)}, u32[]{:S(2)}, u32[]{:S(2)}) collective-permute-start(bf16[64,2176]{1,0:T(8,128)(2,1)S(1)} %collective-permute-done.7.refs_7_.refs_23_), channel_id=1, source_target_pairs={{0,2},{2,0},{4,6},{6,4},{8,10},{10,8},{12,14},{14,12},{16,18},{18,... | collective-permute-start | bytes 835592 | tf_op jit(solution)/shard_map/ppermute | solution.py:920
  63.7 25.1 %collective-permute-start.16 = (bf16[384,1024]{1,0:T(8,128)(2,1)}, bf16[384,1024]{1,0:T(8,128)(2,1)S(1)}, u32[]{:S(2)}, u32[]{:S(2)}) collective-permute-start(bf16[384,1024]{1,0:T(8,128)(2,1)} %param.16), channel_id=1, source_target_pairs={{0,1},{1,0},{2,3},{3,2},{4,5},{5,4},{6,7},{7,6},{8,9},{9,8},{10,11... | collective-permute-start | bytes 2359304 | tf_op jit(solution)/shard_map/ppermute | solution.py:963
  88.8 36.7 %collective-permute-start.17 = (bf16[768,1024]{1,0:T(8,128)(2,1)}, bf16[768,1024]{1,0:T(8,128)(2,1)S(1)}, u32[]{:S(2)}, u32[]{:S(2)}) collective-permute-start(bf16[768,1024]{1,0:T(8,128)(2,1)} %get-tuple-element.72.own_ref), channel_id=1, source_target_pairs={{0,1},{1,0},{2,3},{3,2},{4,5},{5,4},{6,7},{7,6},{8,9},{9,8},{10,11... | collective-permute-start | bytes 4718600 | tf_op jit(solution)/shard_map/ppermute | solution.py:963
  146.8 35.9 %collective-permute-start.18 = (bf16[768,1024]{1,0:T(8,128)(2,1)}, bf16[768,1024]{1,0:T(8,128)(2,1)S(1)}, u32[]{:S(2)}, u32[]{:S(2)}) collective-permute-start(bf16[768,1024]{1,0:T(8,128)(2,1)} %get-tuple-element.84.own_ref), channel_id=1, source_target_pairs={{0,1},{1,0},{2,3},{3,2},{4,5},{5,4},{6,7},{7,6},{8,9},{9,8},{10,11... | collective-permute-start | bytes 4718600 | tf_op jit(solution)/shard_map/ppermute | solution.py:963
  216.9 10.9 %collective-permute-start.19 = (bf16[512,1536]{1,0:T(8,128)(2,1)}, bf16[512,1536]{1,0:T(8,128)(2,1)}, u32[]{:S(2)}, u32[]{:S(2)}) collective-permute-start(bf16[512,1536]{1,0:T(8,128)(2,1)} %convolution_convert_fusion.1), channel_id=1, source_target_pairs={{0,2},{2,0},{4,6},{6,4},{8,10},{10,8},{12,14},{14,12},{16,18},{18,... | collective-permute-start | bytes 4718600 | tf_op jit(solution)/shard_map/ppermute | solution.py:920
  220.1 5.9 %collective-permute-start.20 = (bf16[512,512]{1,0:T(8,128)(2,1)}, bf16[512,512]{1,0:T(8,128)(2,1)}, u32[]{:S(2)}, u32[]{:S(2)}) collective-permute-start(bf16[512,512]{1,0:T(8,128)(2,1)} %convolution_convert_fusion.2), channel_id=1, source_target_pairs={{0,2},{2,0},{4,6},{6,4},{8,10},{10,8},{12,14},{14,12},{16,18},{18,... | collective-permute-start | bytes 1572872 | tf_op jit(solution)/shard_map/ppermute | solution.py:920
  220.6 4.1 %collective-permute-start.21 = (f32[16,768]{1,0:T(8,128)S(1)}, f32[16,768]{1,0:T(8,128)S(1)}, u32[]{:S(2)}, u32[]{:S(2)}) collective-permute-start(f32[16,768]{1,0:T(8,128)S(1)} %fusion.33), channel_id=1, source_target_pairs={{0,1},{1,0},{2,3},{3,2},{4,5},{5,4},{6,7},{7,6},{8,9},{9,8},{10,11... | collective-permute-start | bytes 147464 | tf_op jit(solution)/shard_map/ppermute | solution.py:963
  230.6 31.2 %collective-permute-start.23 = (bf16[256,2048]{1,0:T(8,128)(2,1)S(1)}, bf16[256,2048]{1,0:T(8,128)(2,1)S(1)}, u32[]{:S(2)}, u32[]{:S(2)}) collective-permute-start(bf16[256,2048]{1,0:T(8,128)(2,1)S(1)} %pad_maximum_fusion.1), channel_id=1, source_target_pairs={{0,4},{2,6},{4,0},{6,2},{8,12},{10,14},{12,8},{14,10},{16,20},{18,... | collective-permute-start | bytes 3145736 | tf_op jit(solution)/shard_map/ppermute | solution.py:920
  232.3 19.4 %collective-permute-start.25 = (bf16[384,1024]{1,0:T(8,128)(2,1)S(1)}, bf16[384,1024]{1,0:T(8,128)(2,1)S(1)}, u32[]{:S(2)}, u32[]{:S(2)}) collective-permute-start(bf16[384,1024]{1,0:T(8,128)(2,1)S(1)} %constant_dynamic-slice_fusion.1), channel_id=1, source_target_pairs={{0,1},{1,0},{2,3},{3,2},{4,5},{5,4},{6,7},{7,6},{8,9},{9,8},{10,11... | collective-permute-start | bytes 2359304 | tf_op jit(solution)/shard_map/ppermute | solution.py:963
  251.7 10.2 %collective-permute-start.24 = (f32[4,768]{1,0:T(4,128)S(1)}, f32[4,768]{1,0:T(4,128)S(1)}, u32[]{:S(2)}, u32[]{:S(2)}) collective-permute-start(f32[4,768]{1,0:T(4,128)S(1)} %slice.184), channel_id=1, source_target_pairs={{0,4},{2,6},{4,0},{6,2},{8,12},{10,14},{12,8},{14,10},{16,20},{18,... | collective-permute-start | bytes 36872 | tf_op jit(solution)/shard_map/ppermute | solution.py:920
  253.2 21.0 %collective-permute-start.26 = (bf16[384,1024]{1,0:T(8,128)(2,1)S(1)}, bf16[384,1024]{1,0:T(8,128)(2,1)S(1)}, u32[]{:S(2)}, u32[]{:S(2)}) collective-permute-start(bf16[384,1024]{1,0:T(8,128)(2,1)S(1)} %constant_dynamic-slice_fusion), channel_id=1, source_target_pairs={{0,1},{1,0},{2,3},{3,2},{4,5},{5,4},{6,7},{7,6},{8,9},{9,8},{10,11... | collective-permute-start | bytes 2359304 | tf_op jit(solution)/shard_map/ppermute | solution.py:963
  265.5 14.0 %collective-permute-start.27 = (f32[1,768]{1,0:T(1,128)S(1)}, f32[1,768]{1,0:T(1,128)S(1)}, u32[]{:S(2)}, u32[]{:S(2)}) collective-permute-start(f32[1,768]{1,0:T(1,128)S(1)} %get-tuple-element.123), channel_id=1, source_target_pairs={{0,16},{2,18},{4,20},{6,22},{8,24},{10,26},{12,28},{14,30},{16,0},... | collective-permute-start | bytes 9224 | tf_op jit(solution)/shard_map/ppermute | solution.py:920
  269.3 12.3 %collective-permute-start.29 = (f32[1,768]{1,0:T(1,128)S(1)}, f32[1,768]{1,0:T(1,128)S(1)}, u32[]{:S(2)}, u32[]{:S(2)}) collective-permute-start(f32[1,768]{1,0:T(1,128)S(1)} %get-tuple-element.124), channel_id=1, source_target_pairs={{0,24},{2,26},{4,28},{6,30},{8,0},{10,2},{12,4},{14,6},{16,8},{18,... | collective-permute-start | bytes 9224 | tf_op jit(solution)/shard_map/ppermute | solution.py:920
  269.9 11.7 %collective-permute-start.28 = (f32[1,768]{1,0:T(1,128)S(1)}, f32[1,768]{1,0:T(1,128)S(1)}, u32[]{:S(2)}, u32[]{:S(2)}) collective-permute-start(f32[1,768]{1,0:T(1,128)S(1)} %get-tuple-element.125), channel_id=1, source_target_pairs={{0,8},{2,10},{4,12},{6,14},{8,16},{10,18},{12,20},{14,22},{16,24},... | collective-permute-start | bytes 9224 | tf_op jit(solution)/shard_map/ppermute | solution.py:920
  272.4 17.8 %collective-permute-start.30 = (bf16[64,2048]{1,0:T(8,128)(2,1)}, bf16[64,2048]{1,0:T(8,128)(2,1)S(1)}, u32[]{:S(2)}, u32[]{:S(2)}) collective-permute-start(bf16[64,2048]{1,0:T(8,128)(2,1)} %get-tuple-element.116), channel_id=1, source_target_pairs={{0,16},{2,18},{4,20},{6,22},{8,24},{10,26},{12,28},{14,30},{16,0},... | collective-permute-start | bytes 786440 | tf_op jit(solution)/shard_map/ppermute | solution.py:920
  274.3 22.5 %collective-permute-start.32 = (bf16[64,2048]{1,0:T(8,128)(2,1)}, bf16[64,2048]{1,0:T(8,128)(2,1)}, u32[]{:S(2)}, u32[]{:S(2)}) collective-permute-start(bf16[64,2048]{1,0:T(8,128)(2,1)} %get-tuple-element.117), channel_id=1, source_target_pairs={{0,24},{2,26},{4,28},{6,30},{8,0},{10,2},{12,4},{14,6},{16,8},{18,... | collective-permute-start | bytes 786440 | tf_op jit(solution)/shard_map/ppermute | solution.py:920
  279.6 17.2 %collective-permute-start.31 = (bf16[64,2048]{1,0:T(8,128)(2,1)}, bf16[64,2048]{1,0:T(8,128)(2,1)S(1)}, u32[]{:S(2)}, u32[]{:S(2)}) collective-permute-start(bf16[64,2048]{1,0:T(8,128)(2,1)} %get-tuple-element.118), channel_id=1, source_target_pairs={{0,8},{2,10},{4,12},{6,14},{8,16},{10,18},{12,20},{14,22},{16,24},... | collective-permute-start | bytes 786440 | tf_op jit(solution)/shard_map/ppermute | solution.py:920
  (39 other events, 393.1 us)
Sparse Core Ops, SparseCore 0:
  41.8 76.6 all-gather.1
  160.2 113.8 reduce-scatter.1

commit v5 on v4

--- a/solution.py
+++ b/solution.py
@@ -411,15 +411,39 @@
         out_ref[rows, :] = jnp.transpose(jnp.concatenate(parts, axis=0)).astype(LOW)
 
 
-def front_kernel(place_ref, own_ref, other_ref, vec_ref, bias_ref, *refs, scale, count):
-    pieces, outs = refs[:count], refs[count : 2 * count]
-    x_ref, xhat_ref, norm_ref, qkv_ref, att_ref, log_ref = refs[2 * count : 2 * count + 6]
-    share_ref, weight_ref, out_ref, joined_ref = refs[2 * count + 6 :]
+def read_vectors(vec_ref, bias_ref, hidden_ref, joined_ref):
+    turned = jnp.transpose(joined_ref[...]).astype(jnp.float32)
+    vec_ref[...] = turned[0:8]
+    bias_ref[...] = turned[8:16]
+    lane = lax.broadcasted_iota(jnp.int32, (1, 128), 1)
+    for pair in range(bias_ref.shape[1] // 128):
+        rows = [turned[10 + q : 11 + q, pair * 128 : pair * 128 + 128] for q in range(4)]
+        flipped = [pltpu.roll(row, 64, 1) for row in rows]
+        for q in (0, 2):
+            start = pair * 512 + q * 64
+            hidden_ref[:, start : start + 128] = jnp.where(lane < 64, rows[q], flipped[q + 1])
+            hidden_ref[:, start + 256 : start + 384] = jnp.where(
+                lane < 64, flipped[q], rows[q + 1]
+            )
+
+
+def front_kernel(place_ref, own_ref, other_ref, *refs, scale, count):
+    pieces, outs, vecs = (refs[i * count : (i + 1) * count] for i in range(3))
+    kept, refs = refs[3 * count : 3 * count + 4], refs[3 * count + 4 :]
+    qkv_ref, att_ref, log_ref, share_ref, weight_ref, vec_ref, hidden_ref = refs[:7]
+    x_ref, xhat_ref, norm_ref, out_ref, joined_ref, bias_ref, lines_ref, sem = refs[7:]
+    pairs = pl.num_programs(0)
+    copies = [
+        pltpu.make_async_copy(source, target, sem.at[index])
+        for index, (source, target) in enumerate(zip((x_ref, xhat_ref, norm_ref, out_ref), kept))
+    ]
     rows_own = own_ref.shape[0]
     step = pl.program_id(0)
 
     @pl.when(step == 0)
     def _():
+        fill_natural(place_ref, lines_ref, vecs)
+        read_vectors(vec_ref, bias_ref, hidden_ref, lines_ref)
         for half, ref in ((place_ref[0], own_ref), (1 - place_ref[0], other_ref)):
             for start in range(0, rows_own, 128):
                 rows = pl.ds(pl.multiple_of(half * rows_own + start, 128), 128)
@@ -429,10 +453,13 @@
                 xhat_ref[rows, :] = xhat.astype(LOW)
                 norm_ref[rows, :] = (xhat * vec_ref[0:1, :] + vec_ref[1:2, :]).astype(LOW)
         fill_natural(place_ref, out_ref, outs)
+        for copy in copies:
+            copy.start()
 
     fill_natural(place_ref, weight_ref, pieces)
+    mine = pl.ds(pl.multiple_of((place_ref[0] * pairs + step) * 128, 128), 128)
     bias = jnp.concatenate(
-        [bias_ref[0:1, :], jnp.zeros((1, 128), jnp.float32), bias_ref[1:2, :]], axis=1
+        [bias_ref[0:1, mine], jnp.zeros((1, 128), jnp.float32), bias_ref[1:2, mine]], axis=1
     )
     qkv_ref[...] = (matmul(norm_ref[...], weight_ref[...]) + bias).astype(LOW)
     attend_pair(qkv_ref, att_ref, log_ref, scale)
@@ -441,9 +468,11 @@
     @pl.when(step == pl.num_programs(0) - 1)
     def _():
         share_ref[...] = contract_last(joined_ref[...], out_ref[...]).astype(LOW)
-
-
-def front(place, own, other, vectors, bias, pieces, pairs, scale):
+        for copy in copies:
+            copy.wait()
+
+
+def front(place, own, other, pieces, pairs, scale):
     length, width = 2 * own.shape[0], own.shape[1]
     once = pl.Buffered(1)
     square = pl.BlockSpec((length, width), lambda *_: (0, 0), pipeline_mode=once)
@@ -456,39 +485,48 @@
             in_specs=[
                 half,
                 half,
-                whole(vectors.shape),
-                pl.BlockSpec((8, 128), lambda p, place: (0, place[0] * pairs + p)),
             ]
             + piece_specs(pieces, 384)
-            + fixed_specs(pieces, pairs * 128, 3),
-            out_specs=[
-                square,
-                square,
-                square,
+            + fixed_specs(pieces, pairs * 128, 3)
+            + fixed_specs(pieces, 128, pairs * 4),
+            out_specs=[pl.BlockSpec(memory_space=pl.ANY)] * 4
+            + [
                 pl.BlockSpec((length, 384), lambda p, _: (0, p)),
                 pl.BlockSpec((length, 128), lambda p, _: (0, p)),
                 pl.BlockSpec((1, 8, length), lambda p, _: (p, 0, 0)),
                 square,
                 pl.BlockSpec((width, 384), lambda p, _: (0, p)),
-                pl.BlockSpec((width, pairs * 128), lambda *_: (0, 0), pipeline_mode=once),
+                whole((8, width)),
+                whole((1, 4 * width)),
             ],
-            scratch_shapes=[pltpu.VMEM((length, pairs * 128), LOW)],
+            scratch_shapes=[
+                pltpu.VMEM((length, width), LOW),
+                pltpu.VMEM((length, width), LOW),
+                pltpu.VMEM((length, width), LOW),
+                pltpu.VMEM((width, pairs * 128), LOW),
+                pltpu.VMEM((length, pairs * 128), LOW),
+                pltpu.VMEM((8, width), jnp.float32),
+                pltpu.VMEM((width, 128), LOW),
+                pltpu.SemaphoreType.DMA((4,)),
+            ],
         ),
         out_shape=[
             jax.ShapeDtypeStruct((length, width), LOW),
             jax.ShapeDtypeStruct((length, width), LOW),
             jax.ShapeDtypeStruct((length, width), LOW),
+            jax.ShapeDtypeStruct((width, pairs * 128), LOW),
             jax.ShapeDtypeStruct((length, pairs * 384), LOW),
             jax.ShapeDtypeStruct((length, pairs * 128), LOW),
             jax.ShapeDtypeStruct((pairs, 8, length), jnp.float32),
             jax.ShapeDtypeStruct((length, width), LOW),
             jax.ShapeDtypeStruct((width, pairs * 384), LOW),
-            jax.ShapeDtypeStruct((width, pairs * 128), LOW),
+            jax.ShapeDtypeStruct((8, width), jnp.float32),
+            jax.ShapeDtypeStruct((1, 4 * width), jnp.float32),
         ],
         compiler_params=settings(56),
         cost_estimate=cost(2 * length * width * pairs * 384 * 4, 12 * length * width),
         name="front",
-    )(place, own, other, vectors, bias, *pieces, *pieces)
+    )(place, own, other, *pieces, *pieces, *pieces)
 
 
 def feed_kernel(
@@ -865,47 +903,6 @@
     )(proj, out, up, down, vec)
 
 
-def vector_kernel(place_ref, *refs):
-    pieces = refs[:-4]
-    vec_ref, bias_ref, hidden_ref, joined_ref = refs[-4:]
-    fill_natural(place_ref, joined_ref, pieces)
-    turned = jnp.transpose(joined_ref[...]).astype(jnp.float32)
-    vec_ref[...] = turned[0:8]
-    bias_ref[...] = turned[8:16]
-    lane = lax.broadcasted_iota(jnp.int32, (1, 128), 1)
-    for pair in range(bias_ref.shape[1] // 128):
-        rows = [turned[10 + q : 11 + q, pair * 128 : pair * 128 + 128] for q in range(4)]
-        flipped = [pltpu.roll(row, 64, 1) for row in rows]
-        for q in (0, 2):
-            start = pair * 512 + q * 64
-            hidden_ref[:, start : start + 128] = jnp.where(lane < 64, rows[q], flipped[q + 1])
-            hidden_ref[:, start + 256 : start + 384] = jnp.where(
-                lane < 64, flipped[q], rows[q + 1]
-            )
-
-
-def spread_vectors(place, pieces, index):
-    width = sum(piece.shape[0] for piece in pieces)
-    return pl.pallas_call(
-        vector_kernel,
-        grid_spec=pltpu.PrefetchScalarGridSpec(
-            num_scalar_prefetch=1,
-            grid=(1,),
-            in_specs=fixed_specs(pieces, 128, index),
-            out_specs=[whole((8, width)), whole((8, width)), whole((1, 4 * width))],
-            scratch_shapes=[pltpu.VMEM((width, 128), LOW)],
-        ),
-        out_shape=[
-            jax.ShapeDtypeStruct((8, width), jnp.float32),
-            jax.ShapeDtypeStruct((8, width), jnp.float32),
-            jax.ShapeDtypeStruct((1, 4 * width), jnp.float32),
-        ],
-        compiler_params=settings(56),
-        cost_estimate=cost(width * 128, 2 * width * 128),
-        name="vectors",
-    )(place, *pieces)
-
-
 def after(value, *events):
     return lax.optimization_barrier((value,) + events)[0]
 
@@ -1016,7 +1013,6 @@
     wide = lax.all_gather(
         after(wide_shard, inputs_other, *narrow_far[1:6]), "dp", axis=0, tiled=True
     )
-    vectors, query_bias, hidden_bias = spread_vectors(place, narrow, 16)
 
     def in_order(own, other):
         return jnp.where(
@@ -1033,16 +1029,9 @@
     def other_rows(value):
         return lax.dynamic_slice_in_dim(value, (1 - side) * rows, rows, 0)
 
-    hidden_in, xhat, norm_one, qkv, attended, logs, share, proj_full, out_full = front(
-        place,
-        inputs,
-        inputs_other,
-        vectors,
-        query_bias,
-        narrow,
-        pairs,
-        scale,
-    )
+    early = front(place, inputs, inputs_other, narrow, pairs, scale)
+    hidden_in, xhat, norm_one, out_full, qkv, attended, logs, share, proj_full = early[:9]
+    vectors, hidden_bias = early[9:]
     cotangent = after(in_order(out_grad, grad_other), share)
     lefts = jnp.stack([cotangent, jnp.zeros_like(cotangent)])
     norm_slot = to_slots(after(norm_one, share))
@@ -1082,24 +1071,20 @@
         precision=lax.Precision.HIGHEST,
         preferred_element_type=jnp.float32,
     )
-    proj_core = reduce_core(norm_slot, after(dqkv, pack), ranks)
+    proj_core = reduce_core(norm_slot, dqkv, ranks)
+    dbranch_slot = to_slots(after(dbranch, pack))
     pack = pack + swap(pack)
-    pack = pack[: ranks // 2] + dp_shift(pack[ranks // 2 :], ranks, 0, 0, 1)
+    out_core = reduce_core(dbranch_slot, attended, ranks)
+    slim_near = jnp.concatenate(
+        [
+            reduce_near(norm_slot, dqkv, proj_core),
+            reduce_near(dbranch_slot, attended, out_core),
+        ],
+        axis=1,
+    )
+    pack = pack[: ranks // 2] + dp_shift(after(pack[ranks // 2 :], slim_near), ranks, 0, 0, 1)
+    slim_near, pack = lax.optimization_barrier((slim_near, pack))
     back_other = swap(other_rows(after(dnorm_one, pack)))
-    dbranch_slot = to_slots(after(dbranch, dattended))
-    out_core = reduce_core(dbranch_slot, attended, ranks)
-    slim_near, pack = lax.optimization_barrier(
-        (
-            jnp.concatenate(
-                [
-                    reduce_near(norm_slot, dqkv, proj_core),
-                    reduce_near(dbranch_slot, attended, out_core),
-                ],
-                axis=1,
-            ),
-            pack,
-        )
-    )
     pack_arrived = dp_shift(pack[ranks // 4 :], ranks, 0, 1, 0)
     slim_arrived = dp_shift(slim_near, ranks, 0, 1, 0)
     own_other = swap(other_rows(after(mixed_share, back_other)))
@@ -1119,12 +1104,11 @@
             pack[: ranks // 4] + pack_arrived,
         )
     )
-    pack = far_sum(pack_total, far_send(pack_total, ranks, jnp.float32)).reshape(-1)
     grad_back = wide_grad[0].T.astype(jnp.float32)
     grad_hidden = wide_grad[1].astype(jnp.float32)
-    slim_grad = far_sum(
-        after(slim_total, grad_back, grad_hidden), far_send(slim_total, ranks)
-    )
+    pack = far_sum(pack_total, far_send(pack_total, ranks, jnp.float32)).reshape(-1)
+    slim_sent = far_send(slim_total, ranks)
+    slim_grad = far_sum(after(slim_total, grad_back, grad_hidden), slim_sent)
     grad_proj = slim_grad[:, :columns]
     grad_out = slim_grad[:, columns:].T
     result = result_product(

time: 308 us -> 302 us (0.981)
  matrix products: 39.3 us -> 35.1 us
    dot_general x6, matrix products: 13.8 us -> 9.44 us  [matmul(): return jnp.dot(left, right, preferred_element_type=jnp.float32)]
  transfers between devices with their start and end apart: 35 -> 35, of which waited for: 15 -> 15; matrix products, arithmetic and copies ran while one was open for 17% -> 16% of each run, Pallas kernels for 18% -> 17%
where the time goes in v5:
time: 302 us
  waiting for transfers between devices  123 us (41%)
  Pallas kernels  73.4 us (24%)
  matrix products  35.1 us (12%)
  starting transfers between devices  30.4 us (10%)
  local copies, waits for them, and re-layouts  19.9 us (7%)
  between operations  14.8 us (5%)
  other arithmetic  5.64 us (2%)
    ppermute x7, waiting for transfers between devices, swap(): return lax.ppermute(value, 'tensor', [(0, 1), (1, 0)])  64.3 us
    ppermute x26, waiting for transfers between devices, dp_shift(): lax.ppermute(value, 'dp', [(rank, goes(rank)) for rank in range(ranks)])  58.3 us
    ppermute x26, starting transfers between devices, dp_shift(): lax.ppermute(value, 'dp', [(rank, goes(rank)) for rank in range(ranks)])  24.9 us
    pallas_call x1, Pallas kernels, feed_product(): pl.pallas_call(feed_kernel, grid_spec=pltpu.PrefetchScalarGridSpec(num_sc...  20.1 us
    pallas_call x1, Pallas kernels, back_product(): pl.pallas_call(functools.partial(back_kernel, scale=scale), grid=(pairs,)...  19.2 us
    pallas_call x1, Pallas kernels, front(): pl.pallas_call(functools.partial(front_kernel, scale=scale, count=len(pie...  18.5 us
    dot_general x1, matrix products, paired(): lax.dot_general(lefts, after(rights, dnorm_share), (((1,), (1,)), ((0,),...  12.4 us
    dot_general x6, matrix products, matmul(): return jnp.dot(left, right, preferred_element_type=jnp.float32)  9.44 us
  transfers between devices with their start and end apart: 35, of which 15 were waited for; matrix products, arithmetic and copies ran while one was open for 16% of the time, Pallas kernels for 17%

profile of v5, /device:TPU:8, one launch (start us, length us, event | category | flops | bytes accessed | tf_op | source)
XLA Modules:
  0.0 301.8 jit_solution(9651673067501213337)
XLA Ops:
  8.0 2.6 concatenate.22.vec_ref
  10.6 2.1 pack.1
  17.7 2.6 collective-permute-start.2
  20.3 14.8 %collective-permute-done.1.refs_1_.refs_17_.refs_33_ = bf16[64,2176]{1,0:T(8,128)(2,1)S(1)} collective-permute-done((bf16[64,2176]{1,0:T(8,128)(2,1)}, bf16[64,2176]{1,0:T(8,128)(2,1)S(1)}, u32[]{:S(2)}, u32[]{:S(2)}) %collective-permute-start.1) | collective-permute-done | bytes 278560 | tf_op jit(solution)/shard_map/ppermute | solution.py:917
  36.6 3.0 collective-permute-done.2.refs_2_.refs_18_.refs_34_
  39.6 2.0 collective-permute-done.5.refs_5_.refs_21_.refs_37_
  45.6 6.9 %collective-permute-done.7.refs_7_.refs_23_.refs_39_ = bf16[64,2176]{1,0:T(8,128)(2,1)S(1)} collective-permute-done((bf16[64,2176]{1,0:T(8,128)(2,1)S(1)}, bf16[64,2176]{1,0:T(8,128)(2,1)S(1)}, u32[]{:S(2)}, u32[]{:S(2)}) %collective-permute-start.7) | collective-permute-done | bytes 278560 | tf_op jit(solution)/shard_map/ppermute | solution.py:917
  52.5 10.7 %collective-permute-done.6.refs_6_.refs_22_.refs_38_ = bf16[64,2176]{1,0:T(8,128)(2,1)S(1)} collective-permute-done((bf16[64,2176]{1,0:T(8,128)(2,1)S(1)}, bf16[64,2176]{1,0:T(8,128)(2,1)S(1)}, u32[]{:S(2)}, u32[]{:S(2)}) %collective-permute-start.6) | collective-permute-done | bytes 278560 | tf_op jit(solution)/shard_map/ppermute | solution.py:917
  66.1 18.5 %front.1 = (bf16[768,1024]{1,0:T(8,128)(2,1)}, bf16[768,1024]{1,0:T(8,128)(2,1)}, bf16[768,1024]{1,0:T(8,128)(2,1)}, bf16[1024,512]{1,0:T(8,128)(2,1)}, bf16[768...) custom-call(s32[20]{0:T(128)} %concatenate.21.place_ref, ...), custom_call_target="tpu_custom_call" | custom-call | flops 9663676416 | bytes 9437184 | tf_op jit(solution)/shard_map/front/pallas_call | solution.py:480
  86.1 4.6 %fusion.13 = bf16[1024,768]{1,0:T(8,128)(2,1)} fusion(bf16[768,1024]{1,0:T(8,128)(2,1)} %get-tuple-element.77, s32[1024]{0:T(1024)S(1)} %add.167), kind=kOutput, calls=%fused_computation.17 | convolution fusion | flops 1613496320 | bytes 3149824 | tf_op jit(solution)/shard_map/dot_general | solution.py:1025
  91.4 2.1 stack.51.grad_ref
  93.5 27.8 %collective-permute-done.17.other_ref = bf16[768,1024]{1,0:T(8,128)(2,1)S(1)} collective-permute-done((bf16[768,1024]{1,0:T(8,128)(2,1)}, bf16[768,1024]{1,0:T(8,128)(2,1)S(1)}, u32[]{:S(2)}, u32[]{:S(2)}) %collective-permute-start.17) | collective-permute-done | bytes 1572896 | tf_op jit(solution)/shard_map/ppermute | solution.py:960
  122.5 20.1 %feed.1 = (bf16[768,1024]{1,0:T(8,128)(2,1)}, bf16[2,768,1024]{2,1,0:T(8,128)(2,1)}, bf16[2,768,2048]{2,1,0:T(8,128)(2,1)}, bf16[768,1024]{1,0:T(8,128)(2,1)}, f32[8,2048]{1,0:T(8,128)}) custom-call(s32[20]{0:T(128)} %concatenate.21.place_ref, bf16[768,1024]{1,0:T(8,128)(2,1)} %get-tuple-element.66.x_ref, ...), custom_call_target="tpu_custom_call", output_to_operand_aliasing={{1}: (6, {})} | custom-call | flops 14495514624 | bytes 31457280 | tf_op jit(solution)/shard_map/feed/pallas_call | solution.py:602
  143.6 12.4 %convolution_convert_fusion = bf16[2,1024,2048]{2,1,0:T(8,128)(2,1)} fusion(bf16[2,768,1024]{2,1,0:T(8,128)(2,1)} %get-tuple-element.81.grad_ref, bf16[2,768,2048]{2,1,0:T(8,128)(2,1)} %get-tuple-element.84), kind=kOutput, calls=%fused_computation | convolution fusion | flops 6446645248 | bytes 17825792 | tf_op jit(solution)/shard_map/dot_general | solution.py:1042
  157.1 6.6 %fusion.19.own_ref = bf16[768,1024]{1,0:T(8,128)(2,1)S(1)} fusion(bf16[1024,4096]{1,0:T(8,128)(2,1)} %all-gather.2.cloned.1.call-done.pair_ref, bf16[2,768,2048]{2,1,0:T(8,128)(2,1)} %get-tuple-element.84), kind=kOutput, calls=%fused_computation.19 | convolution fusion | flops 3222011904 | bytes 8912896 | tf_op jit(solution)/shard_map/dot_general | solution.py:43
  163.7 14.7 %collective-permute-done.18.other_ref = bf16[768,1024]{1,0:T(8,128)(2,1)S(1)} collective-permute-done((bf16[768,1024]{1,0:T(8,128)(2,1)}, bf16[768,1024]{1,0:T(8,128)(2,1)S(1)}, u32[]{:S(2)}, u32[]{:S(2)}) %collective-permute-start.18) | collective-permute-done | bytes 1572896 | tf_op jit(solution)/shard_map/ppermute | solution.py:960
  179.5 7.0 %mid.1 = (bf16[768,1024]{1,0:T(8,128)(2,1)}, bf16[768,512]{1,0:T(8,128)(2,1)}, f32[8,1024]{1,0:T(8,128)}) custom-call(bf16[768,1024]{1,0:T(8,128)(2,1)} %get-tuple-element.106.resid_ref, bf16[768,1024]{1,0:T(8,128)(2,1)} %get-tuple-element.82.own_ref, bf16[768,1024]{1,0:T(8,128)(2,1)} %copy-done.25, bf16[2,768,1024]{2,1,0:T(8,128)(2,1)} %get-tuple-element.81.grad_ref, ...), custom_call_target="tpu_custom_call" | custom-call | flops 12884901888 | bytes 12582912 | tf_op jit(solution)/shard_map/mid/pallas_call | solution.py:663
  186.6 19.2 %back.1 = (bf16[768,1536]{1,0:T(8,128)(2,1)}, bf16[768,1024]{1,0:T(8,128)(2,1)}, f32[4,8,384]{2,1,0:T(8,128)}, f32[8,1024]{1,0:T(8,128)}) custom-call(bf16[768,1024]{1,0:T(8,128)(2,1)} %get-tuple-element.78.xhat_ref, bf16[768,1536]{1,0:T(8,128)(2,1)} %get-tuple-element.79.qkv_ref, bf16[768,512]{1,0:T(8,128)(2,1)} %get-tuple-element.87.grad_ref, ...), custom_call_target="tpu_custom_call" | custom-call | flops 115964116992 | bytes 9437184 | tf_op jit(solution)/shard_map/back/pallas_call | solution.py:789
  207.9 3.2 %convolution_convert_fusion.1 = bf16[512,1536]{1,0:T(8,128)(2,1)S(1)} fusion(bf16[768,1536]{1,0:T(8,128)(2,1)} %get-tuple-element.90, bf16[1024,768]{1,0:T(8,128)(2,1)S(1)} %copy-done.17), kind=kOutput, calls=%fused_computation.7 | convolution fusion | flops 1208745984 | bytes 4718592 | tf_op jit(solution)/shard_map/dot_general | solution.py:33
  215.1 3.5 %collective-permute-done.21 = f32[16,768]{1,0:T(8,128)S(1)} collective-permute-done((f32[16,768]{1,0:T(8,128)S(1)}, f32[16,768]{1,0:T(8,128)S(1)}, u32[]{:S(2)}, u32[]{:S(2)}) %collective-permute-start.21) | collective-permute-done | bytes 49184 | tf_op jit(solution)/shard_map/ppermute | solution.py:960
  219.0 2.1 fusion.10
  226.3 18.3 %collective-permute-done.25.other_ref = bf16[384,1024]{1,0:T(8,128)(2,1)S(1)} collective-permute-done((bf16[384,1024]{1,0:T(8,128)(2,1)S(1)}, bf16[384,1024]{1,0:T(8,128)(2,1)S(1)}, u32[]{:S(2)}, u32[]{:S(2)}) %collective-permute-start.25) | collective-permute-done | bytes 786464 | tf_op jit(solution)/shard_map/ppermute | solution.py:960
  246.0 8.8 %collective-permute-done.24 = f32[4,768]{1,0:T(4,128)S(1)} collective-permute-done((f32[4,768]{1,0:T(4,128)S(1)}, f32[4,768]{1,0:T(4,128)S(1)}, u32[]{:S(2)}, u32[]{:S(2)}) %collective-permute-start.24) | collective-permute-done | bytes 12320 | tf_op jit(solution)/shard_map/ppermute | solution.py:917
  258.2 4.9 %collective-permute-start.27 = (f32[1,768]{1,0:T(1,128)S(1)}, f32[1,768]{1,0:T(1,128)S(1)}, u32[]{:S(2)}, u32[]{:S(2)}) collective-permute-start(f32[1,768]{1,0:T(1,128)S(1)} %get-tuple-element.121), channel_id=1, source_target_pairs={{0,16},{2,18},{4,20},{6,22},{8,24},{10,26},{12,28},{14,30},{16,0},... | collective-permute-start | bytes 9224 | tf_op jit(solution)/shard_map/ppermute | solution.py:917
  263.1 2.0 collective-permute-start.28
  266.2 1.9 collective-permute-start.30
  268.1 3.0 %last.1 = f32[384,1024]{1,0:T(8,128)} custom-call(s32[20]{0:T(128)S(1)} %copy-done.6, bf16[384,1024]{1,0:T(8,128)(2,1)S(1)} %copy-done.4, bf16[768,1024]{1,0:T(8,128)(2,1)S(1)} %copy-done.3, bf16[768,1024]{1,0:T(8,128)(2,1)S(1)} %copy-done, bf16[384,1024]{1,0:T(8,128)(2,1)S(1)} %collective-permute-done.25.other_ref, f32[8,1024]{1,0:T(8,128)S(1)} %copy-done.5), custom_call_target="tpu_custom_call" | custom-call | flops 15728640 | bytes 125829120 | tf_op jit(solution)/shard_map/last/pallas_call | solution.py:835
  271.1 2.0 collective-permute-start.31
  276.4 3.6 %result.1 = bf16[384,1024]{1,0:T(8,128)(2,1)} custom-call(s32[20]{0:T(128)S(1)} %copy-done.6, bf16[768,1024]{1,0:T(8,128)(2,1)S(1)} %copy-done.1, bf16[768,1024]{1,0:T(8,128)(2,1)S(1)} %fusion.19.own_ref, bf16[384,1024]{1,0:T(8,128)(2,1)} %collective-permute-done.26.other_ref, f32[8,1024]{1,0:T(8,128)S(1)} %copy-done.5), custom_call_target="tpu_custom_call" | custom-call | flops 3932160 | bytes 125829120 | tf_op jit(solution)/shard_map/result/pallas_call | solution.py:862
  279.9 2.1 fusion.32
  282.0 2.4 collective-permute-done.30
  284.5 7.1 %collective-permute-done.32 = bf16[64,2048]{1,0:T(8,128)(2,1)} collective-permute-done((bf16[64,2048]{1,0:T(8,128)(2,1)}, bf16[64,2048]{1,0:T(8,128)(2,1)}, u32[]{:S(2)}, u32[]{:S(2)}) %collective-permute-start.32) | collective-permute-done | bytes 262176 | tf_op jit(solution)/shard_map/ppermute | solution.py:917
  (194 shorter events, 44.5 us)
Async XLA Ops:
  7.2 114.1 %all-gather.2.cloned.1.call-start = ((), (), s32[]{:S(2)}) async-start(), calls=%async_computation.1 | async-start | bytes 8912896 | tf_op jit(solution)/shard_map/all_gather | solution.py:1013
  12.7 29.0 %collective-permute-start = (bf16[384,1024]{1,0:T(8,128)(2,1)}, bf16[384,1024]{1,0:T(8,128)(2,1)S(1)}, u32[]{:S(2)}, u32[]{:S(2)}) collective-permute-start(bf16[384,1024]{1,0:T(8,128)(2,1)} %x_ref.1), channel_id=1, source_target_pairs={{0,1},{1,0},{2,3},{3,2},{4,5},{5,4},{6,7},{7,6},{8,9},{9,8},{10,11... | collective-permute-start | bytes 2359304 | tf_op jit(solution)/shard_map/ppermute | solution.py:960
  14.2 20.9 %collective-permute-start.1 = (bf16[64,2176]{1,0:T(8,128)(2,1)}, bf16[64,2176]{1,0:T(8,128)(2,1)S(1)}, u32[]{:S(2)}, u32[]{:S(2)}) collective-permute-start(bf16[64,2176]{1,0:T(8,128)(2,1)} %get-tuple-element.63.refs_0_.refs_16_.refs_32_), channel_id=1, source_target_pairs={{0,8},{2,10},{4,12},{6,14},{8,16},{10,18},{12,20},{14,22},{16,24},... | collective-permute-start | bytes 835592 | tf_op jit(solution)/shard_map/ppermute | solution.py:917
  15.7 20.9 %collective-permute-start.4 = (bf16[64,2176]{1,0:T(8,128)(2,1)}, bf16[64,2176]{1,0:T(8,128)(2,1)S(1)}, u32[]{:S(2)}, u32[]{:S(2)}) collective-permute-start(bf16[64,2176]{1,0:T(8,128)(2,1)} %get-tuple-element.63.refs_0_.refs_16_.refs_32_), channel_id=1, source_target_pairs={{0,4},{2,6},{4,0},{6,2},{8,12},{10,14},{12,8},{14,10},{16,20},{18,... | collective-permute-start | bytes 835592 | tf_op jit(solution)/shard_map/ppermute | solution.py:917
  17.3 19.4 %collective-permute-start.3 = (bf16[64,2176]{1,0:T(8,128)(2,1)}, bf16[64,2176]{1,0:T(8,128)(2,1)S(1)}, u32[]{:S(2)}, u32[]{:S(2)}) collective-permute-start(bf16[64,2176]{1,0:T(8,128)(2,1)} %get-tuple-element.63.refs_0_.refs_16_.refs_32_), channel_id=1, source_target_pairs={{0,24},{2,26},{4,28},{6,30},{8,0},{10,2},{12,4},{14,6},{16,8},{18,... | collective-permute-start | bytes 835592 | tf_op jit(solution)/shard_map/ppermute | solution.py:917
  17.7 21.9 %collective-permute-start.2 = (bf16[64,2176]{1,0:T(8,128)(2,1)}, bf16[64,2176]{1,0:T(8,128)(2,1)S(1)}, u32[]{:S(2)}, u32[]{:S(2)}) collective-permute-start(bf16[64,2176]{1,0:T(8,128)(2,1)} %get-tuple-element.63.refs_0_.refs_16_.refs_32_), channel_id=1, source_target_pairs={{0,16},{2,18},{4,20},{6,22},{8,24},{10,26},{12,28},{14,30},{16,0},... | collective-permute-start | bytes 835592 | tf_op jit(solution)/shard_map/ppermute | solution.py:917
  35.1 6.5 %collective-permute-start.5 = (bf16[64,2176]{1,0:T(8,128)(2,1)S(1)}, bf16[64,2176]{1,0:T(8,128)(2,1)S(1)}, u32[]{:S(2)}, u32[]{:S(2)}) collective-permute-start(bf16[64,2176]{1,0:T(8,128)(2,1)S(1)} %collective-permute-done.1.refs_1_.refs_17_.refs_33_), channel_id=1, source_target_pairs={{0,4},{2,6},{4,0},{6,2},{8,12},{10,14},{12,8},{14,10},{16,20},{18,... | collective-permute-start | bytes 835592 | tf_op jit(solution)/shard_map/ppermute | solution.py:917
  41.7 238.3 %reduce-scatter.2.cloned.1.call-start = ((), (), s32[]{:S(2)}) async-start(), calls=%async_computation.2 | async-start | bytes 8912896 | tf_op jit(solution)/shard_map/reduce_scatter | solution.py:1048
  41.7 3.2 %collective-permute-start.8 = (bf16[64,2176]{1,0:T(8,128)(2,1)}, bf16[64,2176]{1,0:T(8,128)(2,1)S(1)}, u32[]{:S(2)}, u32[]{:S(2)}) collective-permute-start(bf16[64,2176]{1,0:T(8,128)(2,1)} %get-tuple-element.63.refs_0_.refs_16_.refs_32_), channel_id=1, source_target_pairs={{0,2},{2,0},{4,6},{6,4},{8,10},{10,8},{12,14},{14,12},{16,18},{18,... | collective-permute-start | bytes 835592 | tf_op jit(solution)/shard_map/ppermute | solution.py:917
  42.5 3.0 collective-permute-start.12
  42.9 9.5 %collective-permute-start.7 = (bf16[64,2176]{1,0:T(8,128)(2,1)S(1)}, bf16[64,2176]{1,0:T(8,128)(2,1)S(1)}, u32[]{:S(2)}, u32[]{:S(2)}) collective-permute-start(bf16[64,2176]{1,0:T(8,128)(2,1)S(1)} %collective-permute-done.3.refs_3_.refs_19_.refs_35_), channel_id=1, source_target_pairs={{0,4},{2,6},{4,0},{6,2},{8,12},{10,14},{12,8},{14,10},{16,20},{18,... | collective-permute-start | bytes 835592 | tf_op jit(solution)/shard_map/ppermute | solution.py:917
  44.5 18.7 %collective-permute-start.6 = (bf16[64,2176]{1,0:T(8,128)(2,1)S(1)}, bf16[64,2176]{1,0:T(8,128)(2,1)S(1)}, u32[]{:S(2)}, u32[]{:S(2)}) collective-permute-start(bf16[64,2176]{1,0:T(8,128)(2,1)S(1)} %collective-permute-done.2.refs_2_.refs_18_.refs_34_), channel_id=1, source_target_pairs={{0,4},{2,6},{4,0},{6,2},{8,12},{10,14},{12,8},{14,10},{16,20},{18,... | collective-permute-start | bytes 835592 | tf_op jit(solution)/shard_map/ppermute | solution.py:917
  45.0 18.2 %collective-permute-start.11 = (bf16[64,2176]{1,0:T(8,128)(2,1)S(1)}, bf16[64,2176]{1,0:T(8,128)(2,1)S(1)}, u32[]{:S(2)}, u32[]{:S(2)}) collective-permute-start(bf16[64,2176]{1,0:T(8,128)(2,1)S(1)} %collective-permute-done.3.refs_3_.refs_19_.refs_35_), channel_id=1, source_target_pairs={{0,2},{2,0},{4,6},{6,4},{8,10},{10,8},{12,14},{14,12},{16,18},{18,... | collective-permute-start | bytes 835592 | tf_op jit(solution)/shard_map/ppermute | solution.py:917
  45.0 18.7 %collective-permute-start.10 = (bf16[64,2176]{1,0:T(8,128)(2,1)S(1)}, bf16[64,2176]{1,0:T(8,128)(2,1)S(1)}, u32[]{:S(2)}, u32[]{:S(2)}) collective-permute-start(bf16[64,2176]{1,0:T(8,128)(2,1)S(1)} %collective-permute-done.2.refs_2_.refs_18_.refs_34_), channel_id=1, source_target_pairs={{0,2},{2,0},{4,6},{6,4},{8,10},{10,8},{12,14},{14,12},{16,18},{18,... | collective-permute-start | bytes 835592 | tf_op jit(solution)/shard_map/ppermute | solution.py:917
  45.5 18.3 %collective-permute-start.9 = (bf16[64,2176]{1,0:T(8,128)(2,1)S(1)}, bf16[64,2176]{1,0:T(8,128)(2,1)S(1)}, u32[]{:S(2)}, u32[]{:S(2)}) collective-permute-start(bf16[64,2176]{1,0:T(8,128)(2,1)S(1)} %collective-permute-done.1.refs_1_.refs_17_.refs_33_), channel_id=1, source_target_pairs={{0,2},{2,0},{4,6},{6,4},{8,10},{10,8},{12,14},{14,12},{16,18},{18,... | collective-permute-start | bytes 835592 | tf_op jit(solution)/shard_map/ppermute | solution.py:917
  52.4 11.3 %collective-permute-start.15 = (bf16[64,2176]{1,0:T(8,128)(2,1)S(1)}, bf16[64,2176]{1,0:T(8,128)(2,1)S(1)}, u32[]{:S(2)}, u32[]{:S(2)}) collective-permute-start(bf16[64,2176]{1,0:T(8,128)(2,1)S(1)} %collective-permute-done.7.refs_7_.refs_23_.refs_39_), channel_id=1, source_target_pairs={{0,2},{2,0},{4,6},{6,4},{8,10},{10,8},{12,14},{14,12},{16,18},{18,... | collective-permute-start | bytes 835592 | tf_op jit(solution)/shard_map/ppermute | solution.py:917
  63.7 20.9 %collective-permute-start.16 = (bf16[384,1024]{1,0:T(8,128)(2,1)}, bf16[384,1024]{1,0:T(8,128)(2,1)S(1)}, u32[]{:S(2)}, u32[]{:S(2)}) collective-permute-start(bf16[384,1024]{1,0:T(8,128)(2,1)} %param.16), channel_id=1, source_target_pairs={{0,1},{1,0},{2,3},{3,2},{4,5},{5,4},{6,7},{7,6},{8,9},{9,8},{10,11... | collective-permute-start | bytes 2359304 | tf_op jit(solution)/shard_map/ppermute | solution.py:960
  84.6 36.7 %collective-permute-start.17 = (bf16[768,1024]{1,0:T(8,128)(2,1)}, bf16[768,1024]{1,0:T(8,128)(2,1)S(1)}, u32[]{:S(2)}, u32[]{:S(2)}) collective-permute-start(bf16[768,1024]{1,0:T(8,128)(2,1)} %get-tuple-element.69.own_ref), channel_id=1, source_target_pairs={{0,1},{1,0},{2,3},{3,2},{4,5},{5,4},{6,7},{7,6},{8,9},{9,8},{10,11... | collective-permute-start | bytes 4718600 | tf_op jit(solution)/shard_map/ppermute | solution.py:960
  142.5 35.9 %collective-permute-start.18 = (bf16[768,1024]{1,0:T(8,128)(2,1)}, bf16[768,1024]{1,0:T(8,128)(2,1)S(1)}, u32[]{:S(2)}, u32[]{:S(2)}) collective-permute-start(bf16[768,1024]{1,0:T(8,128)(2,1)} %get-tuple-element.82.own_ref), channel_id=1, source_target_pairs={{0,1},{1,0},{2,3},{3,2},{4,5},{5,4},{6,7},{7,6},{8,9},{9,8},{10,11... | collective-permute-start | bytes 4718600 | tf_op jit(solution)/shard_map/ppermute | solution.py:960
  211.1 7.9 %collective-permute-start.19 = (bf16[512,1536]{1,0:T(8,128)(2,1)S(1)}, bf16[512,1536]{1,0:T(8,128)(2,1)S(1)}, u32[]{:S(2)}, u32[]{:S(2)}) collective-permute-start(bf16[512,1536]{1,0:T(8,128)(2,1)S(1)} %convolution_convert_fusion.1), channel_id=1, source_target_pairs={{0,2},{2,0},{4,6},{6,4},{8,10},{10,8},{12,14},{14,12},{16,18},{18,... | collective-permute-start | bytes 4718600 | tf_op jit(solution)/shard_map/ppermute | solution.py:917
  214.0 4.7 %collective-permute-start.20 = (bf16[512,512]{1,0:T(8,128)(2,1)S(1)}, bf16[512,512]{1,0:T(8,128)(2,1)S(1)}, u32[]{:S(2)}, u32[]{:S(2)}) collective-permute-start(bf16[512,512]{1,0:T(8,128)(2,1)S(1)} %convolution_convert_fusion.2), channel_id=1, source_target_pairs={{0,2},{2,0},{4,6},{6,4},{8,10},{10,8},{12,14},{14,12},{16,18},{18,... | collective-permute-start | bytes 1572872 | tf_op jit(solution)/shard_map/ppermute | solution.py:917
  214.5 4.1 %collective-permute-start.21 = (f32[16,768]{1,0:T(8,128)S(1)}, f32[16,768]{1,0:T(8,128)S(1)}, u32[]{:S(2)}, u32[]{:S(2)}) collective-permute-start(f32[16,768]{1,0:T(8,128)S(1)} %fusion.33), channel_id=1, source_target_pairs={{0,1},{1,0},{2,3},{3,2},{4,5},{5,4},{6,7},{7,6},{8,9},{9,8},{10,11... | collective-permute-start | bytes 147464 | tf_op jit(solution)/shard_map/ppermute | solution.py:960
  223.5 31.2 %collective-permute-start.23 = (bf16[256,2048]{1,0:T(8,128)(2,1)}, bf16[256,2048]{1,0:T(8,128)(2,1)S(1)}, u32[]{:S(2)}, u32[]{:S(2)}) collective-permute-start(bf16[256,2048]{1,0:T(8,128)(2,1)} %pad_maximum_fusion.1), channel_id=1, source_target_pairs={{0,4},{2,6},{4,0},{6,2},{8,12},{10,14},{12,8},{14,10},{16,20},{18,... | collective-permute-start | bytes 3145736 | tf_op jit(solution)/shard_map/ppermute | solution.py:917
  225.2 19.4 %collective-permute-start.25 = (bf16[384,1024]{1,0:T(8,128)(2,1)S(1)}, bf16[384,1024]{1,0:T(8,128)(2,1)S(1)}, u32[]{:S(2)}, u32[]{:S(2)}) collective-permute-start(bf16[384,1024]{1,0:T(8,128)(2,1)S(1)} %constant_dynamic-slice_fusion.1), channel_id=1, source_target_pairs={{0,1},{1,0},{2,3},{3,2},{4,5},{5,4},{6,7},{7,6},{8,9},{9,8},{10,11... | collective-permute-start | bytes 2359304 | tf_op jit(solution)/shard_map/ppermute | solution.py:960
  225.7 29.0 %collective-permute-start.24 = (f32[4,768]{1,0:T(4,128)S(1)}, f32[4,768]{1,0:T(4,128)S(1)}, u32[]{:S(2)}, u32[]{:S(2)}) collective-permute-start(f32[4,768]{1,0:T(4,128)S(1)} %slice.184), channel_id=1, source_target_pairs={{0,4},{2,6},{4,0},{6,2},{8,12},{10,14},{12,8},{14,10},{16,20},{18,... | collective-permute-start | bytes 36872 | tf_op jit(solution)/shard_map/ppermute | solution.py:917
  245.5 29.5 %collective-permute-start.26 = (bf16[384,1024]{1,0:T(8,128)(2,1)}, bf16[384,1024]{1,0:T(8,128)(2,1)}, u32[]{:S(2)}, u32[]{:S(2)}) collective-permute-start(bf16[384,1024]{1,0:T(8,128)(2,1)} %constant_dynamic-slice_fusion), channel_id=1, source_target_pairs={{0,1},{1,0},{2,3},{3,2},{4,5},{5,4},{6,7},{7,6},{8,9},{9,8},{10,11... | collective-permute-start | bytes 2359304 | tf_op jit(solution)/shard_map/ppermute | solution.py:960
  258.2 12.9 %collective-permute-start.27 = (f32[1,768]{1,0:T(1,128)S(1)}, f32[1,768]{1,0:T(1,128)S(1)}, u32[]{:S(2)}, u32[]{:S(2)}) collective-permute-start(f32[1,768]{1,0:T(1,128)S(1)} %get-tuple-element.121), channel_id=1, source_target_pairs={{0,16},{2,18},{4,20},{6,22},{8,24},{10,26},{12,28},{14,30},{16,0},... | collective-permute-start | bytes 9224 | tf_op jit(solution)/shard_map/ppermute | solution.py:917
  263.1 8.0 %collective-permute-start.29 = (f32[1,768]{1,0:T(1,128)S(1)}, f32[1,768]{1,0:T(1,128)S(1)}, u32[]{:S(2)}, u32[]{:S(2)}) collective-permute-start(f32[1,768]{1,0:T(1,128)S(1)} %get-tuple-element.122), channel_id=1, source_target_pairs={{0,24},{2,26},{4,28},{6,30},{8,0},{10,2},{12,4},{14,6},{16,8},{18,... | collective-permute-start | bytes 9224 | tf_op jit(solution)/shard_map/ppermute | solution.py:917
  263.1 10.1 %collective-permute-start.28 = (f32[1,768]{1,0:T(1,128)S(1)}, f32[1,768]{1,0:T(1,128)S(1)}, u32[]{:S(2)}, u32[]{:S(2)}) collective-permute-start(f32[1,768]{1,0:T(1,128)S(1)} %get-tuple-element.123), channel_id=1, source_target_pairs={{0,8},{2,10},{4,12},{6,14},{8,16},{10,18},{12,20},{14,22},{16,24},... | collective-permute-start | bytes 9224 | tf_op jit(solution)/shard_map/ppermute | solution.py:917
  266.2 18.3 %collective-permute-start.30 = (bf16[64,2048]{1,0:T(8,128)(2,1)}, bf16[64,2048]{1,0:T(8,128)(2,1)S(1)}, u32[]{:S(2)}, u32[]{:S(2)}) collective-permute-start(bf16[64,2048]{1,0:T(8,128)(2,1)} %get-tuple-element.114), channel_id=1, source_target_pairs={{0,16},{2,18},{4,20},{6,22},{8,24},{10,26},{12,28},{14,30},{16,0},... | collective-permute-start | bytes 786440 | tf_op jit(solution)/shard_map/ppermute | solution.py:917
  271.1 20.5 %collective-permute-start.32 = (bf16[64,2048]{1,0:T(8,128)(2,1)}, bf16[64,2048]{1,0:T(8,128)(2,1)}, u32[]{:S(2)}, u32[]{:S(2)}) collective-permute-start(bf16[64,2048]{1,0:T(8,128)(2,1)} %get-tuple-element.115), channel_id=1, source_target_pairs={{0,24},{2,26},{4,28},{6,30},{8,0},{10,2},{12,4},{14,6},{16,8},{18,... | collective-permute-start | bytes 786440 | tf_op jit(solution)/shard_map/ppermute | solution.py:917
  271.1 20.5 %collective-permute-start.31 = (bf16[64,2048]{1,0:T(8,128)(2,1)}, bf16[64,2048]{1,0:T(8,128)(2,1)}, u32[]{:S(2)}, u32[]{:S(2)}) collective-permute-start(bf16[64,2048]{1,0:T(8,128)(2,1)} %get-tuple-element.116), channel_id=1, source_target_pairs={{0,8},{2,10},{4,12},{6,14},{8,16},{10,18},{12,20},{14,22},{16,24},... | collective-permute-start | bytes 786440 | tf_op jit(solution)/shard_map/ppermute | solution.py:917
  (45 other events, 485.9 us)
Sparse Core Ops, SparseCore 0:
  41.8 76.6 all-gather.1
  156.1 114.8 reduce-scatter.1

commit v6 on v5

--- a/solution.py
+++ b/solution.py
@@ -652,7 +652,7 @@
     dbranch = dresid.astype(LOW)
     dbranch_ref[...] = dbranch
     datt_ref[...] = matmul(dbranch, weight_ref[...]).astype(LOW)
-    for row, value in enumerate((dnorm * xhat, dnorm, dbranch.astype(jnp.float32), grad)):
+    for row, value in enumerate((dbranch.astype(jnp.float32), dnorm * xhat, dnorm, grad)):
         sum_ref[row : row + 1, :] += 0.5 * jnp.sum(value, axis=0, keepdims=True)
 
 
@@ -740,7 +740,7 @@
 
 
 def back_kernel(
-    xhat_ref,
+    xhat_all_ref,
     qkv_ref,
     grad_ref,
     log_ref,
@@ -752,15 +752,21 @@
     dkey_ref,
     dvalue_ref,
     acc_ref,
+    xhat_ref,
+    sem,
     *,
     scale,
 ):
     step = pl.program_id(0)
+    fetch = pltpu.make_async_copy(xhat_all_ref, xhat_ref, sem.at[0])
+
+    @pl.when(step == 0)
+    def _():
+        fetch.start()
+
     attend_back_pair(qkv_ref, grad_ref, log_ref, dqkv_ref, dkey_ref, dvalue_ref, scale)
     dnorm = contract_last(dqkv_ref[...], weight_ref[...])
-    sum_ref[...] = jnp.broadcast_to(
-        jnp.sum(dqkv_ref[...].astype(jnp.float32), axis=0, keepdims=True)[None], sum_ref.shape
-    )
+    sum_ref[0] = jnp.sum(dqkv_ref[...].astype(jnp.float32), axis=0, keepdims=True)
 
     @pl.when(step == 0)
     def _():
@@ -772,12 +778,11 @@
 
     @pl.when(step == pl.num_programs(0) - 1)
     def _():
+        fetch.wait()
         total = acc_ref[...] + dnorm
         dnorm_ref[...] = total.astype(LOW)
         vec_ref[0:1, :] = jnp.sum(total * xhat_ref[...].astype(jnp.float32), axis=0, keepdims=True)
-        vec_ref[1:8, :] = jnp.broadcast_to(
-            jnp.sum(total, axis=0, keepdims=True), (7, total.shape[1])
-        )
+        vec_ref[1:2, :] = jnp.sum(total, axis=0, keepdims=True)
 
 
 def back_product(xhat, qkv, grad, logs, weight, scale):
@@ -790,7 +795,7 @@
         functools.partial(back_kernel, scale=scale),
         grid=(pairs,),
         in_specs=[
-            square,
+            pl.BlockSpec(memory_space=pl.ANY),
             pl.BlockSpec((length, 384), lambda p: (0, p)),
             pl.BlockSpec((length, 128), lambda p: (0, p)),
             pl.BlockSpec((1, 8, length), lambda p: (p, 0, 0)),
@@ -799,19 +804,21 @@
         out_specs=[
             pl.BlockSpec((length, 384), lambda p: (0, p)),
             square,
-            pl.BlockSpec((1, 8, 384), lambda p: (p, 0, 0)),
-            whole((8, width)),
+            pl.BlockSpec((1, 1, 384), lambda p: (p, 0, 0)),
+            whole((2, width)),
         ],
         out_shape=[
             jax.ShapeDtypeStruct((length, columns), LOW),
             jax.ShapeDtypeStruct((length, width), LOW),
-            jax.ShapeDtypeStruct((pairs, 8, 384), jnp.float32),
-            jax.ShapeDtypeStruct((8, width), jnp.float32),
+            jax.ShapeDtypeStruct((pairs, 1, 384), jnp.float32),
+            jax.ShapeDtypeStruct((2, width), jnp.float32),
         ],
         scratch_shapes=[
             pltpu.VMEM((length, 128), jnp.float32),
             pltpu.VMEM((length, 128), jnp.float32),
             pltpu.VMEM((length, width), jnp.float32),
+            pltpu.VMEM((length, width), LOW),
+            pltpu.SemaphoreType.DMA((1,)),
         ],
         compiler_params=settings(56),
         cost_estimate=cost(2 * length * width * columns * 48, 12 * length * width),
@@ -874,22 +881,62 @@
     )(place, resid, own, other, vectors)
 
 
-def pack_kernel(proj_ref, out_ref, up_ref, down_ref, vec_ref, narrow_ref, wide_ref):
+def finish_kernel(own_ref, one_ref, two_ref, three_ref, proj_ref, out_ref):
+    total = own_ref[...]
+    for ref in (one_ref, two_ref, three_ref):
+        total = total + ref[...].astype(jnp.float32)
+    columns = out_ref.shape[1]
+    for pair in range(columns // 128):
+        for kind in range(3):
+            start = (pair * 3 + kind) * 128
+            proj_ref[kind, :, pair * 128 : pair * 128 + 128] = total[:, start : start + 128]
+    out_ref[...] = total[:, 3 * columns :]
+
+
+def finish(total, sent):
+    rows, columns = sent[0].shape
+    return pl.pallas_call(
+        finish_kernel,
+        grid=(1,),
+        in_specs=[whole((rows, columns))] * 4,
+        out_specs=[whole((3, rows, columns // 4)), whole((rows, columns // 4))],
+        out_shape=[
+            jax.ShapeDtypeStruct((3, rows, columns // 4), jnp.float32),
+            jax.ShapeDtypeStruct((rows, columns // 4), jnp.float32),
+        ],
+        compiler_params=settings(16),
+        cost_estimate=cost(4 * rows * columns, 14 * rows * columns),
+        name="finish",
+    )(total, *sent)
+
+
+def pack_kernel(proj_ref, out_ref, up_ref, down_ref, *refs):
+    singles, pair_ref, ups_ref = refs[:6], refs[6], refs[7]
+    narrow_ref, wide_ref, rows_ref = refs[8:]
     columns = proj_ref.shape[2]
     for pair in range(columns // 128):
         for kind in range(3):
             start = (pair * 3 + kind) * 128
             narrow_ref[:, start : start + 128] = proj_ref[kind, :, pair * 128 : pair * 128 + 128]
     narrow_ref[:, 3 * columns : 4 * columns] = out_ref[...]
-    turned = jnp.transpose(vec_ref[...].astype(jnp.float32))
-    turned = jnp.concatenate([turned, jnp.zeros((SLOT, 112), jnp.float32)], axis=1)
-    narrow_ref[:, 4 * columns :] = turned.astype(LOW)
+    rows_ref[...] = jnp.zeros_like(rows_ref)
+    for index, ref in enumerate(singles):
+        rows_ref[index : index + 1, 0:SLOT] = ref[...].astype(jnp.float32).reshape(1, SLOT)
+    rows_ref[8:10, 0:SLOT] = pair_ref[...].astype(jnp.float32)
+    ups = ups_ref[...].astype(jnp.float32).reshape(2, 128)
+    for half in range(2):
+        rows_ref[10 + 2 * half : 11 + 2 * half, :] = ups[half : half + 1, :]
+        rows_ref[11 + 2 * half : 12 + 2 * half, :] = pltpu.roll(ups[half : half + 1, :], SLOT, 1)
+    turned = jnp.transpose(rows_ref[...])[0:SLOT]
+    narrow_ref[:, 4 * columns :] = jnp.concatenate(
+        [turned, jnp.zeros((SLOT, 112), jnp.float32)], axis=1
+    ).astype(LOW)
     hidden = up_ref.shape[1]
     wide_ref[:, :hidden] = up_ref[...]
     wide_ref[:, hidden:] = down_ref[...]
 
 
-def pack_shards(proj, out, up, down, vec):
+def pack_shards(proj, out, up, down, singles, pair, ups):
     rows, columns = out.shape
     return pl.pallas_call(
         pack_kernel,
@@ -897,10 +944,11 @@
             jax.ShapeDtypeStruct((rows, 4 * columns + 128), LOW),
             jax.ShapeDtypeStruct((rows, 2 * up.shape[1]), LOW),
         ],
+        scratch_shapes=[pltpu.VMEM((16, 128), jnp.float32)],
         compiler_params=settings(56),
         cost_estimate=cost(0, 4 * rows * (4 * columns + 2 * up.shape[1])),
         name="pack",
-    )(proj, out, up, down, vec)
+    )(proj, out, up, down, *singles, pair, ups)
 
 
 def after(value, *events):
@@ -919,9 +967,9 @@
 
 def dp_gather(shard, ranks, event):
     far = [shard] + [dp_shift(shard, ranks, k, 0, 0) for k in (1, 2, 3)]
-    sent = far[:2] + [after(far[2], event)] + far[3:]
-    near = [dp_shift(piece, ranks, 0, 1, 0) for piece in sent]
-    pieces = far + near
+    near = [dp_shift(piece, ranks, 0, 1, 0) for piece in (far[0], far[1], far[3])]
+    second = dp_shift(after(far[2], event, near[2]), ranks, 0, 1, 0)
+    pieces = far + [near[0], near[1], second, near[2]]
     return pieces + [dp_shift(piece, ranks, 0, 0, 1) for piece in pieces], pieces
 
 
@@ -946,7 +994,7 @@
 def far_send(total, ranks, wire=LOW):
     rows = total.shape[0] // 4
     low = total.astype(wire)
-    return [dp_shift(low[k * rows : (k + 1) * rows], ranks, -k, 0, 0) for k in (2, 3, 1)]
+    return [dp_shift(low[k * rows : (k + 1) * rows], ranks, -k, 0, 0) for k in (1, 3, 2)]
 
 
 def far_sum(total, sent):
@@ -1001,17 +1049,15 @@
     to_local = (jnp.arange(width, dtype=jnp.int32)[:, None] == feature[None, :]).astype(LOW)
     slot_of = (slots[:, None] == source[None, :]).astype(jnp.float32)
 
-    zero = jnp.zeros_like(ln1_gain)
-    vec = [ln1_gain, ln1_bias, attn_out_bias, ln2_gain, ln2_bias, down_bias, zero, zero]
-    vec = jnp.concatenate(
-        [jnp.stack(vec), qv_bias, up_bias.reshape(4, shard), jnp.zeros((2, shard), LOW)], axis=0
-    )
-    narrow_shard, wide_shard = pack_shards(w_qkv, w_attn_out.T, w_up, w_down.T, vec)
+    singles = [ln1_gain, ln1_bias, attn_out_bias, ln2_gain, ln2_bias, down_bias]
+    narrow_shard, wide_shard = pack_shards(
+        w_qkv, w_attn_out.T, w_up, w_down.T, singles, qv_bias, up_bias
+    )
     narrow, narrow_far = dp_gather(narrow_shard, ranks, place)
     inputs_other = swap(after(inputs, narrow_shard))
     grad_other = swap(after(out_grad, inputs_other))
     wide = lax.all_gather(
-        after(wide_shard, inputs_other, *narrow_far[1:6]), "dp", axis=0, tiled=True
+        after(wide_shard, inputs_other, *narrow_far[1:6], narrow_far[7]), "dp", axis=0, tiled=True
     )
 
     def in_order(own, other):
@@ -1053,7 +1099,7 @@
     dqkv, dnorm_one, dqkv_sum, front_sum = back_product(
         xhat, qkv, dattended, logs, proj_full, scale
     )
-    dqkv_sum = dqkv_sum[:, 0].reshape(pairs, 3, 128)
+    dqkv_sum = dqkv_sum.reshape(pairs, 3, 128)
     placed = [
         place_block(value, 2 * value.shape[0], side * value.shape[0]).reshape(ranks, -1)
         for value in (
@@ -1062,7 +1108,7 @@
             dpre_sum[0],
         )
     ]
-    pack = jnp.stack([front_sum[0], front_sum[1], mid_sum[2], mid_sum[0], mid_sum[1], mid_sum[3]])
+    pack = jnp.concatenate([front_sum, mid_sum[:4]], axis=0)
     pack = pack.reshape(6, ranks, shard).transpose(1, 0, 2).reshape(ranks, -1)
     pack = lax.dot_general(
         slot_of,
@@ -1073,7 +1119,7 @@
     )
     proj_core = reduce_core(norm_slot, dqkv, ranks)
     dbranch_slot = to_slots(after(dbranch, pack))
-    pack = pack + swap(pack)
+    pack_other = swap(pack)
     out_core = reduce_core(dbranch_slot, attended, ranks)
     slim_near = jnp.concatenate(
         [
@@ -1082,7 +1128,8 @@
         ],
         axis=1,
     )
-    pack = pack[: ranks // 2] + dp_shift(after(pack[ranks // 2 :], slim_near), ranks, 0, 0, 1)
+    pack = pack + after(pack_other, slim_near)
+    pack = pack[: ranks // 2] + dp_shift(pack[ranks // 2 :], ranks, 0, 0, 1)
     slim_near, pack = lax.optimization_barrier((slim_near, pack))
     back_other = swap(other_rows(after(dnorm_one, pack)))
     pack_arrived = dp_shift(pack[ranks // 4 :], ranks, 0, 1, 0)
@@ -1106,19 +1153,16 @@
     )
     grad_back = wide_grad[0].T.astype(jnp.float32)
     grad_hidden = wide_grad[1].astype(jnp.float32)
+    slim_sent = far_send(slim_total, ranks)
     pack = far_sum(pack_total, far_send(pack_total, ranks, jnp.float32)).reshape(-1)
-    slim_sent = far_send(slim_total, ranks)
-    slim_grad = far_sum(after(slim_total, grad_back, grad_hidden), slim_sent)
-    grad_proj = slim_grad[:, :columns]
-    grad_out = slim_grad[:, columns:].T
+    grad_proj, grad_out = finish(after(slim_total, grad_back, grad_hidden), slim_sent)
+    grad_out = grad_out.T
     result = result_product(
         place, after(resid, slim_total), mixed_share, own_other, vectors
     )
     input_grad = last_product(
         place, inputs, dbranch, dnorm_one, after(back_other, slim_total), vectors
     )
-    grad_proj = grad_proj.reshape(shard, pairs, 3, 128).transpose(2, 0, 1, 3)
-    grad_proj = grad_proj.reshape(3, shard, heads_width)
     vector_grads = [pack[i * shard : (i + 1) * shard] for i in range(6)]
     return (
         result,

time: 302 us -> 291 us (0.964)
  waiting for transfers between devices: 123 us -> 113 us
  starting transfers between devices: 30.4 us -> 36.1 us
  local copies, waits for them, and re-layouts: 19.9 us -> 14.6 us
    ppermute x26, waiting for transfers between devices: 58.3 us -> 50.7 us  [dp_shift(): lax.ppermute(value, 'dp', [(rank, goes(rank)) for rank in range(ranks)])]
    ppermute x7, waiting for transfers between devices: 64.3 us -> 59.2 us  [swap(): return lax.ppermute(value, 'tensor', [(0, 1), (1, 0)])]
    ppermute x7, starting transfers between devices: 5.45 us -> 9.01 us  [swap(): return lax.ppermute(value, 'tensor', [(0, 1), (1, 0)])]
    all_gather x1, waiting for transfers between devices: 0.01 us -> 3.24 us  [paired(): lax.all_gather(after(wide_shard, inputs_other, *narrow_far[1:6], narrow_f...]
where the time goes in v6:
time: 291 us
  waiting for transfers between devices  113 us (39%)
  Pallas kernels  73.2 us (25%)
  starting transfers between devices  36.1 us (12%)
  matrix products  34 us (12%)
  between operations  14.7 us (5%)
  local copies, waits for them, and re-layouts  14.6 us (5%)
  other arithmetic  5.01 us (2%)
    ppermute x7, waiting for transfers between devices, swap(): return lax.ppermute(value, 'tensor', [(0, 1), (1, 0)])  59.2 us
    ppermute x26, waiting for transfers between devices, dp_shift(): lax.ppermute(value, 'dp', [(rank, goes(rank)) for rank in range(ranks)])  50.7 us
    ppermute x26, starting transfers between devices, dp_shift(): lax.ppermute(value, 'dp', [(rank, goes(rank)) for rank in range(ranks)])  27 us
    pallas_call x1, Pallas kernels, feed_product(): pl.pallas_call(feed_kernel, grid_spec=pltpu.PrefetchScalarGridSpec(num_sc...  20.1 us
    pallas_call x1, Pallas kernels, front(): pl.pallas_call(functools.partial(front_kernel, scale=scale, count=len(pie...  18.4 us
    pallas_call x1, Pallas kernels, back_product(): pl.pallas_call(functools.partial(back_kernel, scale=scale), grid=(pairs,)...  18.4 us
    dot_general x1, matrix products, paired(): lax.dot_general(lefts, after(rights, dnorm_share), (((1,), (1,)), ((0,),...  12.3 us
    ppermute x7, starting transfers between devices, swap(): return lax.ppermute(value, 'tensor', [(0, 1), (1, 0)])  9.01 us
  transfers between devices with their start and end apart: 35, of which 15 were waited for; matrix products, arithmetic and copies ran while one was open for 16% of the time, Pallas kernels for 17%

profile of v6, /device:TPU:8, one launch (start us, length us, event | category | flops | bytes accessed | tf_op | source)
XLA Modules:
  0.0 290.7 jit_solution(10916113083619823082)
XLA Ops:
  7.2 2.2 pack.1
  14.5 4.4 %collective-permute-start.2 = (bf16[64,2176]{1,0:T(8,128)(2,1)}, bf16[64,2176]{1,0:T(8,128)(2,1)S(1)}, u32[]{:S(2)}, u32[]{:S(2)}) collective-permute-start(bf16[64,2176]{1,0:T(8,128)(2,1)} %get-tuple-element.65.refs_0_.refs_16_.refs_32_), channel_id=1, source_target_pairs={{0,16},{2,18},{4,20},{6,22},{8,24},{10,26},{12,28},{14,30},{16,0},... | collective-permute-start | bytes 835592 | tf_op jit(solution)/shard_map/ppermute | solution.py:965
  18.9 13.8 %collective-permute-done.3.refs_3_.refs_19_.refs_35_ = bf16[64,2176]{1,0:T(8,128)(2,1)S(1)} collective-permute-done((bf16[64,2176]{1,0:T(8,128)(2,1)}, bf16[64,2176]{1,0:T(8,128)(2,1)S(1)}, u32[]{:S(2)}, u32[]{:S(2)}) %collective-permute-start.3) | collective-permute-done | bytes 278560 | tf_op jit(solution)/shard_map/ppermute | solution.py:965
  34.7 1.8 collective-permute-done.2.refs_2_.refs_18_.refs_34_
  36.5 2.7 collective-permute-done.6.refs_7_.refs_23_.refs_39_
  39.2 3.0 %collective-permute-done.5.refs_5_.refs_21_.refs_37_ = bf16[64,2176]{1,0:T(8,128)(2,1)S(1)} collective-permute-done((bf16[64,2176]{1,0:T(8,128)(2,1)S(1)}, bf16[64,2176]{1,0:T(8,128)(2,1)S(1)}, u32[]{:S(2)}, u32[]{:S(2)}) %collective-permute-start.5) | collective-permute-done | bytes 278560 | tf_op jit(solution)/shard_map/ppermute | solution.py:965
  46.1 8.0 %collective-permute-done.7.refs_6_.refs_22_.refs_38_ = bf16[64,2176]{1,0:T(8,128)(2,1)S(1)} collective-permute-done((bf16[64,2176]{1,0:T(8,128)(2,1)S(1)}, bf16[64,2176]{1,0:T(8,128)(2,1)S(1)}, u32[]{:S(2)}, u32[]{:S(2)}) %collective-permute-start.7) | collective-permute-done | bytes 278560 | tf_op jit(solution)/shard_map/ppermute | solution.py:965
  56.5 18.4 %front.1 = (bf16[768,1024]{1,0:T(8,128)(2,1)}, bf16[768,1024]{1,0:T(8,128)(2,1)}, bf16[768,1024]{1,0:T(8,128)(2,1)}, bf16[1024,512]{1,0:T(8,128)(2,1)}, bf16[768...) custom-call(s32[20]{0:T(128)} %concatenate.21.place_ref, ...), custom_call_target="tpu_custom_call" | custom-call | flops 9663676416 | bytes 9437184 | tf_op jit(solution)/shard_map/front/pallas_call | solution.py:480
  76.5 4.5 %fusion.13 = bf16[1024,768]{1,0:T(8,128)(2,1)} fusion(bf16[768,1024]{1,0:T(8,128)(2,1)} %get-tuple-element.79, s32[1024]{0:T(1024)S(1)} %add.158), kind=kOutput, calls=%fused_computation.17 | convolution fusion | flops 1613496320 | bytes 3149824 | tf_op jit(solution)/shard_map/dot_general | solution.py:1071
  81.7 2.2 stack.23.grad_ref
  83.9 27.8 %collective-permute-done.17.other_ref = bf16[768,1024]{1,0:T(8,128)(2,1)S(1)} collective-permute-done((bf16[768,1024]{1,0:T(8,128)(2,1)}, bf16[768,1024]{1,0:T(8,128)(2,1)S(1)}, u32[]{:S(2)}, u32[]{:S(2)}) %collective-permute-start.17) | collective-permute-done | bytes 1572896 | tf_op jit(solution)/shard_map/ppermute | solution.py:1008
  111.6 3.2 %all-gather.2.cloned.1.call-done.pair_ref = bf16[1024,4096]{1,0:T(8,128)(2,1)} async-done(((bf16[64,4096]{1,0:T(8,128)(2,1)}), bf16[1024,4096]{1,0:T(8,128)(2,1)}) %all-gather.2.cloned.1.call-update) | async-done | bytes 8388624 | tf_op jit(solution)/shard_map/all_gather | solution.py:1059
  114.9 20.1 %feed.1 = (bf16[768,1024]{1,0:T(8,128)(2,1)}, bf16[2,768,1024]{2,1,0:T(8,128)(2,1)}, bf16[2,768,2048]{2,1,0:T(8,128)(2,1)}, bf16[768,1024]{1,0:T(8,128)(2,1)}, f32[8,2048]{1,0:T(8,128)}) custom-call(s32[20]{0:T(128)} %concatenate.21.place_ref, bf16[768,1024]{1,0:T(8,128)(2,1)} %get-tuple-element.68.x_ref, ...), custom_call_target="tpu_custom_call", output_to_operand_aliasing={{1}: (6, {})} | custom-call | flops 14495514624 | bytes 31457280 | tf_op jit(solution)/shard_map/feed/pallas_call | solution.py:602
  136.5 12.3 %convolution_convert_fusion = bf16[2,1024,2048]{2,1,0:T(8,128)(2,1)} fusion(bf16[2,768,1024]{2,1,0:T(8,128)(2,1)} %get-tuple-element.83.grad_ref, bf16[2,768,2048]{2,1,0:T(8,128)(2,1)} %get-tuple-element.86), kind=kOutput, calls=%fused_computation | convolution fusion | flops 6446645248 | bytes 17825792 | tf_op jit(solution)/shard_map/dot_general | solution.py:1088
  150.1 6.9 %fusion.19.own_ref = bf16[768,1024]{1,0:T(8,128)(2,1)S(1)} fusion(bf16[1024,4096]{1,0:T(8,128)(2,1)} %all-gather.2.cloned.1.call-done.pair_ref, bf16[2,768,2048]{2,1,0:T(8,128)(2,1)} %get-tuple-element.86), kind=kOutput, calls=%fused_computation.19 | convolution fusion | flops 3222011904 | bytes 8912896 | tf_op jit(solution)/shard_map/dot_general | solution.py:43
  157.0 14.9 %collective-permute-done.18.other_ref = bf16[768,1024]{1,0:T(8,128)(2,1)S(1)} collective-permute-done((bf16[768,1024]{1,0:T(8,128)(2,1)}, bf16[768,1024]{1,0:T(8,128)(2,1)S(1)}, u32[]{:S(2)}, u32[]{:S(2)}) %collective-permute-start.18) | collective-permute-done | bytes 1572896 | tf_op jit(solution)/shard_map/ppermute | solution.py:1008
  173.0 7.0 %mid.1 = (bf16[768,1024]{1,0:T(8,128)(2,1)}, bf16[768,512]{1,0:T(8,128)(2,1)}, f32[8,1024]{1,0:T(8,128)}) custom-call(bf16[768,1024]{1,0:T(8,128)(2,1)} %get-tuple-element.108.resid_ref, bf16[768,1024]{1,0:T(8,128)(2,1)} %get-tuple-element.84.own_ref, bf16[768,1024]{1,0:T(8,128)(2,1)} %copy-done.27, bf16[2,768,1024]{2,1,0:T(8,128)(2,1)} %get-tuple-element.83.grad_ref, ...), custom_call_target="tpu_custom_call" | custom-call | flops 12884901888 | bytes 12582912 | tf_op jit(solution)/shard_map/mid/pallas_call | solution.py:663
  180.0 18.4 %back.1 = (bf16[768,1536]{1,0:T(8,128)(2,1)}, bf16[768,1024]{1,0:T(8,128)(2,1)}, f32[4,1,384]{2,1,0:T(1,128)}, f32[2,1024]{1,0:T(2,128)}) custom-call(bf16[768,1024]{1,0:T(8,128)(2,1)} %get-tuple-element.80.xhat_all_ref, bf16[768,1536]{1,0:T(8,128)(2,1)} %get-tuple-element.81.qkv_ref, bf16[768,512]{1,0:T(8,128)(2,1)} %get-tuple-element.89.grad_ref, ...), custom_call_target="tpu_custom_call" | custom-call | flops 115964116992 | bytes 9437184 | tf_op jit(solution)/shard_map/back/pallas_call | solution.py:794
  200.3 3.2 %convolution_convert_fusion.1 = bf16[512,1536]{1,0:T(8,128)(2,1)S(1)} fusion(bf16[768,1536]{1,0:T(8,128)(2,1)} %get-tuple-element.92, bf16[1024,768]{1,0:T(8,128)(2,1)S(1)} %copy-done.19), kind=kOutput, calls=%fused_computation.7 | convolution fusion | flops 1208745984 | bytes 4718592 | tf_op jit(solution)/shard_map/dot_general | solution.py:33
  203.9 1.9 fusion.16
  216.1 16.6 %collective-permute-done.25.other_ref = bf16[384,1024]{1,0:T(8,128)(2,1)S(1)} collective-permute-done((bf16[384,1024]{1,0:T(8,128)(2,1)S(1)}, bf16[384,1024]{1,0:T(8,128)(2,1)S(1)}, u32[]{:S(2)}, u32[]{:S(2)}) %collective-permute-start.25) | collective-permute-done | bytes 786464 | tf_op jit(solution)/shard_map/ppermute | solution.py:1008
  235.2 10.0 %collective-permute-done.24 = f32[4,768]{1,0:T(4,128)S(1)} collective-permute-done((f32[4,768]{1,0:T(4,128)S(1)}, f32[4,768]{1,0:T(4,128)S(1)}, u32[]{:S(2)}, u32[]{:S(2)}) %collective-permute-start.24) | collective-permute-done | bytes 12320 | tf_op jit(solution)/shard_map/ppermute | solution.py:965
  246.5 1.8 fusion.9
  248.5 3.7 %collective-permute-start.27 = (f32[1,768]{1,0:T(1,128)S(1)}, f32[1,768]{1,0:T(1,128)S(1)}, u32[]{:S(2)}, u32[]{:S(2)}) collective-permute-start(f32[1,768]{1,0:T(1,128)S(1)} %get-tuple-element.123), channel_id=1, source_target_pairs={{0,24},{2,26},{4,28},{6,30},{8,0},{10,2},{12,4},{14,6},{16,8},{18,... | collective-permute-start | bytes 9224 | tf_op jit(solution)/shard_map/ppermute | solution.py:965
  253.5 2.8 collective-permute-start.28
  258.8 3.0 %last.1 = f32[384,1024]{1,0:T(8,128)} custom-call(s32[20]{0:T(128)S(1)} %copy-done.9, bf16[384,1024]{1,0:T(8,128)(2,1)S(1)} %copy-done.7, bf16[768,1024]{1,0:T(8,128)(2,1)S(1)} %copy-done.6, bf16[768,1024]{1,0:T(8,128)(2,1)S(1)} %copy-done.3, bf16[384,1024]{1,0:T(8,128)(2,1)S(1)} %collective-permute-done.25.other_ref, f32[8,1024]{1,0:T(8,128)S(1)} %copy-done.8), custom_call_target="tpu_custom_call" | custom-call | flops 15728640 | bytes 125829120 | tf_op jit(solution)/shard_map/last/pallas_call | solution.py:842
  261.9 2.0 collective-permute-start.30
  268.6 2.2 result.1
  270.8 2.1 fusion.32
  272.9 7.4 %collective-permute-done.31.two_ref = bf16[64,2048]{1,0:T(8,128)(2,1)S(1)} collective-permute-done((bf16[64,2048]{1,0:T(8,128)(2,1)}, bf16[64,2048]{1,0:T(8,128)(2,1)S(1)}, u32[]{:S(2)}, u32[]{:S(2)}) %collective-permute-start.31) | collective-permute-done | bytes 262176 | tf_op jit(solution)/shard_map/ppermute | solution.py:965
  280.3 1.7 collective-permute-done.30.one_ref
  282.0 1.8 finish.1
  (187 shorter events, 44.1 us)
Async XLA Ops:
  7.2 107.7 %all-gather.2.cloned.1.call-start = ((), (), s32[]{:S(2)}) async-start(), calls=%async_computation.1 | async-start | bytes 8912896 | tf_op jit(solution)/shard_map/all_gather | solution.py:1059
  9.4 32.8 %collective-permute-start = (bf16[384,1024]{1,0:T(8,128)(2,1)}, bf16[384,1024]{1,0:T(8,128)(2,1)S(1)}, u32[]{:S(2)}, u32[]{:S(2)}) collective-permute-start(bf16[384,1024]{1,0:T(8,128)(2,1)} %x_ref.1), channel_id=1, source_target_pairs={{0,1},{1,0},{2,3},{3,2},{4,5},{5,4},{6,7},{7,6},{8,9},{9,8},{10,11... | collective-permute-start | bytes 2359304 | tf_op jit(solution)/shard_map/ppermute | solution.py:1008
  10.9 21.7 %collective-permute-start.3 = (bf16[64,2176]{1,0:T(8,128)(2,1)}, bf16[64,2176]{1,0:T(8,128)(2,1)S(1)}, u32[]{:S(2)}, u32[]{:S(2)}) collective-permute-start(bf16[64,2176]{1,0:T(8,128)(2,1)} %get-tuple-element.65.refs_0_.refs_16_.refs_32_), channel_id=1, source_target_pairs={{0,24},{2,26},{4,28},{6,30},{8,0},{10,2},{12,4},{14,6},{16,8},{18,... | collective-permute-start | bytes 835592 | tf_op jit(solution)/shard_map/ppermute | solution.py:965
  11.4 22.8 %collective-permute-start.1 = (bf16[64,2176]{1,0:T(8,128)(2,1)}, bf16[64,2176]{1,0:T(8,128)(2,1)S(1)}, u32[]{:S(2)}, u32[]{:S(2)}) collective-permute-start(bf16[64,2176]{1,0:T(8,128)(2,1)} %get-tuple-element.65.refs_0_.refs_16_.refs_32_), channel_id=1, source_target_pairs={{0,8},{2,10},{4,12},{6,14},{8,16},{10,18},{12,20},{14,22},{16,24},... | collective-permute-start | bytes 835592 | tf_op jit(solution)/shard_map/ppermute | solution.py:965
  12.9 21.7 %collective-permute-start.4 = (bf16[64,2176]{1,0:T(8,128)(2,1)}, bf16[64,2176]{1,0:T(8,128)(2,1)S(1)}, u32[]{:S(2)}, u32[]{:S(2)}) collective-permute-start(bf16[64,2176]{1,0:T(8,128)(2,1)} %get-tuple-element.65.refs_0_.refs_16_.refs_32_), channel_id=1, source_target_pairs={{0,4},{2,6},{4,0},{6,2},{8,12},{10,14},{12,8},{14,10},{16,20},{18,... | collective-permute-start | bytes 835592 | tf_op jit(solution)/shard_map/ppermute | solution.py:965
  14.5 22.1 %collective-permute-start.2 = (bf16[64,2176]{1,0:T(8,128)(2,1)}, bf16[64,2176]{1,0:T(8,128)(2,1)S(1)}, u32[]{:S(2)}, u32[]{:S(2)}) collective-permute-start(bf16[64,2176]{1,0:T(8,128)(2,1)} %get-tuple-element.65.refs_0_.refs_16_.refs_32_), channel_id=1, source_target_pairs={{0,16},{2,18},{4,20},{6,22},{8,24},{10,26},{12,28},{14,30},{16,0},... | collective-permute-start | bytes 835592 | tf_op jit(solution)/shard_map/ppermute | solution.py:965
  32.6 6.5 %collective-permute-start.6 = (bf16[64,2176]{1,0:T(8,128)(2,1)S(1)}, bf16[64,2176]{1,0:T(8,128)(2,1)S(1)}, u32[]{:S(2)}, u32[]{:S(2)}) collective-permute-start(bf16[64,2176]{1,0:T(8,128)(2,1)S(1)} %collective-permute-done.3.refs_3_.refs_19_.refs_35_), channel_id=1, source_target_pairs={{0,4},{2,6},{4,0},{6,2},{8,12},{10,14},{12,8},{14,10},{16,20},{18,... | collective-permute-start | bytes 835592 | tf_op jit(solution)/shard_map/ppermute | solution.py:965
  34.2 8.0 %collective-permute-start.5 = (bf16[64,2176]{1,0:T(8,128)(2,1)S(1)}, bf16[64,2176]{1,0:T(8,128)(2,1)S(1)}, u32[]{:S(2)}, u32[]{:S(2)}) collective-permute-start(bf16[64,2176]{1,0:T(8,128)(2,1)S(1)} %collective-permute-done.1.refs_1_.refs_17_.refs_33_), channel_id=1, source_target_pairs={{0,4},{2,6},{4,0},{6,2},{8,12},{10,14},{12,8},{14,10},{16,20},{18,... | collective-permute-start | bytes 835592 | tf_op jit(solution)/shard_map/ppermute | solution.py:965
  42.2 228.6 %reduce-scatter.2.cloned.1.call-start = ((), (), s32[]{:S(2)}) async-start(), calls=%async_computation.2 | async-start | bytes 8912896 | tf_op jit(solution)/shard_map/reduce_scatter | solution.py:1094
  42.3 3.0 %collective-permute-start.8 = (bf16[64,2176]{1,0:T(8,128)(2,1)}, bf16[64,2176]{1,0:T(8,128)(2,1)S(1)}, u32[]{:S(2)}, u32[]{:S(2)}) collective-permute-start(bf16[64,2176]{1,0:T(8,128)(2,1)} %get-tuple-element.65.refs_0_.refs_16_.refs_32_), channel_id=1, source_target_pairs={{0,2},{2,0},{4,6},{6,4},{8,10},{10,8},{12,14},{14,12},{16,18},{18,... | collective-permute-start | bytes 835592 | tf_op jit(solution)/shard_map/ppermute | solution.py:965
  43.0 2.6 collective-permute-start.12
  43.5 2.3 collective-permute-start.11
  43.6 10.5 %collective-permute-start.7 = (bf16[64,2176]{1,0:T(8,128)(2,1)S(1)}, bf16[64,2176]{1,0:T(8,128)(2,1)S(1)}, u32[]{:S(2)}, u32[]{:S(2)}) collective-permute-start(bf16[64,2176]{1,0:T(8,128)(2,1)S(1)} %collective-permute-done.2.refs_2_.refs_18_.refs_34_), channel_id=1, source_target_pairs={{0,4},{2,6},{4,0},{6,2},{8,12},{10,14},{12,8},{14,10},{16,20},{18,... | collective-permute-start | bytes 835592 | tf_op jit(solution)/shard_map/ppermute | solution.py:965
  45.1 9.0 %collective-permute-start.10 = (bf16[64,2176]{1,0:T(8,128)(2,1)S(1)}, bf16[64,2176]{1,0:T(8,128)(2,1)S(1)}, u32[]{:S(2)}, u32[]{:S(2)}) collective-permute-start(bf16[64,2176]{1,0:T(8,128)(2,1)S(1)} %collective-permute-done.2.refs_2_.refs_18_.refs_34_), channel_id=1, source_target_pairs={{0,2},{2,0},{4,6},{6,4},{8,10},{10,8},{12,14},{14,12},{16,18},{18,... | collective-permute-start | bytes 835592 | tf_op jit(solution)/shard_map/ppermute | solution.py:965
  45.2 9.0 %collective-permute-start.9 = (bf16[64,2176]{1,0:T(8,128)(2,1)S(1)}, bf16[64,2176]{1,0:T(8,128)(2,1)S(1)}, u32[]{:S(2)}, u32[]{:S(2)}) collective-permute-start(bf16[64,2176]{1,0:T(8,128)(2,1)S(1)} %collective-permute-done.1.refs_1_.refs_17_.refs_33_), channel_id=1, source_target_pairs={{0,2},{2,0},{4,6},{6,4},{8,10},{10,8},{12,14},{14,12},{16,18},{18,... | collective-permute-start | bytes 835592 | tf_op jit(solution)/shard_map/ppermute | solution.py:965
  45.6 8.6 %collective-permute-start.15 = (bf16[64,2176]{1,0:T(8,128)(2,1)S(1)}, bf16[64,2176]{1,0:T(8,128)(2,1)S(1)}, u32[]{:S(2)}, u32[]{:S(2)}) collective-permute-start(bf16[64,2176]{1,0:T(8,128)(2,1)S(1)} %collective-permute-done.6.refs_7_.refs_23_.refs_39_), channel_id=1, source_target_pairs={{0,2},{2,0},{4,6},{6,4},{8,10},{10,8},{12,14},{14,12},{16,18},{18,... | collective-permute-start | bytes 835592 | tf_op jit(solution)/shard_map/ppermute | solution.py:965
  45.8 8.5 %collective-permute-start.13 = (bf16[64,2176]{1,0:T(8,128)(2,1)S(1)}, bf16[64,2176]{1,0:T(8,128)(2,1)S(1)}, u32[]{:S(2)}, u32[]{:S(2)}) collective-permute-start(bf16[64,2176]{1,0:T(8,128)(2,1)S(1)} %collective-permute-done.5.refs_5_.refs_21_.refs_37_), channel_id=1, source_target_pairs={{0,2},{2,0},{4,6},{6,4},{8,10},{10,8},{12,14},{14,12},{16,18},{18,... | collective-permute-start | bytes 835592 | tf_op jit(solution)/shard_map/ppermute | solution.py:965
  54.1 20.8 %collective-permute-start.16 = (bf16[384,1024]{1,0:T(8,128)(2,1)}, bf16[384,1024]{1,0:T(8,128)(2,1)S(1)}, u32[]{:S(2)}, u32[]{:S(2)}) collective-permute-start(bf16[384,1024]{1,0:T(8,128)(2,1)} %param.16), channel_id=1, source_target_pairs={{0,1},{1,0},{2,3},{3,2},{4,5},{5,4},{6,7},{7,6},{8,9},{9,8},{10,11... | collective-permute-start | bytes 2359304 | tf_op jit(solution)/shard_map/ppermute | solution.py:1008
  74.9 36.7 %collective-permute-start.17 = (bf16[768,1024]{1,0:T(8,128)(2,1)}, bf16[768,1024]{1,0:T(8,128)(2,1)S(1)}, u32[]{:S(2)}, u32[]{:S(2)}) collective-permute-start(bf16[768,1024]{1,0:T(8,128)(2,1)} %get-tuple-element.71.own_ref), channel_id=1, source_target_pairs={{0,1},{1,0},{2,3},{3,2},{4,5},{5,4},{6,7},{7,6},{8,9},{9,8},{10,11... | collective-permute-start | bytes 4718600 | tf_op jit(solution)/shard_map/ppermute | solution.py:1008
  135.0 36.8 %collective-permute-start.18 = (bf16[768,1024]{1,0:T(8,128)(2,1)}, bf16[768,1024]{1,0:T(8,128)(2,1)S(1)}, u32[]{:S(2)}, u32[]{:S(2)}) collective-permute-start(bf16[768,1024]{1,0:T(8,128)(2,1)} %get-tuple-element.84.own_ref), channel_id=1, source_target_pairs={{0,1},{1,0},{2,3},{3,2},{4,5},{5,4},{6,7},{7,6},{8,9},{9,8},{10,11... | collective-permute-start | bytes 4718600 | tf_op jit(solution)/shard_map/ppermute | solution.py:1008
  203.5 5.3 %collective-permute-start.19 = (bf16[512,1536]{1,0:T(8,128)(2,1)S(1)}, bf16[512,1536]{1,0:T(8,128)(2,1)S(1)}, u32[]{:S(2)}, u32[]{:S(2)}) collective-permute-start(bf16[512,1536]{1,0:T(8,128)(2,1)S(1)} %convolution_convert_fusion.1), channel_id=1, source_target_pairs={{0,2},{2,0},{4,6},{6,4},{8,10},{10,8},{12,14},{14,12},{16,18},{18,... | collective-permute-start | bytes 4718600 | tf_op jit(solution)/shard_map/ppermute | solution.py:965
  206.9 4.2 %collective-permute-start.21 = (f32[16,768]{1,0:T(8,128)S(1)}, f32[16,768]{1,0:T(8,128)S(1)}, u32[]{:S(2)}, u32[]{:S(2)}) collective-permute-start(f32[16,768]{1,0:T(8,128)S(1)} %fusion.33), channel_id=1, source_target_pairs={{0,1},{1,0},{2,3},{3,2},{4,5},{5,4},{6,7},{7,6},{8,9},{9,8},{10,11... | collective-permute-start | bytes 147464 | tf_op jit(solution)/shard_map/ppermute | solution.py:1008
  212.5 32.7 %collective-permute-start.23 = (bf16[256,2048]{1,0:T(8,128)(2,1)}, bf16[256,2048]{1,0:T(8,128)(2,1)S(1)}, u32[]{:S(2)}, u32[]{:S(2)}) collective-permute-start(bf16[256,2048]{1,0:T(8,128)(2,1)} %pad_maximum_fusion.1), channel_id=1, source_target_pairs={{0,4},{2,6},{4,0},{6,2},{8,12},{10,14},{12,8},{14,10},{16,20},{18,... | collective-permute-start | bytes 3145736 | tf_op jit(solution)/shard_map/ppermute | solution.py:965
  213.2 19.6 %collective-permute-start.25 = (bf16[384,1024]{1,0:T(8,128)(2,1)S(1)}, bf16[384,1024]{1,0:T(8,128)(2,1)S(1)}, u32[]{:S(2)}, u32[]{:S(2)}) collective-permute-start(bf16[384,1024]{1,0:T(8,128)(2,1)S(1)} %constant_dynamic-slice_fusion.1), channel_id=1, source_target_pairs={{0,1},{1,0},{2,3},{3,2},{4,5},{5,4},{6,7},{7,6},{8,9},{9,8},{10,11... | collective-permute-start | bytes 2359304 | tf_op jit(solution)/shard_map/ppermute | solution.py:1008
  214.7 30.4 %collective-permute-start.24 = (f32[4,768]{1,0:T(4,128)S(1)}, f32[4,768]{1,0:T(4,128)S(1)}, u32[]{:S(2)}, u32[]{:S(2)}) collective-permute-start(f32[4,768]{1,0:T(4,128)S(1)} %slice.155), channel_id=1, source_target_pairs={{0,4},{2,6},{4,0},{6,2},{8,12},{10,14},{12,8},{14,10},{16,20},{18,... | collective-permute-start | bytes 36872 | tf_op jit(solution)/shard_map/ppermute | solution.py:965
  233.7 32.1 %collective-permute-start.26 = (bf16[384,1024]{1,0:T(8,128)(2,1)}, bf16[384,1024]{1,0:T(8,128)(2,1)S(1)}, u32[]{:S(2)}, u32[]{:S(2)}) collective-permute-start(bf16[384,1024]{1,0:T(8,128)(2,1)} %constant_dynamic-slice_fusion), channel_id=1, source_target_pairs={{0,1},{1,0},{2,3},{3,2},{4,5},{5,4},{6,7},{7,6},{8,9},{9,8},{10,11... | collective-permute-start | bytes 2359304 | tf_op jit(solution)/shard_map/ppermute | solution.py:1008
  248.5 13.3 %collective-permute-start.27 = (f32[1,768]{1,0:T(1,128)S(1)}, f32[1,768]{1,0:T(1,128)S(1)}, u32[]{:S(2)}, u32[]{:S(2)}) collective-permute-start(f32[1,768]{1,0:T(1,128)S(1)} %get-tuple-element.123), channel_id=1, source_target_pairs={{0,24},{2,26},{4,28},{6,30},{8,0},{10,2},{12,4},{14,6},{16,8},{18,... | collective-permute-start | bytes 9224 | tf_op jit(solution)/shard_map/ppermute | solution.py:965
  252.2 9.7 %collective-permute-start.29 = (f32[1,768]{1,0:T(1,128)S(1)}, f32[1,768]{1,0:T(1,128)S(1)}, u32[]{:S(2)}, u32[]{:S(2)}) collective-permute-start(f32[1,768]{1,0:T(1,128)S(1)} %get-tuple-element.124), channel_id=1, source_target_pairs={{0,16},{2,18},{4,20},{6,22},{8,24},{10,26},{12,28},{14,30},{16,0},... | collective-permute-start | bytes 9224 | tf_op jit(solution)/shard_map/ppermute | solution.py:965
  253.5 10.4 %collective-permute-start.28 = (f32[1,768]{1,0:T(1,128)S(1)}, f32[1,768]{1,0:T(1,128)S(1)}, u32[]{:S(2)}, u32[]{:S(2)}) collective-permute-start(f32[1,768]{1,0:T(1,128)S(1)} %get-tuple-element.125), channel_id=1, source_target_pairs={{0,8},{2,10},{4,12},{6,14},{8,16},{10,18},{12,20},{14,22},{16,24},... | collective-permute-start | bytes 9224 | tf_op jit(solution)/shard_map/ppermute | solution.py:965
  257.4 15.4 %collective-permute-start.32 = (bf16[64,2048]{1,0:T(8,128)(2,1)}, bf16[64,2048]{1,0:T(8,128)(2,1)S(1)}, u32[]{:S(2)}, u32[]{:S(2)}) collective-permute-start(bf16[64,2048]{1,0:T(8,128)(2,1)} %get-tuple-element.118), channel_id=1, source_target_pairs={{0,16},{2,18},{4,20},{6,22},{8,24},{10,26},{12,28},{14,30},{16,0},... | collective-permute-start | bytes 786440 | tf_op jit(solution)/shard_map/ppermute | solution.py:965
  261.9 18.4 %collective-permute-start.31 = (bf16[64,2048]{1,0:T(8,128)(2,1)}, bf16[64,2048]{1,0:T(8,128)(2,1)S(1)}, u32[]{:S(2)}, u32[]{:S(2)}) collective-permute-start(bf16[64,2048]{1,0:T(8,128)(2,1)} %get-tuple-element.119), channel_id=1, source_target_pairs={{0,8},{2,10},{4,12},{6,14},{8,16},{10,18},{12,20},{14,22},{16,24},... | collective-permute-start | bytes 786440 | tf_op jit(solution)/shard_map/ppermute | solution.py:965
  261.9 20.1 %collective-permute-start.30 = (bf16[64,2048]{1,0:T(8,128)(2,1)}, bf16[64,2048]{1,0:T(8,128)(2,1)}, u32[]{:S(2)}, u32[]{:S(2)}) collective-permute-start(bf16[64,2048]{1,0:T(8,128)(2,1)} %get-tuple-element.120), channel_id=1, source_target_pairs={{0,24},{2,26},{4,28},{6,30},{8,0},{10,2},{12,4},{14,6},{16,8},{18,... | collective-permute-start | bytes 786440 | tf_op jit(solution)/shard_map/ppermute | solution.py:965
  (47 other events, 488.8 us)
Sparse Core Ops, SparseCore 0:
  42.3 72.4 all-gather.1
  149.0 112.0 reduce-scatter.1

commit v7 on v6

--- a/solution.py
+++ b/solution.py
@@ -881,16 +881,14 @@
     )(place, resid, own, other, vectors)
 
 
-def finish_kernel(own_ref, one_ref, two_ref, three_ref, proj_ref, out_ref):
+def finish_kernel(own_ref, one_ref, two_ref, three_ref, proj_ref):
     total = own_ref[...]
     for ref in (one_ref, two_ref, three_ref):
         total = total + ref[...].astype(jnp.float32)
-    columns = out_ref.shape[1]
-    for pair in range(columns // 128):
+    for pair in range(proj_ref.shape[2] // 128):
         for kind in range(3):
             start = (pair * 3 + kind) * 128
             proj_ref[kind, :, pair * 128 : pair * 128 + 128] = total[:, start : start + 128]
-    out_ref[...] = total[:, 3 * columns :]
 
 
 def finish(total, sent):
@@ -899,11 +897,8 @@
         finish_kernel,
         grid=(1,),
         in_specs=[whole((rows, columns))] * 4,
-        out_specs=[whole((3, rows, columns // 4)), whole((rows, columns // 4))],
-        out_shape=[
-            jax.ShapeDtypeStruct((3, rows, columns // 4), jnp.float32),
-            jax.ShapeDtypeStruct((rows, columns // 4), jnp.float32),
-        ],
+        out_specs=whole((3, rows, columns // 3)),
+        out_shape=jax.ShapeDtypeStruct((3, rows, columns // 3), jnp.float32),
         compiler_params=settings(16),
         cost_estimate=cost(4 * rows * columns, 14 * rows * columns),
         name="finish",
@@ -1121,42 +1116,33 @@
     dbranch_slot = to_slots(after(dbranch, pack))
     pack_other = swap(pack)
     out_core = reduce_core(dbranch_slot, attended, ranks)
-    slim_near = jnp.concatenate(
-        [
-            reduce_near(norm_slot, dqkv, proj_core),
-            reduce_near(dbranch_slot, attended, out_core),
-        ],
-        axis=1,
-    )
-    pack = pack + after(pack_other, slim_near)
+    proj_near = reduce_near(norm_slot, dqkv, proj_core)
+    pack = pack + after(pack_other, proj_near)
     pack = pack[: ranks // 2] + dp_shift(pack[ranks // 2 :], ranks, 0, 0, 1)
-    slim_near, pack = lax.optimization_barrier((slim_near, pack))
+    proj_near, pack = lax.optimization_barrier((proj_near, pack))
+    pack_arrived = dp_shift(pack[ranks // 4 :], ranks, 0, 1, 0)
+    proj_arrived = dp_shift(proj_near, ranks, 0, 1, 0)
     back_other = swap(other_rows(after(dnorm_one, pack)))
-    pack_arrived = dp_shift(pack[ranks // 4 :], ranks, 0, 1, 0)
-    slim_arrived = dp_shift(slim_near, ranks, 0, 1, 0)
+    out_near = reduce_near(dbranch_slot, attended, after(out_core, proj_near))
+    out_arrived = dp_shift(out_near, ranks, 0, 1, 0)
     own_other = swap(other_rows(after(mixed_share, back_other)))
-    slim_arrived, pack_arrived, back_other = lax.optimization_barrier(
-        (slim_arrived, pack_arrived, back_other)
-    )
-    columns = 3 * heads_width
+    proj_arrived, pack_arrived, back_other = lax.optimization_barrier(
+        (proj_arrived, pack_arrived, back_other)
+    )
     slim_total, pack_total = lax.optimization_barrier(
         (
-            jnp.concatenate(
-                [
-                    reduce_sum(norm_slot, dqkv, proj_core, slim_arrived[:, :columns]),
-                    reduce_sum(dbranch_slot, attended, out_core, slim_arrived[:, columns:]),
-                ],
-                axis=1,
-            ),
+            reduce_sum(norm_slot, dqkv, proj_core, proj_arrived),
             pack[: ranks // 4] + pack_arrived,
         )
     )
+    slim_sent = far_send(slim_total, ranks)
+    pack = far_sum(pack_total, far_send(pack_total, ranks, jnp.float32)).reshape(-1)
+    out_total = reduce_sum(dbranch_slot, attended, out_core, after(out_arrived, *slim_sent))
+    out_sent = far_send(out_total, ranks)
     grad_back = wide_grad[0].T.astype(jnp.float32)
     grad_hidden = wide_grad[1].astype(jnp.float32)
-    slim_sent = far_send(slim_total, ranks)
-    pack = far_sum(pack_total, far_send(pack_total, ranks, jnp.float32)).reshape(-1)
-    grad_proj, grad_out = finish(after(slim_total, grad_back, grad_hidden), slim_sent)
-    grad_out = grad_out.T
+    grad_proj = finish(after(slim_total, grad_back, grad_hidden), slim_sent)
+    grad_out = far_sum(out_total, out_sent).T
     result = result_product(
         place, after(resid, slim_total), mixed_share, own_other, vectors
     )

time: 291 us -> 307 us (1.055); the launches traced: 291 us -> 302 us
  waiting for transfers between devices: 113 us -> 124 us
    ppermute x26 -> x30, waiting for transfers between devices: 50.7 us -> 60.7 us  [dp_shift(): lax.ppermute(value, 'dp', [(rank, goes(rank)) for rank in range(ranks)])]
    ppermute x26 -> x30, starting transfers between devices: 27 us -> 28.2 us  [dp_shift(): lax.ppermute(value, 'dp', [(rank, goes(rank)) for rank in range(ranks)])]
  transfers between devices with their start and end apart: 35 -> 39, of which waited for: 15 -> 16; matrix products, arithmetic and copies ran while one was open for 16% -> 15% of each run, Pallas kernels for 17% -> 17%
where the time goes in v7:
time: 307 us; the launch traced here: 302 us
  waiting for transfers between devices  124 us (40%)
  Pallas kernels  73.6 us (24%)
  starting transfers between devices  36.4 us (12%)
  matrix products  35.9 us (12%)
  between operations  14.7 us (5%)
  local copies, waits for them, and re-layouts  13.3 us (4%)
  other arithmetic  4.69 us (2%)
    ppermute x30, waiting for transfers between devices, dp_shift(): lax.ppermute(value, 'dp', [(rank, goes(rank)) for rank in range(ranks)])  60.7 us
    ppermute x7, waiting for transfers between devices, swap(): return lax.ppermute(value, 'tensor', [(0, 1), (1, 0)])  60 us
    ppermute x30, starting transfers between devices, dp_shift(): lax.ppermute(value, 'dp', [(rank, goes(rank)) for rank in range(ranks)])  28.2 us
    pallas_call x1, Pallas kernels, feed_product(): pl.pallas_call(feed_kernel, grid_spec=pltpu.PrefetchScalarGridSpec(num_sc...  20.1 us
    pallas_call x1, Pallas kernels, front(): pl.pallas_call(functools.partial(front_kernel, scale=scale, count=len(pie...  18.5 us
    pallas_call x1, Pallas kernels, back_product(): pl.pallas_call(functools.partial(back_kernel, scale=scale), grid=(pairs,)...  18.4 us
    dot_general x1, matrix products, paired(): lax.dot_general(lefts, after(rights, dnorm_share), (((1,), (1,)), ((0,),...  12.4 us
    dot_general x6, matrix products, matmul(): return jnp.dot(left, right, preferred_element_type=jnp.float32)  10.3 us
  transfers between devices with their start and end apart: 39, of which 16 were waited for; matrix products, arithmetic and copies ran while one was open for 15% of the time, Pallas kernels for 17%

profile of v7, /device:TPU:8, one launch (start us, length us, event | category | flops | bytes accessed | tf_op | source)
XLA Modules:
  0.0 302.5 jit_solution(14322020888748372384)
XLA Ops:
  7.2 2.2 pack.1
  14.5 4.4 %collective-permute-start.2 = (bf16[64,2176]{1,0:T(8,128)(2,1)}, bf16[64,2176]{1,0:T(8,128)(2,1)S(1)}, u32[]{:S(2)}, u32[]{:S(2)}) collective-permute-start(bf16[64,2176]{1,0:T(8,128)(2,1)} %get-tuple-element.65.refs_0_.refs_16_.refs_32_), channel_id=1, source_target_pairs={{0,16},{2,18},{4,20},{6,22},{8,24},{10,26},{12,28},{14,30},{16,0},... | collective-permute-start | bytes 835592 | tf_op jit(solution)/shard_map/ppermute | solution.py:960
  18.9 13.8 %collective-permute-done.3.refs_3_.refs_19_.refs_35_ = bf16[64,2176]{1,0:T(8,128)(2,1)S(1)} collective-permute-done((bf16[64,2176]{1,0:T(8,128)(2,1)}, bf16[64,2176]{1,0:T(8,128)(2,1)S(1)}, u32[]{:S(2)}, u32[]{:S(2)}) %collective-permute-start.3) | collective-permute-done | bytes 278560 | tf_op jit(solution)/shard_map/ppermute | solution.py:960
  36.5 2.7 collective-permute-done.6.refs_7_.refs_23_.refs_39_
  39.2 3.0 collective-permute-done.5.refs_5_.refs_21_.refs_37_
  46.1 8.0 %collective-permute-done.7.refs_6_.refs_22_.refs_38_ = bf16[64,2176]{1,0:T(8,128)(2,1)S(1)} collective-permute-done((bf16[64,2176]{1,0:T(8,128)(2,1)S(1)}, bf16[64,2176]{1,0:T(8,128)(2,1)S(1)}, u32[]{:S(2)}, u32[]{:S(2)}) %collective-permute-start.7) | collective-permute-done | bytes 278560 | tf_op jit(solution)/shard_map/ppermute | solution.py:960
  56.5 18.5 %front.1 = (bf16[768,1024]{1,0:T(8,128)(2,1)}, bf16[768,1024]{1,0:T(8,128)(2,1)}, bf16[768,1024]{1,0:T(8,128)(2,1)}, bf16[1024,512]{1,0:T(8,128)(2,1)}, bf16[768...) custom-call(s32[20]{0:T(128)} %concatenate.15.place_ref, ...), custom_call_target="tpu_custom_call" | custom-call | flops 9663676416 | bytes 9437184 | tf_op jit(solution)/shard_map/front/pallas_call | solution.py:480
  76.5 4.5 %fusion.13 = bf16[1024,768]{1,0:T(8,128)(2,1)} fusion(bf16[768,1024]{1,0:T(8,128)(2,1)} %get-tuple-element.79, s32[1024]{0:T(1024)S(1)} %add.167), kind=kOutput, calls=%fused_computation.16 | convolution fusion | flops 1613496320 | bytes 3149824 | tf_op jit(solution)/shard_map/dot_general | solution.py:1066
  81.7 2.1 stack.23.grad_ref
  83.9 27.8 %collective-permute-done.17.other_ref = bf16[768,1024]{1,0:T(8,128)(2,1)S(1)} collective-permute-done((bf16[768,1024]{1,0:T(8,128)(2,1)}, bf16[768,1024]{1,0:T(8,128)(2,1)S(1)}, u32[]{:S(2)}, u32[]{:S(2)}) %collective-permute-start.17) | collective-permute-done | bytes 1572896 | tf_op jit(solution)/shard_map/ppermute | solution.py:1003
  111.7 3.2 %all-gather.2.cloned.1.call-done.pair_ref = bf16[1024,4096]{1,0:T(8,128)(2,1)} async-done(((bf16[64,4096]{1,0:T(8,128)(2,1)}), bf16[1024,4096]{1,0:T(8,128)(2,1)}) %all-gather.2.cloned.1.call-update) | async-done | bytes 8388624 | tf_op jit(solution)/shard_map/all_gather | solution.py:1054
  114.9 20.1 %feed.1 = (bf16[768,1024]{1,0:T(8,128)(2,1)}, bf16[2,768,1024]{2,1,0:T(8,128)(2,1)}, bf16[2,768,2048]{2,1,0:T(8,128)(2,1)}, bf16[768,1024]{1,0:T(8,128)(2,1)}, f32[8,2048]{1,0:T(8,128)}) custom-call(s32[20]{0:T(128)} %concatenate.15.place_ref, bf16[768,1024]{1,0:T(8,128)(2,1)} %get-tuple-element.68.x_ref, ...), custom_call_target="tpu_custom_call", output_to_operand_aliasing={{1}: (6, {})} | custom-call | flops 14495514624 | bytes 31457280 | tf_op jit(solution)/shard_map/feed/pallas_call | solution.py:602
  136.5 12.4 %convolution_convert_fusion = bf16[2,1024,2048]{2,1,0:T(8,128)(2,1)} fusion(bf16[2,768,1024]{2,1,0:T(8,128)(2,1)} %get-tuple-element.83.grad_ref, bf16[2,768,2048]{2,1,0:T(8,128)(2,1)} %get-tuple-element.86), kind=kOutput, calls=%fused_computation | convolution fusion | flops 6446645248 | bytes 17825792 | tf_op jit(solution)/shard_map/dot_general | solution.py:1083
  148.9 6.6 %fusion.19.own_ref = bf16[768,1024]{1,0:T(8,128)(2,1)S(1)} fusion(bf16[1024,4096]{1,0:T(8,128)(2,1)} %all-gather.2.cloned.1.call-done.pair_ref, bf16[2,768,2048]{2,1,0:T(8,128)(2,1)} %get-tuple-element.86), kind=kOutput, calls=%fused_computation.18 | convolution fusion | flops 3222011904 | bytes 8912896 | tf_op jit(solution)/shard_map/dot_general | solution.py:43
  155.5 16.3 %collective-permute-done.18.other_ref = bf16[768,1024]{1,0:T(8,128)(2,1)S(1)} collective-permute-done((bf16[768,1024]{1,0:T(8,128)(2,1)}, bf16[768,1024]{1,0:T(8,128)(2,1)S(1)}, u32[]{:S(2)}, u32[]{:S(2)}) %collective-permute-start.18) | collective-permute-done | bytes 1572896 | tf_op jit(solution)/shard_map/ppermute | solution.py:1003
  173.0 7.0 %mid.1 = (bf16[768,1024]{1,0:T(8,128)(2,1)}, bf16[768,512]{1,0:T(8,128)(2,1)}, f32[8,1024]{1,0:T(8,128)}) custom-call(bf16[768,1024]{1,0:T(8,128)(2,1)} %get-tuple-element.105.resid_ref, bf16[768,1024]{1,0:T(8,128)(2,1)} %get-tuple-element.84.own_ref, bf16[768,1024]{1,0:T(8,128)(2,1)} %copy-done.23, bf16[2,768,1024]{2,1,0:T(8,128)(2,1)} %get-tuple-element.83.grad_ref, ...), custom_call_target="tpu_custom_call" | custom-call | flops 12884901888 | bytes 12582912 | tf_op jit(solution)/shard_map/mid/pallas_call | solution.py:663
  180.0 18.4 %back.1 = (bf16[768,1536]{1,0:T(8,128)(2,1)}, bf16[768,1024]{1,0:T(8,128)(2,1)}, f32[4,1,384]{2,1,0:T(1,128)}, f32[2,1024]{1,0:T(2,128)}) custom-call(bf16[768,1024]{1,0:T(8,128)(2,1)} %get-tuple-element.80.xhat_all_ref, bf16[768,1536]{1,0:T(8,128)(2,1)} %get-tuple-element.81.qkv_ref, bf16[768,512]{1,0:T(8,128)(2,1)} %get-tuple-element.89.grad_ref, ...), custom_call_target="tpu_custom_call" | custom-call | flops 115964116992 | bytes 9437184 | tf_op jit(solution)/shard_map/back/pallas_call | solution.py:794
  198.4 4.4 %convolution_convert_fusion.1 = bf16[512,1536]{1,0:T(8,128)(2,1)} fusion(bf16[768,1536]{1,0:T(8,128)(2,1)} %get-tuple-element.92, bf16[1024,768]{1,0:T(8,128)(2,1)S(1)} %copy-done.13), kind=kOutput, calls=%fused_computation.7 | convolution fusion | flops 1208745984 | bytes 4718592 | tf_op jit(solution)/shard_map/dot_general | solution.py:33
  208.5 1.9 fusion.10
  215.7 15.8 %collective-permute-done.24.other_ref = bf16[384,1024]{1,0:T(8,128)(2,1)S(1)} collective-permute-done((bf16[384,1024]{1,0:T(8,128)(2,1)S(1)}, bf16[384,1024]{1,0:T(8,128)(2,1)S(1)}, u32[]{:S(2)}, u32[]{:S(2)}) %collective-permute-start.24) | collective-permute-done | bytes 786464 | tf_op jit(solution)/shard_map/ppermute | solution.py:1003
  231.6 5.7 %collective-permute-done.23 = f32[4,768]{1,0:T(4,128)S(1)} collective-permute-done((f32[4,768]{1,0:T(4,128)S(1)}, f32[4,768]{1,0:T(4,128)S(1)}, u32[]{:S(2)}, u32[]{:S(2)}) %collective-permute-start.23) | collective-permute-done | bytes 12320 | tf_op jit(solution)/shard_map/ppermute | solution.py:960
  237.2 1.9 fusion.9.own_ref
  239.2 2.3 collective-permute-start.26
  243.2 2.8 collective-permute-start.27
  248.6 3.0 %last.1 = f32[384,1024]{1,0:T(8,128)} custom-call(s32[20]{0:T(128)S(1)} %copy-done.9, bf16[384,1024]{1,0:T(8,128)(2,1)S(1)} %copy-done.4, bf16[768,1024]{1,0:T(8,128)(2,1)S(1)} %copy-done.3, bf16[768,1024]{1,0:T(8,128)(2,1)S(1)} %copy-done, bf16[384,1024]{1,0:T(8,128)(2,1)S(1)} %collective-permute-done.24.other_ref, f32[8,1024]{1,0:T(8,128)S(1)} %copy-done.7), custom_call_target="tpu_custom_call" | custom-call | flops 15728640 | bytes 125829120 | tf_op jit(solution)/shard_map/last/pallas_call | solution.py:842
  252.6 2.0 collective-permute-start.29
  255.8 9.5 %collective-permute-done.31.three_ref = bf16[64,1536]{1,0:T(8,128)(2,1)S(1)} collective-permute-done((bf16[64,1536]{1,0:T(8,128)(2,1)S(1)}, bf16[64,1536]{1,0:T(8,128)(2,1)S(1)}, u32[]{:S(2)}, u32[]{:S(2)}) %collective-permute-start.31) | collective-permute-done | bytes 196640 | tf_op jit(solution)/shard_map/ppermute | solution.py:960
  265.3 8.3 %collective-permute-done.30.two_ref = bf16[64,1536]{1,0:T(8,128)(2,1)S(1)} collective-permute-done((bf16[64,1536]{1,0:T(8,128)(2,1)S(1)}, bf16[64,1536]{1,0:T(8,128)(2,1)S(1)}, u32[]{:S(2)}, u32[]{:S(2)}) %collective-permute-start.30) | collective-permute-done | bytes 196640 | tf_op jit(solution)/shard_map/ppermute | solution.py:960
  273.6 2.4 collective-permute-done.29.one_ref
  281.2 4.0 %collective-permute-done.34 = bf16[64,512]{1,0:T(8,128)(2,1)} collective-permute-done((bf16[64,512]{1,0:T(8,128)(2,1)}, bf16[64,512]{1,0:T(8,128)(2,1)}, u32[]{:S(2)}, u32[]{:S(2)}) %collective-permute-start.34) | collective-permute-done | bytes 65568 | tf_op jit(solution)/shard_map/ppermute | solution.py:960
  289.1 3.6 %result.1 = bf16[384,1024]{1,0:T(8,128)(2,1)} custom-call(s32[20]{0:T(128)S(1)} %copy-done.9, bf16[768,1024]{1,0:T(8,128)(2,1)S(1)} %copy-done.1, bf16[768,1024]{1,0:T(8,128)(2,1)S(1)} %fusion.19.own_ref, bf16[384,1024]{1,0:T(8,128)(2,1)} %collective-permute-done.25.other_ref, f32[8,1024]{1,0:T(8,128)S(1)} %copy-done.8), custom_call_target="tpu_custom_call" | custom-call | flops 3932160 | bytes 125829120 | tf_op jit(solution)/shard_map/result/pallas_call | solution.py:869
  292.7 2.1 fusion.32
  (187 shorter events, 47.0 us)
Async XLA Ops:
  7.2 107.7 %all-gather.2.cloned.1.call-start = ((), (), s32[]{:S(2)}) async-start(), calls=%async_computation.1 | async-start | bytes 8912896 | tf_op jit(solution)/shard_map/all_gather | solution.py:1054
  9.4 32.8 %collective-permute-start = (bf16[384,1024]{1,0:T(8,128)(2,1)}, bf16[384,1024]{1,0:T(8,128)(2,1)S(1)}, u32[]{:S(2)}, u32[]{:S(2)}) collective-permute-start(bf16[384,1024]{1,0:T(8,128)(2,1)} %x_ref.1), channel_id=1, source_target_pairs={{0,1},{1,0},{2,3},{3,2},{4,5},{5,4},{6,7},{7,6},{8,9},{9,8},{10,11... | collective-permute-start | bytes 2359304 | tf_op jit(solution)/shard_map/ppermute | solution.py:1003
  10.9 21.7 %collective-permute-start.3 = (bf16[64,2176]{1,0:T(8,128)(2,1)}, bf16[64,2176]{1,0:T(8,128)(2,1)S(1)}, u32[]{:S(2)}, u32[]{:S(2)}) collective-permute-start(bf16[64,2176]{1,0:T(8,128)(2,1)} %get-tuple-element.65.refs_0_.refs_16_.refs_32_), channel_id=1, source_target_pairs={{0,24},{2,26},{4,28},{6,30},{8,0},{10,2},{12,4},{14,6},{16,8},{18,... | collective-permute-start | bytes 835592 | tf_op jit(solution)/shard_map/ppermute | solution.py:960
  11.4 22.8 %collective-permute-start.1 = (bf16[64,2176]{1,0:T(8,128)(2,1)}, bf16[64,2176]{1,0:T(8,128)(2,1)S(1)}, u32[]{:S(2)}, u32[]{:S(2)}) collective-permute-start(bf16[64,2176]{1,0:T(8,128)(2,1)} %get-tuple-element.65.refs_0_.refs_16_.refs_32_), channel_id=1, source_target_pairs={{0,8},{2,10},{4,12},{6,14},{8,16},{10,18},{12,20},{14,22},{16,24},... | collective-permute-start | bytes 835592 | tf_op jit(solution)/shard_map/ppermute | solution.py:960
  12.9 21.7 %collective-permute-start.4 = (bf16[64,2176]{1,0:T(8,128)(2,1)}, bf16[64,2176]{1,0:T(8,128)(2,1)S(1)}, u32[]{:S(2)}, u32[]{:S(2)}) collective-permute-start(bf16[64,2176]{1,0:T(8,128)(2,1)} %get-tuple-element.65.refs_0_.refs_16_.refs_32_), channel_id=1, source_target_pairs={{0,4},{2,6},{4,0},{6,2},{8,12},{10,14},{12,8},{14,10},{16,20},{18,... | collective-permute-start | bytes 835592 | tf_op jit(solution)/shard_map/ppermute | solution.py:960
  14.5 22.1 %collective-permute-start.2 = (bf16[64,2176]{1,0:T(8,128)(2,1)}, bf16[64,2176]{1,0:T(8,128)(2,1)S(1)}, u32[]{:S(2)}, u32[]{:S(2)}) collective-permute-start(bf16[64,2176]{1,0:T(8,128)(2,1)} %get-tuple-element.65.refs_0_.refs_16_.refs_32_), channel_id=1, source_target_pairs={{0,16},{2,18},{4,20},{6,22},{8,24},{10,26},{12,28},{14,30},{16,0},... | collective-permute-start | bytes 835592 | tf_op jit(solution)/shard_map/ppermute | solution.py:960
  32.6 6.5 %collective-permute-start.6 = (bf16[64,2176]{1,0:T(8,128)(2,1)S(1)}, bf16[64,2176]{1,0:T(8,128)(2,1)S(1)}, u32[]{:S(2)}, u32[]{:S(2)}) collective-permute-start(bf16[64,2176]{1,0:T(8,128)(2,1)S(1)} %collective-permute-done.3.refs_3_.refs_19_.refs_35_), channel_id=1, source_target_pairs={{0,4},{2,6},{4,0},{6,2},{8,12},{10,14},{12,8},{14,10},{16,20},{18,... | collective-permute-start | bytes 835592 | tf_op jit(solution)/shard_map/ppermute | solution.py:960
  34.2 8.0 %collective-permute-start.5 = (bf16[64,2176]{1,0:T(8,128)(2,1)S(1)}, bf16[64,2176]{1,0:T(8,128)(2,1)S(1)}, u32[]{:S(2)}, u32[]{:S(2)}) collective-permute-start(bf16[64,2176]{1,0:T(8,128)(2,1)S(1)} %collective-permute-done.1.refs_1_.refs_17_.refs_33_), channel_id=1, source_target_pairs={{0,4},{2,6},{4,0},{6,2},{8,12},{10,14},{12,8},{14,10},{16,20},{18,... | collective-permute-start | bytes 835592 | tf_op jit(solution)/shard_map/ppermute | solution.py:960
  42.2 250.4 %reduce-scatter.2.cloned.1.call-start = ((), (), s32[]{:S(2)}) async-start(), calls=%async_computation.2 | async-start | bytes 8912896 | tf_op jit(solution)/shard_map/reduce_scatter | solution.py:1089
  43.6 10.5 %collective-permute-start.7 = (bf16[64,2176]{1,0:T(8,128)(2,1)S(1)}, bf16[64,2176]{1,0:T(8,128)(2,1)S(1)}, u32[]{:S(2)}, u32[]{:S(2)}) collective-permute-start(bf16[64,2176]{1,0:T(8,128)(2,1)S(1)} %collective-permute-done.2.refs_2_.refs_18_.refs_34_), channel_id=1, source_target_pairs={{0,4},{2,6},{4,0},{6,2},{8,12},{10,14},{12,8},{14,10},{16,20},{18,... | collective-permute-start | bytes 835592 | tf_op jit(solution)/shard_map/ppermute | solution.py:960
  45.1 9.0 %collective-permute-start.10 = (bf16[64,2176]{1,0:T(8,128)(2,1)S(1)}, bf16[64,2176]{1,0:T(8,128)(2,1)S(1)}, u32[]{:S(2)}, u32[]{:S(2)}) collective-permute-start(bf16[64,2176]{1,0:T(8,128)(2,1)S(1)} %collective-permute-done.2.refs_2_.refs_18_.refs_34_), channel_id=1, source_target_pairs={{0,2},{2,0},{4,6},{6,4},{8,10},{10,8},{12,14},{14,12},{16,18},{18,... | collective-permute-start | bytes 835592 | tf_op jit(solution)/shard_map/ppermute | solution.py:960
  45.2 9.0 %collective-permute-start.9 = (bf16[64,2176]{1,0:T(8,128)(2,1)S(1)}, bf16[64,2176]{1,0:T(8,128)(2,1)S(1)}, u32[]{:S(2)}, u32[]{:S(2)}) collective-permute-start(bf16[64,2176]{1,0:T(8,128)(2,1)S(1)} %collective-permute-done.1.refs_1_.refs_17_.refs_33_), channel_id=1, source_target_pairs={{0,2},{2,0},{4,6},{6,4},{8,10},{10,8},{12,14},{14,12},{16,18},{18,... | collective-permute-start | bytes 835592 | tf_op jit(solution)/shard_map/ppermute | solution.py:960
  45.6 8.6 %collective-permute-start.15 = (bf16[64,2176]{1,0:T(8,128)(2,1)S(1)}, bf16[64,2176]{1,0:T(8,128)(2,1)S(1)}, u32[]{:S(2)}, u32[]{:S(2)}) collective-permute-start(bf16[64,2176]{1,0:T(8,128)(2,1)S(1)} %collective-permute-done.6.refs_7_.refs_23_.refs_39_), channel_id=1, source_target_pairs={{0,2},{2,0},{4,6},{6,4},{8,10},{10,8},{12,14},{14,12},{16,18},{18,... | collective-permute-start | bytes 835592 | tf_op jit(solution)/shard_map/ppermute | solution.py:960
  45.8 8.5 %collective-permute-start.13 = (bf16[64,2176]{1,0:T(8,128)(2,1)S(1)}, bf16[64,2176]{1,0:T(8,128)(2,1)S(1)}, u32[]{:S(2)}, u32[]{:S(2)}) collective-permute-start(bf16[64,2176]{1,0:T(8,128)(2,1)S(1)} %collective-permute-done.5.refs_5_.refs_21_.refs_37_), channel_id=1, source_target_pairs={{0,2},{2,0},{4,6},{6,4},{8,10},{10,8},{12,14},{14,12},{16,18},{18,... | collective-permute-start | bytes 835592 | tf_op jit(solution)/shard_map/ppermute | solution.py:960
  54.1 20.8 %collective-permute-start.16 = (bf16[384,1024]{1,0:T(8,128)(2,1)}, bf16[384,1024]{1,0:T(8,128)(2,1)S(1)}, u32[]{:S(2)}, u32[]{:S(2)}) collective-permute-start(bf16[384,1024]{1,0:T(8,128)(2,1)} %param.16), channel_id=1, source_target_pairs={{0,1},{1,0},{2,3},{3,2},{4,5},{5,4},{6,7},{7,6},{8,9},{9,8},{10,11... | collective-permute-start | bytes 2359304 | tf_op jit(solution)/shard_map/ppermute | solution.py:1003
  74.9 36.7 %collective-permute-start.17 = (bf16[768,1024]{1,0:T(8,128)(2,1)}, bf16[768,1024]{1,0:T(8,128)(2,1)S(1)}, u32[]{:S(2)}, u32[]{:S(2)}) collective-permute-start(bf16[768,1024]{1,0:T(8,128)(2,1)} %get-tuple-element.71.own_ref), channel_id=1, source_target_pairs={{0,1},{1,0},{2,3},{3,2},{4,5},{5,4},{6,7},{7,6},{8,9},{9,8},{10,11... | collective-permute-start | bytes 4718600 | tf_op jit(solution)/shard_map/ppermute | solution.py:1003
  135.0 36.8 %collective-permute-start.18 = (bf16[768,1024]{1,0:T(8,128)(2,1)}, bf16[768,1024]{1,0:T(8,128)(2,1)S(1)}, u32[]{:S(2)}, u32[]{:S(2)}) collective-permute-start(bf16[768,1024]{1,0:T(8,128)(2,1)} %get-tuple-element.84.own_ref), channel_id=1, source_target_pairs={{0,1},{1,0},{2,3},{3,2},{4,5},{5,4},{6,7},{7,6},{8,9},{9,8},{10,11... | collective-permute-start | bytes 4718600 | tf_op jit(solution)/shard_map/ppermute | solution.py:1003
  202.8 5.3 %collective-permute-start.19 = (bf16[512,1536]{1,0:T(8,128)(2,1)}, bf16[512,1536]{1,0:T(8,128)(2,1)}, u32[]{:S(2)}, u32[]{:S(2)}) collective-permute-start(bf16[512,1536]{1,0:T(8,128)(2,1)} %convolution_convert_fusion.1), channel_id=1, source_target_pairs={{0,2},{2,0},{4,6},{6,4},{8,10},{10,8},{12,14},{14,12},{16,18},{18,... | collective-permute-start | bytes 4718600 | tf_op jit(solution)/shard_map/ppermute | solution.py:960
  204.8 5.6 %collective-permute-start.20 = (f32[16,768]{1,0:T(8,128)S(1)}, f32[16,768]{1,0:T(8,128)S(1)}, u32[]{:S(2)}, u32[]{:S(2)}) collective-permute-start(f32[16,768]{1,0:T(8,128)S(1)} %fusion.36), channel_id=1, source_target_pairs={{0,1},{1,0},{2,3},{3,2},{4,5},{5,4},{6,7},{7,6},{8,9},{9,8},{10,11... | collective-permute-start | bytes 147464 | tf_op jit(solution)/shard_map/ppermute | solution.py:1003
  211.9 19.7 %collective-permute-start.24 = (bf16[384,1024]{1,0:T(8,128)(2,1)S(1)}, bf16[384,1024]{1,0:T(8,128)(2,1)S(1)}, u32[]{:S(2)}, u32[]{:S(2)}) collective-permute-start(bf16[384,1024]{1,0:T(8,128)(2,1)S(1)} %constant_dynamic-slice_fusion.1), channel_id=1, source_target_pairs={{0,1},{1,0},{2,3},{3,2},{4,5},{5,4},{6,7},{7,6},{8,9},{9,8},{10,11... | collective-permute-start | bytes 2359304 | tf_op jit(solution)/shard_map/ppermute | solution.py:1003
  212.6 24.6 %collective-permute-start.22 = (bf16[256,1536]{1,0:T(8,128)(2,1)S(1)}, bf16[256,1536]{1,0:T(8,128)(2,1)S(1)}, u32[]{:S(2)}, u32[]{:S(2)}) collective-permute-start(bf16[256,1536]{1,0:T(8,128)(2,1)S(1)} %fusion.10), channel_id=1, source_target_pairs={{0,4},{2,6},{4,0},{6,2},{8,12},{10,14},{12,8},{14,10},{16,20},{18,... | collective-permute-start | bytes 2359304 | tf_op jit(solution)/shard_map/ppermute | solution.py:960
  213.2 24.0 %collective-permute-start.23 = (f32[4,768]{1,0:T(4,128)S(1)}, f32[4,768]{1,0:T(4,128)S(1)}, u32[]{:S(2)}, u32[]{:S(2)}) collective-permute-start(f32[4,768]{1,0:T(4,128)S(1)} %slice.158), channel_id=1, source_target_pairs={{0,4},{2,6},{4,0},{6,2},{8,12},{10,14},{12,8},{14,10},{16,20},{18,... | collective-permute-start | bytes 36872 | tf_op jit(solution)/shard_map/ppermute | solution.py:960
  215.1 40.7 %collective-permute-start.33 = (bf16[256,512]{1,0:T(8,128)(2,1)S(1)}, bf16[256,512]{1,0:T(8,128)(2,1)S(1)}, u32[]{:S(2)}, u32[]{:S(2)}) collective-permute-start(bf16[256,512]{1,0:T(8,128)(2,1)S(1)} %fusion.25), channel_id=1, source_target_pairs={{0,4},{2,6},{4,0},{6,2},{8,12},{10,14},{12,8},{14,10},{16,20},{18,... | collective-permute-start | bytes 786440 | tf_op jit(solution)/shard_map/ppermute | solution.py:960
  239.2 12.5 %collective-permute-start.26 = (f32[1,768]{1,0:T(1,128)S(1)}, f32[1,768]{1,0:T(1,128)S(1)}, u32[]{:S(2)}, u32[]{:S(2)}) collective-permute-start(f32[1,768]{1,0:T(1,128)S(1)} %get-tuple-element.126), channel_id=1, source_target_pairs={{0,24},{2,26},{4,28},{6,30},{8,0},{10,2},{12,4},{14,6},{16,8},{18,... | collective-permute-start | bytes 9224 | tf_op jit(solution)/shard_map/ppermute | solution.py:960
  241.5 11.1 %collective-permute-start.28 = (f32[1,768]{1,0:T(1,128)S(1)}, f32[1,768]{1,0:T(1,128)S(1)}, u32[]{:S(2)}, u32[]{:S(2)}) collective-permute-start(f32[1,768]{1,0:T(1,128)S(1)} %get-tuple-element.127), channel_id=1, source_target_pairs={{0,16},{2,18},{4,20},{6,22},{8,24},{10,26},{12,28},{14,30},{16,0},... | collective-permute-start | bytes 9224 | tf_op jit(solution)/shard_map/ppermute | solution.py:960
  243.2 9.4 %collective-permute-start.27 = (f32[1,768]{1,0:T(1,128)S(1)}, f32[1,768]{1,0:T(1,128)S(1)}, u32[]{:S(2)}, u32[]{:S(2)}) collective-permute-start(f32[1,768]{1,0:T(1,128)S(1)} %get-tuple-element.128), channel_id=1, source_target_pairs={{0,8},{2,10},{4,12},{6,14},{8,16},{10,18},{12,20},{14,22},{16,24},... | collective-permute-start | bytes 9224 | tf_op jit(solution)/shard_map/ppermute | solution.py:960
  247.1 39.8 %collective-permute-start.25 = (bf16[384,1024]{1,0:T(8,128)(2,1)}, bf16[384,1024]{1,0:T(8,128)(2,1)}, u32[]{:S(2)}, u32[]{:S(2)}) collective-permute-start(bf16[384,1024]{1,0:T(8,128)(2,1)} %constant_dynamic-slice_fusion), channel_id=1, source_target_pairs={{0,1},{1,0},{2,3},{3,2},{4,5},{5,4},{6,7},{7,6},{8,9},{9,8},{10,11... | collective-permute-start | bytes 2359304 | tf_op jit(solution)/shard_map/ppermute | solution.py:1003
  251.7 13.6 %collective-permute-start.31 = (bf16[64,1536]{1,0:T(8,128)(2,1)S(1)}, bf16[64,1536]{1,0:T(8,128)(2,1)S(1)}, u32[]{:S(2)}, u32[]{:S(2)}) collective-permute-start(bf16[64,1536]{1,0:T(8,128)(2,1)S(1)} %get-tuple-element.118), channel_id=1, source_target_pairs={{0,16},{2,18},{4,20},{6,22},{8,24},{10,26},{12,28},{14,30},{16,0},... | collective-permute-start | bytes 589832 | tf_op jit(solution)/shard_map/ppermute | solution.py:960
  252.6 21.0 %collective-permute-start.30 = (bf16[64,1536]{1,0:T(8,128)(2,1)S(1)}, bf16[64,1536]{1,0:T(8,128)(2,1)S(1)}, u32[]{:S(2)}, u32[]{:S(2)}) collective-permute-start(bf16[64,1536]{1,0:T(8,128)(2,1)S(1)} %get-tuple-element.119), channel_id=1, source_target_pairs={{0,8},{2,10},{4,12},{6,14},{8,16},{10,18},{12,20},{14,22},{16,24},... | collective-permute-start | bytes 589832 | tf_op jit(solution)/shard_map/ppermute | solution.py:960
  252.6 23.4 %collective-permute-start.29 = (bf16[64,1536]{1,0:T(8,128)(2,1)S(1)}, bf16[64,1536]{1,0:T(8,128)(2,1)S(1)}, u32[]{:S(2)}, u32[]{:S(2)}) collective-permute-start(bf16[64,1536]{1,0:T(8,128)(2,1)S(1)} %get-tuple-element.120), channel_id=1, source_target_pairs={{0,24},{2,26},{4,28},{6,30},{8,0},{10,2},{12,4},{14,6},{16,8},{18,... | collective-permute-start | bytes 589832 | tf_op jit(solution)/shard_map/ppermute | solution.py:960
  278.5 6.7 %collective-permute-start.34 = (bf16[64,512]{1,0:T(8,128)(2,1)}, bf16[64,512]{1,0:T(8,128)(2,1)}, u32[]{:S(2)}, u32[]{:S(2)}) collective-permute-start(bf16[64,512]{1,0:T(8,128)(2,1)} %get-tuple-element.123), channel_id=1, source_target_pairs={{0,24},{2,26},{4,28},{6,30},{8,0},{10,2},{12,4},{14,6},{16,8},{18,... | collective-permute-start | bytes 196616 | tf_op jit(solution)/shard_map/ppermute | solution.py:960
  278.5 6.7 %collective-permute-start.36 = (bf16[64,512]{1,0:T(8,128)(2,1)}, bf16[64,512]{1,0:T(8,128)(2,1)}, u32[]{:S(2)}, u32[]{:S(2)}) collective-permute-start(bf16[64,512]{1,0:T(8,128)(2,1)} %get-tuple-element.124), channel_id=1, source_target_pairs={{0,16},{2,18},{4,20},{6,22},{8,24},{10,26},{12,28},{14,30},{16,0},... | collective-permute-start | bytes 196616 | tf_op jit(solution)/shard_map/ppermute | solution.py:960
  (47 other events, 290.9 us)
Sparse Core Ops, SparseCore 0:
  42.3 72.4 all-gather.1
  149.0 117.3 reduce-scatter.1
